TPU v7x, 32 devices: a whole 2x2x4 slice. The times are simulated.
32 devices in a mesh: dp: 16 (over z, y, x), seq: 2 (over core).
Axes of the slice: x: 2, y: 2, z: 4, core: 2. Of those that a mesh axis runs over, the one named last changes fastest.
Arguments:
- tokens: bfloat16 [64, 512, 768], P('dp', 'seq'), may hold values from -6 to 6
- lengths: int32 [64, 6], P('dp'), may hold values from 1 to 192, 512 in all within a row
- w_qkv: bfloat16 [768, 2304], replicated, may hold values from -0.21875 to 0.21875
- w_out: bfloat16 [768, 768], replicated, may hold values from -1.75 to 1.75
- w_in: bfloat16 [768, 3072], replicated, may hold values from -0.21875 to 0.21875
- w_back: bfloat16 [3072, 768], replicated, may hold values from -0.109375 to 0.109375
- bias_q: float32 [768], replicated, may hold values from -3 to 3
- value_bias_vector: float32 [768], replicated, may hold values from -3 to 3
- bias_out: float32 [768], replicated, may hold values from -3 to 3
- gain1: float32 [768], replicated, may hold values from 0.25 to 1.75
- shift1: float32 [768], replicated, may hold values from -3 to 3
- bias_in: float32 [3072], replicated, may hold values from -3 to 3
- bias_back: float32 [768], replicated, may hold values from -3 to 3
- gain2: float32 [768], replicated, may hold values from 0.25 to 1.75
- shift2: float32 [768], replicated, may hold values from -3 to 3
- cotangent: bfloat16 [64, 512, 768], P('dp', 'seq'), may hold values from -6 to 6
Outputs:
- layer_output: bfloat16 [64, 512, 768], P('dp', 'seq')
- cls_vectors: bfloat16 [64, 6, 768], P('dp')
- input_grad: bfloat16 [64, 512, 768], P('dp', 'seq')
- grad_qkv: float32 [1769472], P(('dp', 'seq'))
- grad_out: float32 [589824], P(('dp', 'seq'))
- grad_in: float32 [2359296], P(('dp', 'seq'))
- grad_back: float32 [2359296], P(('dp', 'seq'))
- vector_grads: float32 [9216], P(('dp', 'seq'))
Inputs may be any that keep to these rules, and one draw needn't show every extreme that they name: Each row's 6 lengths sum to 512, and the longest in every row is exactly 192; a passage's first position holds its CLS token.
All inputs are finite; a program needn't handle non-finite values.
Results may differ from a plain program's by a relative error of at most 0.015.
Values may be sent and summed in bfloat16 or wider, within the bound.
No kernel may reach another device: no remote copies, remote signals or barrier semaphores. Data moves between devices by JAX's collectives and lax.ppermute only.
A program may use at most 192 MiB of HBM per device.

v0:
```python
from functools import partial

import jax
import jax.numpy as jnp
from jax import lax
from jax.sharding import PartitionSpec as P

HEADS = 12
MB = 2


EPS = 1e-12


def normalize(hidden):
    center = hidden - jnp.mean(hidden, axis=-1, keepdims=True)
    feature_variance = jnp.mean(center * center, axis=-1, keepdims=True)
    inverse = lax.rsqrt(feature_variance + EPS)
    return (center * inverse, inverse)


def norm_backward(grad_hat, normed, inverse):
    first = jnp.mean(grad_hat, axis=-1, keepdims=True)
    second = jnp.mean(grad_hat * normed, axis=-1, keepdims=True)
    return inverse * (grad_hat - first - normed * second)


def segment_table(row_lengths, positions):
    starts = jnp.cumsum(row_lengths, axis=1) - row_lengths
    return jnp.sum((positions[None, :, None] >= starts[:, None, :]).astype(jnp.int32), axis=-1) - 1


def column_sum(values):
    return jnp.sum(values.astype(jnp.float32), axis=0)


def on_device(
    tokens,
    lengths,
    w_qkv,
    w_out,
    w_in,
    w_back,
    bias_q,
    value_bias_vector,
    bias_out,
    gain1,
    shift1,
    bias_in,
    bias_back,
    gain2,
    shift2,
    cotangent,
):
    rows_local, local_length, model_width = tokens.shape
    pair_size = lax.axis_size("seq")
    full_length = local_length * pair_size
    head_count = HEADS
    head_size = model_width // head_count
    micro_count = MB
    batch_rows = rows_local // micro_count
    score_scale = head_size ** (-0.5)
    offset = lax.axis_index("seq") * local_length
    query_positions = offset + jnp.arange(local_length, dtype=jnp.int32)
    key_position_list = jnp.arange(full_length, dtype=jnp.int32)
    outputs_list = []
    cls_list = []
    grad_list = []
    totals = None
    for step_index in range(micro_count):
        lower = step_index * batch_rows
        micro_tokens = tokens[lower : lower + batch_rows]
        microbatch_cotangent = cotangent[lower : lower + batch_rows]
        row_lengths = lengths[lower : lower + batch_rows]
        work_tokens, work_cot, work_lengths, work_positions = (
            micro_tokens,
            microbatch_cotangent,
            row_lengths,
            query_positions,
        )
        work_rows = work_tokens.shape[0]
        work_length = work_tokens.shape[1]
        flat_rows = work_tokens.reshape(-1, model_width)
        query_segment = segment_table(work_lengths, work_positions)
        key_segment = segment_table(work_lengths, key_position_list)
        same_segment = (query_segment[:, :, None] == key_segment[:, None, :])[:, None]
        projected = jnp.dot(flat_rows, w_qkv, preferred_element_type=jnp.float32)
        queries = (projected[:, :model_width] + bias_q).astype(jnp.bfloat16)
        keys_local = projected[:, model_width : 2 * model_width].astype(jnp.bfloat16)
        values_local = (projected[:, 2 * model_width :] + value_bias_vector).astype(jnp.bfloat16)
        keys_rows = keys_local.reshape(work_rows, work_length, model_width)
        values_rows = values_local.reshape(work_rows, work_length, model_width)
        all_keys, all_values = (
            lax.all_gather(keys_rows, "seq", axis=1, tiled=True),
            lax.all_gather(values_rows, "seq", axis=1, tiled=True),
        )
        query_heads = queries.reshape(work_rows, work_length, head_count, head_size)
        key_heads = all_keys.reshape(work_rows, full_length, head_count, head_size)
        value_head_split = all_values.reshape(work_rows, full_length, head_count, head_size)
        scores = (
            jnp.einsum(
                "bqhd,bkhd->bhqk", query_heads, key_heads, preferred_element_type=jnp.float32
            )
            * score_scale
        )
        masked = jnp.where(same_segment, scores, -1e30)
        top_score = jnp.max(masked, axis=-1, keepdims=True)
        raw_weight = jnp.where(same_segment, jnp.exp(masked - top_score), 0.0)
        row_total = jnp.sum(raw_weight, axis=-1, keepdims=True)
        log_total = top_score + jnp.log(row_total)
        weights_low = (raw_weight / row_total).astype(jnp.bfloat16)
        mixed = jnp.einsum(
            "bhqk,bkhd->bqhd", weights_low, value_head_split, preferred_element_type=jnp.float32
        )
        mixed = mixed.reshape(-1, model_width).astype(jnp.bfloat16)
        pre_first = (
            flat_rows.astype(jnp.float32)
            + jnp.dot(mixed, w_out, preferred_element_type=jnp.float32)
            + bias_out
        )
        hat_first, inverse_first = normalize(pre_first)
        normed_first = hat_first * gain1 + shift1
        normed_low = normed_first.astype(jnp.bfloat16)
        inner_pre = jnp.dot(normed_low, w_in, preferred_element_type=jnp.float32) + bias_in
        activation, gelu_backward = jax.vjp(partial(jax.nn.gelu, approximate=False), inner_pre)
        activation_low = activation.astype(jnp.bfloat16)
        pre_second = (
            normed_first
            + jnp.dot(activation_low, w_back, preferred_element_type=jnp.float32)
            + bias_back
        )
        hat_second, inverse_second = normalize(pre_second)
        output_low = (hat_second * gain2 + shift2).astype(jnp.bfloat16)
        output_row_block = output_low.reshape(work_rows, work_length, model_width)
        starts = jnp.cumsum(work_lengths, axis=1) - work_lengths
        classifier_token_select = (starts[:, :, None] == work_positions[None, None, :]).astype(
            jnp.bfloat16
        )
        picked = jnp.einsum(
            "jwz,jzo->jwo",
            classifier_token_select,
            output_row_block,
            preferred_element_type=jnp.float32,
        )
        cls_list.append(lax.psum(picked.astype(jnp.bfloat16), "seq"))
        grad_output = work_cot.reshape(-1, model_width).astype(jnp.float32)
        grad_gain2 = jnp.sum(grad_output * hat_second, axis=0)
        grad_shift2 = jnp.sum(grad_output, axis=0)
        gradient_second_preactivation = norm_backward(
            grad_output * gain2, hat_second, inverse_second
        )
        grad_feed = gradient_second_preactivation.astype(jnp.bfloat16)
        grad_bias_back = column_sum(grad_feed)
        grad_w_back = jnp.einsum(
            "tf,td->fd", activation_low, grad_feed, preferred_element_type=jnp.float32
        )
        grad_activation = jnp.einsum(
            "td,fd->tf", grad_feed, w_back, preferred_element_type=jnp.float32
        )
        grad_inner = gelu_backward(grad_activation)[0].astype(jnp.bfloat16)
        grad_bias_in = column_sum(grad_inner)
        grad_w_in = jnp.einsum(
            "td,tf->df", normed_low, grad_inner, preferred_element_type=jnp.float32
        )
        grad_normed1 = gradient_second_preactivation + jnp.einsum(
            "tf,df->td", grad_inner, w_in, preferred_element_type=jnp.float32
        )
        grad_gain1 = jnp.sum(grad_normed1 * hat_first, axis=0)
        grad_shift1 = jnp.sum(grad_normed1, axis=0)
        grad_pre1 = norm_backward(grad_normed1 * gain1, hat_first, inverse_first)
        grad_branch = grad_pre1.astype(jnp.bfloat16)
        grad_bias_out = column_sum(grad_branch)
        grad_w_out = jnp.einsum("tc,td->cd", mixed, grad_branch, preferred_element_type=jnp.float32)
        grad_mixed = jnp.einsum(
            "td,cd->tc", grad_branch, w_out, preferred_element_type=jnp.float32
        ).astype(jnp.bfloat16)
        grad_mixed_heads = grad_mixed.reshape(work_rows, work_length, head_count, head_size)
        scores_again = (
            jnp.einsum(
                "bqhd,bkhd->bhqk", query_heads, key_heads, preferred_element_type=jnp.float32
            )
            * score_scale
        )
        probs = jnp.where(
            same_segment, jnp.exp(jnp.where(same_segment, scores_again, 0.0) - log_total), 0.0
        )
        grad_probs = jnp.einsum(
            "bqhd,bkhd->bhqk",
            grad_mixed_heads,
            value_head_split,
            preferred_element_type=jnp.float32,
        )
        row_delta = jnp.sum(probs * grad_probs, axis=-1, keepdims=True)
        grad_scores = (probs * (grad_probs - row_delta)).astype(jnp.bfloat16)
        grad_query = (
            jnp.einsum(
                "bhqk,bkhd->bqhd", grad_scores, key_heads, preferred_element_type=jnp.float32
            )
            * score_scale
        )
        grad_query = grad_query.reshape(-1, model_width).astype(jnp.bfloat16)
        key_term = (
            jnp.einsum(
                "bhqk,bqhd->bkhd", grad_scores, query_heads, preferred_element_type=jnp.float32
            )
            * score_scale
        )
        value_term = jnp.einsum(
            "bhqk,bqhd->bkhd",
            probs.astype(jnp.bfloat16),
            grad_mixed_heads,
            preferred_element_type=jnp.float32,
        )
        key_term = key_term.reshape(work_rows, full_length, model_width)
        value_term = value_term.reshape(work_rows, full_length, model_width)
        key_sum, value_sum = (
            lax.psum_scatter(
                key_term.astype(jnp.bfloat16), "seq", scatter_dimension=1, tiled=True
            ).astype(jnp.float32),
            lax.psum_scatter(
                value_term.astype(jnp.bfloat16), "seq", scatter_dimension=1, tiled=True
            ).astype(jnp.float32),
        )
        grad_key = key_sum.reshape(-1, model_width).astype(jnp.bfloat16)
        grad_value = value_sum.reshape(-1, model_width).astype(jnp.bfloat16)
        grad_projected = jnp.concatenate([grad_query, grad_key, grad_value], axis=1)
        grad_bias_q = column_sum(grad_query)
        grad_bias_v = column_sum(grad_value)
        grad_w_qkv = jnp.einsum(
            "td,te->de", flat_rows, grad_projected, preferred_element_type=jnp.float32
        )
        grad_input = grad_pre1 + jnp.einsum(
            "te,de->td", grad_projected, w_qkv, preferred_element_type=jnp.float32
        )
        grad_rows = grad_input.astype(jnp.bfloat16).reshape(work_rows, work_length, model_width)
        outputs_list.append(output_row_block)
        grad_list.append(grad_rows)
        vector_terms = jnp.concatenate(
            [
                grad_bias_q,
                grad_bias_v,
                grad_bias_out,
                grad_gain1,
                grad_shift1,
                grad_bias_in,
                grad_bias_back,
                grad_gain2,
                grad_shift2,
            ],
            axis=0,
        )
        micro_grads = [
            grad_w_qkv.reshape(-1),
            grad_w_out.reshape(-1),
            grad_w_in.reshape(-1),
            grad_w_back.reshape(-1),
            vector_terms,
        ]
        if totals is None:
            totals = micro_grads
        else:
            totals = [earlier + later for earlier, later in zip(totals, micro_grads)]
    totals = list(
        (
            lax.psum_scatter(totals[0], ("dp", "seq"), scatter_dimension=0, tiled=True),
            lax.psum_scatter(totals[1], ("dp", "seq"), scatter_dimension=0, tiled=True),
            lax.psum_scatter(totals[2], ("dp", "seq"), scatter_dimension=0, tiled=True),
            lax.psum_scatter(totals[3], ("dp", "seq"), scatter_dimension=0, tiled=True),
            lax.psum_scatter(totals[4], ("dp", "seq"), scatter_dimension=0, tiled=True),
        )
    )
    layer_output = jnp.concatenate(outputs_list, axis=0)
    cls_vectors = jnp.concatenate(cls_list, axis=0)
    input_grad = jnp.concatenate(grad_list, axis=0)
    return (
        layer_output,
        cls_vectors,
        input_grad,
        totals[0],
        totals[1],
        totals[2],
        totals[3],
        totals[4],
    )


def solution(mesh):
    in_specs = (
        P("dp", "seq", None),
        P("dp", None),
        P(),
        P(),
        P(),
        P(),
        P(),
        P(),
        P(),
        P(),
        P(),
        P(),
        P(),
        P(),
        P(),
        P("dp", "seq", None),
    )
    out_specs = (
        P("dp", "seq", None),
        P("dp", None, None),
        P("dp", "seq", None),
        P(("dp", "seq")),
        P(("dp", "seq")),
        P(("dp", "seq")),
        P(("dp", "seq")),
        P(("dp", "seq")),
    )
    return jax.shard_map(
        on_device, mesh=mesh, in_specs=in_specs, out_specs=out_specs, check_vma=False
    )
```

profile of v0, /device:TPU:0, one launch (start us, length us, event | category | flops | bytes accessed | tf_op | source)
XLA Modules:
  0.0 821.8 jit_solution(5690308346378670319)
XLA Ops:
  63.0 7.8 fusion.48
  87.3 5.2 fusion.1
  95.1 7.7 fusion.49
  108.1 34.6 %multiply_convert_fusion.3 = (bf16[512,3072]{1,0:T(8,128)(2,1)S(1)}, f32[512,3072]{1,0:T(8,128)}, bf16[512,3072]{1,0:T(8,128)(2,1)S(1)}, f32[512,3072]{1,0:T(8,128)}, f32[512,3072]{1,0:T(8,128)}) fusion(f32[3072]{0:T(1024)S(1)} %copy-done.74, f32[512,3072]{1,0:T(8,128)S(1)} %fusion.104, bf16[768,3072]{1,0:T(8,128)(2,1)S(1)} %bitcast.205, ...), kind=kOutput, calls=%fused_computation.41 | convolution fusion | flops 2625503232 | bytes 37771264 | tf_op jit(solution)/shard_map/dot_general | solution.py:124
  153.9 10.5 %convert_reduce_fusion.1 = (f32[3072]{0:T(1024)}, bf16[512,3072]{1,0:T(8,128)(2,1)}) fusion(f32[512,3072]{1,0:T(8,128)} %get-tuple-element.77, bf16[3072,768]{1,0:T(8,128)(2,1)S(1)} %bitcast.203, f32[512,768]{1,0:T(8,128)S(1)} %get-tuple-element.88, f32[512,3072]{1,0:T(8,128)} %get-tuple-element.111, f32[3072]{0:T(1024)S(1)} %copy-done.74), kind=kOutput, calls=%fused_computation.21 | convolution fusion | flops 2443047936 | bytes 22044672 | tf_op jit(solution)/shard_map/td,fd->tf/dot_general | solution.py:157
  164.4 8.0 multiply_reduce_fusion.3
  172.4 8.4 %convert_reduce_fusion = (f32[3072]{0:T(1024)}, bf16[512,3072]{1,0:T(8,128)(2,1)S(1)}) fusion(f32[512,3072]{1,0:T(8,128)} %get-tuple-element.92, bf16[3072,768]{1,0:T(8,128)(2,1)S(1)} %bitcast.203, f32[512,768]{1,0:T(8,128)S(1)} %get-tuple-element.69, f32[512,3072]{1,0:T(8,128)} %copy-done.77, f32[3072]{0:T(1024)S(1)} %copy-done.74), kind=kOutput, calls=%fused_computation.20 | convolution fusion | flops 2443047936 | bytes 22044672 | tf_op jit(solution)/shard_map/td,fd->tf/dot_general | solution.py:157
  180.8 9.2 %convert_reduce_fusion.9 = (f32[768]{0:T(1024)}, f32[512,768]{1,0:T(8,128)S(1)}, f32[768]{0:T(1024)}, f32[512]{0:T(512)}, f32[512]{0:T(512)}, /*index=5*/f32[768]{0:T(1024)}, f32[512,768]{1,0:T(8,128)}) fusion(f32[512]{0:T(512)S(1)} %broadcast_multiply_fusion.3, f32[512,768]{1,0:T(8,128)S(1)} %copy-done.44, f32[512]{0:T(512)S(1)} %copy-done.62, ...), kind=kOutput, calls=%fused_computation.107 | convolution fusion | flops 2423780096 | bytes 17330176 | tf_op jit(solution)/shard_map/tf,df->td/dot_general | solution.py:165
  198.1 8.5 %multiply_reduce_fusion.1 = (f32[2,12,256]{2,1,0:T(8,128)S(1)}, f32[2,12,256,512]{3,2,1,0:T(8,128)S(1)}) fusion(f32[2,12,256]{2,1,0:T(8,128)} %log_add_fusion.1, f32[2,12,256,512]{3,2,1,0:T(8,128)} %copy-done.2, pred[2,256,512]{2,1,0:T(8,128)(4,1)} %broadcast_compare_fusion.1, bf16[2,512,12,64]{1,3,2,0:T(8,128)(2,1)} %bitcast.188, ...), kind=kOutput, calls=%fused_computation.4 | convolution fusion | flops 421521408 | bytes 27836416 | tf_op jit(solution)/shard_map/bqhd,bkhd->bhqk/dot_general | solution.py:187
  206.6 7.0 multiply_convert_fusion.1
  234.5 8.0 fusion.20
  246.7 8.5 %multiply_reduce_fusion = (f32[2,12,256]{2,1,0:T(8,128)S(1)}, f32[2,12,256,512]{3,2,1,0:T(8,128)S(1)}) fusion(f32[2,12,256]{2,1,0:T(8,128)} %log_add_fusion, f32[2,12,256,512]{3,2,1,0:T(8,128)} %copy-done.1, pred[2,256,512]{2,1,0:T(8,128)(4,1)} %broadcast_compare_fusion, bf16[2,512,12,64]{1,3,2,0:T(8,128)(2,1)} %bitcast.186, ...), kind=kOutput, calls=%fused_computation.1 | convolution fusion | flops 421521408 | bytes 27836416 | tf_op jit(solution)/shard_map/bqhd,bkhd->bhqk/dot_general | solution.py:187
  255.2 7.2 multiply_convert_fusion
  270.1 8.0 fusion.23
  280.8 5.3 fusion.87
  286.1 5.3 convolution_add_fusion
  291.4 10.8 %add.301 = f32[2359296]{0:T(1024)} reshape(f32[3072,768]{1,0:T(8,128)} %convolution_add_fusion) | data formatting | bytes 18874368 | tf_op jit(solution)/shard_map/add | solution.py:262
  302.5 5.5 fusion.106
  311.2 5.9 copy.137
  324.3 5.5 convert_reduce_fusion.11
  356.8 8.0 copy.129
  364.8 7.9 add.295
  410.1 43.8 %all-reduce.4 = f32[9216]{0:T(1024)} all-reduce(f32[9216]{0:T(1024)} %add.302), channel_id=10, replica_groups=mesh['dp'=16,'seq'=2] {'dp','seq'}, use_global_device_ids=true, to_apply=%region_56.57.clone | all-reduce | flops 9216 | bytes 73728
  463.7 344.7 %all-reduce.9.cloned.1.call-done = (f32[1769472]{0:T(1024)}, f32[589824]{0:T(1024)}, f32[2359296]{0:T(1024)}, f32[2359296]{0:T(1024)}) async-done(((f32[1769472]{0:T(1024)}, f32[589824]{0:T(1024)}, f32[2359296]{0:T(1024)}, f32[2359296]{0:T(1024)}), (f32[1769472]{0:T(1024)}, f32[589824]{0:T(1024)}, f32[2359296]{0:T(1024)}, f32[2359296]{0:T(1024)})) %all-reduce.9.cloned.1.call-update) | async-done | bytes 28311568
  (326 shorter events, 225.4 us)
Async XLA Ops:
  7.2 40.1 %all-gather.7.cloned.1.call-start = ((), (), s32[]{:S(2)}) async-start(), calls=%async_computation.5 | async-start | bytes 2359296 | tf_op jit(solution)/shard_map/all_gather | solution.py:94
  14.9 45.5 %all-gather.5.cloned.1.call-start = ((), (), s32[]{:S(2)}) async-start(), calls=%async_computation.4 | async-start | bytes 2359296 | tf_op jit(solution)/shard_map/all_gather | solution.py:95
  21.5 19.4 %copy-start.56 = (f32[768]{0:T(1024)S(1)}, f32[768]{0:T(1024)}, u32[]{:S(2)}) copy-start(f32[768]{0:T(1024)} %param.29) | copy-start | bytes 9220
  21.5 54.2 %all-gather.11.cloned.1.call-start = ((), (), s32[]{:S(2)}) async-start(), calls=%async_computation.7 | async-start | bytes 2359296 | tf_op jit(solution)/shard_map/all_gather | solution.py:94
  24.0 68.5 %all-gather.9.cloned.1.call-start = ((), (), s32[]{:S(2)}) async-start(), calls=%async_computation.6 | async-start | bytes 2359296 | tf_op jit(solution)/shard_map/all_gather | solution.py:95
  24.6 313.9 %reduce-scatter.5.cloned.1.call-start = ((), (), s32[]{:S(2)}) async-start(), calls=%async_computation.8 | async-start | bytes 2359296 | tf_op jit(solution)/shard_map/reduce_scatter | solution.py:217
  63.0 9.7 %copy-start.48 = (bf16[2,256,768]{2,1,0:T(8,128)(2,1)S(1)}, bf16[2,256,768]{2,1,0:T(8,128)(2,1)}, u32[]{:S(2)}) copy-start(bf16[2,256,768]{2,1,0:T(8,128)(2,1)} %copy-done.47) | copy-start | bytes 2359300
  63.0 9.7 %copy-start.71 = (bf16[768,768]{1,0:T(8,128)(2,1)S(1)}, bf16[768,768]{1,0:T(8,128)(2,1)}, u32[]{:S(2)}) copy-start(bf16[768,768]{1,0:T(8,128)(2,1)} %param.19) | copy-start | bytes 3538948
  63.0 9.7 %copy-start.75 = (f32[768]{0:T(1024)S(1)}, f32[768]{0:T(1024)}, u32[]{:S(2)}) copy-start(f32[768]{0:T(1024)} %param.24) | copy-start | bytes 9220
  95.1 10.1 %slice-start.2 = ((s8[4718592]{0:T(1024)(128)(4,1)}), s8[4194304]{0:T(1024)(128)(4,1)S(1)}, s32[]{:S(2)}) async-start(s8[4718592]{0:T(1024)(128)(4,1)} %bitcast.204), calls=%async_computation.15 | async-start | bytes 8388608
  95.1 10.1 %slice-start.3 = ((s8[4718592]{0:T(1024)(128)(4,1)}), s8[524288]{0:T(1024)(128)(4,1)S(1)}, s32[]{:S(2)}) async-start(s8[4718592]{0:T(1024)(128)(4,1)} %bitcast.204), calls=%async_computation.16 | async-start | bytes 1048576
  104.8 76.0 %copy-start.5 = (f32[512,768]{1,0:T(8,128)}, f32[512,768]{1,0:T(8,128)S(1)}, u32[]{:S(2)}) copy-start(f32[512,768]{1,0:T(8,128)S(1)} %get-tuple-element.110) | copy-start | bytes 4718596
  105.3 37.5 %slice-start = ((s8[4718592]{0:T(1024)(128)(4,1)}), s8[4194304]{0:T(1024)(128)(4,1)S(1)}, s32[]{:S(2)}) async-start(s8[4718592]{0:T(1024)(128)(4,1)} %bitcast.202), calls=%async_computation.13 | async-start | bytes 8388608
  108.0 34.7 %copy-start.77 = (f32[512,3072]{1,0:T(8,128)}, f32[512,3072]{1,0:T(8,128)S(1)}, u32[]{:S(2)}) copy-start(f32[512,3072]{1,0:T(8,128)S(1)} %fusion.104) | copy-start | bytes 18874372
  108.1 34.7 %slice-start.1 = ((s8[4718592]{0:T(1024)(128)(4,1)}), s8[524288]{0:T(1024)(128)(4,1)S(1)}, s32[]{:S(2)}) async-start(s8[4718592]{0:T(1024)(128)(4,1)} %bitcast.202), calls=%async_computation.14 | async-start | bytes 1048576
  108.1 34.7 %copy-start.76 = (f32[768]{0:T(1024)S(1)}, f32[768]{0:T(1024)}, u32[]{:S(2)}) copy-start(f32[768]{0:T(1024)} %param.28) | copy-start | bytes 9220
  153.9 10.5 %copy-start.17 = (f32[512,768]{1,0:T(8,128)}, f32[512,768]{1,0:T(8,128)S(1)}, u32[]{:S(2)}) copy-start(f32[512,768]{1,0:T(8,128)S(1)} %get-tuple-element.88) | copy-start | bytes 4718596
  153.9 26.9 %copy-start.15 = (f32[512,768]{1,0:T(8,128)}, f32[512,768]{1,0:T(8,128)S(1)}, u32[]{:S(2)}) copy-start(f32[512,768]{1,0:T(8,128)S(1)} %get-tuple-element.69) | copy-start | bytes 4718596
  206.6 9.7 %copy-start.14 = (bf16[2,256,12,64]{1,0,3,2:T(2,128)(2,1)S(1)}, bf16[2,256,12,64]{1,0,3,2:T(2,128)(2,1)}, u32[]{:S(2)}) copy-start(bf16[2,256,12,64]{1,0,3,2:T(2,128)(2,1)} %reshape.274) | copy-start | bytes 2359300
  221.2 119.6 %reduce-scatter.7.cloned.1.call-start = ((), (), s32[]{:S(2)}) async-start(), calls=%async_computation.9 | async-start | bytes 2359296 | tf_op jit(solution)/shard_map/reduce_scatter | solution.py:220
  246.6 96.5 %reduce-scatter.9.cloned.1.call-start = ((), (), s32[]{:S(2)}) async-start(), calls=%async_computation.10 | async-start | bytes 2359296 | tf_op jit(solution)/shard_map/reduce_scatter | solution.py:217
  255.2 9.8 %copy-start.13 = (bf16[2,256,12,64]{1,0,3,2:T(2,128)(2,1)S(1)}, bf16[2,256,12,64]{1,0,3,2:T(2,128)(2,1)}, u32[]{:S(2)}) copy-start(bf16[2,256,12,64]{1,0,3,2:T(2,128)(2,1)} %reshape.281) | copy-start | bytes 2359300
  269.9 75.5 %reduce-scatter.11.cloned.1.call-start = ((), (), s32[]{:S(2)}) async-start(), calls=%async_computation.11 | async-start | bytes 2359296 | tf_op jit(solution)/shard_map/reduce_scatter | solution.py:220
  302.2 506.2 %all-reduce.9.cloned.1.call-start = ((), (), s32[]{:S(2)}) async-start(), calls=%async_computation.12 | async-start | bytes 56623104
  (67 other events, 266.4 us)
Sparse Core Ops, SparseCore 0:
  15.0 12.4 all-gather.6
  29.7 10.9 all-gather.4
  42.2 10.9 all-gather.10
  54.6 10.9 all-gather.8
  221.3 11.5 reduce-scatter.4
  246.7 11.3 reduce-scatter.6
  270.0 11.3 reduce-scatter.8
  302.3 11.3 reduce-scatter.10
  372.9 435.5 all-reduce.8
where the time goes:
time: 828 us; the launch traced here: 822 us
  waiting for transfers between devices  345 us (42%)
  matrix products  204 us (25%)
  local copies, waits for them, and re-layouts  151 us (18%)
  other arithmetic  56.1 us (7%)
  blocking collectives  48.8 us (6%)
  between operations  15.2 us (2%)
    unnamed x10, waiting for transfers between devices  345 us
    unnamed x192, local copies, waits for them, and re-layouts  57.3 us
    unnamed x1, blocking collectives  43.8 us
    dot_general x2, matrix products, on_device(): jnp.dot(normed_low, w_in, preferred_element_type=jnp.float32) + bias_in  37.4 us
    add x4, local copies, waits for them, and re-layouts, on_device(): totals = [earlier + later for earlier, later in zip(totals, micro_grads)]  30.2 us
    dot_general x2, matrix products, on_device(): jnp.einsum('td,fd->tf', grad_feed, w_back, preferred_element_type=jnp.flo...  18.9 us
    dot_general x2, matrix products, on_device(): jnp.einsum('tf,df->td', grad_inner, w_in, preferred_element_type=jnp.floa...  17.2 us
    dot_general x2, matrix products, on_device(): jnp.einsum('bqhd,bkhd->bhqk', grad_mixed_heads, value_head_split, preferr...  17 us
  transfers between devices with their start and end apart: 9, of which 1 were waited for; matrix products, arithmetic and copies ran while one was open for 28% of the time, Pallas kernels for 0%

commit v1 on v0

v1 whole, which is shorter than its diff:
```python
from functools import partial

import jax
import jax.numpy as jnp
from jax import lax
from jax.sharding import PartitionSpec as P

HEADS = 12
EPS = 1e-12
BF = jnp.bfloat16
F32 = jnp.float32


def normalize(hidden):
    center = hidden - jnp.mean(hidden, axis=-1, keepdims=True)
    variance = jnp.mean(center * center, axis=-1, keepdims=True)
    inverse = lax.rsqrt(variance + EPS)
    return center * inverse, inverse


def norm_backward(grad_hat, normed, inverse):
    first = jnp.mean(grad_hat, axis=-1, keepdims=True)
    second = jnp.mean(grad_hat * normed, axis=-1, keepdims=True)
    return inverse * (grad_hat - first - normed * second)


def swap(value):
    return lax.ppermute(value, "seq", [(0, 1), (1, 0)])


def pick(value, index, axis):
    return lax.dynamic_index_in_dim(value, index, axis, keepdims=False)


def reduce_stages(part, order, dp_bits, dp):
    me = lax.axis_index("dp")
    n_halving = dp_bits - 2
    shape = part.shape[1:]
    current = part.reshape((2,) * dp_bits + shape)
    left = list(range(dp_bits - 1, -1, -1))
    for bit in order[:n_halving]:
        axis = left.index(bit)
        mine = (me >> bit) & 1
        pairs = [(i, i ^ (1 << bit)) for i in range(dp)]
        send = pick(current, 1 - mine, axis).astype(BF)
        got = lax.ppermute(send, "dp", pairs)
        keep = pick(current, mine, axis)
        current = keep.astype(F32) + got.astype(F32)
        left.remove(bit)
    high, low = left
    group = (((me >> high) & 1) << 1) | ((me >> low) & 1)
    current = current.reshape((4,) + shape)
    total = pick(current, group, 0).astype(F32)
    for other in (1, 2, 3):
        flip = ((other >> 1) << high) | ((other & 1) << low)
        pairs = [(i, i ^ flip) for i in range(dp)]
        send = pick(current, group ^ other, 0).astype(BF)
        total = total + lax.ppermute(send, "dp", pairs).astype(F32)
    return total


def reduce_scatter(grad, order, dp, dp_bits):
    core = lax.axis_index("seq")
    rows = grad.shape[0] // (2 * dp)
    blocks = grad.reshape(dp, 2, rows, grad.shape[1])
    send = pick(blocks, 1 - core, 1).astype(BF)
    keep = pick(blocks, core, 1)
    part = keep.astype(F32) + swap(send).astype(F32)
    return reduce_stages(part, order, dp_bits, dp)


def on_device(tokens, lengths, w_qkv, w_out, w_in, w_back, bias_q, value_bias, bias_out, gain1, shift1, bias_in, bias_back, gain2, shift2, cotangent):
    rows_local, half, width = tokens.shape
    dp = lax.axis_size("dp")
    dp_bits = dp.bit_length() - 1
    core = lax.axis_index("seq")
    rows = rows_local // 2
    length = 2 * half
    head_size = width // HEADS
    scale = head_size ** -0.5

    def gather_rows(value):
        own = lax.dynamic_slice_in_dim(value, core * rows, rows, 0)
        other = swap(lax.dynamic_slice_in_dim(value, (1 - core) * rows, rows, 0))
        return jnp.concatenate([own, other], axis=1)

    def spread_rows(value):
        got = swap(value[:, half:])
        out = jnp.zeros((rows_local, half, width), value.dtype)
        out = lax.dynamic_update_slice_in_dim(out, value[:, :half], core * rows, 0)
        return lax.dynamic_update_slice_in_dim(out, got, (1 - core) * rows, 0)

    tok = gather_rows(tokens)
    cot = gather_rows(cotangent)
    row_lengths = lax.dynamic_slice_in_dim(lengths, core * rows, rows, 0)
    local = jnp.arange(half, dtype=jnp.int32)
    positions = jnp.concatenate([core * half + local, (1 - core) * half + local])
    starts = jnp.cumsum(row_lengths, axis=1) - row_lengths
    segment = jnp.sum((positions[None, :, None] >= starts[:, None, :]).astype(jnp.int32), axis=-1)
    same = (segment[:, :, None] == segment[:, None, :])[:, None]

    flat = tok.reshape(-1, width)
    projected = jnp.dot(flat, w_qkv, preferred_element_type=F32)
    q = (projected[:, :width] + bias_q).astype(BF)
    k = projected[:, width : 2 * width].astype(BF)
    v = (projected[:, 2 * width :] + value_bias).astype(BF)
    qh, kh, vh = (x.reshape(rows, length, HEADS, head_size) for x in (q, k, v))
    scores = jnp.einsum("bqhd,bkhd->bhqk", qh, kh, preferred_element_type=F32) * scale
    masked = jnp.where(same, scores, -1e30)
    weight = jnp.exp(masked - jnp.max(masked, axis=-1, keepdims=True))
    probs = (weight / jnp.sum(weight, axis=-1, keepdims=True)).astype(BF)
    mixed = jnp.einsum("bhqk,bkhd->bqhd", probs, vh, preferred_element_type=F32)
    mixed = mixed.reshape(-1, width).astype(BF)
    hat1, inv1 = normalize(flat.astype(F32) + jnp.dot(mixed, w_out, preferred_element_type=F32) + bias_out)
    normed1 = hat1 * gain1 + shift1
    normed_low = normed1.astype(BF)
    inner = jnp.dot(normed_low, w_in, preferred_element_type=F32) + bias_in
    act, gelu_back = jax.vjp(partial(jax.nn.gelu, approximate=False), inner)
    act_low = act.astype(BF)
    hat2, inv2 = normalize(normed1 + jnp.dot(act_low, w_back, preferred_element_type=F32) + bias_back)
    output = (hat2 * gain2 + shift2).astype(BF).reshape(rows, length, width)
    choose = (starts[:, :, None] == positions[None, None, :]).astype(BF)
    cls_own = jnp.einsum("rsp,rpd->rsd", choose, output, preferred_element_type=F32).astype(BF)
    cls_other = swap(cls_own)
    cls = jnp.zeros((rows_local,) + cls_own.shape[1:], BF)
    cls = lax.dynamic_update_slice_in_dim(cls, cls_own, core * rows, 0)
    cls = lax.dynamic_update_slice_in_dim(cls, cls_other, (1 - core) * rows, 0)

    dy = cot.reshape(-1, width).astype(F32)
    g_gain2 = jnp.sum(dy * hat2, axis=0)
    g_shift2 = jnp.sum(dy, axis=0)
    dpre2 = norm_backward(dy * gain2, hat2, inv2)
    dfeed = dpre2.astype(BF)
    g_bias_back = jnp.sum(dfeed.astype(F32), axis=0)
    g_back = jnp.einsum("tf,td->fd", act_low, dfeed, preferred_element_type=F32)
    r_back = reduce_scatter(g_back, (0, 1) + tuple(range(2, dp_bits)), dp, dp_bits)
    dact = jnp.einsum("td,fd->tf", dfeed, w_back, preferred_element_type=F32)
    dinner = gelu_back(dact)[0].astype(BF)
    g_bias_in = jnp.sum(dinner.astype(F32), axis=0)
    g_in = jnp.einsum("td,tf->df", normed_low, dinner, preferred_element_type=F32)
    r_in = reduce_scatter(g_in, (1, 0) + tuple(range(2, dp_bits)), dp, dp_bits)
    dnormed1 = dpre2 + jnp.einsum("tf,df->td", dinner, w_in, preferred_element_type=F32)
    g_gain1 = jnp.sum(dnormed1 * hat1, axis=0)
    g_shift1 = jnp.sum(dnormed1, axis=0)
    dpre1 = norm_backward(dnormed1 * gain1, hat1, inv1)
    dbranch = dpre1.astype(BF)
    g_bias_out = jnp.sum(dbranch.astype(F32), axis=0)
    g_out = jnp.einsum("tc,td->cd", mixed, dbranch, preferred_element_type=F32)
    r_out = reduce_scatter(g_out, (0, 1) + tuple(range(2, dp_bits)), dp, dp_bits)
    dmixed = jnp.einsum("td,cd->tc", dbranch, w_out, preferred_element_type=F32).astype(BF)
    dmh = dmixed.reshape(rows, length, HEADS, head_size)
    dprobs = jnp.einsum("bqhd,bkhd->bhqk", dmh, vh, preferred_element_type=F32)
    pf = probs.astype(F32)
    delta = jnp.sum(pf * dprobs, axis=-1, keepdims=True)
    dscores = (pf * (dprobs - delta)).astype(BF)
    dq = (jnp.einsum("bhqk,bkhd->bqhd", dscores, kh, preferred_element_type=F32) * scale).astype(BF)
    dk = (jnp.einsum("bhqk,bqhd->bkhd", dscores, qh, preferred_element_type=F32) * scale).astype(BF)
    dv = jnp.einsum("bhqk,bqhd->bkhd", probs, dmh, preferred_element_type=F32).astype(BF)
    dproj = jnp.concatenate([x.reshape(-1, width) for x in (dq, dk, dv)], axis=1)
    g_proj_bias = jnp.sum(dproj.astype(F32), axis=0)
    g_qkv = jnp.einsum("td,te->de", flat, dproj, preferred_element_type=F32)
    vectors = jnp.concatenate([g_proj_bias[:width], g_proj_bias[2 * width :], g_bias_out, g_gain1, g_shift1, g_bias_in, g_bias_back, g_gain2, g_shift2])
    vectors = vectors.reshape(2 * dp, 1, -1)
    n_vec = vectors.shape[-1]
    vectors = jnp.pad(vectors, ((0, 0), (0, 7), (0, g_qkv.shape[1] - n_vec)))
    joined = jnp.concatenate([g_qkv.reshape(2 * dp, -1, g_qkv.shape[1]), vectors], axis=1)
    r_qkv = reduce_scatter(joined.reshape(-1, g_qkv.shape[1]), (1, 0) + tuple(range(2, dp_bits)), dp, dp_bits)
    r_vec = r_qkv[-8, :n_vec]
    r_qkv = r_qkv[:-8]
    dinput = dpre1 + jnp.einsum("te,de->td", dproj, w_qkv, preferred_element_type=F32)
    dinput = dinput.astype(BF).reshape(rows, length, width)
    return (
        spread_rows(output),
        cls,
        spread_rows(dinput),
        r_qkv.reshape(-1),
        r_out.reshape(-1),
        r_in.reshape(-1),
        r_back.reshape(-1),
        r_vec,
    )


def solution(mesh):
    row = P("dp", "seq", None)
    both = P(("dp", "seq"))
    return jax.shard_map(
        on_device,
        mesh=mesh,
        in_specs=(row, P("dp", None)) + (P(),) * 13 + (row,),
        out_specs=(row, P("dp", None, None), row, both, both, both, both, both),
        check_vma=False,
    )
```

time: 828 us -> 480 us (0.58)
  waiting for transfers between devices: 345 us -> 82.4 us
  blocking collectives: 48.8 us -> 0 us
  local copies, waits for them, and re-layouts: 151 us -> 113 us
  starting transfers between devices: 1.33 us -> 35.9 us
  matrix products: 204 us -> 174 us
  between operations: 15.2 us -> 1.98 us
  other arithmetic: 56.1 us -> 67.4 us
    unnamed x10 -> x0, waiting for transfers between devices: 345 us -> none
    ppermute x0 -> x29, waiting for transfers between devices: none -> 82.4 us  [the longest x8 63 us: reduce_stages(): got = lax.ppermute(send, 'dp', pairs)]
    dot_general x38 -> x18, matrix products: 204 us -> 157 us  [the longest x1 35.2 us: on_device(): inner = jnp.dot(normed_low, w_in, preferred_element_type=F32) + bias_in]
    unnamed x1 -> x0, blocking collectives: 43.8 us -> none
    ppermute x0 -> x29, starting transfers between devices: none -> 35.9 us  [the longest x12 22.3 us: reduce_stages(): total = total + lax.ppermute(send, 'dp', pairs).astype(F32)]
    unnamed x192 -> x138, local copies, waits for them, and re-layouts: 57.3 us -> 27 us
    add x4 -> x0, local copies, waits for them, and re-layouts: 30.2 us -> none  [on_device(): totals = [earlier + later for earlier, later in zip(totals, micro_grads)]]
    reshape x4 -> x11, local copies, waits for them, and re-layouts: 11.7 us -> 29.8 us  [the longest x3 11.5 us: on_device(): qh, kh, vh = (x.reshape(rows, length, HEADS, head_size) for x in (q, k, v))]
  transfers between devices with their start and end apart: 9 -> 29, of which waited for: 1 -> 14; matrix products, arithmetic and copies ran while one was open for 28% -> 15% of each run, Pallas kernels for 0% -> 0%
where the time goes in v1:
time: 480 us; the launch traced here: 475 us
  matrix products  174 us (36%)
  local copies, waits for them, and re-layouts  113 us (24%)
  waiting for transfers between devices  82.4 us (17%)
  other arithmetic  67.4 us (14%)
  starting transfers between devices  35.9 us (7%)
    ppermute x8, waiting for transfers between devices, reduce_stages(): got = lax.ppermute(send, 'dp', pairs)  63 us
    dot_general x1, matrix products, on_device(): inner = jnp.dot(normed_low, w_in, preferred_element_type=F32) + bias_in  35.2 us
    unnamed x138, local copies, waits for them, and re-layouts  27 us
    ppermute x12, starting transfers between devices, reduce_stages(): total = total + lax.ppermute(send, 'dp', pairs).astype(F32)  22.3 us
    convert_element_type x1, other arithmetic, on_device(): dscores = (pf * (dprobs - delta)).astype(BF)  21.2 us
    dot_general x1, matrix products, on_device(): dact = jnp.einsum('td,fd->tf', dfeed, w_back, preferred_element_type=F32)  19.7 us
    ppermute x12, waiting for transfers between devices, reduce_stages(): total = total + lax.ppermute(send, 'dp', pairs).astype(F32)  19 us
    sub x1, matrix products, on_device(): weight = jnp.exp(masked - jnp.max(masked, axis=-1, keepdims=True))  16.4 us
  transfers between devices with their start and end apart: 29, of which 14 were waited for; matrix products, arithmetic and copies ran while one was open for 15% of the time, Pallas kernels for 0%

profile of v1, /device:TPU:0, one launch (start us, length us, event | category | flops | bytes accessed | tf_op | source)
XLA Modules:
  0.0 474.7 jit_solution(10261469594266809041)
XLA Ops:
  39.8 16.4 %fusion.104 = (f32[2,12,512]{2,1,0:T(8,128)}, f32[2,12,512,512]{2,3,1,0:T(8,128)}) fusion(pred[2,512,512]{1,2,0:T(8,128)(4,1)} %broadcast_compare_fusion, bf16[2,512,12,64]{1,0,3,2:T(2,128)(2,1)} %reshape.196, bf16[2,512,12,64]{1,0,3,2:T(2,128)(2,1)} %reshape.195), kind=kOutput, calls=%fused_computation.219 | convolution fusion | flops 830472704 | bytes 28884992 | tf_op jit(solution)/shard_map/sub | solution.py:110
  56.3 10.5 %divide_convert_fusion = bf16[2,12,512,512]{2,3,1,0:T(8,128)(2,1)S(1)} fusion(f32[2,12,512,512]{2,3,1,0:T(8,128)} %get-tuple-element.48, f32[2,12,512]{2,1,0:T(8,128)} %get-tuple-element.47), kind=kLoop, calls=%fused_computation.5 | loop fusion | flops 12582912 | bytes 37797888 | tf_op jit(solution)/shard_map/convert_element_type | solution.py:111
  77.8 35.2 %multiply_convert_fusion = (bf16[1024,3072]{1,0:T(8,128)(2,1)S(1)}, f32[1024,3072]{1,0:T(8,128)}, f32[1024,3072]{1,0:T(8,128)}) fusion(f32[3072]{0:T(1024)S(1)} %copy-done.52, bf16[768,3072]{1,0:T(8,128)(2,1)S(1)} %bitcast.252, f32[1024,768]{1,0:T(8,128)S(1)} %get-tuple-element.23, f32[768]{0:T(1024)S(1)} %copy-done.33, f32[768]{0:T(1024)S(1)} %copy-done.30, ...), kind=kOutput, calls=%fused_computation.13 | convolution fusion | flops 5043388416 | bytes 39348224 | tf_op jit(solution)/shard_map/dot_general | solution.py:117
  113.1 5.5 %fusion.113 = (f32[1024]{0:T(1024)S(1)}, f32[1024,768]{1,0:T(8,128)S(1)}) fusion(f32[768]{0:T(1024)S(1)} %copy-done.54, bf16[1024,3072]{1,0:T(8,128)(2,1)S(1)} %get-tuple-element.20, bf16[3072,768]{1,0:T(8,128)(2,1)S(1)} %bitcast.250, f32[768]{0:T(1024)S(1)} %copy-done.33, f32[768]{0:T(1024)S(1)} %copy-done.30, f32[1024]{0:T(1024)S(1)} %add_rsqrt_fusion.1, ...), kind=kOutput, calls=%fused_computation.220 | convolution fusion | flops 4837342208 | bytes 17323008 | tf_op jit(solution)/shard_map/dot_general | solution.py:120
  126.7 7.8 %fusion.90 = f32[3072,768]{1,0:T(8,128)} fusion(bf16[1024,3072]{1,0:T(8,128)(2,1)S(1)} %get-tuple-element.20, f32[1024,768]{1,0:T(8,128)S(1)} %get-tuple-element.17), kind=kOutput, calls=%fused_computation.209 | convolution fusion | flops 4832624640 | bytes 18874368 | tf_op jit(solution)/shard_map/tf,td->fd/dot_general | solution.py:135
  134.6 19.7 %convert_reduce_fusion = (f32[3072]{0:T(1024)}, bf16[1024,3072]{1,0:T(8,128)(2,1)}) fusion(f32[1024,3072]{1,0:T(8,128)} %get-tuple-element.21, bf16[3072,768]{1,0:T(8,128)(2,1)} %param.21, f32[1024,768]{1,0:T(8,128)} %copy-done.18, f32[1024,3072]{1,0:T(8,128)} %get-tuple-element.49, f32[3072]{0:T(1024)S(1)} %copy-done.52), kind=kOutput, calls=%fused_computation.11 | convolution fusion | flops 4886098944 | bytes 39346176 | tf_op jit(solution)/shard_map/td,fd->tf/dot_general | solution.py:137
  154.3 11.6 %multiply_reduce_fusion = (f32[768]{0:T(1024)}, f32[1024]{0:T(1024)S(1)}, f32[1024]{0:T(1024)S(1)}, f32[768]{0:T(1024)}, f32[1024,768]{1,0:T(8,128)S(1)}) fusion(f32[1024,768]{1,0:T(8,128)} %copy-done.2, f32[1024]{0:T(1024)S(1)} %add_rsqrt_fusion.1, f32[1024]{0:T(1024)S(1)} %broadcast_multiply_fusion.4, f32[768]{0:T(1024)S(1)} %copy-done.30, ...), kind=kOutput, calls=%fused_computation.60 | convolution fusion | flops 4839698432 | bytes 20472832 | tf_op jit(solution)/shard_map/tf,df->td/dot_general | solution.py:142
  165.8 8.6 %fusion.95 = f32[768,3072]{1,0:T(8,128)} fusion(bf16[1024,3072]{1,0:T(8,128)(2,1)S(1)} %copy-done.11, f32[1024,768]{1,0:T(8,128)S(1)} %copy-done.3, f32[768]{0:T(1024)S(1)} %copy-done.33, f32[768]{0:T(1024)S(1)} %copy-done.30, f32[1024]{0:T(1024)S(1)} %add_rsqrt_fusion.1, f32[1024]{0:T(1024)S(1)} %broadcast_multiply_fusion.4), kind=kOutput, calls=%fused_computation.214 | convolution fusion | flops 4835770368 | bytes 18888704 | tf_op jit(solution)/shard_map/td,tf->df/dot_general | solution.py:140
  187.0 9.1 %fusion.33 = bf16[2,512,12,64]{1,3,2,0:T(8,128)(2,1)S(1)} fusion(bf16[2,12,512,512]{2,3,1,0:T(8,128)(2,1)} %copy-done.1, bf16[2,512,12,64]{1,0,3,2:T(2,128)(2,1)} %reshape.198), kind=kOutput, calls=%fused_computation.95 | convolution fusion | flops 806092800 | bytes 15728640 | tf_op jit(solution)/shard_map/bhqk,bqhd->bkhd/dot_general | solution.py:158
  196.1 12.9 %fusion.1 = (f32[2,12,512]{2,1,0:T(8,128)S(1)}, f32[2,12,512,512]{2,3,1,0:T(8,128)}) fusion(bf16[2,12,512,512]{2,3,1,0:T(8,128)(2,1)} %copy-done.1, bf16[2,512,12,64]{1,0,3,2:T(2,128)(2,1)S(1)} %copy-done.6, bf16[2,512,12,64]{1,0,3,2:T(2,128)(2,1)S(1)} %copy-done.7), kind=kOutput, calls=%fused_computation.3 | convolution fusion | flops 824168448 | bytes 40943616 | tf_op jit(solution)/shard_map/bqhd,bkhd->bhqk/dot_general | solution.py:152
  209.1 21.2 %fusion.2 = bf16[2,12,512,512]{2,3,1,0:T(8,128)(2,1)} fusion(f32[2,12,512,512]{2,3,1,0:T(8,128)} %get-tuple-element.54, f32[2,12,512]{2,1,0:T(8,128)S(1)} %get-tuple-element.53, f32[2,12,512,512]{2,3,1,0:T(8,128)} %get-tuple-element.48, f32[2,12,512]{2,1,0:T(8,128)S(1)} %copy-done.28), kind=kLoop, calls=%fused_computation.4 | loop fusion | flops 37748736 | bytes 63012864 | tf_op jit(solution)/shard_map/convert_element_type | solution.py:155
  230.3 9.8 %fusion.35 = bf16[2,512,12,64]{1,3,2,0:T(8,128)(2,1)} fusion(bf16[2,12,512,512]{2,3,1,0:T(8,128)(2,1)} %fusion.2, bf16[2,512,12,64]{1,0,3,2:T(2,128)(2,1)S(1)} %copy-done.17), kind=kOutput, calls=%fused_computation.97 | convolution fusion | flops 806879232 | bytes 15728640 | tf_op jit(solution)/shard_map/bhqk,bqhd->bkhd/dot_general | solution.py:157
  240.1 7.9 %fusion.34 = bf16[2,512,12,64]{1,3,2,0:T(8,128)(2,1)} fusion(bf16[2,12,512,512]{2,3,1,0:T(8,128)(2,1)} %fusion.2, bf16[2,512,12,64]{1,0,3,2:T(2,128)(2,1)S(1)} %copy-done.10), kind=kOutput, calls=%fused_computation.96 | convolution fusion | flops 806879232 | bytes 15728640 | tf_op jit(solution)/shard_map/bhqk,bkhd->bqhd/dot_general | solution.py:156
  268.3 8.5 %add_convert_fusion.1 = bf16[1024,768]{1,0:T(8,128)(2,1)} fusion(f32[1024,768]{1,0:T(8,128)} %copy-done.19, bf16[768,2304]{1,0:T(8,128)(2,1)S(1)} %copy-done, bf16[1024,768]{1,0:T(8,128)(2,1)} %copy.90, bf16[1024,768]{1,0:T(8,128)(2,1)} %copy.89, bf16[1024,768]{1,0:T(8,128)(2,1)} %copy.88), kind=kOutput, calls=%fused_computation.62 | convolution fusion | flops 3639607296 | bytes 12976128 | tf_op jit(solution)/shard_map/te,de->td/dot_general | solution.py:170
  307.7 6.7 %fusion.13 = f32[32,24,2304]{2,1,0:T(8,128)S(1)} fusion(bf16[32,24,1024]{2,1,0:T(8,128)(2,1)} %bitcast.243, bf16[1024,768]{1,0:T(8,128)(2,1)} %copy.90, bf16[1024,768]{1,0:T(8,128)(2,1)} %copy.89, bf16[1024,768]{1,0:T(8,128)(2,1)} %copy.88), kind=kOutput, calls=%fused_computation.37 | convolution fusion | flops 3638034432 | bytes 13369344 | tf_op jit(solution)/shard_map/td,te->de/dot_general | solution.py:161
  317.5 6.2 %fusion.28 = bf16[16,24,3072]{2,1,0:T(8,128)(2,1)} fusion(f32[16,2,24,3072]{3,2,1,0:T(8,128)} %bitcast.208, s32[]{:T(128)S(6)} %select_n.99), kind=kLoop, calls=%fused_computation.78 | loop fusion | bytes 4718596 | tf_op jit(solution)/shard_map/convert_element_type | solution.py:66
  331.2 4.3 collective-permute-done.12
  370.0 16.4 %collective-permute-done.24 = bf16[2,2,2,96,768]{4,3,2,1,0:T(8,128)(2,1)S(1)} collective-permute-done((bf16[2,2,2,96,768]{4,3,2,1,0:T(8,128)(2,1)S(1)}, bf16[2,2,2,96,768]{4,3,2,1,0:T(8,128)(2,1)S(1)}, u32[]{:S(2)}, u32[]{:S(2)}) %collective-permute-start.24) | collective-permute-done | bytes 1179680 | tf_op jit(solution)/shard_map/ppermute | solution.py:46
  388.4 5.7 %collective-permute-done.6 = bf16[2,2,2,32,2304]{4,3,2,1,0:T(8,128)(2,1)S(1)} collective-permute-done((bf16[2,2,2,32,2304]{4,3,2,1,0:T(8,128)(2,1)S(1)}, bf16[2,2,2,32,2304]{4,3,2,1,0:T(8,128)(2,1)S(1)}, u32[]{:S(2)}, u32[]{:S(2)}) %collective-permute-start.6) | collective-permute-done | bytes 1179680 | tf_op jit(solution)/shard_map/ppermute | solution.py:46
  395.2 24.1 %collective-permute-done.18 = bf16[2,2,2,24,3072]{4,3,2,1,0:T(8,128)(2,1)S(1)} collective-permute-done((bf16[2,2,2,24,3072]{4,3,2,1,0:T(8,128)(2,1)S(1)}, bf16[2,2,2,24,3072]{4,3,2,1,0:T(8,128)(2,1)S(1)}, u32[]{:S(2)}, u32[]{:S(2)}) %collective-permute-start.18) | collective-permute-done | bytes 1179680 | tf_op jit(solution)/shard_map/ppermute | solution.py:46
  420.6 8.8 %collective-permute-done.25 = bf16[2,2,96,768]{3,2,1,0:T(8,128)(2,1)S(1)} collective-permute-done((bf16[2,2,96,768]{3,2,1,0:T(8,128)(2,1)S(1)}, bf16[2,2,96,768]{3,2,1,0:T(8,128)(2,1)S(1)}, u32[]{:S(2)}, u32[]{:S(2)}) %collective-permute-start.25) | collective-permute-done | bytes 589856 | tf_op jit(solution)/shard_map/ppermute | solution.py:46
  438.6 4.5 collective-permute-done.8
  447.1 6.5 %collective-permute-start.20 = (bf16[24,3072]{1,0:T(8,128)(2,1)}, bf16[24,3072]{1,0:T(8,128)(2,1)}, u32[]{:S(2)}, u32[]{:S(2)}) collective-permute-start(bf16[24,3072]{1,0:T(8,128)(2,1)} %get-tuple-element.38), channel_id=1, source_target_pairs={{0,8},{2,10},{4,12},{6,14},{8,0},{10,2},{12,4},{14,6},{16,24},{18,... | collective-permute-start | bytes 442376 | tf_op jit(solution)/shard_map/ppermute | solution.py:58
  466.2 4.4 collective-permute-done.21
  (290 shorter events, 200.6 us)
Async XLA Ops:
  3.5 7.6 %collective-permute-start = (bf16[2,256,768]{2,1,0:T(8,128)(2,1)}, bf16[2,256,768]{2,1,0:T(8,128)(2,1)}, u32[]{:S(2)}, u32[]{:S(2)}) collective-permute-start(bf16[2,256,768]{2,1,0:T(8,128)(2,1)} %get-tuple-element.34), channel_id=1, source_target_pairs={{0,1},{1,0},{2,3},{3,2},{4,5},{5,4},{6,7},{7,6},{8,9},{9,8},{10,11... | collective-permute-start | bytes 2359304 | tf_op jit(solution)/shard_map/ppermute | solution.py:28
  285.7 49.9 %collective-permute-start.2 = (bf16[2,6,768]{2,1,0:T(8,128)(2,1)}, bf16[2,6,768]{2,1,0:T(8,128)(2,1)}, u32[]{:S(2)}, u32[]{:S(2)}) collective-permute-start(bf16[2,6,768]{2,1,0:T(8,128)(2,1)} %convolution_convert_fusion.3), channel_id=1, source_target_pairs={{0,1},{1,0},{2,3},{3,2},{4,5},{5,4},{6,7},{7,6},{8,9},{9,8},{10,11... | collective-permute-start | bytes 55304 | tf_op jit(solution)/shard_map/ppermute | solution.py:28
  285.8 56.2 %collective-permute-start.1 = (bf16[2,256,768]{2,1,0:T(8,128)(2,1)}, bf16[2,256,768]{2,1,0:T(8,128)(2,1)}, u32[]{:S(2)}, u32[]{:S(2)}) collective-permute-start(bf16[2,256,768]{2,1,0:T(8,128)(2,1)} %get-tuple-element.31), channel_id=1, source_target_pairs={{0,1},{1,0},{2,3},{3,2},{4,5},{5,4},{6,7},{7,6},{8,9},{9,8},{10,11... | collective-permute-start | bytes 2359304 | tf_op jit(solution)/shard_map/ppermute | solution.py:28
  289.9 34.0 %collective-permute-start.11 = (bf16[16,24,768]{2,1,0:T(8,128)(2,1)}, bf16[16,24,768]{2,1,0:T(8,128)(2,1)}, u32[]{:S(2)}, u32[]{:S(2)}) collective-permute-start(bf16[16,24,768]{2,1,0:T(8,128)(2,1)} %fusion.58), channel_id=1, source_target_pairs={{0,1},{1,0},{2,3},{3,2},{4,5},{5,4},{6,7},{7,6},{8,9},{9,8},{10,11... | collective-permute-start | bytes 1769480 | tf_op jit(solution)/shard_map/ppermute | solution.py:28
  294.1 61.7 %collective-permute-start.23 = (bf16[16,96,768]{2,1,0:T(8,128)(2,1)}, bf16[16,96,768]{2,1,0:T(8,128)(2,1)}, u32[]{:S(2)}, u32[]{:S(2)}) collective-permute-start(bf16[16,96,768]{2,1,0:T(8,128)(2,1)} %fusion.29), channel_id=1, source_target_pairs={{0,1},{1,0},{2,3},{3,2},{4,5},{5,4},{6,7},{7,6},{8,9},{9,8},{10,11... | collective-permute-start | bytes 7077896 | tf_op jit(solution)/shard_map/ppermute | solution.py:28
  323.7 37.5 %collective-permute-start.5 = (bf16[16,32,2304]{2,1,0:T(8,128)(2,1)}, bf16[16,32,2304]{2,1,0:T(8,128)(2,1)}, u32[]{:S(2)}, u32[]{:S(2)}) collective-permute-start(bf16[16,32,2304]{2,1,0:T(8,128)(2,1)} %fusion.27), channel_id=1, source_target_pairs={{0,1},{1,0},{2,3},{3,2},{4,5},{5,4},{6,7},{7,6},{8,9},{9,8},{10,11... | collective-permute-start | bytes 7077896 | tf_op jit(solution)/shard_map/ppermute | solution.py:28
  325.2 10.3 %collective-permute-start.12 = (bf16[2,2,2,24,768]{4,3,2,1,0:T(8,128)(2,1)S(1)}, bf16[2,2,2,24,768]{4,3,2,1,0:T(8,128)(2,1)S(1)}, u32[]{:S(2)}, u32[]{:S(2)}) collective-permute-start(bf16[2,2,2,24,768]{4,3,2,1,0:T(8,128)(2,1)S(1)} %fusion.61), channel_id=1, source_target_pairs={{0,2},{2,0},{4,6},{6,4},{8,10},{10,8},{12,14},{14,12},{16,18},{18,... | collective-permute-start | bytes 884744 | tf_op jit(solution)/shard_map/ppermute | solution.py:46
  335.5 10.5 %collective-permute-start.4 = (bf16[2,256,768]{2,1,0:T(8,128)(2,1)S(1)}, bf16[2,256,768]{2,1,0:T(8,128)(2,1)S(1)}, u32[]{:S(2)}, u32[]{:S(2)}) collective-permute-start(bf16[2,256,768]{2,1,0:T(8,128)(2,1)S(1)} %get-tuple-element.27), channel_id=1, source_target_pairs={{0,1},{1,0},{2,3},{3,2},{4,5},{5,4},{6,7},{7,6},{8,9},{9,8},{10,11... | collective-permute-start | bytes 2359304 | tf_op jit(solution)/shard_map/ppermute | solution.py:28
  341.9 24.7 %collective-permute-start.17 = (bf16[16,24,3072]{2,1,0:T(8,128)(2,1)}, bf16[16,24,3072]{2,1,0:T(8,128)(2,1)}, u32[]{:S(2)}, u32[]{:S(2)}) collective-permute-start(bf16[16,24,3072]{2,1,0:T(8,128)(2,1)} %fusion.28), channel_id=1, source_target_pairs={{0,1},{1,0},{2,3},{3,2},{4,5},{5,4},{6,7},{7,6},{8,9},{9,8},{10,11... | collective-permute-start | bytes 7077896 | tf_op jit(solution)/shard_map/ppermute | solution.py:28
  359.7 26.7 %collective-permute-start.24 = (bf16[2,2,2,96,768]{4,3,2,1,0:T(8,128)(2,1)S(1)}, bf16[2,2,2,96,768]{4,3,2,1,0:T(8,128)(2,1)S(1)}, u32[]{:S(2)}, u32[]{:S(2)}) collective-permute-start(bf16[2,2,2,96,768]{4,3,2,1,0:T(8,128)(2,1)S(1)} %fusion.56), channel_id=1, source_target_pairs={{0,2},{2,0},{4,6},{6,4},{8,10},{10,8},{12,14},{14,12},{16,18},{18,... | collective-permute-start | bytes 3538952 | tf_op jit(solution)/shard_map/ppermute | solution.py:46
  365.1 29.0 %collective-permute-start.6 = (bf16[2,2,2,32,2304]{4,3,2,1,0:T(8,128)(2,1)S(1)}, bf16[2,2,2,32,2304]{4,3,2,1,0:T(8,128)(2,1)S(1)}, u32[]{:S(2)}, u32[]{:S(2)}) collective-permute-start(bf16[2,2,2,32,2304]{4,3,2,1,0:T(8,128)(2,1)S(1)} %fusion.54), channel_id=1, source_target_pairs={{0,4},{2,6},{4,0},{6,2},{8,12},{10,14},{12,8},{14,10},{16,20},{18,... | collective-permute-start | bytes 3538952 | tf_op jit(solution)/shard_map/ppermute | solution.py:46
  369.5 49.8 %collective-permute-start.18 = (bf16[2,2,2,24,3072]{4,3,2,1,0:T(8,128)(2,1)S(1)}, bf16[2,2,2,24,3072]{4,3,2,1,0:T(8,128)(2,1)S(1)}, u32[]{:S(2)}, u32[]{:S(2)}) collective-permute-start(bf16[2,2,2,24,3072]{4,3,2,1,0:T(8,128)(2,1)S(1)} %fusion.55), channel_id=1, source_target_pairs={{0,4},{2,6},{4,0},{6,2},{8,12},{10,14},{12,8},{14,10},{16,20},{18,... | collective-permute-start | bytes 3538952 | tf_op jit(solution)/shard_map/ppermute | solution.py:46
  386.8 42.7 %collective-permute-start.25 = (bf16[2,2,96,768]{3,2,1,0:T(8,128)(2,1)S(1)}, bf16[2,2,96,768]{3,2,1,0:T(8,128)(2,1)S(1)}, u32[]{:S(2)}, u32[]{:S(2)}) collective-permute-start(bf16[2,2,96,768]{3,2,1,0:T(8,128)(2,1)S(1)} %fusion.60), channel_id=1, source_target_pairs={{0,4},{2,6},{4,0},{6,2},{8,12},{10,14},{12,8},{14,10},{16,20},{18,... | collective-permute-start | bytes 1769480 | tf_op jit(solution)/shard_map/ppermute | solution.py:46
  394.3 38.6 %collective-permute-start.7 = (bf16[2,2,32,2304]{3,2,1,0:T(8,128)(2,1)S(1)}, bf16[2,2,32,2304]{3,2,1,0:T(8,128)(2,1)S(1)}, u32[]{:S(2)}, u32[]{:S(2)}) collective-permute-start(bf16[2,2,32,2304]{3,2,1,0:T(8,128)(2,1)S(1)} %fusion.57), channel_id=1, source_target_pairs={{0,2},{2,0},{4,6},{6,4},{8,10},{10,8},{12,14},{14,12},{16,18},{18,... | collective-permute-start | bytes 1769480 | tf_op jit(solution)/shard_map/ppermute | solution.py:46
  419.7 15.4 %collective-permute-start.19 = (bf16[2,2,24,3072]{3,2,1,0:T(8,128)(2,1)S(1)}, bf16[2,2,24,3072]{3,2,1,0:T(8,128)(2,1)S(1)}, u32[]{:S(2)}, u32[]{:S(2)}) collective-permute-start(bf16[2,2,24,3072]{3,2,1,0:T(8,128)(2,1)S(1)} %fusion.59), channel_id=1, source_target_pairs={{0,2},{2,0},{4,6},{6,4},{8,10},{10,8},{12,14},{14,12},{16,18},{18,... | collective-permute-start | bytes 1769480 | tf_op jit(solution)/shard_map/ppermute | solution.py:46
  429.6 30.2 %collective-permute-start.26 = (bf16[96,768]{1,0:T(8,128)(2,1)S(1)}, bf16[96,768]{1,0:T(8,128)(2,1)S(1)}, u32[]{:S(2)}, u32[]{:S(2)}) collective-permute-start(bf16[96,768]{1,0:T(8,128)(2,1)S(1)} %get-tuple-element.35), channel_id=1, source_target_pairs={{0,8},{2,10},{4,12},{6,14},{8,0},{10,2},{12,4},{14,6},{16,24},{18,... | collective-permute-start | bytes 442376 | tf_op jit(solution)/shard_map/ppermute | solution.py:58
  430.1 29.8 %collective-permute-start.28 = (bf16[96,768]{1,0:T(8,128)(2,1)S(1)}, bf16[96,768]{1,0:T(8,128)(2,1)S(1)}, u32[]{:S(2)}, u32[]{:S(2)}) collective-permute-start(bf16[96,768]{1,0:T(8,128)(2,1)S(1)} %get-tuple-element.36), channel_id=1, source_target_pairs={{0,24},{2,26},{4,28},{6,30},{8,16},{10,18},{12,20},{14,22},{16,8},... | collective-permute-start | bytes 442376 | tf_op jit(solution)/shard_map/ppermute | solution.py:58
  433.1 10.0 %collective-permute-start.8 = (bf16[32,2304]{1,0:T(8,128)(2,1)S(1)}, bf16[32,2304]{1,0:T(8,128)(2,1)S(1)}, u32[]{:S(2)}, u32[]{:S(2)}) collective-permute-start(bf16[32,2304]{1,0:T(8,128)(2,1)S(1)} %get-tuple-element.41), channel_id=1, source_target_pairs={{0,8},{2,10},{4,12},{6,14},{8,0},{10,2},{12,4},{14,6},{16,24},{18,... | collective-permute-start | bytes 442376 | tf_op jit(solution)/shard_map/ppermute | solution.py:58
  434.2 12.9 %collective-permute-start.10 = (bf16[32,2304]{1,0:T(8,128)(2,1)S(1)}, bf16[32,2304]{1,0:T(8,128)(2,1)S(1)}, u32[]{:S(2)}, u32[]{:S(2)}) collective-permute-start(bf16[32,2304]{1,0:T(8,128)(2,1)S(1)} %get-tuple-element.42), channel_id=1, source_target_pairs={{0,24},{2,26},{4,28},{6,30},{8,16},{10,18},{12,20},{14,22},{16,8},... | collective-permute-start | bytes 442376 | tf_op jit(solution)/shard_map/ppermute | solution.py:58
  435.1 21.2 %collective-permute-start.9 = (bf16[32,2304]{1,0:T(8,128)(2,1)S(1)}, bf16[32,2304]{1,0:T(8,128)(2,1)S(1)}, u32[]{:S(2)}, u32[]{:S(2)}) collective-permute-start(bf16[32,2304]{1,0:T(8,128)(2,1)S(1)} %get-tuple-element.43), channel_id=1, source_target_pairs={{0,16},{2,18},{4,20},{6,22},{8,24},{10,26},{12,28},{14,30},{16,0},... | collective-permute-start | bytes 442376 | tf_op jit(solution)/shard_map/ppermute | solution.py:58
  443.1 17.7 %collective-permute-start.27 = (bf16[96,768]{1,0:T(8,128)(2,1)S(1)}, bf16[96,768]{1,0:T(8,128)(2,1)S(1)}, u32[]{:S(2)}, u32[]{:S(2)}) collective-permute-start(bf16[96,768]{1,0:T(8,128)(2,1)S(1)} %get-tuple-element.37), channel_id=1, source_target_pairs={{0,16},{2,18},{4,20},{6,22},{8,24},{10,26},{12,28},{14,30},{16,0},... | collective-permute-start | bytes 442376 | tf_op jit(solution)/shard_map/ppermute | solution.py:58
  447.1 19.1 %collective-permute-start.20 = (bf16[24,3072]{1,0:T(8,128)(2,1)}, bf16[24,3072]{1,0:T(8,128)(2,1)}, u32[]{:S(2)}, u32[]{:S(2)}) collective-permute-start(bf16[24,3072]{1,0:T(8,128)(2,1)} %get-tuple-element.38), channel_id=1, source_target_pairs={{0,8},{2,10},{4,12},{6,14},{8,0},{10,2},{12,4},{14,6},{16,24},{18,... | collective-permute-start | bytes 442376 | tf_op jit(solution)/shard_map/ppermute | solution.py:58
  456.2 10.0 %collective-permute-start.22 = (bf16[24,3072]{1,0:T(8,128)(2,1)}, bf16[24,3072]{1,0:T(8,128)(2,1)}, u32[]{:S(2)}, u32[]{:S(2)}) collective-permute-start(bf16[24,3072]{1,0:T(8,128)(2,1)} %get-tuple-element.39), channel_id=1, source_target_pairs={{0,24},{2,26},{4,28},{6,30},{8,16},{10,18},{12,20},{14,22},{16,8},... | collective-permute-start | bytes 442376 | tf_op jit(solution)/shard_map/ppermute | solution.py:58
  459.8 10.8 %collective-permute-start.21 = (bf16[24,3072]{1,0:T(8,128)(2,1)}, bf16[24,3072]{1,0:T(8,128)(2,1)}, u32[]{:S(2)}, u32[]{:S(2)}) collective-permute-start(bf16[24,3072]{1,0:T(8,128)(2,1)} %get-tuple-element.40), channel_id=1, source_target_pairs={{0,16},{2,18},{4,20},{6,22},{8,24},{10,26},{12,28},{14,30},{16,0},... | collective-permute-start | bytes 442376 | tf_op jit(solution)/shard_map/ppermute | solution.py:58
  (67 other events, 566.7 us)

commit v2 on v1

v2 whole, which is shorter than its diff:
```python
from functools import partial

import jax
import jax.numpy as jnp
from jax import lax
from jax.experimental import pallas as pl
from jax.experimental.pallas import tpu as pltpu
from jax.sharding import PartitionSpec as P

HEADS = 12
EPS = 1e-12
BF = jnp.bfloat16
F32 = jnp.float32
VMEM_LIMIT = 60 << 20
RSQRT2 = 0.7071067811865476
RSQRT2PI = 0.3989422804014327


def row_dot(left, right):
    return lax.dot_general(left, right, (((1,), (0,)), ((), ())), preferred_element_type=F32)


def row_dot_t(left, right):
    return lax.dot_general(left, right, (((1,), (1,)), ((), ())), preferred_element_type=F32)


def col_dot(left, right):
    return lax.dot_general(left, right, (((0,), (0,)), ((), ())), preferred_element_type=F32)


def gelu_pair(value):
    expo = jnp.exp(value * value * -0.5)
    t = 1.0 / (1.0 + (0.3275911 * RSQRT2) * jnp.abs(value))
    poly = t * (0.5 * 0.254829592 + t * (0.5 * -0.284496736 + t * (0.5 * 1.421413741 + t * (0.5 * -1.453152027 + t * (0.5 * 1.061405429)))))
    tail = poly * expo
    phi = jnp.where(value < 0.0, tail, 1.0 - tail)
    return value * phi, phi + value * expo * RSQRT2PI


def forward_kernel(
    core_ref, len_ref, own_ref, other_ref, cot_own_ref, cot_other_ref, wqkv_hbm, wout_hbm, win_hbm, wback_hbm,
    bq_ref, bv_ref, bo_ref, g1_ref, s1_ref, bi_ref, bb_ref, g2_ref, s2_ref,
    qkv_ref, probs_hbm, mixed_ref, low_ref, hat1_ref, inv1_ref, act_ref, slope_ref, out_ref, out_other_ref, cls_ref, dfeed_ref,
    gg2_ref, gs2_ref, gbb_ref,
    x_ref, cot_ref, bias_ref, normed_ref, acc_ref, outf_ref, wqkv_ref, wout_ref, win_ref, wback_ref, p_ref, w_sem, p_sem,
):
    step = pl.program_id(0)
    core = core_ref[0]
    rows = pl.num_programs(0)
    half, width = own_ref.shape[1:]
    length = 2 * half
    pairs = width // 128
    block = 256
    hidden = win_ref.shape[1]
    chunk = 512

    copies = [
        pltpu.make_async_copy(src, dst, w_sem.at[i])
        for i, (src, dst) in enumerate(
            ((wqkv_hbm, wqkv_ref), (wout_hbm, wout_ref), (win_hbm, win_ref), (wback_hbm, wback_ref))
        )
    ]

    @pl.when(step == 0)
    def _():
        for copy in copies:
            copy.start()
        gg2_ref[...] = jnp.zeros_like(gg2_ref)
        gs2_ref[...] = jnp.zeros_like(gs2_ref)
        gbb_ref[...] = jnp.zeros_like(gbb_ref)

    own_at = pl.multiple_of(core * half, half)
    other_at = pl.multiple_of((1 - core) * half, half)
    x_ref[pl.ds(own_at, half), :] = own_ref[0]
    x_ref[pl.ds(other_at, half), :] = other_ref[0]
    cot_ref[pl.ds(own_at, half), :] = cot_own_ref[0]
    cot_ref[pl.ds(other_at, half), :] = cot_other_ref[0]

    row = core * rows + step
    count = len_ref.shape[1]
    starts = [jnp.int32(0)]
    for j in range(count - 1):
        starts.append(starts[-1] + len_ref[row, j])
    down = lax.broadcasted_iota(jnp.int32, (length, 1), 0)
    across = lax.broadcasted_iota(jnp.int32, (1, length), 1)
    seg_down = jnp.zeros((length, 1), jnp.int32)
    seg_across = jnp.zeros((1, length), jnp.int32)
    for j in range(1, count):
        seg_down += (down >= starts[j]).astype(jnp.int32)
        seg_across += (across >= starts[j]).astype(jnp.int32)
    bias_ref[...] = jnp.where(seg_down == seg_across, 0.0, -1e30)

    @pl.when(step == 0)
    def _():
        copies[0].wait()

    for n in range(3):
        part = row_dot(x_ref[...], wqkv_ref[:, n * width : (n + 1) * width])
        if n == 0:
            part = (part + bq_ref[...]) * (width // HEADS) ** -0.5
        if n == 2:
            part = part + bv_ref[...]
        qkv_ref[0, :, n * width : (n + 1) * width] = part.astype(BF)

    lane = lax.broadcasted_iota(jnp.int32, (1, 128), 1)
    first = lane < 64

    def pair_body(pair, carry):
        slot = lax.rem(pair, 2)
        out_copy = pltpu.make_async_copy(p_ref.at[slot], probs_hbm.at[step, pair], p_sem.at[slot])

        @pl.when(pair >= 2)
        def _():
            out_copy.wait()

        q_at = pl.multiple_of(pair * 128, 128)
        k_pair = qkv_ref[0, :, pl.ds(pl.multiple_of(width + pair * 128, 128), 128)]
        v_pair = qkv_ref[0, :, pl.ds(pl.multiple_of(2 * width + pair * 128, 128), 128)]
        for b in range(length // block):
            q_pair = qkv_ref[0, b * block : (b + 1) * block, pl.ds(q_at, 128)]
            outs = []
            for h in range(2):
                q_one = jnp.where(first if h == 0 else jnp.logical_not(first), q_pair, jnp.zeros_like(q_pair))
                s = row_dot_t(q_one, k_pair) + bias_ref[b * block : (b + 1) * block, :]
                e = jnp.exp(s - jnp.max(s, axis=-1, keepdims=True))
                p = (e * (1.0 / jnp.sum(e, axis=-1, keepdims=True))).astype(BF)
                p_ref[slot, h, b * block : (b + 1) * block, :] = p
                outs.append(row_dot(p, v_pair))
            mixed_ref[0, b * block : (b + 1) * block, pl.ds(q_at, 128)] = jnp.where(first, outs[0], outs[1]).astype(BF)
        out_copy.start()
        return carry

    lax.fori_loop(0, pairs, pair_body, 0)
    for tail in (pairs - 2, pairs - 1):
        pltpu.make_async_copy(p_ref.at[tail % 2], probs_hbm.at[step, tail], p_sem.at[tail % 2]).wait()

    @pl.when(step == 0)
    def _():
        for copy in copies[1:]:
            copy.wait()

    def token_body(b, carry):
        at = pl.ds(pl.multiple_of(b * block, block), block)
        pre = x_ref[at, :].astype(F32) + row_dot(mixed_ref[0, at, :], wout_ref[...]) + bo_ref[...]
        center = pre - jnp.mean(pre, axis=-1, keepdims=True)
        inv = lax.rsqrt(jnp.mean(center * center, axis=-1, keepdims=True) + EPS)
        hat = center * inv
        hat1_ref[0, at, :] = hat.astype(BF)
        inv1_ref[0, at, :] = inv
        normed = hat * g1_ref[...] + s1_ref[...]
        normed_ref[...] = normed + bb_ref[...]
        low_ref[0, at, :] = normed.astype(BF)
        for c in range(hidden // chunk):
            cols = slice(c * chunk, (c + 1) * chunk)
            inner = row_dot(low_ref[0, at, :], win_ref[:, cols]) + bi_ref[:, cols]
            act, slope = gelu_pair(inner)
            act_ref[0, at, cols] = act.astype(BF)
            slope_ref[0, at, cols] = slope.astype(BF)
        pre = normed_ref[...] + row_dot(act_ref[0, at, :], wback_ref[...])
        center = pre - jnp.mean(pre, axis=-1, keepdims=True)
        inv = lax.rsqrt(jnp.mean(center * center, axis=-1, keepdims=True) + EPS)
        hat = center * inv
        outf_ref[at, :] = (hat * g2_ref[...] + s2_ref[...]).astype(BF)
        dy = cot_ref[at, :].astype(F32)
        gg2_ref[...] += jnp.sum(dy * hat, axis=0, keepdims=True)
        gs2_ref[...] += jnp.sum(dy, axis=0, keepdims=True)
        g = dy * g2_ref[...]
        dpre = inv * (g - jnp.mean(g, axis=-1, keepdims=True) - hat * jnp.mean(g * hat, axis=-1, keepdims=True))
        dfeed = dpre.astype(BF)
        dfeed_ref[0, at, :] = dfeed
        gbb_ref[...] += jnp.sum(dfeed.astype(F32), axis=0, keepdims=True)
        return carry

    lax.fori_loop(0, length // block, token_body, 0)
    out_ref[0] = outf_ref[pl.ds(own_at, half), :]
    out_other_ref[0] = outf_ref[pl.ds(other_at, half), :]
    which = lax.broadcasted_iota(jnp.int32, (8, 1), 0)
    start_down = jnp.full((8, 1), -1, jnp.int32)
    for j in range(count):
        start_down = jnp.where(which == j, starts[j], start_down)
    choose = (start_down == across).astype(F32).astype(BF)
    cls_ref[0] = row_dot(choose, outf_ref[...]).astype(BF)


def whole(shape):
    return pl.BlockSpec(shape, lambda *_: (0,) * len(shape))


ANY = pl.BlockSpec(memory_space=pl.ANY)


def forward_call(core, lengths, tokens, other, cot, cot_other, weights, vectors):
    rows_local, half, width = tokens.shape
    rows = rows_local // 2
    length = 2 * half
    hidden = weights[2].shape[1]
    own_row = pl.BlockSpec((1, half, width), lambda r, core, lens: (core[0] * rows + r, 0, 0))
    plain_row = pl.BlockSpec((1, half, width), lambda r, *_: (r, 0, 0))

    def full(n):
        return pl.BlockSpec((1, length, n), lambda r, *_: (r, 0, 0))

    shapes = [
        jax.ShapeDtypeStruct((rows, length, 3 * width), BF),
        jax.ShapeDtypeStruct((rows, HEADS // 2, 2, length, length), BF),
        jax.ShapeDtypeStruct((rows, length, width), BF),
        jax.ShapeDtypeStruct((rows, length, width), BF),
        jax.ShapeDtypeStruct((rows, length, width), BF),
        jax.ShapeDtypeStruct((rows, length, 1), F32),
        jax.ShapeDtypeStruct((rows, length, hidden), BF),
        jax.ShapeDtypeStruct((rows, length, hidden), BF),
        jax.ShapeDtypeStruct((rows_local, half, width), BF),
        jax.ShapeDtypeStruct((rows, half, width), BF),
        jax.ShapeDtypeStruct((rows, 8, width), BF),
        jax.ShapeDtypeStruct((rows, length, width), BF),
    ] + [jax.ShapeDtypeStruct((1, width), F32)] * 3
    out_specs = [full(3 * width), ANY, full(width), full(width), full(width), full(1), full(hidden), full(hidden), own_row, plain_row,
                 pl.BlockSpec((1, 8, width), lambda r, *_: (r, 0, 0)), full(width)] + [whole((1, width))] * 3
    flops = 2 * rows * length * width * (3 * width + width + 2 * hidden) + 4 * rows * length * length * width
    return pl.pallas_call(
        forward_kernel,
        name="forward_rows",
        out_shape=shapes,
        grid_spec=pltpu.PrefetchScalarGridSpec(
            num_scalar_prefetch=2,
            grid=(rows,),
            in_specs=[own_row, plain_row, own_row, plain_row, ANY, ANY, ANY, ANY] + [whole(v.shape) for v in vectors],
            out_specs=out_specs,
            scratch_shapes=[
                pltpu.VMEM((length, width), BF),
                pltpu.VMEM((length, width), BF),
                pltpu.VMEM((length, length), F32),
                pltpu.VMEM((256, width), F32),
                pltpu.VMEM((8, 128), F32),
                pltpu.VMEM((length, width), BF),
            ]
            + [pltpu.VMEM(w.shape, BF) for w in weights]
            + [pltpu.VMEM((2, 2, length, length), BF), pltpu.SemaphoreType.DMA((4,)), pltpu.SemaphoreType.DMA((2,))],
        ),
        compiler_params=pltpu.CompilerParams(vmem_limit_bytes=VMEM_LIMIT),
        cost_estimate=pl.CostEstimate(flops=flops, bytes_accessed=50 << 20, transcendentals=rows * length * hidden * 2),
    )(core, lengths, tokens, other, cot, cot_other, *weights, *vectors)


def weight_grad(left, right, block_m, block_n, name):
    total, m = left.shape
    n = right.shape[1]

    def body(l_ref, r_ref, o_ref, t_ref):
        @pl.when(pl.program_id(1) == 0)
        def _():
            t_ref[...] = l_ref[...].T

        o_ref[...] = row_dot(t_ref[...], r_ref[...]).astype(BF)

    return pl.pallas_call(
        body,
        name=name,
        out_shape=jax.ShapeDtypeStruct((m, n), BF),
        grid=(m // block_m, n // block_n),
        in_specs=[pl.BlockSpec((total, block_m), lambda i, j: (0, i)), pl.BlockSpec((total, block_n), lambda i, j: (0, j))],
        out_specs=pl.BlockSpec((block_m, block_n), lambda i, j: (i, j)),
        scratch_shapes=[pltpu.VMEM((block_m, total), BF)],
        compiler_params=pltpu.CompilerParams(vmem_limit_bytes=VMEM_LIMIT),
        cost_estimate=pl.CostEstimate(flops=2 * total * m * n, bytes_accessed=2 * (total * (m + n) + m * n), transcendentals=0),
    )(left, right)


def inner_grad(dfeed, slope, w_back):
    total, width = dfeed.shape
    hidden = slope.shape[1]
    block = 512

    def body(d_ref, s_ref, w_ref, o_ref, b_ref):
        value = (row_dot_t(d_ref[...], w_ref[...]) * s_ref[...].astype(F32)).astype(BF)
        o_ref[...] = value
        b_ref[...] = jnp.sum(value.astype(F32), axis=0, keepdims=True)

    return pl.pallas_call(
        body,
        name="inner_grad",
        out_shape=[jax.ShapeDtypeStruct((total, hidden), BF), jax.ShapeDtypeStruct((1, hidden), F32)],
        grid=(hidden // block,),
        in_specs=[whole((total, width)), pl.BlockSpec((total, block), lambda j: (0, j)), pl.BlockSpec((block, width), lambda j: (j, 0))],
        out_specs=[pl.BlockSpec((total, block), lambda j: (0, j)), pl.BlockSpec((1, block), lambda j: (0, j))],
        compiler_params=pltpu.CompilerParams(vmem_limit_bytes=VMEM_LIMIT),
        cost_estimate=pl.CostEstimate(flops=2 * total * width * hidden, bytes_accessed=20 << 20, transcendentals=0),
    )(dfeed, slope, w_back)


def branch_grad(dinner, dfeed, hat1, inv1, w_in, w_out, gain1):
    total, width = dfeed.shape
    hidden = dinner.shape[1]
    block = 256

    def body(i_ref, f_ref, h_ref, v_ref, wi_ref, wo_ref, g_ref, branch_ref, mixed_ref, gg_ref, gs_ref, gb_ref):
        @pl.when(pl.program_id(0) == 0)
        def _():
            gg_ref[...] = jnp.zeros_like(gg_ref)
            gs_ref[...] = jnp.zeros_like(gs_ref)
            gb_ref[...] = jnp.zeros_like(gb_ref)

        dn = f_ref[...].astype(F32) + row_dot_t(i_ref[...], wi_ref[...])
        hat = h_ref[...].astype(F32)
        gg_ref[...] += jnp.sum(dn * hat, axis=0, keepdims=True)
        gs_ref[...] += jnp.sum(dn, axis=0, keepdims=True)
        g = dn * g_ref[...]
        dpre = v_ref[...] * (g - jnp.mean(g, axis=-1, keepdims=True) - hat * jnp.mean(g * hat, axis=-1, keepdims=True))
        branch = dpre.astype(BF)
        branch_ref[...] = branch
        gb_ref[...] += jnp.sum(branch.astype(F32), axis=0, keepdims=True)
        mixed_ref[...] = row_dot_t(branch, wo_ref[...]).astype(BF)

    def rows(n):
        return pl.BlockSpec((block, n), lambda i: (i, 0))

    one = jax.ShapeDtypeStruct((1, width), F32)
    return pl.pallas_call(
        body,
        name="branch_grad",
        out_shape=[jax.ShapeDtypeStruct((total, width), BF), jax.ShapeDtypeStruct((total, width), BF), one, one, one],
        grid=(total // block,),
        in_specs=[rows(hidden), rows(width), rows(width), rows(1), whole(w_in.shape), whole(w_out.shape), whole(gain1.shape)],
        out_specs=[rows(width), rows(width)] + [whole((1, width))] * 3,
        compiler_params=pltpu.CompilerParams(vmem_limit_bytes=VMEM_LIMIT),
        cost_estimate=pl.CostEstimate(flops=2 * total * width * (hidden + width), bytes_accessed=20 << 20, transcendentals=0),
    )(dinner, dfeed, hat1, inv1, w_in, w_out, gain1)


def attention_grad(qkv, probs, mixed, dmixed):
    rows, length, width = mixed.shape
    pairs = width // 128
    scale = (width // HEADS) ** -0.5

    def body(q_ref, k_ref, v_ref, p_ref, m_ref, d_ref, dq_ref, dk_ref, dv_ref, bq_ref, bv_ref):
        @pl.when(pl.program_id(1) == 0)
        def _():
            bq_ref[...] = jnp.zeros_like(bq_ref)
            bv_ref[...] = jnp.zeros_like(bv_ref)

        lane = lax.broadcasted_iota(jnp.int32, (1, 128), 1)
        first = lane < 64
        q, k, v, d = q_ref[0], k_ref[0], v_ref[0], d_ref[0]
        product = d.astype(F32) * m_ref[0].astype(F32)
        q_t, d_t = q.T, d.T
        dqs, dks, dvs = [], [], []
        for h in range(2):
            on = first if h == 0 else jnp.logical_not(first)
            delta = jnp.sum(jnp.where(on, product, 0.0), axis=-1, keepdims=True)
            dprobs = row_dot_t(jnp.where(on, d, jnp.zeros_like(d)), v)
            p = p_ref[0, 0, h]
            ds = (p.astype(F32) * (dprobs - delta)).astype(BF)
            dqs.append(row_dot(ds, k))
            half = slice(h * 64, (h + 1) * 64)
            dks.append(row_dot(q_t[half], ds))
            dvs.append(row_dot(d_t[half], p))
        dq = (jnp.where(first, dqs[0], dqs[1]) * scale).astype(BF)
        dk = jnp.concatenate(dks, axis=0).T.astype(BF)
        dv = jnp.concatenate(dvs, axis=0).T.astype(BF)
        dq_ref[0] = dq
        dk_ref[0] = dk
        dv_ref[0] = dv
        bq_ref[...] += jnp.sum(dq.astype(F32), axis=0, keepdims=True)
        bv_ref[...] += jnp.sum(dv.astype(F32), axis=0, keepdims=True)

    def cols(base):
        return pl.BlockSpec((1, length, 128), lambda p, r: (r, 0, base + p))

    vec = pl.BlockSpec((1, 128), lambda p, r: (0, p))
    out = jax.ShapeDtypeStruct((rows, length, width), BF)
    one = jax.ShapeDtypeStruct((1, width), F32)
    return pl.pallas_call(
        body,
        name="attention_grad",
        out_shape=[out, out, out, one, one],
        grid=(pairs, rows),
        in_specs=[cols(0), cols(pairs), cols(2 * pairs), pl.BlockSpec((1, 1, 2, length, length), lambda p, r: (r, p, 0, 0, 0)), cols(0), cols(0)],
        out_specs=[cols(0), cols(0), cols(0), vec, vec],
        compiler_params=pltpu.CompilerParams(vmem_limit_bytes=VMEM_LIMIT),
        cost_estimate=pl.CostEstimate(flops=8 * rows * length * length * width, bytes_accessed=30 << 20, transcendentals=0),
    )(qkv, qkv, qkv, probs, mixed, dmixed)


def input_grad_call(dq, dk, dv, dpre, w_qkv):
    total, width = dpre.shape
    block = 256

    def body(q_ref, k_ref, v_ref, d_ref, w_ref, o_ref):
        total = d_ref[...].astype(F32)
        for n, ref in enumerate((q_ref, k_ref, v_ref)):
            total = total + row_dot_t(ref[...], w_ref[:, n * width : (n + 1) * width])
        o_ref[...] = total.astype(BF)

    rows = pl.BlockSpec((block, width), lambda i: (i, 0))
    return pl.pallas_call(
        body,
        name="input_grad",
        out_shape=jax.ShapeDtypeStruct((total, width), BF),
        grid=(total // block,),
        in_specs=[rows, rows, rows, rows, whole(w_qkv.shape)],
        out_specs=rows,
        compiler_params=pltpu.CompilerParams(vmem_limit_bytes=VMEM_LIMIT),
        cost_estimate=pl.CostEstimate(flops=6 * total * width * width, bytes_accessed=10 << 20, transcendentals=0),
    )(dq, dk, dv, dpre, w_qkv)


def swap(value):
    return lax.ppermute(value, "seq", [(0, 1), (1, 0)])


def pick(value, index, axis):
    return lax.dynamic_index_in_dim(value, index, axis, keepdims=False)


def reduce_stages(part, order, dp_bits, dp):
    me = lax.axis_index("dp")
    n_halving = dp_bits - 2
    shape = part.shape[1:]
    current = part.reshape((2,) * dp_bits + shape)
    left = list(range(dp_bits - 1, -1, -1))
    for bit in order[:n_halving]:
        axis = left.index(bit)
        mine = (me >> bit) & 1
        pairs = [(i, i ^ (1 << bit)) for i in range(dp)]
        send = pick(current, 1 - mine, axis).astype(BF)
        got = lax.ppermute(send, "dp", pairs)
        keep = pick(current, mine, axis)
        current = (keep.astype(F32) + got.astype(F32)).astype(BF)
        left.remove(bit)
    high, low = left
    group = (((me >> high) & 1) << 1) | ((me >> low) & 1)
    current = current.reshape((4,) + shape)
    total = pick(current, group, 0).astype(F32)
    for other in (1, 2, 3):
        flip = ((other >> 1) << high) | ((other & 1) << low)
        pairs = [(i, i ^ flip) for i in range(dp)]
        send = pick(current, group ^ other, 0).astype(BF)
        total = total + lax.ppermute(send, "dp", pairs).astype(F32)
    return total


def reduce_scatter(grad, order, dp, dp_bits):
    core = lax.axis_index("seq")
    rows = grad.shape[0] // (2 * dp)
    blocks = grad.reshape(dp, 2, rows, grad.shape[1])
    send = pick(blocks, 1 - core, 1).astype(BF)
    keep = pick(blocks, core, 1)
    part = (keep.astype(F32) + swap(send).astype(F32)).astype(BF)
    return reduce_stages(part, order, dp_bits, dp)


def on_device(tokens, lengths, w_qkv, w_out, w_in, w_back, bias_q, value_bias, bias_out, gain1, shift1, bias_in, bias_back, gain2, shift2, cotangent):
    rows_local, half, width = tokens.shape
    dp = lax.axis_size("dp")
    dp_bits = dp.bit_length() - 1
    core = lax.axis_index("seq")
    rows = rows_local // 2
    length = 2 * half
    total = rows * length
    order_a = (0, 1) + tuple(range(2, dp_bits))
    order_b = (1, 0) + tuple(range(2, dp_bits))

    def send_rows(value):
        return swap(lax.dynamic_slice_in_dim(value, (1 - core) * rows, rows, 0))

    other = send_rows(tokens)
    cot_other = send_rows(cotangent)
    vectors = [v.reshape(1, -1) for v in (bias_q, value_bias, bias_out, gain1, shift1, bias_in, bias_back, gain2, shift2)]
    (qkv, probs, mixed, low, hat1, inv1, act, slope, output, output_other, cls_own, dfeed, g_gain2, g_shift2, g_bias_back) = forward_call(
        core.reshape(1).astype(jnp.int32), lengths, tokens, other, cotangent, cot_other, (w_qkv, w_out, w_in, w_back), vectors
    )

    def flat(value):
        return value.reshape(total, value.shape[-1])

    g_back = weight_grad(flat(act), flat(dfeed), 512, width, "grad_back")
    r_back = reduce_scatter(g_back, order_a, dp, dp_bits)
    dinner, g_bias_in = inner_grad(flat(dfeed), flat(slope), w_back)
    g_in = weight_grad(flat(low), dinner, width, 512, "grad_in")
    r_in = reduce_scatter(g_in, order_b, dp, dp_bits)
    dpre1, dmixed, g_gain1, g_shift1, g_bias_out = branch_grad(dinner, flat(dfeed), flat(hat1), flat(inv1), w_in, w_out, vectors[3])
    g_out = weight_grad(flat(mixed), dpre1, width, width, "grad_out")
    r_out = reduce_scatter(g_out, order_a, dp, dp_bits)
    dq, dk, dv, g_bias_q, g_bias_v = attention_grad(qkv, probs, mixed, dmixed.reshape(rows, length, width))

    own_first = tokens_global = None
    own = lax.dynamic_slice_in_dim(tokens, core * rows, rows, 0)
    front = jnp.where(core == 0, own, other)
    rear = jnp.where(core == 0, other, own)
    full_tokens = jnp.concatenate([front, rear], axis=1).reshape(total, width)
    g_parts = [weight_grad(full_tokens, flat(d), width, width, "grad_qkv") for d in (dq, dk, dv)]
    g_qkv = jnp.concatenate(g_parts, axis=1)
    vector_parts = [g_bias_q, g_bias_v, g_bias_out, g_gain1, g_shift1, g_bias_in, g_bias_back, g_gain2, g_shift2]
    joined = jnp.concatenate([v.reshape(-1) for v in vector_parts]).reshape(2 * dp, 1, -1)
    n_vec = joined.shape[-1]
    joined = jnp.pad(joined, ((0, 0), (0, 7), (0, g_qkv.shape[1] - n_vec))).astype(BF)
    joined = jnp.concatenate([g_qkv.reshape(2 * dp, -1, g_qkv.shape[1]), joined], axis=1)
    r_qkv = reduce_scatter(joined.reshape(-1, g_qkv.shape[1]), order_b, dp, dp_bits)
    r_vec = r_qkv[-8, :n_vec]
    r_qkv = r_qkv[:-8]
    dinput = input_grad_call(flat(dq), flat(dk), flat(dv), dpre1, w_qkv).reshape(rows, length, width)

    out_got = swap(output_other)
    output = lax.dynamic_update_slice_in_dim(output, out_got, (1 - core) * rows, 0)
    count = lengths.shape[1]
    cls_own = cls_own[:, :count]
    cls_got = swap(cls_own)
    cls = jnp.where(core == 0, jnp.concatenate([cls_own, cls_got], axis=0), jnp.concatenate([cls_got, cls_own], axis=0))
    in_own = lax.dynamic_slice_in_dim(dinput, core * half, half, 1)
    in_got = swap(lax.dynamic_slice_in_dim(dinput, (1 - core) * half, half, 1))
    input_grad = jnp.where(core == 0, jnp.concatenate([in_own, in_got], axis=0), jnp.concatenate([in_got, in_own], axis=0))
    return (
        output,
        cls,
        input_grad,
        r_qkv.reshape(-1),
        r_out.reshape(-1),
        r_in.reshape(-1),
        r_back.reshape(-1),
        r_vec,
    )


def solution(mesh):
    row = P("dp", "seq", None)
    both = P(("dp", "seq"))
    return jax.shard_map(
        on_device,
        mesh=mesh,
        in_specs=(row, P("dp", None)) + (P(),) * 13 + (row,),
        out_specs=(row, P("dp", None, None), row, both, both, both, both, both),
        check_vma=False,
    )
```

time: 480 us -> 325 us (0.68)
  matrix products: 174 us -> 0 us
  Pallas kernels: 0 us -> 156 us
  local copies, waits for them, and re-layouts: 113 us -> 28.1 us
  other arithmetic: 67.4 us -> 20 us
    dot_general x18 -> x0, matrix products: 157 us -> none  [the longest x1 35.2 us: on_device(): inner = jnp.dot(normed_low, w_in, preferred_element_type=F32) + bias_in]
    pallas_call x0 -> x11, Pallas kernels: none -> 156 us  [the longest x1 64 us: forward_call(): pl.pallas_call(forward_kernel, name='forward_rows', out_shape=shapes, gri...]
    convert_element_type x23 -> x0, local copies, waits for them, and re-layouts: 32.2 us -> none  [the longest x4 13.1 us: reduce_scatter(): send = pick(blocks, 1 - core, 1).astype(BF)]
    convert_element_type x3 -> x12, other arithmetic: 34 us -> 11.3 us  [the longest x4 9.76 us: reduce_scatter(): part = (keep.astype(F32) + swap(send).astype(F32)).astype(BF)]
    unnamed x138 -> x68, local copies, waits for them, and re-layouts: 27 us -> 5.74 us
    reshape x8 -> x9, local copies, waits for them, and re-layouts: 25 us -> 4.78 us  [the longest x8 4.67 us: on_device(): v.reshape(1, -1)]
    sub x1 -> x0, matrix products: 16.4 us -> none  [on_device(): weight = jnp.exp(masked - jnp.max(masked, axis=-1, keepdims=True))]
    reduce_sum x8 -> x0, other arithmetic: 13.5 us -> none  [the longest x1 3.92 us: on_device(): g_bias_back = jnp.sum(dfeed.astype(F32), axis=0)]
  transfers between devices with their start and end apart: 29 -> 29, of which waited for: 14 -> 11; matrix products, arithmetic and copies ran while one was open for 15% -> 12% of each run, Pallas kernels for 0% -> 25%
where the time goes in v2:
time: 325 us; the launch traced here: 324 us
  Pallas kernels  156 us (48%)
  waiting for transfers between devices  82.4 us (25%)
  starting transfers between devices  36.3 us (11%)
  local copies, waits for them, and re-layouts  28.1 us (9%)
  other arithmetic  20 us (6%)
    pallas_call x1, Pallas kernels, forward_call(): pl.pallas_call(forward_kernel, name='forward_rows', out_shape=shapes, gri...  64 us
    ppermute x8, waiting for transfers between devices, reduce_stages(): got = lax.ppermute(send, 'dp', pairs)  56.4 us
    pallas_call x6, Pallas kernels, weight_grad(): pl.pallas_call(body, name=name, out_shape=jax.ShapeDtypeStruct((m, n), BF...  37.6 us
    ppermute x12, starting transfers between devices, reduce_stages(): total = total + lax.ppermute(send, 'dp', pairs).astype(F32)  24.1 us
    ppermute x12, waiting for transfers between devices, reduce_stages(): total = total + lax.ppermute(send, 'dp', pairs).astype(F32)  21.9 us
    pallas_call x1, Pallas kernels, attention_grad(): pl.pallas_call(body, name='attention_grad', out_shape=[out, out, out, one...  18.8 us
    pallas_call x1, Pallas kernels, branch_grad(): pl.pallas_call(body, name='branch_grad', out_shape=[jax.ShapeDtypeStruct(...  15 us
    pallas_call x1, Pallas kernels, inner_grad(): pl.pallas_call(body, name='inner_grad', out_shape=[jax.ShapeDtypeStruct((...  11.7 us
  transfers between devices with their start and end apart: 29, of which 11 were waited for; matrix products, arithmetic and copies ran while one was open for 12% of the time, Pallas kernels for 25%

profile of v2, /device:TPU:0, one launch (start us, length us, event | category | flops | bytes accessed | tf_op | source)
XLA Modules:
  0.0 323.6 jit_solution(15409897683866695931)
XLA Ops:
  9.6 64.0 %forward_rows.1 = (bf16[2,512,2304]{2,1,0:T(8,128)(2,1)}, bf16[2,6,2,512,512]{4,3,2,1,0:T(8,128)(2,1)}, bf16[2,512,768]{2,1,0:T(8,128)(2,1)}, bf16[2,512,768]{2,...) custom-call(s32[1]{0:T(128)} %bitcast.core_ref, ...), custom_call_target="tpu_custom_call" | custom-call | flops 16106127360 | bytes 52428800 | tf_op jit(solution)/shard_map/forward_rows/pallas_call | solution.py:220
  73.7 10.0 %grad_back.1 = bf16[3072,768]{1,0:T(8,128)(2,1)} custom-call(bf16[1024,3072]{1,0:T(8,128)(2,1)} %bitcast.175, bf16[1024,768]{1,0:T(8,128)(2,1)} %bitcast.178), custom_call_target="tpu_custom_call" | custom-call | flops 4831838208 | bytes 12582912 | tf_op jit(solution)/shard_map/grad_back/pallas_call | solution.py:256
  83.7 3.2 dynamic-slice_bitcast_fusion
  87.3 11.7 %inner_grad.1 = (bf16[1024,3072]{1,0:T(8,128)(2,1)}, f32[1,3072]{1,0:T(1,128)}) custom-call(bf16[1024,768]{1,0:T(8,128)(2,1)} %bitcast.179, bf16[1024,3072]{1,0:T(8,128)(2,1)} %bitcast.174, bf16[3072,768]{1,0:T(8,128)(2,1)} %w_ref.2), custom_call_target="tpu_custom_call" | custom-call | flops 4831838208 | bytes 20971520 | tf_op jit(solution)/shard_map/inner_grad/pallas_call | solution.py:279
  99.0 15.0 %branch_grad.1 = (bf16[1024,768]{1,0:T(8,128)(2,1)}, bf16[1024,768]{1,0:T(8,128)(2,1)}, f32[1,768]{1,0:T(1,128)}, f32[1,768]{1,0:T(1,128)}, f32[1,768]{1,0:T(1,128)}) custom-call(bf16[1024,3072]{1,0:T(8,128)(2,1)} %get-tuple-element.43.i_ref.r_ref, bf16[1024,768]{1,0:T(8,128)(2,1)} %bitcast.180, bf16[1024,768]{1,0:T(8,128)(2,1)} %bitcast.177, ...), custom_call_target="tpu_custom_call" | custom-call | flops 6039797760 | bytes 20971520 | tf_op jit(solution)/shard_map/branch_grad/pallas_call | solution.py:318
  114.1 4.3 %grad_out.1 = bf16[768,768]{1,0:T(8,128)(2,1)} custom-call(bf16[1024,768]{1,0:T(8,128)(2,1)} %bitcast.154, bf16[1024,768]{1,0:T(8,128)(2,1)} %get-tuple-element.50.d_ref.r_ref), custom_call_target="tpu_custom_call" | custom-call | flops 1207959552 | bytes 4325376 | tf_op jit(solution)/shard_map/grad_out/pallas_call | solution.py:256
  120.6 18.8 %attention_grad.1 = (bf16[2,512,768]{2,1,0:T(8,128)(2,1)}, bf16[2,512,768]{2,1,0:T(8,128)(2,1)}, bf16[2,512,768]{2,1,0:T(8,128)(2,1)}, f32[1,768]{1,0:T(1,128)}, f32[1,768]{1,0:T(1,128)}) custom-call(bf16[2,512,2304]{2,1,0:T(8,128)(2,1)} %get-tuple-element.38.q_ref.k_ref.v_ref, bf16[2,512,2304]{2,1,0:T(8,128)(2,1)} %get-tuple-element.38.q_ref.k_ref.v_ref, ...), custom_call_target="tpu_custom_call" | custom-call | flops 3221225472 | bytes 31457280 | tf_op jit(solution)/shard_map/attention_grad/pallas_call | solution.py:372
  143.6 4.3 %grad_qkv.3 = bf16[768,768]{1,0:T(8,128)(2,1)} custom-call(bf16[1024,768]{1,0:T(8,128)(2,1)} %bitcast.157, bf16[1024,768]{1,0:T(8,128)(2,1)} %bitcast.167), custom_call_target="tpu_custom_call" | custom-call | flops 1207959552 | bytes 4325376 | tf_op jit(solution)/shard_map/grad_qkv/pallas_call | solution.py:256
  147.9 4.4 %grad_qkv.4 = bf16[768,768]{1,0:T(8,128)(2,1)} custom-call(bf16[1024,768]{1,0:T(8,128)(2,1)} %bitcast.158, bf16[1024,768]{1,0:T(8,128)(2,1)} %bitcast.169), custom_call_target="tpu_custom_call" | custom-call | flops 1207959552 | bytes 4325376 | tf_op jit(solution)/shard_map/grad_qkv/pallas_call | solution.py:256
  152.3 4.3 %grad_qkv.5 = bf16[768,768]{1,0:T(8,128)(2,1)} custom-call(bf16[1024,768]{1,0:T(8,128)(2,1)} %bitcast.159, bf16[1024,768]{1,0:T(8,128)(2,1)} %bitcast.171), custom_call_target="tpu_custom_call" | custom-call | flops 1207959552 | bytes 4325376 | tf_op jit(solution)/shard_map/grad_qkv/pallas_call | solution.py:256
  160.9 10.3 %grad_in.1 = bf16[768,3072]{1,0:T(8,128)(2,1)} custom-call(bf16[1024,768]{1,0:T(8,128)(2,1)} %bitcast.176, bf16[1024,3072]{1,0:T(8,128)(2,1)} %get-tuple-element.43.i_ref.r_ref), custom_call_target="tpu_custom_call" | custom-call | flops 4831838208 | bytes 12582912 | tf_op jit(solution)/shard_map/grad_in/pallas_call | solution.py:256
  177.1 8.5 %input_grad.1 = bf16[1024,768]{1,0:T(8,128)(2,1)} custom-call(bf16[1024,768]{1,0:T(8,128)(2,1)} %bitcast.168, bf16[1024,768]{1,0:T(8,128)(2,1)} %bitcast.170, bf16[1024,768]{1,0:T(8,128)(2,1)} %bitcast.172, bf16[1024,768]{1,0:T(8,128)(2,1)} %get-tuple-element.50.d_ref.r_ref, bf16[768,2304]{1,0:T(8,128)(2,1)} %w_ref.3), custom_call_target="tpu_custom_call" | custom-call | flops 3623878656 | bytes 10485760 | tf_op jit(solution)/shard_map/input_grad/pallas_call | solution.py:395
  188.4 4.1 %collective-permute-done.3 = bf16[2,6,768]{2,1,0:T(8,128)(2,1)S(1)} collective-permute-done((bf16[2,6,768]{2,1,0:T(8,128)(2,1)S(1)}, bf16[2,6,768]{2,1,0:T(8,128)(2,1)S(1)}, u32[]{:S(2)}, u32[]{:S(2)}) %collective-permute-start.3) | collective-permute-done | bytes 18464 | tf_op jit(solution)/shard_map/ppermute | solution.py:408
  194.0 3.3 %dynamic-slice_bitcast_fusion.1 = bf16[16,24,3072]{2,1,0:T(8,128)(2,1)} fusion(bf16[16,2,24,3072]{3,2,1,0:T(8,128)(2,1)} %bitcast.142, s32[]{:T(128)S(6)} %select_n.130), kind=kLoop, calls=%fused_computation.22 | loop fusion | bytes 4718596 | tf_op jit(solution)/shard_map/jit(dynamic_index_in_dim)/squeeze | solution.py:412
  206.8 3.0 collective-permute-done.16
  212.0 3.1 fusion
  224.1 17.9 %collective-permute-done.24 = bf16[2,2,2,96,768]{4,3,2,1,0:T(8,128)(2,1)S(1)} collective-permute-done((bf16[2,2,2,96,768]{4,3,2,1,0:T(8,128)(2,1)S(1)}, bf16[2,2,2,96,768]{4,3,2,1,0:T(8,128)(2,1)S(1)}, u32[]{:S(2)}, u32[]{:S(2)}) %collective-permute-start.24) | collective-permute-done | bytes 1179680 | tf_op jit(solution)/shard_map/ppermute | solution.py:426
  243.9 4.3 %collective-permute-done.6 = bf16[2,2,2,32,2304]{4,3,2,1,0:T(8,128)(2,1)S(1)} collective-permute-done((bf16[2,2,2,32,2304]{4,3,2,1,0:T(8,128)(2,1)S(1)}, bf16[2,2,2,32,2304]{4,3,2,1,0:T(8,128)(2,1)S(1)}, u32[]{:S(2)}, u32[]{:S(2)}) %collective-permute-start.6) | collective-permute-done | bytes 1179680 | tf_op jit(solution)/shard_map/ppermute | solution.py:426
  249.1 24.3 %collective-permute-done.18 = bf16[2,2,2,24,3072]{4,3,2,1,0:T(8,128)(2,1)S(1)} collective-permute-done((bf16[2,2,2,24,3072]{4,3,2,1,0:T(8,128)(2,1)S(1)}, bf16[2,2,2,24,3072]{4,3,2,1,0:T(8,128)(2,1)S(1)}, u32[]{:S(2)}, u32[]{:S(2)}) %collective-permute-start.18) | collective-permute-done | bytes 1179680 | tf_op jit(solution)/shard_map/ppermute | solution.py:426
  274.5 9.4 %collective-permute-done.25 = bf16[2,2,96,768]{3,2,1,0:T(8,128)(2,1)S(1)} collective-permute-done((bf16[2,2,96,768]{3,2,1,0:T(8,128)(2,1)S(1)}, bf16[2,2,96,768]{3,2,1,0:T(8,128)(2,1)S(1)}, u32[]{:S(2)}, u32[]{:S(2)}) %collective-permute-start.25) | collective-permute-done | bytes 589856 | tf_op jit(solution)/shard_map/ppermute | solution.py:426
  291.1 5.5 %collective-permute-done.10 = bf16[32,2304]{1,0:T(8,128)(2,1)S(1)} collective-permute-done((bf16[32,2304]{1,0:T(8,128)(2,1)S(1)}, bf16[32,2304]{1,0:T(8,128)(2,1)S(1)}, u32[]{:S(2)}, u32[]{:S(2)}) %collective-permute-start.10) | collective-permute-done | bytes 147488 | tf_op jit(solution)/shard_map/ppermute | solution.py:438
  298.8 8.5 %collective-permute-start.20 = (bf16[24,3072]{1,0:T(8,128)(2,1)S(1)}, bf16[24,3072]{1,0:T(8,128)(2,1)S(1)}, u32[]{:S(2)}, u32[]{:S(2)}) collective-permute-start(bf16[24,3072]{1,0:T(8,128)(2,1)S(1)} %get-tuple-element.85), channel_id=1, source_target_pairs={{0,8},{2,10},{4,12},{6,14},{8,0},{10,2},{12,4},{14,6},{16,24},{18,... | collective-permute-start | bytes 442376 | tf_op jit(solution)/shard_map/ppermute | solution.py:438
  307.4 5.6 %collective-permute-done.9 = bf16[32,2304]{1,0:T(8,128)(2,1)S(1)} collective-permute-done((bf16[32,2304]{1,0:T(8,128)(2,1)S(1)}, bf16[32,2304]{1,0:T(8,128)(2,1)S(1)}, u32[]{:S(2)}, u32[]{:S(2)}) %collective-permute-start.9) | collective-permute-done | bytes 147488 | tf_op jit(solution)/shard_map/ppermute | solution.py:438
  315.0 7.0 %collective-permute-done.21 = bf16[24,3072]{1,0:T(8,128)(2,1)S(1)} collective-permute-done((bf16[24,3072]{1,0:T(8,128)(2,1)S(1)}, bf16[24,3072]{1,0:T(8,128)(2,1)S(1)}, u32[]{:S(2)}, u32[]{:S(2)}) %collective-permute-start.21) | collective-permute-done | bytes 147488 | tf_op jit(solution)/shard_map/ppermute | solution.py:438
  (178 shorter events, 67.5 us)
Async XLA Ops:
  1.9 6.5 %collective-permute-start = (bf16[2,256,768]{2,1,0:T(8,128)(2,1)S(1)}, bf16[2,256,768]{2,1,0:T(8,128)(2,1)S(1)}, u32[]{:S(2)}, u32[]{:S(2)}) collective-permute-start(bf16[2,256,768]{2,1,0:T(8,128)(2,1)S(1)} %constant_dynamic-slice_fusion.3), channel_id=1, source_target_pairs={{0,1},{1,0},{2,3},{3,2},{4,5},{5,4},{6,7},{7,6},{8,9},{9,8},{10,11... | collective-permute-start | bytes 2359304 | tf_op jit(solution)/shard_map/ppermute | solution.py:408
  86.9 125.1 %collective-permute-start.23 = (bf16[16,96,768]{2,1,0:T(8,128)(2,1)}, bf16[16,96,768]{2,1,0:T(8,128)(2,1)}, u32[]{:S(2)}, u32[]{:S(2)}) collective-permute-start(bf16[16,96,768]{2,1,0:T(8,128)(2,1)} %dynamic-slice_bitcast_fusion), channel_id=1, source_target_pairs={{0,1},{1,0},{2,3},{3,2},{4,5},{5,4},{6,7},{7,6},{8,9},{9,8},{10,11... | collective-permute-start | bytes 7077896 | tf_op jit(solution)/shard_map/ppermute | solution.py:408
  120.3 50.9 %collective-permute-start.11 = (bf16[16,24,768]{2,1,0:T(8,128)(2,1)}, bf16[16,24,768]{2,1,0:T(8,128)(2,1)}, u32[]{:S(2)}, u32[]{:S(2)}) collective-permute-start(bf16[16,24,768]{2,1,0:T(8,128)(2,1)} %dynamic-slice_bitcast_fusion.7), channel_id=1, source_target_pairs={{0,1},{1,0},{2,3},{3,2},{4,5},{5,4},{6,7},{7,6},{8,9},{9,8},{10,11... | collective-permute-start | bytes 1769480 | tf_op jit(solution)/shard_map/ppermute | solution.py:408
  174.2 13.7 %collective-permute-start.12 = (bf16[2,2,2,24,768]{4,3,2,1,0:T(8,128)(2,1)}, bf16[2,2,2,24,768]{4,3,2,1,0:T(8,128)(2,1)S(1)}, u32[]{:S(2)}, u32[]{:S(2)}) collective-permute-start(bf16[2,2,2,24,768]{4,3,2,1,0:T(8,128)(2,1)} %dynamic-slice_bitcast_fusion.9), channel_id=1, source_target_pairs={{0,2},{2,0},{4,6},{6,4},{8,10},{10,8},{12,14},{14,12},{16,18},{18,... | collective-permute-start | bytes 884744 | tf_op jit(solution)/shard_map/ppermute | solution.py:426
  185.6 30.2 %collective-permute-start.5 = (bf16[16,32,2304]{2,1,0:T(8,128)(2,1)}, bf16[16,32,2304]{2,1,0:T(8,128)(2,1)}, u32[]{:S(2)}, u32[]{:S(2)}) collective-permute-start(bf16[16,32,2304]{2,1,0:T(8,128)(2,1)} %fusion.4), channel_id=1, source_target_pairs={{0,1},{1,0},{2,3},{3,2},{4,5},{5,4},{6,7},{7,6},{8,9},{9,8},{10,11... | collective-permute-start | bytes 7077896 | tf_op jit(solution)/shard_map/ppermute | solution.py:408
  187.2 11.2 %collective-permute-start.4 = (bf16[2,256,768]{2,1,0:T(8,128)(2,1)S(1)}, bf16[2,256,768]{2,1,0:T(8,128)(2,1)S(1)}, u32[]{:S(2)}, u32[]{:S(2)}) collective-permute-start(bf16[2,256,768]{2,1,0:T(8,128)(2,1)S(1)} %get-tuple-element.81), channel_id=1, source_target_pairs={{0,1},{1,0},{2,3},{3,2},{4,5},{5,4},{6,7},{7,6},{8,9},{9,8},{10,11... | collective-permute-start | bytes 2359304 | tf_op jit(solution)/shard_map/ppermute | solution.py:408
  187.7 13.8 %collective-permute-start.2 = (bf16[2,256,768]{2,1,0:T(8,128)(2,1)S(1)}, bf16[2,256,768]{2,1,0:T(8,128)(2,1)S(1)}, u32[]{:S(2)}, u32[]{:S(2)}) collective-permute-start(bf16[2,256,768]{2,1,0:T(8,128)(2,1)S(1)} %copy-done.25), channel_id=1, source_target_pairs={{0,1},{1,0},{2,3},{3,2},{4,5},{5,4},{6,7},{7,6},{8,9},{9,8},{10,11... | collective-permute-start | bytes 2359304 | tf_op jit(solution)/shard_map/ppermute | solution.py:408
  192.5 5.9 %collective-permute-start.13 = (bf16[2,2,24,768]{3,2,1,0:T(8,128)(2,1)S(1)}, bf16[2,2,24,768]{3,2,1,0:T(8,128)(2,1)S(1)}, u32[]{:S(2)}, u32[]{:S(2)}) collective-permute-start(bf16[2,2,24,768]{3,2,1,0:T(8,128)(2,1)S(1)} %dynamic-slice_bitcast_fusion.16), channel_id=1, source_target_pairs={{0,4},{2,6},{4,0},{6,2},{8,12},{10,14},{12,8},{14,10},{16,20},{18,... | collective-permute-start | bytes 442376 | tf_op jit(solution)/shard_map/ppermute | solution.py:426
  198.4 22.4 %collective-permute-start.17 = (bf16[16,24,3072]{2,1,0:T(8,128)(2,1)}, bf16[16,24,3072]{2,1,0:T(8,128)(2,1)}, u32[]{:S(2)}, u32[]{:S(2)}) collective-permute-start(bf16[16,24,3072]{2,1,0:T(8,128)(2,1)} %dynamic-slice_bitcast_fusion.1), channel_id=1, source_target_pairs={{0,1},{1,0},{2,3},{3,2},{4,5},{5,4},{6,7},{7,6},{8,9},{9,8},{10,11... | collective-permute-start | bytes 7077896 | tf_op jit(solution)/shard_map/ppermute | solution.py:408
  215.2 26.7 %collective-permute-start.24 = (bf16[2,2,2,96,768]{4,3,2,1,0:T(8,128)(2,1)S(1)}, bf16[2,2,2,96,768]{4,3,2,1,0:T(8,128)(2,1)S(1)}, u32[]{:S(2)}, u32[]{:S(2)}) collective-permute-start(bf16[2,2,2,96,768]{4,3,2,1,0:T(8,128)(2,1)S(1)} %dynamic-slice_bitcast_fusion.2), channel_id=1, source_target_pairs={{0,2},{2,0},{4,6},{6,4},{8,10},{10,8},{12,14},{14,12},{16,18},{18,... | collective-permute-start | bytes 3538952 | tf_op jit(solution)/shard_map/ppermute | solution.py:426
  219.2 29.0 %collective-permute-start.6 = (bf16[2,2,2,32,2304]{4,3,2,1,0:T(8,128)(2,1)S(1)}, bf16[2,2,2,32,2304]{4,3,2,1,0:T(8,128)(2,1)S(1)}, u32[]{:S(2)}, u32[]{:S(2)}) collective-permute-start(bf16[2,2,2,32,2304]{4,3,2,1,0:T(8,128)(2,1)S(1)} %dynamic-slice_bitcast_fusion.4), channel_id=1, source_target_pairs={{0,4},{2,6},{4,0},{6,2},{8,12},{10,14},{12,8},{14,10},{16,20},{18,... | collective-permute-start | bytes 3538952 | tf_op jit(solution)/shard_map/ppermute | solution.py:426
  223.5 50.0 %collective-permute-start.18 = (bf16[2,2,2,24,3072]{4,3,2,1,0:T(8,128)(2,1)S(1)}, bf16[2,2,2,24,3072]{4,3,2,1,0:T(8,128)(2,1)S(1)}, u32[]{:S(2)}, u32[]{:S(2)}) collective-permute-start(bf16[2,2,2,24,3072]{4,3,2,1,0:T(8,128)(2,1)S(1)} %dynamic-slice_bitcast_fusion.3), channel_id=1, source_target_pairs={{0,4},{2,6},{4,0},{6,2},{8,12},{10,14},{12,8},{14,10},{16,20},{18,... | collective-permute-start | bytes 3538952 | tf_op jit(solution)/shard_map/ppermute | solution.py:426
  242.3 41.6 %collective-permute-start.25 = (bf16[2,2,96,768]{3,2,1,0:T(8,128)(2,1)S(1)}, bf16[2,2,96,768]{3,2,1,0:T(8,128)(2,1)S(1)}, u32[]{:S(2)}, u32[]{:S(2)}) collective-permute-start(bf16[2,2,96,768]{3,2,1,0:T(8,128)(2,1)S(1)} %dynamic-slice_bitcast_fusion.5), channel_id=1, source_target_pairs={{0,4},{2,6},{4,0},{6,2},{8,12},{10,14},{12,8},{14,10},{16,20},{18,... | collective-permute-start | bytes 1769480 | tf_op jit(solution)/shard_map/ppermute | solution.py:426
  248.5 37.7 %collective-permute-start.7 = (bf16[2,2,32,2304]{3,2,1,0:T(8,128)(2,1)S(1)}, bf16[2,2,32,2304]{3,2,1,0:T(8,128)(2,1)S(1)}, u32[]{:S(2)}, u32[]{:S(2)}) collective-permute-start(bf16[2,2,32,2304]{3,2,1,0:T(8,128)(2,1)S(1)} %dynamic-slice_bitcast_fusion.8), channel_id=1, source_target_pairs={{0,2},{2,0},{4,6},{6,4},{8,10},{10,8},{12,14},{14,12},{16,18},{18,... | collective-permute-start | bytes 1769480 | tf_op jit(solution)/shard_map/ppermute | solution.py:426
  273.9 14.9 %collective-permute-start.19 = (bf16[2,2,24,3072]{3,2,1,0:T(8,128)(2,1)S(1)}, bf16[2,2,24,3072]{3,2,1,0:T(8,128)(2,1)S(1)}, u32[]{:S(2)}, u32[]{:S(2)}) collective-permute-start(bf16[2,2,24,3072]{3,2,1,0:T(8,128)(2,1)S(1)} %dynamic-slice_bitcast_fusion.6), channel_id=1, source_target_pairs={{0,2},{2,0},{4,6},{6,4},{8,10},{10,8},{12,14},{14,12},{16,18},{18,... | collective-permute-start | bytes 1769480 | tf_op jit(solution)/shard_map/ppermute | solution.py:426
  284.1 29.0 %collective-permute-start.26 = (bf16[96,768]{1,0:T(8,128)(2,1)S(1)}, bf16[96,768]{1,0:T(8,128)(2,1)S(1)}, u32[]{:S(2)}, u32[]{:S(2)}) collective-permute-start(bf16[96,768]{1,0:T(8,128)(2,1)S(1)} %get-tuple-element.82), channel_id=1, source_target_pairs={{0,8},{2,10},{4,12},{6,14},{8,0},{10,2},{12,4},{14,6},{16,24},{18,... | collective-permute-start | bytes 442376 | tf_op jit(solution)/shard_map/ppermute | solution.py:438
  284.2 29.4 %collective-permute-start.27 = (bf16[96,768]{1,0:T(8,128)(2,1)S(1)}, bf16[96,768]{1,0:T(8,128)(2,1)S(1)}, u32[]{:S(2)}, u32[]{:S(2)}) collective-permute-start(bf16[96,768]{1,0:T(8,128)(2,1)S(1)} %get-tuple-element.84), channel_id=1, source_target_pairs={{0,16},{2,18},{4,20},{6,22},{8,24},{10,26},{12,28},{14,30},{16,0},... | collective-permute-start | bytes 442376 | tf_op jit(solution)/shard_map/ppermute | solution.py:438
  286.4 10.2 %collective-permute-start.10 = (bf16[32,2304]{1,0:T(8,128)(2,1)S(1)}, bf16[32,2304]{1,0:T(8,128)(2,1)S(1)}, u32[]{:S(2)}, u32[]{:S(2)}) collective-permute-start(bf16[32,2304]{1,0:T(8,128)(2,1)S(1)} %get-tuple-element.89), channel_id=1, source_target_pairs={{0,24},{2,26},{4,28},{6,30},{8,16},{10,18},{12,20},{14,22},{16,8},... | collective-permute-start | bytes 442376 | tf_op jit(solution)/shard_map/ppermute | solution.py:438
  288.8 10.0 %collective-permute-start.8 = (bf16[32,2304]{1,0:T(8,128)(2,1)S(1)}, bf16[32,2304]{1,0:T(8,128)(2,1)S(1)}, u32[]{:S(2)}, u32[]{:S(2)}) collective-permute-start(bf16[32,2304]{1,0:T(8,128)(2,1)S(1)} %get-tuple-element.88), channel_id=1, source_target_pairs={{0,8},{2,10},{4,12},{6,14},{8,0},{10,2},{12,4},{14,6},{16,24},{18,... | collective-permute-start | bytes 442376 | tf_op jit(solution)/shard_map/ppermute | solution.py:438
  288.8 24.1 %collective-permute-start.9 = (bf16[32,2304]{1,0:T(8,128)(2,1)S(1)}, bf16[32,2304]{1,0:T(8,128)(2,1)S(1)}, u32[]{:S(2)}, u32[]{:S(2)}) collective-permute-start(bf16[32,2304]{1,0:T(8,128)(2,1)S(1)} %get-tuple-element.90), channel_id=1, source_target_pairs={{0,16},{2,18},{4,20},{6,22},{8,24},{10,26},{12,28},{14,30},{16,0},... | collective-permute-start | bytes 442376 | tf_op jit(solution)/shard_map/ppermute | solution.py:438
  296.6 17.0 %collective-permute-start.28 = (bf16[96,768]{1,0:T(8,128)(2,1)S(1)}, bf16[96,768]{1,0:T(8,128)(2,1)S(1)}, u32[]{:S(2)}, u32[]{:S(2)}) collective-permute-start(bf16[96,768]{1,0:T(8,128)(2,1)S(1)} %get-tuple-element.83), channel_id=1, source_target_pairs={{0,24},{2,26},{4,28},{6,30},{8,16},{10,18},{12,20},{14,22},{16,8},... | collective-permute-start | bytes 442376 | tf_op jit(solution)/shard_map/ppermute | solution.py:438
  298.8 16.2 %collective-permute-start.20 = (bf16[24,3072]{1,0:T(8,128)(2,1)S(1)}, bf16[24,3072]{1,0:T(8,128)(2,1)S(1)}, u32[]{:S(2)}, u32[]{:S(2)}) collective-permute-start(bf16[24,3072]{1,0:T(8,128)(2,1)S(1)} %get-tuple-element.85), channel_id=1, source_target_pairs={{0,8},{2,10},{4,12},{6,14},{8,0},{10,2},{12,4},{14,6},{16,24},{18,... | collective-permute-start | bytes 442376 | tf_op jit(solution)/shard_map/ppermute | solution.py:438
  313.0 9.1 %collective-permute-start.21 = (bf16[24,3072]{1,0:T(8,128)(2,1)S(1)}, bf16[24,3072]{1,0:T(8,128)(2,1)S(1)}, u32[]{:S(2)}, u32[]{:S(2)}) collective-permute-start(bf16[24,3072]{1,0:T(8,128)(2,1)S(1)} %get-tuple-element.87), channel_id=1, source_target_pairs={{0,16},{2,18},{4,20},{6,22},{8,24},{10,26},{12,28},{14,30},{16,0},... | collective-permute-start | bytes 442376 | tf_op jit(solution)/shard_map/ppermute | solution.py:438
  313.1 9.0 %collective-permute-start.22 = (bf16[24,3072]{1,0:T(8,128)(2,1)S(1)}, bf16[24,3072]{1,0:T(8,128)(2,1)S(1)}, u32[]{:S(2)}, u32[]{:S(2)}) collective-permute-start(bf16[24,3072]{1,0:T(8,128)(2,1)S(1)} %get-tuple-element.86), channel_id=1, source_target_pairs={{0,24},{2,26},{4,28},{6,30},{8,16},{10,18},{12,20},{14,22},{16,8},... | collective-permute-start | bytes 442376 | tf_op jit(solution)/shard_map/ppermute | solution.py:438
  (34 other events, 219.8 us)

commit v3 on v1

v3 whole, which is shorter than its diff:
```python
from functools import partial

import jax
import jax.numpy as jnp
from jax import lax
from jax.experimental import pallas as pl
from jax.experimental.pallas import tpu as pltpu
from jax.sharding import PartitionSpec as P

HEADS = 12
EPS = 1e-12
BF = jnp.bfloat16
F32 = jnp.float32
VMEM_LIMIT = 60 << 20
RSQRT2 = 0.7071067811865476
RSQRT2PI = 0.3989422804014327


def row_dot(left, right):
    return lax.dot_general(left, right, (((1,), (0,)), ((), ())), preferred_element_type=F32)


def row_dot_t(left, right):
    return lax.dot_general(left, right, (((1,), (1,)), ((), ())), preferred_element_type=F32)


def col_dot(left, right):
    return lax.dot_general(left, right, (((0,), (0,)), ((), ())), preferred_element_type=F32)


def gelu_pair(value):
    expo = jnp.exp(value * value * -0.5)
    phi = 0.5 + 0.5 * lax.erf(value * RSQRT2)
    return value * phi, phi + value * expo * RSQRT2PI


def whole(shape):
    return pl.BlockSpec(shape, lambda *_: (0,) * len(shape))


ANY = pl.BlockSpec(memory_space=pl.ANY)
HBM = pl.BlockSpec(memory_space=pltpu.HBM)


def params(mib):
    return pltpu.CompilerParams(vmem_limit_bytes=mib << 20)


def row_starts(len_ref, row):
    starts = [jnp.int32(0)]
    for j in range(len_ref.shape[1] - 1):
        starts.append(starts[-1] + len_ref[row, j])
    return starts


def attention_kernel(
    core_ref, len_ref, own_ref, other_ref, wqkv_hbm, wout_hbm, bq_ref, bv_ref, bo_ref, g1_ref, s1_ref,
    qkv_hbm, probs_hbm, x_ref, mixed_ref, low_ref, hat1_ref, inv1_ref, scale_ref,
    bias_ref, qkv_ref, wqkv_ref, wout_ref, p_ref, w_sem, p_sem, q_sem,
):
    step = pl.program_id(0)
    core = core_ref[0]
    rows = pl.num_programs(0)
    half, width = own_ref.shape[1:]
    length = 2 * half
    pairs = width // 128
    parts = [slice(n * width, (n + 1) * width) for n in range(3)]
    copies = [pltpu.make_async_copy(wqkv_hbm.at[:, part], wqkv_ref.at[:, part], w_sem.at[n]) for n, part in enumerate(parts)]
    copies.append(pltpu.make_async_copy(wout_hbm, wout_ref, w_sem.at[3]))

    @pl.when(step == 0)
    def _():
        for copy in copies:
            copy.start()

    x_ref[0, pl.ds(pl.multiple_of(core * half, half), half), :] = own_ref[0]
    x_ref[0, pl.ds(pl.multiple_of((1 - core) * half, half), half), :] = other_ref[0]
    starts = row_starts(len_ref, core * rows + step)
    down = lax.broadcasted_iota(jnp.int32, (length, 1), 0)
    across = lax.broadcasted_iota(jnp.int32, (1, length), 1)
    seg_down = jnp.zeros((length, 1), jnp.int32)
    seg_across = jnp.zeros((1, length), jnp.int32)
    for start in starts[1:]:
        seg_down += (down >= start).astype(jnp.int32)
        seg_across += (across >= start).astype(jnp.int32)
    bias_ref[...] = jnp.where(seg_down == seg_across, 0.0, -1e30)

    for n, part in enumerate(parts):
        @pl.when(step == 0)
        def _():
            copies[n].wait()

        value = row_dot(x_ref[0], wqkv_ref[:, part])
        if n == 0:
            value = (value + bq_ref[...]) * (width // HEADS) ** -0.5
        if n == 2:
            value = value + bv_ref[...]
        qkv_ref[:, part] = value.astype(BF)
    save = pltpu.make_async_copy(qkv_ref, qkv_hbm.at[step], q_sem)
    save.start()

    first = lax.broadcasted_iota(jnp.int32, (1, 128), 1) < 64

    def pair_body(pair, carry):
        slot = lax.rem(pair, 2)
        out_copy = pltpu.make_async_copy(p_ref.at[slot], probs_hbm.at[step, pair], p_sem.at[slot])

        @pl.when(pair >= 2)
        def _():
            out_copy.wait()

        at = pl.ds(pl.multiple_of(pair * 128, 128), 128)
        q_pair = qkv_ref[:, at]
        k_pair = qkv_ref[:, pl.ds(pl.multiple_of(width + pair * 128, 128), 128)]
        v_pair = qkv_ref[:, pl.ds(pl.multiple_of(2 * width + pair * 128, 128), 128)]
        outs = []
        for h in range(2):
            on = first if h == 0 else jnp.logical_not(first)
            s = row_dot_t(jnp.where(on, q_pair, jnp.zeros_like(q_pair)), k_pair) + bias_ref[...]
            e = jnp.exp(s - jnp.max(s, axis=-1, keepdims=True)).astype(BF)
            p_ref[slot, h] = e
            outs.append(row_dot(e, jnp.where(on, v_pair, jnp.ones_like(v_pair))))
        sums = pltpu.roll(jnp.where(first, outs[1], outs[0]), 64, 1)
        inverse = 1.0 / sums
        scale_ref[0, :, at] = inverse
        mixed_ref[0, :, at] = (jnp.where(first, outs[0], outs[1]) * inverse).astype(BF)
        out_copy.start()
        return carry

    lax.fori_loop(0, pairs, pair_body, 0)
    for tail in (pairs - 2, pairs - 1):
        pltpu.make_async_copy(p_ref.at[tail % 2], probs_hbm.at[step, tail], p_sem.at[tail % 2]).wait()

    @pl.when(step == 0)
    def _():
        copies[3].wait()

    pre = x_ref[0].astype(F32) + row_dot(mixed_ref[0], wout_ref[...]) + bo_ref[...]
    center = pre - jnp.mean(pre, axis=-1, keepdims=True)
    inv = lax.rsqrt(jnp.mean(center * center, axis=-1, keepdims=True) + EPS)
    hat = center * inv
    hat1_ref[0] = hat.astype(BF)
    inv1_ref[0] = inv
    low_ref[0] = (hat * g1_ref[...] + s1_ref[...]).astype(BF)
    save.wait()


def attention_call(core, lengths, tokens, other, w_qkv, w_out, vectors):
    rows_local, half, width = tokens.shape
    rows = rows_local // 2
    length = 2 * half
    pairs = width // 128

    def full(n):
        return pl.BlockSpec((1, length, n), lambda r, *_: (r, 0, 0))

    def row(n, kind=BF):
        return jax.ShapeDtypeStruct((rows, length, n), kind)

    return pl.pallas_call(
        attention_kernel,
        name="attention_rows",
        out_shape=[
            row(3 * width), jax.ShapeDtypeStruct((rows, pairs, 2, length, length), BF), row(width), row(width), row(width), row(width),
            row(1, F32), row(width, F32),
        ],
        grid_spec=pltpu.PrefetchScalarGridSpec(
            num_scalar_prefetch=2,
            grid=(rows,),
            in_specs=[
                pl.BlockSpec((1, half, width), lambda r, core, lens: (core[0] * rows + r, 0, 0)),
                pl.BlockSpec((1, half, width), lambda r, *_: (r, 0, 0)),
                ANY,
                ANY,
            ]
            + [whole(v.shape) for v in vectors],
            out_specs=[HBM, HBM] + [full(width)] * 4 + [full(1), full(width)],
            scratch_shapes=[
                pltpu.VMEM((length, length), F32),
                pltpu.VMEM((length, 3 * width), BF),
                pltpu.VMEM(w_qkv.shape, BF),
                pltpu.VMEM(w_out.shape, BF),
                pltpu.VMEM((2, 2, length, length), BF),
                pltpu.SemaphoreType.DMA((4,)),
                pltpu.SemaphoreType.DMA((2,)),
                pltpu.SemaphoreType.DMA,
            ],
        ),
        compiler_params=params(54),
        cost_estimate=pl.CostEstimate(
            flops=8 * rows * length * width * width + 4 * rows * length * length * width,
            bytes_accessed=35 << 20,
            transcendentals=rows * HEADS * length * length,
        ),
    )(core, lengths, tokens, other, w_qkv, w_out, *vectors)


def feed_forward_kernel(
    split, rows, core_ref, len_ref, low_ref, win_ref, wback_ref, bi_ref, bb_ref, g2_ref, s2_ref, cot_hbm, cot_other_hbm,
    slope_ref, out_hbm, other_hbm, cls_ref, dfeed_ref, gg_ref, gs_ref, gb_ref, *rest
):
    if split:
        keep_ref, send_ref, act_ref, acc_ref, cot_ref, out_ref, grad_ref, c_sem, o_sem = rest
    else:
        act_hbm, act_ref, acc_ref, cot_ref, out_ref, c_sem, o_sem = rest
    step = pl.program_id(0)
    core = core_ref[0]
    total, width = low_ref.shape
    group, length = cot_ref.shape[:2]
    half = length // 2
    own_at = pl.ds(pl.multiple_of(core * half, half), half)
    other_at = pl.ds(pl.multiple_of((1 - core) * half, half), half)
    chunk = win_ref.shape[1]
    chunks = act_ref.shape[1] // chunk
    loads, stores = [], []
    for r in range(group):
        loads.append(pltpu.make_async_copy(cot_hbm.at[core * group + r], cot_ref.at[r, own_at], c_sem.at[r]))
        loads.append(pltpu.make_async_copy(cot_other_hbm.at[r], cot_ref.at[r, other_at], c_sem.at[group + r]))
        stores.append(pltpu.make_async_copy(out_ref.at[r, other_at], other_hbm.at[r], o_sem.at[group + r]))
        stores.append(pltpu.make_async_copy(out_ref.at[r, own_at], out_hbm.at[core * group + r], o_sem.at[r]))

    @pl.when(step == 0)
    def _():
        for load in loads:
            load.start()

    @pl.when(step < chunks)
    def _():
        base = pl.multiple_of(step * chunk, chunk)
        piece = 256
        for n in range(chunk // piece):
            cols = slice(n * piece, (n + 1) * piece)
            inner = row_dot(low_ref[...], win_ref[:, cols]) + bi_ref[:, cols]
            act, slope = gelu_pair(inner)
            act_ref[:, pl.ds(base + n * piece, piece)] = act.astype(BF)
            slope_ref[:, cols] = slope.astype(BF)
        value = row_dot(act_ref[:, pl.ds(base, chunk)], wback_ref[...])

        @pl.when(step == 0)
        def _():
            acc_ref[...] = value + bb_ref[...]

        @pl.when(step > 0)
        def _():
            acc_ref[...] += value

    @pl.when(step == chunks - 1)
    def _():
        for load in loads:
            load.wait()
        gg_ref[...] = jnp.zeros_like(gg_ref)
        gs_ref[...] = jnp.zeros_like(gs_ref)
        gb_ref[...] = jnp.zeros_like(gb_ref)
        block = 256
        per = length // block

        def token_body(i, carry):
            at = pl.ds(pl.multiple_of(i * block, block), block)
            row = lax.div(i, per)
            inside = pl.ds(pl.multiple_of(lax.rem(i, per) * block, block), block)
            pre = low_ref[at, :].astype(F32) + acc_ref[at, :]
            center = pre - jnp.mean(pre, axis=-1, keepdims=True)
            inv = lax.rsqrt(jnp.mean(center * center, axis=-1, keepdims=True) + EPS)
            hat = center * inv
            out_ref[row, inside, :] = (hat * g2_ref[...] + s2_ref[...]).astype(BF)
            dy = cot_ref[row, inside, :].astype(F32)
            gg_ref[...] += jnp.sum(dy * hat, axis=0, keepdims=True)
            gs_ref[...] += jnp.sum(dy, axis=0, keepdims=True)
            g = dy * g2_ref[...]
            dpre = inv * (g - jnp.mean(g, axis=-1, keepdims=True) - hat * jnp.mean(g * hat, axis=-1, keepdims=True))
            dfeed = dpre.astype(BF)
            dfeed_ref[at, :] = dfeed
            gb_ref[...] += jnp.sum(dfeed.astype(F32), axis=0, keepdims=True)
            return carry

        lax.fori_loop(0, total // block, token_body, 0)
        for store in stores:
            store.start()
        which = lax.broadcasted_iota(jnp.int32, (8, 1), 0)
        across = lax.broadcasted_iota(jnp.int32, (1, length), 1)
        for r in range(group):
            down = jnp.full((8, 1), -1, jnp.int32)
            for j, start in enumerate(row_starts(len_ref, core * group + r)):
                down = jnp.where(which == j, start, down)
            cls_ref[r] = row_dot((down == across).astype(F32).astype(BF), out_ref[r]).astype(BF)
        if not split:
            save = pltpu.make_async_copy(act_ref, act_hbm, o_sem.at[2 * group])
            save.start()
            save.wait()
            for store in stores:
                store.wait()

    if split:
        @pl.when(step >= chunks)
        def _():
            at = pl.ds(pl.multiple_of((step - chunks) * grad_ref.shape[0], 128), grad_ref.shape[0])
            grad_ref[...] = col_dot(act_ref[:, at], dfeed_ref[...])
            split_store(grad_ref, keep_ref, send_ref, core, rows, width // LANES)

        @pl.when(step == pl.num_programs(0) - 1)
        def _():
            for store in stores:
                store.wait()


def feed_forward_call(core, lengths, low, w_in, w_back, vectors, cot, cot_other, dp, split):
    total, width = low.shape
    rows_local, half, _ = cot.shape
    group = rows_local // 2
    length = 2 * half
    hidden = w_in.shape[1]
    chunk = width
    chunks = hidden // chunk
    rows = hidden // (2 * dp)
    bias_in, bias_back, gain2, shift2 = vectors

    def at(j):
        return jnp.minimum(j, chunks - 1)

    one = jax.ShapeDtypeStruct((1, width), F32)
    shapes = [
        jax.ShapeDtypeStruct((total, hidden), BF),
        jax.ShapeDtypeStruct(cot.shape, BF),
        jax.ShapeDtypeStruct(cot_other.shape, BF),
        jax.ShapeDtypeStruct((group, 8, width), BF),
        jax.ShapeDtypeStruct((total, width), BF),
        one,
        one,
        one,
    ]
    specs = [pl.BlockSpec((total, chunk), lambda j, *_: (0, at(j))), HBM, HBM, whole((group, 8, width)), whole((total, width))] + [whole((1, width))] * 3
    scratch = [
        pltpu.VMEM((total, hidden), BF),
        pltpu.VMEM((total, width), F32),
        pltpu.VMEM((group, length, width), BF),
        pltpu.VMEM((group, length, width), BF),
    ]
    if split:
        devices = 4
        half_shape = jax.ShapeDtypeStruct((width // LANES, dp, rows, LANES), BF)
        half_spec = pl.BlockSpec((width // LANES, devices, rows, LANES), lambda j, *_: (0, jnp.maximum(j - chunks, 0), 0, 0))
        shapes += [half_shape] * 2
        specs += [half_spec] * 2
        scratch.append(pltpu.VMEM((devices * 2 * rows, width), F32))
        steps = chunks + dp // devices
    else:
        shapes.append(jax.ShapeDtypeStruct((total, hidden), BF))
        specs.append(HBM)
        steps = chunks
    scratch += [pltpu.SemaphoreType.DMA((2 * group,)), pltpu.SemaphoreType.DMA((2 * group + 1,))]
    return pl.pallas_call(
        partial(feed_forward_kernel, split, rows),
        name="feed_forward",
        out_shape=shapes,
        grid_spec=pltpu.PrefetchScalarGridSpec(
            num_scalar_prefetch=2,
            grid=(steps,),
            in_specs=[
                whole((total, width)),
                pl.BlockSpec((width, chunk), lambda j, *_: (0, at(j))),
                pl.BlockSpec((chunk, width), lambda j, *_: (at(j), 0)),
                pl.BlockSpec((1, chunk), lambda j, *_: (0, at(j))),
                whole((width,)),
                whole((width,)),
                whole((width,)),
                ANY,
                ANY,
            ],
            out_specs=specs,
            scratch_shapes=scratch,
        ),
        compiler_params=params(57),
        cost_estimate=pl.CostEstimate(flops=6 * total * width * hidden, bytes_accessed=30 << 20, transcendentals=2 * total * hidden),
    )(core, lengths, low, w_in, w_back, bias_in, bias_back, gain2, shift2, cot, cot_other)


def weight_grad(left, right, block_m, block_n, name):
    total, m = left.shape
    n = right.shape[1]

    def body(l_ref, r_ref, o_ref, t_ref):
        @pl.when(pl.program_id(1) == 0)
        def _():
            t_ref[...] = l_ref[...].T

        o_ref[...] = row_dot(t_ref[...], r_ref[...]).astype(BF)

    return pl.pallas_call(
        body,
        name=name,
        out_shape=jax.ShapeDtypeStruct((m, n), BF),
        grid=(m // block_m, n // block_n),
        in_specs=[pl.BlockSpec((total, block_m), lambda i, j: (0, i)), pl.BlockSpec((total, block_n), lambda i, j: (0, j))],
        out_specs=pl.BlockSpec((block_m, block_n), lambda i, j: (i, j)),
        scratch_shapes=[pltpu.VMEM((block_m, total), BF)],
        compiler_params=params(60),
        cost_estimate=pl.CostEstimate(flops=2 * total * m * n, bytes_accessed=2 * (total * (m + n) + m * n), transcendentals=0),
    )(left, right)


def branch_grad(core, dfeed, slope, low, mixed, hat1, inv1, w_in, w_back, w_out, gain1, dp, split):
    total, width = dfeed.shape
    hidden = slope.shape[1]
    chunk = width
    chunks = hidden // chunk
    steps = chunks + (1 if split else 0)
    rows = width // (2 * dp)

    def body(core_ref, f_ref, s_ref, l_ref, m_ref, h_ref, v_ref, wb_ref, wi_ref, wo_ref, g_ref, branch_ref, mixed_ref, gi_ref, gg_ref, gs_ref, gb_ref, *rest):
        step = pl.program_id(0)
        if split:
            keep_ref, send_ref, acc_ref, inner_ref, grad_ref = rest
        else:
            inner_ref, acc_ref = rest

        @pl.when(step < chunks)
        def _():
            inner = (row_dot_t(f_ref[...], wb_ref[...]) * s_ref[...].astype(F32)).astype(BF)
            inner_ref[...] = inner
            gi_ref[...] = jnp.sum(inner.astype(F32), axis=0, keepdims=True)
            value = row_dot_t(inner_ref[...], wi_ref[...])

            @pl.when(step == 0)
            def _():
                acc_ref[...] = value

            @pl.when(step > 0)
            def _():
                acc_ref[...] += value

            if split:
                grad_ref[...] = col_dot(l_ref[...], inner_ref[...])
                split_store(grad_ref, keep_ref, send_ref, core_ref[0], rows, 2)

        @pl.when(step == chunks - 1)
        def _():
            gg_ref[...] = jnp.zeros_like(gg_ref)
            gs_ref[...] = jnp.zeros_like(gs_ref)
            gb_ref[...] = jnp.zeros_like(gb_ref)
            block = 256

            def token_body(i, carry):
                at = pl.ds(pl.multiple_of(i * block, block), block)
                dn = f_ref[at, :].astype(F32) + acc_ref[at, :]
                hat = h_ref[at, :].astype(F32)
                gg_ref[...] += jnp.sum(dn * hat, axis=0, keepdims=True)
                gs_ref[...] += jnp.sum(dn, axis=0, keepdims=True)
                g = dn * g_ref[...]
                dpre = v_ref[at, :] * (g - jnp.mean(g, axis=-1, keepdims=True) - hat * jnp.mean(g * hat, axis=-1, keepdims=True))
                branch = dpre.astype(BF)
                branch_ref[at, :] = branch
                gb_ref[...] += jnp.sum(branch.astype(F32), axis=0, keepdims=True)
                return carry

            lax.fori_loop(0, total // block, token_body, 0)
            mixed_ref[...] = row_dot_t(branch_ref[...], wo_ref[...]).astype(BF)

        if split:
            @pl.when(step == chunks)
            def _():
                grad_ref[...] = col_dot(m_ref[...], branch_ref[...])
                split_store(grad_ref, keep_ref, send_ref, core_ref[0], rows, 2)

    def at(j):
        return jnp.minimum(j, chunks - 1)

    one = jax.ShapeDtypeStruct((1, width), F32)
    row = jax.ShapeDtypeStruct((total, width), BF)
    shapes = [row, row, jax.ShapeDtypeStruct((1, hidden), F32), one, one, one]
    specs = [whole((total, width))] * 2 + [pl.BlockSpec((1, chunk), lambda j, *_: (0, at(j)))] + [whole((1, width))] * 3
    scratch = [pltpu.VMEM((total, width), F32)]
    if split:
        shapes += [jax.ShapeDtypeStruct((2 * steps, dp, rows, LANES), BF)] * 2
        specs += [pl.BlockSpec((2, dp, rows, LANES), lambda j, *_: (j, 0, 0, 0))] * 2
        scratch += [pltpu.VMEM((total, chunk), BF), pltpu.VMEM((width, chunk), F32)]
    else:
        shapes.append(jax.ShapeDtypeStruct((total, hidden), BF))
        specs.append(pl.BlockSpec((total, chunk), lambda j, *_: (0, at(j))))
    return pl.pallas_call(
        body,
        name="branch_grad",
        out_shape=shapes,
        grid_spec=pltpu.PrefetchScalarGridSpec(
            num_scalar_prefetch=1,
            grid=(steps,),
            in_specs=[
                whole((total, width)),
                pl.BlockSpec((total, chunk), lambda j, *_: (0, at(j))),
                whole((total, width)),
                whole((total, width)),
                whole((total, width)),
                whole((total, 1)),
                pl.BlockSpec((chunk, width), lambda j, *_: (at(j), 0)),
                pl.BlockSpec((width, chunk), lambda j, *_: (0, at(j))),
                whole(w_out.shape),
                whole(gain1.shape),
            ],
            out_specs=specs,
            scratch_shapes=scratch,
        ),
        compiler_params=params(52),
        cost_estimate=pl.CostEstimate(flops=2 * total * width * (3 * hidden + width), bytes_accessed=30 << 20, transcendentals=0),
    )(core, dfeed, slope, low, mixed, hat1, inv1, w_back, w_in, w_out, gain1)


def attention_grad(qkv, probs, mixed, dmixed, inverse, lower, count, partial_out=None):
    rows, length, width = mixed.shape
    pairs = width // 128
    scale = (width // HEADS) ** -0.5

    def body(q_ref, k_ref, v_ref, p_ref, m_ref, d_ref, i_ref, *rest):
        out_ref, bq_ref, bv_ref = rest[-3:]

        @pl.when(pl.program_id(1) == 0)
        def _():
            bq_ref[...] = jnp.zeros_like(bq_ref)
            bv_ref[...] = jnp.zeros_like(bv_ref)

        lane = lax.broadcasted_iota(jnp.int32, (1, 128), 1)
        first = lane < 64
        q, k, v = q_ref[0], k_ref[0], v_ref[0]
        scaled = d_ref[0].astype(F32) * i_ref[0]
        d = scaled.astype(BF)
        product = scaled * m_ref[0].astype(F32)
        q_t, d_t, k_t = q.T, d.T, k.T
        dqs, dks, dvs = [], [], []
        for h in range(2):
            on = first if h == 0 else jnp.logical_not(first)
            delta = jnp.sum(jnp.where(on, product, 0.0), axis=-1, keepdims=True)
            dprobs = row_dot_t(jnp.where(on, d, jnp.zeros_like(d)), v)
            p = p_ref[0, 0, h]
            ds = (p.astype(F32) * (dprobs - delta)).astype(BF)
            half = slice(h * 64, (h + 1) * 64)
            dqs.append(row_dot_t(k_t[half], ds))
            dks.append(row_dot(q_t[half], ds))
            dvs.append(row_dot(d_t[half], p))
        dq = (jnp.concatenate(dqs, axis=0) * scale).T.astype(BF)
        dk = jnp.concatenate(dks, axis=0).T.astype(BF)
        dv = jnp.concatenate(dvs, axis=0).T.astype(BF)
        out_ref[0, 0] = dq
        out_ref[1, 0] = dk
        out_ref[2, 0] = dv
        bq_ref[...] += jnp.sum(dq.astype(F32), axis=0, keepdims=True)
        bv_ref[...] += jnp.sum(dv.astype(F32), axis=0, keepdims=True)

    def cols(base):
        return pl.BlockSpec((1, length, 128), lambda p, r: (lower + r, 0, base + p))

    vec = pl.BlockSpec((1, 128), lambda p, r: (0, p))
    out = jax.ShapeDtypeStruct((3, rows, length, width), BF)
    one = jax.ShapeDtypeStruct((1, width), F32)
    more = [] if partial_out is None else [partial_out]
    return pl.pallas_call(
        body,
        name="attention_grad",
        out_shape=[out, one, one],
        grid=(pairs, count),
        input_output_aliases={7: 0} if more else {},
        in_specs=[cols(0), cols(pairs), cols(2 * pairs), pl.BlockSpec((1, 1, 2, length, length), lambda p, r: (lower + r, p, 0, 0, 0)), cols(0), cols(0), cols(0)] + [ANY] * len(more),
        out_specs=[pl.BlockSpec((3, 1, length, 128), lambda p, r: (0, lower + r, 0, p)), vec, vec],
        compiler_params=params(32),
        cost_estimate=pl.CostEstimate(flops=8 * count * length * length * width, bytes_accessed=(15 * count) << 20, transcendentals=0),
    )(qkv, qkv, qkv, probs, mixed, dmixed, inverse, *more)


def input_grad_call(core, dproj, dpre, w_qkv, half):
    _, total, width = dproj.shape
    length = 2 * half
    group = total // length

    def body(core_ref, p_ref, d_ref, w_ref, own_hbm, other_hbm, acc_ref, out_ref, sem):
        step = pl.program_id(0)
        core = core_ref[0]
        value = row_dot_t(p_ref[0], w_ref[...])

        @pl.when(step == 0)
        def _():
            acc_ref[...] = value + d_ref[...].astype(F32)

        @pl.when(step == 1)
        def _():
            acc_ref[...] += value

        @pl.when(step == 2)
        def _():
            out_ref[...] = (acc_ref[...] + value).astype(BF)
            stores = []
            for r in range(group):
                other = pl.ds(pl.multiple_of(r * length + (1 - core) * half, half), half)
                own = pl.ds(pl.multiple_of(r * length + core * half, half), half)
                stores.append(pltpu.make_async_copy(out_ref.at[other], other_hbm.at[r], sem.at[r]))
                stores.append(pltpu.make_async_copy(out_ref.at[own], own_hbm.at[core * group + r], sem.at[group + r]))
            for store in stores:
                store.start()
            for store in stores:
                store.wait()

    return pl.pallas_call(
        body,
        name="input_grad",
        out_shape=[jax.ShapeDtypeStruct((2 * group, half, width), BF), jax.ShapeDtypeStruct((group, half, width), BF)],
        grid_spec=pltpu.PrefetchScalarGridSpec(
            num_scalar_prefetch=1,
            grid=(3,),
            in_specs=[
                pl.BlockSpec((1, total, width), lambda n, *_: (n, 0, 0)),
                whole((total, width)),
                pl.BlockSpec((width, width), lambda n, *_: (0, n)),
            ],
            out_specs=[HBM, HBM],
            scratch_shapes=[pltpu.VMEM((total, width), F32), pltpu.VMEM((total, width), BF), pltpu.SemaphoreType.DMA((2 * group,))],
        ),
        compiler_params=params(32),
        cost_estimate=pl.CostEstimate(flops=6 * total * width * width, bytes_accessed=10 << 20, transcendentals=0),
    )(core, dproj, dpre, w_qkv)


def vector_exchange(parts, devices):
    total = sum(p.shape[1] for p in parts)
    cut = total // devices
    stretch = cut
    while stretch % 128:
        stretch *= 2
    per = stretch // cut

    def body(*refs):
        *ins, out = refs
        joined = jnp.concatenate([ref[...] for ref in ins], axis=1)
        for d in range(devices // per):
            out[d * per : (d + 1) * per, :] = jnp.broadcast_to(joined[:, d * stretch : (d + 1) * stretch], (per, stretch))

    table = pl.pallas_call(
        body,
        name="vector_table",
        out_shape=jax.ShapeDtypeStruct((devices, stretch), F32),
        compiler_params=params(16),
    )(*parts)
    return jnp.sum(lax.all_to_all(table, ("dp", "seq"), 0, 0, tiled=True), axis=0)


def swap(value):
    return lax.ppermute(value, "seq", [(0, 1), (1, 0)])


def pick(value, index, axis):
    return lax.dynamic_index_in_dim(value, index, axis, keepdims=False)


def reduce_stages(part, order, dp_bits, dp):
    me = lax.axis_index("dp")
    n_halving = dp_bits - 2
    shape = part.shape[1:]
    current = part.reshape((2,) * dp_bits + shape)
    left = list(range(dp_bits - 1, -1, -1))
    for bit in order[:n_halving]:
        axis = left.index(bit)
        mine = (me >> bit) & 1
        pairs = [(i, i ^ (1 << bit)) for i in range(dp)]
        send = pick(current, 1 - mine, axis).astype(BF)
        got = lax.ppermute(send, "dp", pairs)
        keep = pick(current, mine, axis)
        current = (keep.astype(F32) + got.astype(F32)).astype(BF)
        left.remove(bit)
    high, low = left
    group = (((me >> high) & 1) << 1) | ((me >> low) & 1)
    current = current.reshape((4,) + shape)
    total = pick(current, group, 0).astype(F32)
    for other in (1, 2, 3):
        flip = ((other >> 1) << high) | ((other & 1) << low)
        pairs = [(i, i ^ flip) for i in range(dp)]
        send = pick(current, group ^ other, 0).astype(BF)
        total = total + lax.ppermute(send, "dp", pairs).astype(F32)
    return total


def reduce_scatter(grad, order, dp, dp_bits):
    core = lax.axis_index("seq")
    rows = grad.shape[0] // (2 * dp)
    blocks = grad.reshape(dp, 2, rows, grad.shape[1])
    send = pick(blocks, 1 - core, 1).astype(BF)
    keep = pick(blocks, core, 1)
    part = (keep.astype(F32) + swap(send).astype(F32)).astype(BF)
    return reduce_stages(part, order, dp_bits, dp)


LANES = 384


def split_store(acc_ref, keep_ref, send_ref, core, rows, parts):
    for d in range(acc_ref.shape[0] // (2 * rows)):
        for ref, side in ((keep_ref, core), (send_ref, 1 - core)):
            value = acc_ref[pl.ds(pl.multiple_of((2 * d + side) * rows, 8), rows), :].astype(BF)
            for c in range(parts):
                ref[c, d] = value[:, c * LANES : (c + 1) * LANES]


def grad_rows(core, left, right, dp, name):
    total, m = left.shape
    n = right.shape[1]
    rows = m // (2 * dp)
    group = 4
    block = group * 2 * rows

    def body(core_ref, l_ref, r_ref, keep_ref, send_ref, acc_ref):
        acc_ref[...] = col_dot(l_ref[...], r_ref[...])
        split_store(acc_ref, keep_ref, send_ref, core_ref[0], rows, n // LANES)

    out = jax.ShapeDtypeStruct((n // LANES, dp, rows, LANES), BF)
    out_spec = pl.BlockSpec((n // LANES, group, rows, LANES), lambda i, *_: (0, i, 0, 0))
    return pl.pallas_call(
        body,
        name=name,
        out_shape=[out, out],
        grid_spec=pltpu.PrefetchScalarGridSpec(
            num_scalar_prefetch=1,
            grid=(dp // group,),
            in_specs=[pl.BlockSpec((total, block), lambda i, *_: (0, i)), whole((total, n))],
            out_specs=[out_spec, out_spec],
            scratch_shapes=[pltpu.VMEM((block, n), F32)],
        ),
        compiler_params=params(60),
        cost_estimate=pl.CostEstimate(flops=2 * total * m * n, bytes_accessed=2 * (total * (m + n) + m * n), transcendentals=0),
    )(core, left, right)


def grad_columns(core, pairs, dp, name):
    counts = [(r.shape[0] if r.ndim == 3 else r.shape[1] // (2 * LANES)) for _, r in pairs]
    bases = [sum(counts[:i]) for i in range(len(counts))]
    blocks = sum(counts)
    total, m = pairs[0][0].shape
    rows = m // (2 * dp)
    n = 2 * LANES

    def body(core_ref, *refs):
        lefts = refs[: len(pairs)]
        rights = refs[len(pairs) : 2 * len(pairs)]
        keep_ref, send_ref, acc_ref = refs[2 * len(pairs) :]
        step = pl.program_id(0)
        for i, count in enumerate(counts):
            @pl.when(jnp.logical_and(step >= bases[i], step < bases[i] + count))
            def _():
                r = rights[i]
                value = r[0] if len(r.shape) == 3 else r[...]
                acc_ref[...] = col_dot(lefts[i][...], value)

        split_store(acc_ref, keep_ref, send_ref, core_ref[0], rows, 2)

    def right_spec(i, r):
        def at(j):
            return jnp.clip(j - bases[i], 0, counts[i] - 1)

        if r.ndim == 3:
            return pl.BlockSpec((1, total, n), lambda j, *_: (at(j), 0, 0))
        return pl.BlockSpec((total, n), lambda j, *_: (0, at(j)))

    out = jax.ShapeDtypeStruct((2 * blocks, dp, rows, LANES), BF)
    out_spec = pl.BlockSpec((2, dp, rows, LANES), lambda j, *_: (j, 0, 0, 0))
    return pl.pallas_call(
        body,
        name=name,
        out_shape=[out, out],
        grid_spec=pltpu.PrefetchScalarGridSpec(
            num_scalar_prefetch=1,
            grid=(blocks,),
            in_specs=[whole((total, m)) for _ in pairs] + [right_spec(i, r) for i, (_, r) in enumerate(pairs)],
            out_specs=[out_spec, out_spec],
            scratch_shapes=[pltpu.VMEM((m, n), F32)],
        ),
        compiler_params=params(32),
        cost_estimate=pl.CostEstimate(flops=2 * total * m * n * blocks, bytes_accessed=2 * blocks * n * (total + m), transcendentals=0),
    )(core, *[l for l, _ in pairs], *[r for _, r in pairs])


def add_pieces(where, inputs, outputs, pieces, piece_shape, name):
    count = len(pieces([jnp.int32(0)] * 3))

    def body(where_ref, *refs):
        ins = refs[: len(inputs)]
        outs = refs[len(inputs) : len(inputs) + len(outputs)]
        k_ref, g_ref, k_sem, g_sem, o_sem = refs[len(inputs) + len(outputs) :]
        table = pieces([where_ref[0], where_ref[1], where_ref[2]])
        loads, stores = [], []
        for i, (a, b, a_at, b_at, o, o_at) in enumerate(table):
            loads.append((pltpu.make_async_copy(ins[a].at[a_at], k_ref.at[i], k_sem.at[i]), pltpu.make_async_copy(ins[b].at[b_at], g_ref.at[i], g_sem.at[i])))
            stores.append(pltpu.make_async_copy(k_ref.at[i], outs[o].at[o_at], o_sem.at[i]))
        for pair in loads:
            pair[0].start()
            pair[1].start()
        for i in range(count):
            loads[i][0].wait()
            loads[i][1].wait()
            k_ref[i] = k_ref[i] + g_ref[i]
            stores[i].start()
        for store in stores:
            store.wait()

    return pl.pallas_call(
        body,
        name=name,
        out_shape=[jax.ShapeDtypeStruct(s, BF) for s in outputs],
        grid_spec=pltpu.PrefetchScalarGridSpec(
            num_scalar_prefetch=1,
            grid=(1,),
            in_specs=[ANY] * len(inputs),
            out_specs=[HBM] * len(outputs),
            scratch_shapes=[pltpu.VMEM((count,) + piece_shape, BF)] * 2 + [pltpu.SemaphoreType.DMA((count,))] * 3,
        ),
        compiler_params=params(16),
    )(where, *inputs)


def fold_first(where, keep, got, name):
    _, blocks, _, _, _, rows, lanes = keep.shape
    every = slice(None)

    def pieces(at):
        z_, y, x = at
        table = []
        for role in (1, 0):
            for z in range(4):
                ax = x if role == 0 else 1 - x
                ay = y if role == 0 else 1 - y
                for half, index in ((0, (0, every, z, every, ax)), (1, (1, every, z, ay))):
                    table.append((0, 1, index, index, 2 * half + (1 - role), (every, z)))
        return table

    shape = (blocks, 4, 2, rows, lanes)
    return add_pieces(where, (keep, got), [shape] * 4, pieces, (blocks, 2, rows, lanes), name)


def fold_second(where, keep_a, got_a, keep_b, got_b, name):
    blocks, _, _, rows, lanes = keep_a.shape
    every = slice(None)

    def pieces(at):
        z_, y, x = at
        table = []
        for role in (1, 0):
            for z in range(4):
                for half, own in ((0, y), (1, x)):
                    index = (every, z, own if role == 0 else 1 - own)
                    table.append((2 * half, 2 * half + 1, index, index, 2 * half + (1 - role), (every, z)))
        return table

    shape = (blocks, 4, rows, lanes)
    return add_pieces(where, (keep_a, got_a, keep_b, got_b), [shape] * 4, pieces, (blocks, rows, lanes), name)


def fold_third(where, keep_a, got_a, keep_b, got_b, name):
    blocks, _, rows, lanes = keep_a.shape
    every = slice(None)

    def pieces(at):
        z, y_, x_ = at
        table = []
        for flip in (1, 2, 3, 0):
            for half in range(2):
                index = (every, z ^ flip)
                table.append((2 * half, 2 * half + 1, index, index, flip, (half,)))
        return table

    shape = (2, blocks, rows, lanes)
    return add_pieces(where, (keep_a, got_a, keep_b, got_b), [shape] * 4, pieces, (blocks, rows, lanes), name)


def fold_last(parts, widths, name):
    _, blocks, rows, lanes = parts[0].shape

    def body(a_ref, b_ref, c_ref, d_ref, *outs):
        base = 0
        for out, width in zip(outs, widths):
            tiles = width // 128
            for t in range(tiles):
                column = base + t * 128
                chunk, at = column // lanes, column % lanes
                half, block = chunk // blocks, chunk % blocks
                total = None
                for ref in (a_ref, b_ref, c_ref, d_ref):
                    value = ref[half, block, :, at : at + 128].astype(F32)
                    total = value if total is None else total + value
                out[pl.ds(t, rows, stride=tiles), :] = total
            base += width

    return pl.pallas_call(
        body,
        name=name,
        out_shape=[jax.ShapeDtypeStruct((rows * w // 128, 128), F32) for w in widths],
        compiler_params=params(16),
    )(*parts)


def after(value, *earlier):
    return lax.optimization_barrier((value,) + earlier)[0]


def sync(*values):
    return lax.optimization_barrier(values)


def flip(value, bits):
    return lax.ppermute(value, "dp", [(i, i ^ bits) for i in range(16)])


def on_device(tokens, lengths, w_qkv, w_out, w_in, w_back, bias_q, value_bias, bias_out, gain1, shift1, bias_in, bias_back, gain2, shift2, cotangent):
    rows_local, half, width = tokens.shape
    dp = lax.axis_size("dp")
    dp_bits = dp.bit_length() - 1
    core = lax.axis_index("seq")
    rows = rows_local // 2
    length = 2 * half
    total = rows * length
    order_a = (0, 1) + tuple(range(2, dp_bits))
    order_b = (1, 0) + tuple(range(2, dp_bits))

    def send_rows(value):
        return swap(lax.dynamic_slice_in_dim(value, (1 - core) * rows, rows, 0))

    other = send_rows(tokens)
    cot_other = send_rows(cotangent)
    bq, bv, bo, g1, s1, bi, bb, g2, s2 = (bias_q, value_bias, bias_out, gain1, shift1, bias_in, bias_back, gain2, shift2)
    core_one = core.reshape(1).astype(jnp.int32)
    me = lax.axis_index("dp")
    fast = dp == 16 and width == 2 * LANES
    qkv, probs, full_tokens, mixed, low, hat1, inv1, inverse = attention_call(core_one, lengths, tokens, other, w_qkv, w_out, (bq, bv, bo, g1, s1))

    def flat(value):
        return value.reshape(total, value.shape[-1])

    full_tokens = flat(full_tokens)
    slope, output, output_other, cls_own, dfeed, g_gain2, g_shift2, g_bias_back, *rest = feed_forward_call(
        core_one, lengths, flat(low), w_in, w_back, (bi.reshape(1, -1), bb, g2, s2), cotangent, cot_other, dp, fast
    )
    pairs = width // 128
    output_got = swap(output_other)
    cls_own = cls_own[:, : lengths.shape[1]]
    cls_got = swap(cls_own)
    if fast:
        where = jnp.stack([me >> 2, (me >> 1) & 1, me & 1]).astype(jnp.int32)

        def view(value):
            return value.reshape((2, value.shape[0] // 2, 4, 2, 2) + value.shape[2:])

        def cross(parts, bit_a, bit_b):
            return flip(parts[0], bit_a), flip(parts[2], bit_b)

        def along_z(parts):
            return [parts[0]] + [flip(parts[f], 4 * f) for f in (1, 2, 3)]

        keep_b, send_b = rest
        got_b = swap(send_b)
        dpre1, dmixed, g_bias_in, g_gain1, g_shift1, g_bias_out, keep_i, send_i = branch_grad(
            core_one, dfeed, slope, flat(low), flat(mixed), flat(hat1), flat(inv1), w_in, w_back, w_out, g1, dp, True
        )
        send_i, keep_b, got_b, output_got, cls_got = sync(send_i, keep_b, got_b, output_got, cls_got)
        back = fold_first(where, view(keep_b), view(got_b), "back_1")
        dmixed, send_i, back = sync(dmixed, send_i, back)
        dmixed = dmixed.reshape(rows, length, width)
        got = cross(back, 1, 2)
        got_i = swap(send_i)
        dproj, *bias_a = attention_grad(qkv, probs, mixed, dmixed, inverse, 0, 1)
        dproj, got, got_i = sync(dproj, got, got_i)
        back = fold_second(where, back[1], got[0], back[3], got[1], "back_2")
        inner = fold_first(where, view(keep_i), view(got_i), "inner_1")
        dmixed, inner, back = sync(dmixed, inner, back)
        got = cross(back, 2, 1)
        got_i = cross(inner, 1, 2)
        dproj, *bias_b = attention_grad(qkv, probs, mixed, dmixed, inverse, 1, 1, dproj)
        dproj = dproj.reshape(3, total, width)
        keep_q, send_q = grad_columns(core_one, [(full_tokens, dproj)], dp, "grad_qkv")
        keep_q, send_q, got, got_i = sync(keep_q, send_q, got, got_i)
        got_q = swap(send_q)
        back = fold_third(where, back[1], got[0], back[3], got[1], "back_3")
        inner = fold_second(where, inner[1], got_i[0], inner[3], got_i[1], "inner_2")
        inner, back, got_q = sync(inner, back, got_q)
        proj = fold_first(where, view(keep_q), view(got_q), "proj_1")
        dproj, inner, proj, back = sync(dproj, inner, proj, back)
        got_q = cross(proj, 1, 2)
        got = cross(inner, 2, 1)
        back = along_z(back)
        dinput, dinput_other = input_grad_call(core_one, dproj, dpre1, w_qkv, half)
        dinput, dinput_other, got, got_q, back = sync(dinput, dinput_other, got, got_q, back)
        dinput_got = swap(dinput_other)
        proj = fold_second(where, proj[1], got_q[0], proj[3], got_q[1], "proj_2")
        inner = fold_third(where, inner[1], got[0], inner[3], got[1], "inner_3")
        proj, inner = sync(proj, inner)
        got_q = cross(proj, 2, 1)
        inner = along_z(inner)
        (r_back,) = fold_last(back, (width,), "back_4")
        g_bias_q, g_bias_v = bias_a[0] + bias_b[0], bias_a[1] + bias_b[1]
        vec_sum = vector_exchange((g_bias_q, g_bias_v, g_bias_out, g_gain1, g_shift1, g_bias_in, g_bias_back, g_gain2, g_shift2), 2 * dp)
        got_q, dinput_got = sync(got_q, dinput_got)
        proj = fold_third(where, proj[1], got_q[0], proj[3], got_q[1], "proj_3")
        proj, inner = sync(along_z(proj), inner)
        r_in, r_out = fold_last(inner, (w_in.shape[1], width), "inner_4")
        (r_qkv,) = fold_last(proj, (3 * width,), "proj_4")
    else:
        (act,) = rest
        g_back = weight_grad(act, dfeed, 512, width, "grad_back")
        r_back = reduce_scatter(g_back, order_a, dp, dp_bits)
        dpre1, dmixed, g_bias_in, g_gain1, g_shift1, g_bias_out, dinner = branch_grad(
            core_one, dfeed, slope, flat(low), flat(mixed), flat(hat1), flat(inv1), w_in, w_back, w_out, g1, dp, False
        )
        g_in = weight_grad(flat(low), dinner, width, 512, "grad_in")
        r_in = reduce_scatter(g_in, order_b, dp, dp_bits)
        g_out = weight_grad(flat(mixed), dpre1, width, width, "grad_out")
        r_out = reduce_scatter(g_out, order_a, dp, dp_bits)
        dproj, g_bias_q, g_bias_v = attention_grad(qkv, probs, mixed, dmixed.reshape(rows, length, width), inverse, 0, rows)
        dproj = dproj.reshape(3, total, width)
        g_qkv = jnp.concatenate([weight_grad(full_tokens, dproj[n], width, width, "grad_qkv") for n in range(3)], axis=1)
        r_qkv = reduce_scatter(g_qkv, order_b, dp, dp_bits)
        dinput, dinput_other = input_grad_call(core_one, dproj, dpre1, w_qkv, half)
        dinput_got = swap(dinput_other)
    if not fast:
        vec_sum = vector_exchange((g_bias_q, g_bias_v, g_bias_out, g_gain1, g_shift1, g_bias_in, g_bias_back, g_gain2, g_shift2), 2 * dp)
    n_vec = (8 * width + w_in.shape[1]) // (2 * dp)
    per = vec_sum.shape[0] // n_vec
    r_vec = lax.dynamic_slice_in_dim(vec_sum, lax.rem(2 * me + core, per) * n_vec, n_vec, 0)

    output = lax.dynamic_update_slice_in_dim(output, output_got, (1 - core) * rows, 0)
    cls = jnp.where(core == 0, jnp.concatenate([cls_own, cls_got], axis=0), jnp.concatenate([cls_got, cls_own], axis=0))
    input_grad = lax.dynamic_update_slice_in_dim(dinput, dinput_got, (1 - core) * rows, 0)
    return (
        output,
        cls,
        input_grad,
        r_qkv.reshape(-1),
        r_out.reshape(-1),
        r_in.reshape(-1),
        r_back.reshape(-1),
        r_vec,
    )


def solution(mesh):
    row = P("dp", "seq", None)
    both = P(("dp", "seq"))
    return jax.shard_map(
        on_device,
        mesh=mesh,
        in_specs=(row, P("dp", None)) + (P(),) * 13 + (row,),
        out_specs=(row, P("dp", None, None), row, both, both, both, both, both),
        check_vma=False,
    )
```

time: 480 us -> 244 us (0.51); the launches traced: 475 us -> 244 us
  matrix products: 174 us -> 0 us
  Pallas kernels: 0 us -> 164 us
  local copies, waits for them, and re-layouts: 113 us -> 12 us
  other arithmetic: 67.4 us -> 1.63 us
  waiting for transfers between devices: 82.4 us -> 28.2 us
    pallas_call x0 -> x20, Pallas kernels: none -> 164 us  [the longest x1 33.5 us: feed_forward_call(): pl.pallas_call(partial(feed_forward_kernel, split, rows), name='feed_forw...]
    dot_general x18 -> x0, matrix products: 157 us -> none  [the longest x1 35.2 us: on_device(): inner = jnp.dot(normed_low, w_in, preferred_element_type=F32) + bias_in]
    ppermute x20 -> x21, waiting for transfers between devices: 82 us -> 26.6 us  [flip(): return lax.ppermute(value, 'dp', [(i, i ^ bits) for i in range(16)])]
    convert_element_type x3 -> x0, other arithmetic: 34 us -> none  [the longest x1 21.2 us: on_device(): dscores = (pf * (dprobs - delta)).astype(BF)]
    convert_element_type x23 -> x0, local copies, waits for them, and re-layouts: 32.2 us -> none  [the longest x4 13.1 us: reduce_scatter(): send = pick(blocks, 1 - core, 1).astype(BF)]
    reshape x11 -> x0, local copies, waits for them, and re-layouts: 29.8 us -> none  [the longest x3 11.5 us: on_device(): qh, kh, vh = (x.reshape(rows, length, HEADS, head_size) for x in (q, k, v))]
    unnamed x138 -> x47, local copies, waits for them, and re-layouts: 27 us -> 5.12 us
    sub x1 -> x0, matrix products: 16.4 us -> none  [on_device(): weight = jnp.exp(masked - jnp.max(masked, axis=-1, keepdims=True))]
  transfers between devices with their start and end apart: 29 -> 30, of which waited for: 14 -> 9; matrix products, arithmetic and copies ran while one was open for 15% -> 3% of each run, Pallas kernels for 0% -> 44%
where the time goes in v3:
time: 244 us
  Pallas kernels  164 us (67%)
  starting transfers between devices  36.8 us (15%)
  waiting for transfers between devices  28.2 us (12%)
  local copies, waits for them, and re-layouts  12 us (5%)
    pallas_call x1, Pallas kernels, feed_forward_call(): pl.pallas_call(partial(feed_forward_kernel, split, rows), name='feed_forw...  33.5 us
    pallas_call x1, Pallas kernels, branch_grad(): pl.pallas_call(body, name='branch_grad', out_shape=shapes, grid_spec=pltp...  33.3 us
    pallas_call x9, Pallas kernels, add_pieces(): pl.pallas_call(body, name=name, out_shape=[jax.ShapeDtypeStruct(s, BF) fo...  32.9 us
    ppermute x21, starting transfers between devices, flip(): return lax.ppermute(value, 'dp', [(i, i ^ bits) for i in range(16)])  32.1 us
    pallas_call x1, Pallas kernels, attention_call(): pl.pallas_call(attention_kernel, name='attention_rows', out_shape=[row(3...  30.2 us
    ppermute x21, waiting for transfers between devices, flip(): return lax.ppermute(value, 'dp', [(i, i ^ bits) for i in range(16)])  26.6 us
    pallas_call x2, Pallas kernels, attention_grad(): pl.pallas_call(body, name='attention_grad', out_shape=[out, one, one], gr...  20.5 us
    pallas_call x1, Pallas kernels, input_grad_call(): pl.pallas_call(body, name='input_grad', out_shape=[jax.ShapeDtypeStruct((...  6.57 us
  transfers between devices with their start and end apart: 30, of which 9 were waited for; matrix products, arithmetic and copies ran while one was open for 3% of the time, Pallas kernels for 44%

profile of v3, /device:TPU:0, one launch (start us, length us, event | category | flops | bytes accessed | tf_op | source)
XLA Modules:
  0.0 244.0 jit_solution(13384162880189299038)
XLA Ops:
  5.3 30.2 %attention_rows.1 = (bf16[2,512,2304]{2,1,0:T(8,128)(2,1)}, bf16[2,6,2,512,512]{4,3,2,1,0:T(8,128)(2,1)}, bf16[2,512,768]{2,1,0:T(8,128)(2,1)}, bf16[2,512,768]{...) custom-call(s32[1]{0:T(128)} %bitcast.core_ref, ...), custom_call_target="tpu_custom_call" | custom-call | flops 6442450944 | bytes 36700160 | tf_op jit(solution)/shard_map/attention_rows/pallas_call | solution.py:160
  36.4 33.5 %feed_forward.1 = (bf16[1024,3072]{1,0:T(8,128)(2,1)}, bf16[4,256,768]{2,1,0:T(8,128)(2,1)}, bf16[2,256,768]{2,1,0:T(8,128)(2,1)}, bf16[2,8,768]{2,1,0:T(8,128)(...) custom-call(s32[1]{0:T(128)} %bitcast.core_ref, ...), custom_call_target="tpu_custom_call" | custom-call | flops 14495514624 | bytes 31457280 | tf_op jit(solution)/shard_map/feed_forward/pallas_call | solution.py:351
  72.2 33.3 %branch_grad.1 = (bf16[1024,768]{1,0:T(8,128)(2,1)}, bf16[1024,768]{1,0:T(8,128)(2,1)}, f32[1,3072]{1,0:T(1,128)S(1)}, f32[1,768]{1,0:T(1,128)S(1)}, f32[1,768]{...) custom-call(s32[1]{0:T(128)} %bitcast.core_ref, ...), custom_call_target="tpu_custom_call" | custom-call | flops 15703474176 | bytes 31457280 | tf_op jit(solution)/shard_map/branch_grad/pallas_call | solution.py:479
  105.6 9.0 %back_1.1 = (bf16[1,4,2,96,384]{4,3,2,1,0:T(8,128)(2,1)S(1)}, bf16[1,4,2,96,384]{4,3,2,1,0:T(8,128)(2,1)S(1)}, bf16[1,4,2,96,384]{4,3,2,1,0:T(8,128)(2,1)S(1)}, bf16[1,4,2,96,384]{4,3,2,1,0:T(8,128)(2,1)S(1)}) custom-call(s32[3]{0:T(128)S(1)} %pad_add_fusion.where_ref, bf16[2,1,4,2,2,96,384]{6,5,4,3,2,1,0:T(8,128)(2,1)S(1)} %bitcast.33, ...), custom_call_target="tpu_custom_call" | custom-call | tf_op jit(solution)/shard_map/back_1/pallas_call | solution.py:797
  114.8 2.9 %collective-permute-start.5 = (bf16[1,4,2,96,384]{4,3,2,1,0:T(8,128)(2,1)S(1)}, bf16[1,4,2,96,384]{4,3,2,1,0:T(8,128)(2,1)S(1)}, u32[]{:S(2)}, u32[]{:S(2)}) collective-permute-start(bf16[1,4,2,96,384]{4,3,2,1,0:T(8,128)(2,1)S(1)} %get-tuple-element.191), channel_id=1, source_target_pairs={{0,2},{2,0},{4,6},{6,4},{8,10},{10,8},{12,14},{14,12},{16,18},{18,... | collective-permute-start | bytes 1769480 | tf_op jit(solution)/shard_map/ppermute | solution.py:901
  120.6 10.3 %attention_grad.2 = (bf16[3,2,512,768]{3,2,1,0:T(8,128)(2,1)S(1)}, f32[1,768]{1,0:T(1,128)S(1)}, f32[1,768]{1,0:T(1,128)S(1)}) custom-call(bf16[2,512,2304]{2,1,0:T(8,128)(2,1)S(1)} %bitcast.25, bf16[2,512,2304]{2,1,0:T(8,128)(2,1)S(1)} %bitcast.25, bf16[2,512,2304]{2,1,0:T(8,128)(2,1)S(1)} %bitcast.25, ...), custom_call_target="tpu_custom_call" | custom-call | flops 1610612736 | bytes 15728640 | tf_op jit(solution)/shard_map/attention_grad/pallas_call | solution.py:553
  132.7 3.4 %inner_1.1 = (bf16[5,4,2,24,384]{4,3,2,1,0:T(8,128)(2,1)S(1)}, bf16[5,4,2,24,384]{4,3,2,1,0:T(8,128)(2,1)S(1)}, bf16[5,4,2,24,384]{4,3,2,1,0:T(8,128)(2,1)S(1)}, bf16[5,4,2,24,384]{4,3,2,1,0:T(8,128)(2,1)S(1)}) custom-call(s32[3]{0:T(128)S(1)} %pad_add_fusion.where_ref, bf16[2,5,4,2,2,24,384]{6,5,4,3,2,1,0:T(8,128)(2,1)S(1)} %bitcast.31, ...), custom_call_target="tpu_custom_call" | custom-call | tf_op jit(solution)/shard_map/inner_1/pallas_call | solution.py:797
  136.1 5.8 %back_2.1 = (bf16[1,4,96,384]{3,2,1,0:T(8,128)(2,1)S(1)}, bf16[1,4,96,384]{3,2,1,0:T(8,128)(2,1)S(1)}, bf16[1,4,96,384]{3,2,1,0:T(8,128)(2,1)S(1)}, bf16[1,4,96,384]{3,2,1,0:T(8,128)(2,1)S(1)}) custom-call(s32[3]{0:T(128)S(1)} %pad_add_fusion.where_ref, bf16[1,4,2,96,384]{4,3,2,1,0:T(8,128)(2,1)S(1)} %get-tuple-element.199.refs_0_, ...), custom_call_target="tpu_custom_call" | custom-call | tf_op jit(solution)/shard_map/back_2/pallas_call | solution.py:797
  146.0 10.2 %attention_grad.3 = (bf16[3,2,512,768]{3,2,1,0:T(8,128)(2,1)S(1)}, f32[1,768]{1,0:T(1,128)S(1)}, f32[1,768]{1,0:T(1,128)S(1)}) custom-call(bf16[2,512,2304]{2,1,0:T(8,128)(2,1)S(1)} %bitcast.25, bf16[2,512,2304]{2,1,0:T(8,128)(2,1)S(1)} %bitcast.25, bf16[2,512,2304]{2,1,0:T(8,128)(2,1)S(1)} %bitcast.25, ...), custom_call_target="tpu_custom_call", output_to_operand_aliasing={{0}: (7, {})} | custom-call | flops 1610612736 | bytes 15728640 | tf_op jit(solution)/shard_map/attention_grad/pallas_call | solution.py:553
  156.2 4.8 %grad_qkv.1 = (bf16[6,16,24,384]{3,2,1,0:T(8,128)(2,1)S(1)}, bf16[6,16,24,384]{3,2,1,0:T(8,128)(2,1)S(1)}) custom-call(s32[1]{0:T(128)} %bitcast.core_ref, bf16[1024,768]{1,0:T(8,128)(2,1)S(1)} %bitcast.38, bf16[3,1024,768]{2,1,0:T(8,128)(2,1)S(1)} %bitcast.29), custom_call_target="tpu_custom_call" | custom-call | flops 3623878656 | bytes 8257536 | tf_op jit(solution)/shard_map/grad_qkv/pallas_call | solution.py:758
  161.1 5.0 %collective-permute-done.8.refs_1_ = bf16[1,4,96,384]{3,2,1,0:T(8,128)(2,1)S(1)} collective-permute-done((bf16[1,4,96,384]{3,2,1,0:T(8,128)(2,1)S(1)}, bf16[1,4,96,384]{3,2,1,0:T(8,128)(2,1)S(1)}, u32[]{:S(2)}, u32[]{:S(2)}) %collective-permute-start.8) | collective-permute-done | bytes 294944 | tf_op jit(solution)/shard_map/ppermute | solution.py:901
  166.1 3.2 %back_3.1 = (bf16[2,1,96,384]{3,2,1,0:T(8,128)(2,1)S(1)}, bf16[2,1,96,384]{3,2,1,0:T(8,128)(2,1)S(1)}, bf16[2,1,96,384]{3,2,1,0:T(8,128)(2,1)S(1)}, bf16[2,1,96,384]{3,2,1,0:T(8,128)(2,1)S(1)}) custom-call(s32[3]{0:T(128)S(1)} %pad_add_fusion.where_ref, bf16[1,4,96,384]{3,2,1,0:T(8,128)(2,1)S(1)} %get-tuple-element.225.refs_0_, ...), custom_call_target="tpu_custom_call" | custom-call | tf_op jit(solution)/shard_map/back_3/pallas_call | solution.py:797
  169.3 2.3 inner_2.1
  171.7 3.2 %proj_1.1 = (bf16[3,4,2,24,384]{4,3,2,1,0:T(8,128)(2,1)S(1)}, bf16[3,4,2,24,384]{4,3,2,1,0:T(8,128)(2,1)S(1)}, bf16[3,4,2,24,384]{4,3,2,1,0:T(8,128)(2,1)S(1)}, bf16[3,4,2,24,384]{4,3,2,1,0:T(8,128)(2,1)S(1)}) custom-call(s32[3]{0:T(128)S(1)} %pad_add_fusion.where_ref, bf16[2,3,4,2,2,24,384]{6,5,4,3,2,1,0:T(8,128)(2,1)S(1)} %bitcast.35, ...), custom_call_target="tpu_custom_call" | custom-call | tf_op jit(solution)/shard_map/proj_1/pallas_call | solution.py:797
  176.5 2.6 %collective-permute-start.18 = (bf16[2,1,96,384]{3,2,1,0:T(8,128)(2,1)S(1)}, bf16[2,1,96,384]{3,2,1,0:T(8,128)(2,1)S(1)}, u32[]{:S(2)}, u32[]{:S(2)}) collective-permute-start(bf16[2,1,96,384]{3,2,1,0:T(8,128)(2,1)S(1)} %get-tuple-element.258), channel_id=1, source_target_pairs={{0,16},{2,18},{4,20},{6,22},{8,24},{10,26},{12,28},{14,30},{16,0},... | collective-permute-start | bytes 442376 | tf_op jit(solution)/shard_map/ppermute | solution.py:901
  186.6 2.5 %collective-permute-start.19 = (bf16[2,1,96,384]{3,2,1,0:T(8,128)(2,1)S(1)}, bf16[2,1,96,384]{3,2,1,0:T(8,128)(2,1)S(1)}, u32[]{:S(2)}, u32[]{:S(2)}) collective-permute-start(bf16[2,1,96,384]{3,2,1,0:T(8,128)(2,1)S(1)} %get-tuple-element.259), channel_id=1, source_target_pairs={{0,24},{2,26},{4,28},{6,30},{8,16},{10,18},{12,20},{14,22},{16,8},... | collective-permute-start | bytes 442376 | tf_op jit(solution)/shard_map/ppermute | solution.py:901
  189.0 6.6 %input_grad.1 = (bf16[4,256,768]{2,1,0:T(8,128)(2,1)}, bf16[2,256,768]{2,1,0:T(8,128)(2,1)S(1)}) custom-call(s32[1]{0:T(128)} %bitcast.core_ref, bf16[3,1024,768]{2,1,0:T(8,128)(2,1)S(1)} %bitcast.30, bf16[1024,768]{1,0:T(8,128)(2,1)S(1)} %copy-done.13, bf16[768,2304]{1,0:T(8,128)(2,1)S(1)} %copy-done.8), custom_call_target="tpu_custom_call" | custom-call | flops 3623878656 | bytes 10485760 | tf_op jit(solution)/shard_map/input_grad/pallas_call | solution.py:598
  195.6 4.5 %collective-permute-done.13.refs_1_ = bf16[5,4,24,384]{3,2,1,0:T(8,128)(2,1)S(1)} collective-permute-done((bf16[5,4,24,384]{3,2,1,0:T(8,128)(2,1)S(1)}, bf16[5,4,24,384]{3,2,1,0:T(8,128)(2,1)S(1)}, u32[]{:S(2)}, u32[]{:S(2)}) %collective-permute-start.13) | collective-permute-done | bytes 368672 | tf_op jit(solution)/shard_map/ppermute | solution.py:901
  202.1 2.5 %proj_2.1 = (bf16[3,4,24,384]{3,2,1,0:T(8,128)(2,1)}, bf16[3,4,24,384]{3,2,1,0:T(8,128)(2,1)S(1)}, bf16[3,4,24,384]{3,2,1,0:T(8,128)(2,1)S(1)}, bf16[3,4,24,384]{3,2,1,0:T(8,128)(2,1)S(1)}) custom-call(s32[3]{0:T(128)S(1)} %pad_add_fusion.where_ref, bf16[3,4,2,24,384]{4,3,2,1,0:T(8,128)(2,1)S(1)} %get-tuple-element.261.refs_0_, ...), custom_call_target="tpu_custom_call" | custom-call | tf_op jit(solution)/shard_map/proj_2/pallas_call | solution.py:797
  207.0 2.6 %all-to-all-start = ((f32[32,1,1152]{2,1,0:T(1,128)}), f32[32,1,1152]{2,1,0:T(1,128)S(1)}, u32[]{:S(2)}, u32[]{:S(2)}) async-start(f32[32,1,1152]{2,1,0:T(1,128)} %copy.26), calls=%async_computation | async-start | bytes 294912 | tf_op jit(solution)/shard_map/all_to_all | solution.py:638
  214.9 2.5 %collective-permute-start.27 = (bf16[2,5,24,384]{3,2,1,0:T(8,128)(2,1)}, bf16[2,5,24,384]{3,2,1,0:T(8,128)(2,1)S(1)}, u32[]{:S(2)}, u32[]{:S(2)}) collective-permute-start(bf16[2,5,24,384]{3,2,1,0:T(8,128)(2,1)} %get-tuple-element.291), channel_id=1, source_target_pairs={{0,16},{2,18},{4,20},{6,22},{8,24},{10,26},{12,28},{14,30},{16,0},... | collective-permute-start | bytes 552968 | tf_op jit(solution)/shard_map/ppermute | solution.py:901
  224.7 3.4 %collective-permute-start.24 = (bf16[2,3,24,384]{3,2,1,0:T(8,128)(2,1)S(1)}, bf16[2,3,24,384]{3,2,1,0:T(8,128)(2,1)S(1)}, u32[]{:S(2)}, u32[]{:S(2)}) collective-permute-start(bf16[2,3,24,384]{3,2,1,0:T(8,128)(2,1)S(1)} %get-tuple-element.287), channel_id=1, source_target_pairs={{0,16},{2,18},{4,20},{6,22},{8,24},{10,26},{12,28},{14,30},{16,0},... | collective-permute-start | bytes 331784 | tf_op jit(solution)/shard_map/ppermute | solution.py:901
  229.7 6.6 %collective-permute-done.27.c_ref = bf16[2,5,24,384]{3,2,1,0:T(8,128)(2,1)S(1)} collective-permute-done((bf16[2,5,24,384]{3,2,1,0:T(8,128)(2,1)}, bf16[2,5,24,384]{3,2,1,0:T(8,128)(2,1)S(1)}, u32[]{:S(2)}, u32[]{:S(2)}) %collective-permute-start.27) | collective-permute-done | bytes 184352 | tf_op jit(solution)/shard_map/ppermute | solution.py:901
  236.3 6.1 %collective-permute-done.24.c_ref = bf16[2,3,24,384]{3,2,1,0:T(8,128)(2,1)S(1)} collective-permute-done((bf16[2,3,24,384]{3,2,1,0:T(8,128)(2,1)S(1)}, bf16[2,3,24,384]{3,2,1,0:T(8,128)(2,1)S(1)}, u32[]{:S(2)}, u32[]{:S(2)}) %collective-permute-start.24) | collective-permute-done | bytes 110624 | tf_op jit(solution)/shard_map/ppermute | solution.py:901
  (115 shorter events, 46.1 us)
Async XLA Ops:
  2.5 32.9 %collective-permute-start.1 = (bf16[2,256,768]{2,1,0:T(8,128)(2,1)S(1)}, bf16[2,256,768]{2,1,0:T(8,128)(2,1)S(1)}, u32[]{:S(2)}, u32[]{:S(2)}) collective-permute-start(bf16[2,256,768]{2,1,0:T(8,128)(2,1)S(1)} %constant_dynamic-slice_fusion), channel_id=1, source_target_pairs={{0,1},{1,0},{2,3},{3,2},{4,5},{5,4},{6,7},{7,6},{8,9},{9,8},{10,11... | collective-permute-start | bytes 2359304 | tf_op jit(solution)/shard_map/ppermute | solution.py:642
  69.9 35.6 %collective-permute-start.2 = (bf16[2,16,96,384]{3,2,1,0:T(8,128)(2,1)}, bf16[2,16,96,384]{3,2,1,0:T(8,128)(2,1)S(1)}, u32[]{:S(2)}, u32[]{:S(2)}) collective-permute-start(bf16[2,16,96,384]{3,2,1,0:T(8,128)(2,1)} %get-tuple-element.172), channel_id=1, source_target_pairs={{0,1},{1,0},{2,3},{3,2},{4,5},{5,4},{6,7},{7,6},{8,9},{9,8},{10,11... | collective-permute-start | bytes 7077896 | tf_op jit(solution)/shard_map/ppermute | solution.py:642
  70.4 35.1 %collective-permute-start.4 = (bf16[2,6,768]{2,1,0:T(8,128)(2,1)}, bf16[2,6,768]{2,1,0:T(8,128)(2,1)S(1)}, u32[]{:S(2)}, u32[]{:S(2)}) collective-permute-start(bf16[2,6,768]{2,1,0:T(8,128)(2,1)} %bitcast.42), channel_id=1, source_target_pairs={{0,1},{1,0},{2,3},{3,2},{4,5},{5,4},{6,7},{7,6},{8,9},{9,8},{10,11... | collective-permute-start | bytes 55304 | tf_op jit(solution)/shard_map/ppermute | solution.py:642
  70.6 34.9 %collective-permute-start.3 = (bf16[2,256,768]{2,1,0:T(8,128)(2,1)}, bf16[2,256,768]{2,1,0:T(8,128)(2,1)S(1)}, u32[]{:S(2)}, u32[]{:S(2)}) collective-permute-start(bf16[2,256,768]{2,1,0:T(8,128)(2,1)} %get-tuple-element.173), channel_id=1, source_target_pairs={{0,1},{1,0},{2,3},{3,2},{4,5},{5,4},{6,7},{7,6},{8,9},{9,8},{10,11... | collective-permute-start | bytes 2359304 | tf_op jit(solution)/shard_map/ppermute | solution.py:642
  114.6 18.2 %collective-permute-start.7 = (bf16[10,16,24,384]{3,2,1,0:T(8,128)(2,1)}, bf16[10,16,24,384]{3,2,1,0:T(8,128)(2,1)S(1)}, u32[]{:S(2)}, u32[]{:S(2)}) collective-permute-start(bf16[10,16,24,384]{3,2,1,0:T(8,128)(2,1)} %get-tuple-element.193), channel_id=1, source_target_pairs={{0,1},{1,0},{2,3},{3,2},{4,5},{5,4},{6,7},{7,6},{8,9},{9,8},{10,11... | collective-permute-start | bytes 8847368 | tf_op jit(solution)/shard_map/ppermute | solution.py:642
  114.8 16.5 %collective-permute-start.5 = (bf16[1,4,2,96,384]{4,3,2,1,0:T(8,128)(2,1)S(1)}, bf16[1,4,2,96,384]{4,3,2,1,0:T(8,128)(2,1)S(1)}, u32[]{:S(2)}, u32[]{:S(2)}) collective-permute-start(bf16[1,4,2,96,384]{4,3,2,1,0:T(8,128)(2,1)S(1)} %get-tuple-element.191), channel_id=1, source_target_pairs={{0,2},{2,0},{4,6},{6,4},{8,10},{10,8},{12,14},{14,12},{16,18},{18,... | collective-permute-start | bytes 1769480 | tf_op jit(solution)/shard_map/ppermute | solution.py:901
  117.6 15.1 %collective-permute-start.6 = (bf16[1,4,2,96,384]{4,3,2,1,0:T(8,128)(2,1)S(1)}, bf16[1,4,2,96,384]{4,3,2,1,0:T(8,128)(2,1)S(1)}, u32[]{:S(2)}, u32[]{:S(2)}) collective-permute-start(bf16[1,4,2,96,384]{4,3,2,1,0:T(8,128)(2,1)S(1)} %get-tuple-element.192), channel_id=1, source_target_pairs={{0,4},{2,6},{4,0},{6,2},{8,12},{10,14},{12,8},{14,10},{16,20},{18,... | collective-permute-start | bytes 1769480 | tf_op jit(solution)/shard_map/ppermute | solution.py:901
  141.9 24.1 %collective-permute-start.10 = (bf16[5,4,2,24,384]{4,3,2,1,0:T(8,128)(2,1)S(1)}, bf16[5,4,2,24,384]{4,3,2,1,0:T(8,128)(2,1)S(1)}, u32[]{:S(2)}, u32[]{:S(2)}) collective-permute-start(bf16[5,4,2,24,384]{4,3,2,1,0:T(8,128)(2,1)S(1)} %get-tuple-element.216), channel_id=1, source_target_pairs={{0,2},{2,0},{4,6},{6,4},{8,10},{10,8},{12,14},{14,12},{16,18},{18,... | collective-permute-start | bytes 2211848 | tf_op jit(solution)/shard_map/ppermute | solution.py:901
  142.3 23.8 %collective-permute-start.11 = (bf16[5,4,2,24,384]{4,3,2,1,0:T(8,128)(2,1)S(1)}, bf16[5,4,2,24,384]{4,3,2,1,0:T(8,128)(2,1)S(1)}, u32[]{:S(2)}, u32[]{:S(2)}) collective-permute-start(bf16[5,4,2,24,384]{4,3,2,1,0:T(8,128)(2,1)S(1)} %get-tuple-element.217), channel_id=1, source_target_pairs={{0,4},{2,6},{4,0},{6,2},{8,12},{10,14},{12,8},{14,10},{16,20},{18,... | collective-permute-start | bytes 2211848 | tf_op jit(solution)/shard_map/ppermute | solution.py:901
  144.0 22.0 %collective-permute-start.8 = (bf16[1,4,96,384]{3,2,1,0:T(8,128)(2,1)S(1)}, bf16[1,4,96,384]{3,2,1,0:T(8,128)(2,1)S(1)}, u32[]{:S(2)}, u32[]{:S(2)}) collective-permute-start(bf16[1,4,96,384]{3,2,1,0:T(8,128)(2,1)S(1)} %get-tuple-element.214), channel_id=1, source_target_pairs={{0,4},{2,6},{4,0},{6,2},{8,12},{10,14},{12,8},{14,10},{16,20},{18,... | collective-permute-start | bytes 884744 | tf_op jit(solution)/shard_map/ppermute | solution.py:901
  144.3 21.7 %collective-permute-start.9 = (bf16[1,4,96,384]{3,2,1,0:T(8,128)(2,1)S(1)}, bf16[1,4,96,384]{3,2,1,0:T(8,128)(2,1)S(1)}, u32[]{:S(2)}, u32[]{:S(2)}) collective-permute-start(bf16[1,4,96,384]{3,2,1,0:T(8,128)(2,1)S(1)} %get-tuple-element.215), channel_id=1, source_target_pairs={{0,2},{2,0},{4,6},{6,4},{8,10},{10,8},{12,14},{14,12},{16,18},{18,... | collective-permute-start | bytes 884744 | tf_op jit(solution)/shard_map/ppermute | solution.py:901
  179.0 21.1 %collective-permute-start.15 = (bf16[3,4,2,24,384]{4,3,2,1,0:T(8,128)(2,1)S(1)}, bf16[3,4,2,24,384]{4,3,2,1,0:T(8,128)(2,1)S(1)}, u32[]{:S(2)}, u32[]{:S(2)}) collective-permute-start(bf16[3,4,2,24,384]{4,3,2,1,0:T(8,128)(2,1)S(1)} %get-tuple-element.254), channel_id=1, source_target_pairs={{0,2},{2,0},{4,6},{6,4},{8,10},{10,8},{12,14},{14,12},{16,18},{18,... | collective-permute-start | bytes 1327112 | tf_op jit(solution)/shard_map/ppermute | solution.py:901
  180.5 19.6 %collective-permute-start.16 = (bf16[3,4,2,24,384]{4,3,2,1,0:T(8,128)(2,1)S(1)}, bf16[3,4,2,24,384]{4,3,2,1,0:T(8,128)(2,1)S(1)}, u32[]{:S(2)}, u32[]{:S(2)}) collective-permute-start(bf16[3,4,2,24,384]{4,3,2,1,0:T(8,128)(2,1)S(1)} %get-tuple-element.255), channel_id=1, source_target_pairs={{0,4},{2,6},{4,0},{6,2},{8,12},{10,14},{12,8},{14,10},{16,20},{18,... | collective-permute-start | bytes 1327112 | tf_op jit(solution)/shard_map/ppermute | solution.py:901
  182.0 18.1 %collective-permute-start.13 = (bf16[5,4,24,384]{3,2,1,0:T(8,128)(2,1)S(1)}, bf16[5,4,24,384]{3,2,1,0:T(8,128)(2,1)S(1)}, u32[]{:S(2)}, u32[]{:S(2)}) collective-permute-start(bf16[5,4,24,384]{3,2,1,0:T(8,128)(2,1)S(1)} %get-tuple-element.252), channel_id=1, source_target_pairs={{0,4},{2,6},{4,0},{6,2},{8,12},{10,14},{12,8},{14,10},{16,20},{18,... | collective-permute-start | bytes 1105928 | tf_op jit(solution)/shard_map/ppermute | solution.py:901
  184.2 15.9 %collective-permute-start.14 = (bf16[5,4,24,384]{3,2,1,0:T(8,128)(2,1)S(1)}, bf16[5,4,24,384]{3,2,1,0:T(8,128)(2,1)S(1)}, u32[]{:S(2)}, u32[]{:S(2)}) collective-permute-start(bf16[5,4,24,384]{3,2,1,0:T(8,128)(2,1)S(1)} %get-tuple-element.253), channel_id=1, source_target_pairs={{0,2},{2,0},{4,6},{6,4},{8,10},{10,8},{12,14},{14,12},{16,18},{18,... | collective-permute-start | bytes 1105928 | tf_op jit(solution)/shard_map/ppermute | solution.py:901
  200.1 22.1 %collective-permute-start.22 = (bf16[2,256,768]{2,1,0:T(8,128)(2,1)S(1)}, bf16[2,256,768]{2,1,0:T(8,128)(2,1)}, u32[]{:S(2)}, u32[]{:S(2)}) collective-permute-start(bf16[2,256,768]{2,1,0:T(8,128)(2,1)S(1)} %get-tuple-element.279), channel_id=1, source_target_pairs={{0,1},{1,0},{2,3},{3,2},{4,5},{5,4},{6,7},{7,6},{8,9},{9,8},{10,11... | collective-permute-start | bytes 2359304 | tf_op jit(solution)/shard_map/ppermute | solution.py:642
  204.6 12.9 %collective-permute-start.20 = (bf16[3,4,24,384]{3,2,1,0:T(8,128)(2,1)}, bf16[3,4,24,384]{3,2,1,0:T(8,128)(2,1)S(1)}, u32[]{:S(2)}, u32[]{:S(2)}) collective-permute-start(bf16[3,4,24,384]{3,2,1,0:T(8,128)(2,1)} %get-tuple-element.277), channel_id=1, source_target_pairs={{0,4},{2,6},{4,0},{6,2},{8,12},{10,14},{12,8},{14,10},{16,20},{18,... | collective-permute-start | bytes 663560 | tf_op jit(solution)/shard_map/ppermute | solution.py:901
  209.6 12.6 %collective-permute-start.21 = (bf16[3,4,24,384]{3,2,1,0:T(8,128)(2,1)S(1)}, bf16[3,4,24,384]{3,2,1,0:T(8,128)(2,1)S(1)}, u32[]{:S(2)}, u32[]{:S(2)}) collective-permute-start(bf16[3,4,24,384]{3,2,1,0:T(8,128)(2,1)S(1)} %get-tuple-element.278), channel_id=1, source_target_pairs={{0,2},{2,0},{4,6},{6,4},{8,10},{10,8},{12,14},{14,12},{16,18},{18,... | collective-permute-start | bytes 663560 | tf_op jit(solution)/shard_map/ppermute | solution.py:901
  211.3 16.8 %collective-permute-start.26 = (bf16[2,5,24,384]{3,2,1,0:T(8,128)(2,1)}, bf16[2,5,24,384]{3,2,1,0:T(8,128)(2,1)S(1)}, u32[]{:S(2)}, u32[]{:S(2)}) collective-permute-start(bf16[2,5,24,384]{3,2,1,0:T(8,128)(2,1)} %get-tuple-element.290), channel_id=1, source_target_pairs={{0,8},{2,10},{4,12},{6,14},{8,0},{10,2},{12,4},{14,6},{16,24},{18,... | collective-permute-start | bytes 552968 | tf_op jit(solution)/shard_map/ppermute | solution.py:901
  214.9 21.4 %collective-permute-start.27 = (bf16[2,5,24,384]{3,2,1,0:T(8,128)(2,1)}, bf16[2,5,24,384]{3,2,1,0:T(8,128)(2,1)S(1)}, u32[]{:S(2)}, u32[]{:S(2)}) collective-permute-start(bf16[2,5,24,384]{3,2,1,0:T(8,128)(2,1)} %get-tuple-element.291), channel_id=1, source_target_pairs={{0,16},{2,18},{4,20},{6,22},{8,24},{10,26},{12,28},{14,30},{16,0},... | collective-permute-start | bytes 552968 | tf_op jit(solution)/shard_map/ppermute | solution.py:901
  217.4 18.9 %collective-permute-start.28 = (bf16[2,5,24,384]{3,2,1,0:T(8,128)(2,1)S(1)}, bf16[2,5,24,384]{3,2,1,0:T(8,128)(2,1)S(1)}, u32[]{:S(2)}, u32[]{:S(2)}) collective-permute-start(bf16[2,5,24,384]{3,2,1,0:T(8,128)(2,1)S(1)} %get-tuple-element.292), channel_id=1, source_target_pairs={{0,24},{2,26},{4,28},{6,30},{8,16},{10,18},{12,20},{14,22},{16,8},... | collective-permute-start | bytes 552968 | tf_op jit(solution)/shard_map/ppermute | solution.py:901
  224.0 12.3 %collective-permute-start.23 = (bf16[2,3,24,384]{3,2,1,0:T(8,128)(2,1)S(1)}, bf16[2,3,24,384]{3,2,1,0:T(8,128)(2,1)S(1)}, u32[]{:S(2)}, u32[]{:S(2)}) collective-permute-start(bf16[2,3,24,384]{3,2,1,0:T(8,128)(2,1)S(1)} %get-tuple-element.286), channel_id=1, source_target_pairs={{0,8},{2,10},{4,12},{6,14},{8,0},{10,2},{12,4},{14,6},{16,24},{18,... | collective-permute-start | bytes 331784 | tf_op jit(solution)/shard_map/ppermute | solution.py:901
  224.7 17.7 %collective-permute-start.24 = (bf16[2,3,24,384]{3,2,1,0:T(8,128)(2,1)S(1)}, bf16[2,3,24,384]{3,2,1,0:T(8,128)(2,1)S(1)}, u32[]{:S(2)}, u32[]{:S(2)}) collective-permute-start(bf16[2,3,24,384]{3,2,1,0:T(8,128)(2,1)S(1)} %get-tuple-element.287), channel_id=1, source_target_pairs={{0,16},{2,18},{4,20},{6,22},{8,24},{10,26},{12,28},{14,30},{16,0},... | collective-permute-start | bytes 331784 | tf_op jit(solution)/shard_map/ppermute | solution.py:901
  228.1 14.3 %collective-permute-start.25 = (bf16[2,3,24,384]{3,2,1,0:T(8,128)(2,1)S(1)}, bf16[2,3,24,384]{3,2,1,0:T(8,128)(2,1)S(1)}, u32[]{:S(2)}, u32[]{:S(2)}) collective-permute-start(bf16[2,3,24,384]{3,2,1,0:T(8,128)(2,1)S(1)} %get-tuple-element.288), channel_id=1, source_target_pairs={{0,24},{2,26},{4,28},{6,30},{8,16},{10,18},{12,20},{14,22},{16,8},... | collective-permute-start | bytes 331784 | tf_op jit(solution)/shard_map/ppermute | solution.py:901
  (29 other events, 435.3 us)

commit v4 on v3

v4 whole, which is shorter than its diff:
```python
from functools import partial

import jax
import jax.numpy as jnp
from jax import lax
from jax.experimental import pallas as pl
from jax.experimental.pallas import tpu as pltpu
from jax.sharding import PartitionSpec as P

HEADS = 12
EPS = 1e-12
BF = jnp.bfloat16
F32 = jnp.float32
VMEM_LIMIT = 60 << 20
RSQRT2 = 0.7071067811865476
RSQRT2PI = 0.3989422804014327


def row_dot(left, right):
    return lax.dot_general(left, right, (((1,), (0,)), ((), ())), preferred_element_type=F32)


def row_dot_t(left, right):
    return lax.dot_general(left, right, (((1,), (1,)), ((), ())), preferred_element_type=F32)


def col_dot(left, right):
    return lax.dot_general(left, right, (((0,), (0,)), ((), ())), preferred_element_type=F32)


def gelu_pair(value):
    expo = jnp.exp(value * value * -0.5)
    phi = 0.5 + 0.5 * lax.erf(value * RSQRT2)
    return value * phi, phi + value * expo * RSQRT2PI


def whole(shape):
    return pl.BlockSpec(shape, lambda *_: (0,) * len(shape))


ANY = pl.BlockSpec(memory_space=pl.ANY)
HBM = pl.BlockSpec(memory_space=pltpu.HBM)


def params(mib):
    return pltpu.CompilerParams(vmem_limit_bytes=mib << 20)


def row_starts(len_ref, row):
    starts = [jnp.int32(0)]
    for j in range(len_ref.shape[1] - 1):
        starts.append(starts[-1] + len_ref[row, j])
    return starts


def attention_kernel(
    core_ref, len_ref, own_ref, other_ref, wqkv_hbm, wout_hbm, bq_ref, bv_ref, bo_ref, g1_ref, s1_ref,
    qkv_hbm, probs_hbm, x_ref, mixed_ref, low_ref, hat1_ref, inv1_ref, scale_ref,
    bias_ref, ahead0_ref, ahead1_ref, qkv_ref, wqkv_ref, wout_ref, p_ref, w_sem, p_sem, q_sem,
):
    step = pl.program_id(0)
    core = core_ref[0]
    rows = pl.num_programs(0)
    half, width = own_ref.shape[1:]
    length = 2 * half
    pairs = width // 128
    parts = [slice(n * width, (n + 1) * width) for n in range(3)]
    copies = [pltpu.make_async_copy(wqkv_hbm.at[:, part], wqkv_ref.at[:, part], w_sem.at[n]) for n, part in enumerate(parts)]
    copies.append(pltpu.make_async_copy(wout_hbm, wout_ref, w_sem.at[3]))

    @pl.when(step == 0)
    def _():
        for copy in copies:
            copy.start()

    x_ref[0, pl.ds(pl.multiple_of(core * half, half), half), :] = own_ref[0]
    x_ref[0, pl.ds(pl.multiple_of((1 - core) * half, half), half), :] = other_ref[0]
    starts = row_starts(len_ref, core * rows + step)
    down = lax.broadcasted_iota(jnp.int32, (length, 1), 0)
    across = lax.broadcasted_iota(jnp.int32, (1, length), 1)
    seg_down = jnp.zeros((length, 1), jnp.int32)
    seg_across = jnp.zeros((1, length), jnp.int32)
    for start in starts[1:]:
        seg_down += (down >= start).astype(jnp.int32)
        seg_across += (across >= start).astype(jnp.int32)
    bias_ref[...] = jnp.where(seg_down == seg_across, 0.0, -1e30)

    for n, part in enumerate(parts):
        @pl.when(step == 0)
        def _():
            copies[n].wait()

        value = row_dot(x_ref[0], wqkv_ref[:, part])
        if n == 0:
            value = (value + bq_ref[...]) * (width // HEADS) ** -0.5
        if n == 2:
            value = value + bv_ref[...]
        qkv_ref[:, part] = value.astype(BF)
    save = pltpu.make_async_copy(qkv_ref, qkv_hbm.at[step], q_sem)
    save.start()

    first = lax.broadcasted_iota(jnp.int32, (1, 128), 1) < 64

    def columns(part, pair):
        return pl.ds(pl.multiple_of(part * width + pair * 128, 128), 128)

    def scores(pair, into):
        q_pair = qkv_ref[:, columns(0, pair)]
        k_pair = qkv_ref[:, columns(1, pair)]
        for h in range(2):
            on = first if h == 0 else jnp.logical_not(first)
            into[h] = row_dot_t(jnp.where(on, q_pair, jnp.zeros_like(q_pair)), k_pair)

    def finish(pair, held, slot):
        out_copy = pltpu.make_async_copy(p_ref.at[slot], probs_hbm.at[step, pair], p_sem.at[slot])

        @pl.when(pair >= 2)
        def _():
            out_copy.wait()

        v_pair = qkv_ref[:, columns(2, pair)]
        outs = []
        for h in range(2):
            on = first if h == 0 else jnp.logical_not(first)
            s = held[h] + bias_ref[...]
            e = jnp.exp(s - jnp.max(s, axis=-1, keepdims=True)).astype(BF)
            p_ref[slot, h] = e
            outs.append(row_dot(e, jnp.where(on, v_pair, jnp.ones_like(v_pair))))
        sums = pltpu.roll(jnp.where(first, outs[1], outs[0]), 64, 1)
        inverse = 1.0 / sums
        scale_ref[0, :, columns(0, pair)] = inverse
        mixed_ref[0, :, columns(0, pair)] = (jnp.where(first, outs[0], outs[1]) * inverse).astype(BF)
        out_copy.start()

    scores(0, ahead0_ref)

    def two_pairs(i, carry):
        scores(2 * i + 1, ahead1_ref)
        finish(2 * i, ahead0_ref, 0)
        scores(jnp.minimum(2 * i + 2, pairs - 1), ahead0_ref)
        finish(2 * i + 1, ahead1_ref, 1)
        return carry

    lax.fori_loop(0, pairs // 2, two_pairs, 0)
    for tail in (pairs - 2, pairs - 1):
        pltpu.make_async_copy(p_ref.at[tail % 2], probs_hbm.at[step, tail], p_sem.at[tail % 2]).wait()

    @pl.when(step == 0)
    def _():
        copies[3].wait()

    pre = x_ref[0].astype(F32) + row_dot(mixed_ref[0], wout_ref[...]) + bo_ref[...]
    center = pre - jnp.mean(pre, axis=-1, keepdims=True)
    inv = lax.rsqrt(jnp.mean(center * center, axis=-1, keepdims=True) + EPS)
    hat = center * inv
    hat1_ref[0] = hat.astype(BF)
    inv1_ref[0] = inv
    low_ref[0] = (hat * g1_ref[...] + s1_ref[...]).astype(BF)
    save.wait()


def attention_call(core, lengths, tokens, other, w_qkv, w_out, vectors):
    rows_local, half, width = tokens.shape
    rows = rows_local // 2
    length = 2 * half
    pairs = width // 128

    def full(n):
        return pl.BlockSpec((1, length, n), lambda r, *_: (r, 0, 0))

    def row(n, kind=BF):
        return jax.ShapeDtypeStruct((rows, length, n), kind)

    return pl.pallas_call(
        attention_kernel,
        name="attention_rows",
        out_shape=[
            row(3 * width), jax.ShapeDtypeStruct((rows, pairs, 2, length, length), BF), row(width), row(width), row(width), row(width),
            row(1, F32), row(width, F32),
        ],
        grid_spec=pltpu.PrefetchScalarGridSpec(
            num_scalar_prefetch=2,
            grid=(rows,),
            in_specs=[
                pl.BlockSpec((1, half, width), lambda r, core, lens: (core[0] * rows + r, 0, 0)),
                pl.BlockSpec((1, half, width), lambda r, *_: (r, 0, 0)),
                ANY,
                ANY,
            ]
            + [whole(v.shape) for v in vectors],
            out_specs=[HBM, HBM] + [full(width)] * 4 + [full(1), full(width)],
            scratch_shapes=[
                pltpu.VMEM((length, length), F32),
                pltpu.VMEM((2, length, length), F32),
                pltpu.VMEM((2, length, length), F32),
                pltpu.VMEM((length, 3 * width), BF),
                pltpu.VMEM(w_qkv.shape, BF),
                pltpu.VMEM(w_out.shape, BF),
                pltpu.VMEM((2, 2, length, length), BF),
                pltpu.SemaphoreType.DMA((4,)),
                pltpu.SemaphoreType.DMA((2,)),
                pltpu.SemaphoreType.DMA,
            ],
        ),
        compiler_params=params(60),
        cost_estimate=pl.CostEstimate(
            flops=8 * rows * length * width * width + 4 * rows * length * length * width,
            bytes_accessed=35 << 20,
            transcendentals=rows * HEADS * length * length,
        ),
    )(core, lengths, tokens, other, w_qkv, w_out, *vectors)


def feed_kernel(
    split, core_ref, len_ref, low_ref, win_hbm, wback_hbm, wout_hbm, mixed_hbm, hat1_hbm, inv1_hbm, scale_hbm, cot_hbm, cot_other_hbm,
    bi_ref, bb_ref, g1_ref, g2_ref, s2_ref,
    out_hbm, other_hbm, cls_ref, dpre_hbm, dmixed_hbm, gi_ref, gg2_ref, gs2_ref, gb2_ref, gg1_ref, gs1_ref, gb1_ref, *rest
):
    n_grads = 4 if split else 2
    grads = rest[:n_grads]
    (win_ref, wback_ref, wout_ref, mixed_ref, hat1_ref, inv1_ref, scale_ref, cot_ref, out_ref, act_ref, slope_ref, acc_ref, dfeed_ref,
     grad_ref, w_sem, v_sem, c_sem, o_sem, d_sem) = rest[n_grads:]
    step = pl.program_id(0)
    core = core_ref[0]
    total, width = low_ref.shape
    length = 2 * cot_other_hbm.shape[1]
    half = length // 2
    group = total // length
    hidden = act_ref.shape[1]
    chunk = width
    chunks = hidden // chunk
    piece = 768
    pieces = [slice(n * piece, (n + 1) * piece) for n in range(chunk // piece)]
    weights = []
    for c in range(chunks):
        part = slice(c * chunk, (c + 1) * chunk)
        weights.append(pltpu.make_async_copy(win_hbm.at[:, part], win_ref.at[:, part], w_sem.at[2 * c]))
        weights.append(pltpu.make_async_copy(wback_hbm.at[part], wback_ref.at[part], w_sem.at[2 * c + 1]))
    values = [
        pltpu.make_async_copy(src, dst, v_sem.at[i])
        for i, (src, dst) in enumerate(
            ((hat1_hbm, hat1_ref), (inv1_hbm, inv1_ref), (wout_hbm, wout_ref), (scale_hbm, scale_ref), (mixed_hbm, mixed_ref))
        )
    ]
    loads, stores = [], []
    for r in range(group):
        own = pl.ds(pl.multiple_of(r * length + core * half, half), half)
        other = pl.ds(pl.multiple_of(r * length + (1 - core) * half, half), half)
        loads.append(pltpu.make_async_copy(cot_hbm.at[core * group + r], cot_ref.at[own], c_sem.at[r]))
        loads.append(pltpu.make_async_copy(cot_other_hbm.at[r], cot_ref.at[other], c_sem.at[group + r]))
        stores.append(pltpu.make_async_copy(out_ref.at[other], other_hbm.at[r], o_sem.at[group + r]))
        stores.append(pltpu.make_async_copy(out_ref.at[own], out_hbm.at[core * group + r], o_sem.at[r]))
    dpre_store = pltpu.make_async_copy(out_ref, dpre_hbm, d_sem.at[0])
    dmixed_store = pltpu.make_async_copy(cot_ref, dmixed_hbm, d_sem.at[1])

    @pl.when(step == 0)
    def _():
        for copy in weights + loads + values:
            copy.start()

    for c in range(chunks):
        @pl.when(step == c)
        def _():
            weights[2 * c].wait()
            weights[2 * c + 1].wait()

    @pl.when(step < chunks)
    def _():
        base = pl.multiple_of(step * chunk, chunk)
        for n in range(len(pieces)):
            cols = pl.ds(base + n * piece, piece)
            act, slope = gelu_pair(row_dot(low_ref[...], win_ref[:, cols]) + bi_ref[:, cols])
            act_ref[:, cols] = act.astype(BF)
            slope_ref[:, cols] = slope.astype(BF)
        rows = pl.ds(base, chunk)

        @pl.when(step == 0)
        def _():
            for cols in pieces:
                acc_ref[:, cols] = row_dot(act_ref[:, rows], wback_ref[rows, cols])

        @pl.when(step > 0)
        def _():
            for cols in pieces:
                acc_ref[:, cols] += row_dot(act_ref[:, rows], wback_ref[rows, cols])

    block = 256

    @pl.when(step == chunks - 1)
    def _():
        for load in loads:
            load.wait()
        gg2_ref[...] = jnp.zeros_like(gg2_ref)
        gs2_ref[...] = jnp.zeros_like(gs2_ref)
        gb2_ref[...] = jnp.zeros_like(gb2_ref)

        def token_body(i, carry):
            at = pl.ds(pl.multiple_of(i * block, block), block)
            pre = low_ref[at, :].astype(F32) + acc_ref[at, :] + bb_ref[...]
            center = pre - jnp.mean(pre, axis=-1, keepdims=True)
            inv = lax.rsqrt(jnp.mean(center * center, axis=-1, keepdims=True) + EPS)
            hat = center * inv
            out_ref[at, :] = (hat * g2_ref[...] + s2_ref[...]).astype(BF)
            dy = cot_ref[at, :].astype(F32)
            gg2_ref[...] += jnp.sum(dy * hat, axis=0, keepdims=True)
            gs2_ref[...] += jnp.sum(dy, axis=0, keepdims=True)
            g = dy * g2_ref[...]
            dpre = inv * (g - jnp.mean(g, axis=-1, keepdims=True) - hat * jnp.mean(g * hat, axis=-1, keepdims=True))
            dfeed = dpre.astype(BF)
            dfeed_ref[at, :] = dfeed
            gb2_ref[...] += jnp.sum(dfeed.astype(F32), axis=0, keepdims=True)
            return carry

        lax.fori_loop(0, total // block, token_body, 0)
        for store in stores:
            store.start()
        which = lax.broadcasted_iota(jnp.int32, (8, 1), 0)
        across = lax.broadcasted_iota(jnp.int32, (1, length), 1)
        for r in range(group):
            down = jnp.full((8, 1), -1, jnp.int32)
            for j, start in enumerate(row_starts(len_ref, core * group + r)):
                down = jnp.where(which == j, start, down)
            choose = (down == across).astype(F32).astype(BF)
            cls_ref[r] = row_dot(choose, out_ref[r * length : (r + 1) * length]).astype(BF)

    def put_grad(value, kept, sent, stack):
        if split:
            grad_ref[...] = value
            split_store(grad_ref, kept, sent, core, 2, stack)
        else:
            kept[...] = value.astype(BF)

    keep_b, keep_i = grads[0], grads[n_grads // 2]
    send_b, send_i = (grads[1], grads[3]) if split else (None, None)

    @pl.when(jnp.logical_and(step >= chunks, step < 2 * chunks))
    def _():
        base = pl.multiple_of((step - chunks) * chunk, chunk)
        rows = pl.ds(base, chunk)
        put_grad(col_dot(act_ref[:, rows], dfeed_ref[...]), keep_b, send_b, chunks)
        for n in range(len(pieces)):
            cols = pl.ds(base + n * piece, piece)
            inner = (row_dot_t(dfeed_ref[...], wback_ref[cols, :]) * slope_ref[:, cols].astype(F32)).astype(BF)
            slope_ref[:, cols] = inner
            gi_ref[:, cols] = jnp.sum(inner.astype(F32), axis=0, keepdims=True)

        @pl.when(step == chunks)
        def _():
            for cols in pieces:
                acc_ref[:, cols] = row_dot_t(slope_ref[:, rows], win_ref[cols, rows])

        @pl.when(step > chunks)
        def _():
            for cols in pieces:
                acc_ref[:, cols] += row_dot_t(slope_ref[:, rows], win_ref[cols, rows])

        put_grad(col_dot(low_ref[...], slope_ref[:, rows]), keep_i, send_i, 1)

    @pl.when(step == 2 * chunks)
    def _():
        for store in stores:
            store.wait()
        for value in values:
            value.wait()
        gg1_ref[...] = jnp.zeros_like(gg1_ref)
        gs1_ref[...] = jnp.zeros_like(gs1_ref)
        gb1_ref[...] = jnp.zeros_like(gb1_ref)

        def token_body(i, carry):
            at = pl.ds(pl.multiple_of(i * block, block), block)
            dn = dfeed_ref[at, :].astype(F32) + acc_ref[at, :]
            hat = hat1_ref[at, :].astype(F32)
            gg1_ref[...] += jnp.sum(dn * hat, axis=0, keepdims=True)
            gs1_ref[...] += jnp.sum(dn, axis=0, keepdims=True)
            g = dn * g1_ref[...]
            dpre = inv1_ref[at, :] * (g - jnp.mean(g, axis=-1, keepdims=True) - hat * jnp.mean(g * hat, axis=-1, keepdims=True))
            branch = dpre.astype(BF)
            out_ref[at, :] = branch
            gb1_ref[...] += jnp.sum(branch.astype(F32), axis=0, keepdims=True)
            return carry

        lax.fori_loop(0, total // block, token_body, 0)
        dpre_store.start()
        for cols in pieces:
            cot_ref[:, cols] = (row_dot_t(out_ref[...], wout_ref[cols, :]) * scale_ref[:, cols]).astype(BF)
        dmixed_store.start()
        put_grad(col_dot(mixed_ref[...], out_ref[...]), keep_i, send_i, 1)
        dpre_store.wait()
        dmixed_store.wait()


def feed_call(core, lengths, low, w_in, w_back, w_out, mixed, hat1, inv1, scale, cot, cot_other, vectors, dp, split):
    total, width = low.shape
    half = cot.shape[1]
    group = cot.shape[0] // 2
    hidden = w_in.shape[1]
    chunks = hidden // width

    def in_back(j):
        return jnp.clip(j - chunks, 0, chunks - 1)

    def in_inner(j):
        return jnp.clip(j - chunks, 0, chunks)

    one = jax.ShapeDtypeStruct((1, width), F32)
    row = jax.ShapeDtypeStruct((total, width), BF)
    shapes = [
        jax.ShapeDtypeStruct(cot.shape, BF),
        jax.ShapeDtypeStruct(cot_other.shape, BF),
        jax.ShapeDtypeStruct((group, 8, width), BF),
        row,
        row,
        jax.ShapeDtypeStruct((1, hidden), F32),
    ] + [one] * 6
    specs = [HBM, HBM, whole((group, 8, width)), HBM, HBM, whole((1, hidden))] + [whole((1, width))] * 6
    if split:
        rows_i = width // (2 * dp)
        devices = dp // chunks
        shapes += [jax.ShapeDtypeStruct((2 * chunks, dp, rows_i, LANES), BF)] * 2
        specs += [pl.BlockSpec((2 * chunks, devices, rows_i, LANES), lambda j, *_: (0, in_back(j), 0, 0))] * 2
        shapes += [jax.ShapeDtypeStruct((2 * (chunks + 1), dp, rows_i, LANES), BF)] * 2
        specs += [pl.BlockSpec((2, dp, rows_i, LANES), lambda j, *_: (in_inner(j), 0, 0, 0))] * 2
    else:
        shapes += [jax.ShapeDtypeStruct((hidden, width), BF), jax.ShapeDtypeStruct((width, hidden + width), BF)]
        specs += [pl.BlockSpec((width, width), lambda j, *_: (in_back(j), 0)), pl.BlockSpec((width, width), lambda j, *_: (0, in_inner(j)))]
    return pl.pallas_call(
        partial(feed_kernel, split),
        name="feed_rows",
        out_shape=shapes,
        grid_spec=pltpu.PrefetchScalarGridSpec(
            num_scalar_prefetch=2,
            grid=(2 * chunks + 1,),
            in_specs=[pl.BlockSpec((total, width), lambda *_: (0, 0), pipeline_mode=pl.Buffered(1))]
            + [ANY] * 9
            + [whole((1, hidden))]
            + [whole((width,))] * 4,
            out_specs=specs,
            scratch_shapes=[
                pltpu.VMEM(w_in.shape, BF),
                pltpu.VMEM(w_back.shape, BF),
                pltpu.VMEM(w_out.shape, BF),
                pltpu.VMEM((total, width), BF),
                pltpu.VMEM((total, width), BF),
                pltpu.VMEM((total, 1), F32),
                pltpu.VMEM((total, width), F32),
                pltpu.VMEM((total, width), BF),
                pltpu.VMEM((total, width), BF),
                pltpu.VMEM((total, hidden), BF),
                pltpu.VMEM((total, hidden), BF),
                pltpu.VMEM((total, width), F32),
                pltpu.VMEM((total, width), BF),
                pltpu.VMEM((width, width), F32),
                pltpu.SemaphoreType.DMA((2 * chunks,)),
                pltpu.SemaphoreType.DMA((5,)),
                pltpu.SemaphoreType.DMA((2 * group,)),
                pltpu.SemaphoreType.DMA((2 * group,)),
                pltpu.SemaphoreType.DMA((2,)),
            ],
        ),
        compiler_params=params(60),
        cost_estimate=pl.CostEstimate(flops=2 * total * width * (6 * hidden + 2 * width), bytes_accessed=40 << 20, transcendentals=2 * total * hidden),
    )(core, lengths, low, w_in, w_back, w_out, mixed, hat1, inv1, scale, cot, cot_other, *vectors)


def weight_grad(left, right, block_m, block_n, name):
    total, m = left.shape
    n = right.shape[1]

    def body(l_ref, r_ref, o_ref, t_ref):
        @pl.when(pl.program_id(1) == 0)
        def _():
            t_ref[...] = l_ref[...].T

        o_ref[...] = row_dot(t_ref[...], r_ref[...]).astype(BF)

    return pl.pallas_call(
        body,
        name=name,
        out_shape=jax.ShapeDtypeStruct((m, n), BF),
        grid=(m // block_m, n // block_n),
        in_specs=[pl.BlockSpec((total, block_m), lambda i, j: (0, i)), pl.BlockSpec((total, block_n), lambda i, j: (0, j))],
        out_specs=pl.BlockSpec((block_m, block_n), lambda i, j: (i, j)),
        scratch_shapes=[pltpu.VMEM((block_m, total), BF)],
        compiler_params=params(63),
        cost_estimate=pl.CostEstimate(flops=2 * total * m * n, bytes_accessed=2 * (total * (m + n) + m * n), transcendentals=0),
    )(left, right)


def attention_grad_kernel(lower, qkv_ref, mixed_ref, d_ref, probs_hbm, *rest):
    out_ref, bq_ref, bv_ref, p_ref, p_sem = rest[-5:]
    step = pl.program_id(0)
    length, width = mixed_ref.shape[1:]
    pairs = width // 128
    scale = (width // HEADS) ** -0.5

    def fetch(pair, slot):
        return pltpu.make_async_copy(probs_hbm.at[lower + step, pair], p_ref.at[slot], p_sem.at[slot])

    fetch(0, 0).start()

    @pl.when(step == 0)
    def _():
        bq_ref[...] = jnp.zeros_like(bq_ref)
        bv_ref[...] = jnp.zeros_like(bv_ref)

    first = lax.broadcasted_iota(jnp.int32, (1, 128), 1) < 64

    def pair_body(pair, carry):
        slot = lax.rem(pair, 2)

        @pl.when(pair + 1 < pairs)
        def _():
            fetch(pair + 1, 1 - slot).start()

        at = pl.ds(pl.multiple_of(pair * 128, 128), 128)
        q = qkv_ref[0, :, at]
        k = qkv_ref[0, :, pl.ds(pl.multiple_of(width + pair * 128, 128), 128)]
        v = qkv_ref[0, :, pl.ds(pl.multiple_of(2 * width + pair * 128, 128), 128)]
        d = d_ref[0, :, at]
        product = d.astype(F32) * mixed_ref[0, :, at].astype(F32)
        q_t, d_t, k_t = q.T, d.T, k.T
        fetch(pair, slot).wait()
        dqs, dks, dvs = [], [], []
        for h in range(2):
            on = first if h == 0 else jnp.logical_not(first)
            part = slice(h * 64, (h + 1) * 64)
            delta = jnp.sum(jnp.where(on, product, 0.0), axis=-1, keepdims=True)
            dprobs = row_dot_t(jnp.where(on, d, jnp.zeros_like(d)), v)
            p = p_ref[slot, h]
            ds = (p.astype(F32) * (dprobs - delta)).astype(BF)
            dqs.append(row_dot_t(k_t[part], ds))
            dks.append(row_dot(q_t[part], ds))
            dvs.append(row_dot(d_t[part], p))
        dq = (jnp.concatenate(dqs, axis=0) * scale).T.astype(BF)
        dv = jnp.concatenate(dvs, axis=0).T.astype(BF)
        out_ref[0, 0, :, at] = dq
        out_ref[1, 0, :, at] = jnp.concatenate(dks, axis=0).T.astype(BF)
        out_ref[2, 0, :, at] = dv
        bq_ref[:, at] += jnp.sum(dq.astype(F32), axis=0, keepdims=True)
        bv_ref[:, at] += jnp.sum(dv.astype(F32), axis=0, keepdims=True)
        return carry

    lax.fori_loop(0, pairs, pair_body, 0)


def attention_grad(qkv, probs, mixed, d, lower, count, partial_out=None):
    rows, length, width = mixed.shape
    more = [] if partial_out is None else [partial_out]

    def full(n):
        return pl.BlockSpec((1, length, n), lambda r: (lower + r, 0, 0))

    one = jax.ShapeDtypeStruct((1, width), F32)
    return pl.pallas_call(
        partial(attention_grad_kernel, lower),
        name="attention_grad",
        out_shape=[jax.ShapeDtypeStruct((3, rows, length, width), BF), one, one],
        grid=(count,),
        input_output_aliases={4: 0} if more else {},
        in_specs=[full(3 * width), full(width), full(width), ANY] + [ANY] * len(more),
        out_specs=[pl.BlockSpec((3, 1, length, width), lambda r: (0, lower + r, 0, 0)), whole((1, width)), whole((1, width))],
        scratch_shapes=[pltpu.VMEM((2, 2, length, length), BF), pltpu.SemaphoreType.DMA((2,))],
        compiler_params=params(63),
        cost_estimate=pl.CostEstimate(flops=8 * count * length * length * width, bytes_accessed=(15 * count) << 20, transcendentals=0),
    )(qkv, mixed, d, probs, *more)


def input_grad_call(core, dproj, dpre, w_qkv, half):
    _, total, width = dproj.shape
    length = 2 * half
    group = total // length

    def body(core_ref, p_ref, d_ref, w_ref, own_hbm, other_hbm, acc_ref, out_ref, sem):
        step = pl.program_id(0)
        core = core_ref[0]
        value = row_dot_t(p_ref[0], w_ref[...])

        @pl.when(step == 0)
        def _():
            acc_ref[...] = value + d_ref[...].astype(F32)

        @pl.when(step == 1)
        def _():
            acc_ref[...] += value

        @pl.when(step == 2)
        def _():
            out_ref[...] = (acc_ref[...] + value).astype(BF)
            stores = []
            for r in range(group):
                other = pl.ds(pl.multiple_of(r * length + (1 - core) * half, half), half)
                own = pl.ds(pl.multiple_of(r * length + core * half, half), half)
                stores.append(pltpu.make_async_copy(out_ref.at[other], other_hbm.at[r], sem.at[r]))
                stores.append(pltpu.make_async_copy(out_ref.at[own], own_hbm.at[core * group + r], sem.at[group + r]))
            for store in stores:
                store.start()
            for store in stores:
                store.wait()

    return pl.pallas_call(
        body,
        name="input_grad",
        out_shape=[jax.ShapeDtypeStruct((2 * group, half, width), BF), jax.ShapeDtypeStruct((group, half, width), BF)],
        grid_spec=pltpu.PrefetchScalarGridSpec(
            num_scalar_prefetch=1,
            grid=(3,),
            in_specs=[
                pl.BlockSpec((1, total, width), lambda n, *_: (n, 0, 0)),
                whole((total, width)),
                pl.BlockSpec((width, width), lambda n, *_: (0, n)),
            ],
            out_specs=[HBM, HBM],
            scratch_shapes=[pltpu.VMEM((total, width), F32), pltpu.VMEM((total, width), BF), pltpu.SemaphoreType.DMA((2 * group,))],
        ),
        compiler_params=params(63),
        cost_estimate=pl.CostEstimate(flops=6 * total * width * width, bytes_accessed=10 << 20, transcendentals=0),
    )(core, dproj, dpre, w_qkv)


def vector_table(parts, devices, more=()):
    cut = sum(p.shape[1] for p in parts) // devices

    def body(*refs):
        *ins, out = refs
        values = [ref[...] for ref in ins[: len(parts)]]
        for i, ref in enumerate(ins[len(parts) :]):
            values[i] = values[i] + ref[...]
        joined = jnp.concatenate(values, axis=1)
        out[...] = jnp.zeros_like(out)
        for d in range(devices):
            out[d : d + 1, :cut] = joined[:, d * cut : (d + 1) * cut]

    return pl.pallas_call(
        body,
        name="vector_table",
        out_shape=jax.ShapeDtypeStruct((devices, LANES), F32),
        compiler_params=params(63),
    )(*parts, *more)


def swap(value):
    return lax.ppermute(value, "seq", [(0, 1), (1, 0)])


def pick(value, index, axis):
    return lax.dynamic_index_in_dim(value, index, axis, keepdims=False)


def reduce_stages(part, order, dp_bits, dp):
    me = lax.axis_index("dp")
    n_halving = dp_bits - 2
    shape = part.shape[1:]
    current = part.reshape((2,) * dp_bits + shape)
    left = list(range(dp_bits - 1, -1, -1))
    for bit in order[:n_halving]:
        axis = left.index(bit)
        mine = (me >> bit) & 1
        pairs = [(i, i ^ (1 << bit)) for i in range(dp)]
        send = pick(current, 1 - mine, axis).astype(BF)
        got = lax.ppermute(send, "dp", pairs)
        keep = pick(current, mine, axis)
        current = (keep.astype(F32) + got.astype(F32)).astype(BF)
        left.remove(bit)
    high, low = left
    group = (((me >> high) & 1) << 1) | ((me >> low) & 1)
    current = current.reshape((4,) + shape)
    total = pick(current, group, 0).astype(F32)
    for other in (1, 2, 3):
        flip = ((other >> 1) << high) | ((other & 1) << low)
        pairs = [(i, i ^ flip) for i in range(dp)]
        send = pick(current, group ^ other, 0).astype(BF)
        total = total + lax.ppermute(send, "dp", pairs).astype(F32)
    return total


def reduce_scatter(grad, order, dp, dp_bits):
    core = lax.axis_index("seq")
    rows = grad.shape[0] // (2 * dp)
    blocks = grad.reshape(dp, 2, rows, grad.shape[1])
    send = pick(blocks, 1 - core, 1).astype(BF)
    keep = pick(blocks, core, 1)
    part = (keep.astype(F32) + swap(send).astype(F32)).astype(BF)
    return reduce_stages(part, order, dp_bits, dp)


LANES = 384


def split_store(acc_ref, keep_ref, send_ref, core, parts, stack):
    rows = keep_ref.shape[2]
    for d in range(acc_ref.shape[0] // (2 * stack * rows)):
        for ref, side in ((keep_ref, core), (send_ref, 1 - core)):
            for r in range(stack):
                value = acc_ref[pl.ds(pl.multiple_of(((2 * d + side) * stack + r) * rows, 8), rows), :].astype(BF)
                for c in range(parts):
                    ref[c * stack + r, d] = value[:, c * LANES : (c + 1) * LANES]


def grad_proj(core, left, right, vectors, more, dp):
    total, m = left.shape
    n = 2 * LANES
    rows = m // (2 * dp)
    deep = rows // 8
    blocks = 3 * deep + 1
    cut = sum(v.shape[1] for v in vectors) // (2 * dp)

    def body(core_ref, l_ref, r_ref, *refs):
        ins = refs[: len(vectors) + len(more)]
        keep_ref, send_ref, acc_ref, table_ref = refs[len(ins) :]
        acc_ref[...] = col_dot(l_ref[...], r_ref[0])
        core = core_ref[0]
        step = pl.program_id(0)
        for ref, side in ((keep_ref, core), (send_ref, 1 - core)):
            for d in range(dp):
                value = acc_ref[pl.ds(pl.multiple_of((2 * d + side) * rows, 8), rows), :].astype(BF)
                for c in range(2):
                    chunk = 2 * step + c
                    first = lax.div(chunk, 3) * blocks + lax.rem(chunk, 3) * deep
                    for r in range(deep):
                        ref[first + r, d] = value[8 * r : 8 * r + 8, c * LANES : (c + 1) * LANES]

        @pl.when(step == 0)
        def _():
            values = [ref[...] for ref in ins[: len(vectors)]]
            for i, ref in enumerate(ins[len(vectors) :]):
                values[i] = values[i] + ref[...]
            joined = jnp.concatenate(values, axis=1)
            table_ref[...] = jnp.zeros_like(table_ref)
            for d in range(2 * dp):
                table_ref[d : d + 1, :cut] = joined[:, d * cut : (d + 1) * cut]
            for ref, side in ((keep_ref, core), (send_ref, 1 - core)):
                for d in range(dp):
                    line = table_ref[pl.ds(2 * d + side, 1), :].astype(BF)
                    ref[blocks - 1, d] = jnp.broadcast_to(line, (8, LANES))
                    ref[2 * blocks - 1, d] = jnp.zeros((8, LANES), BF)

    out = jax.ShapeDtypeStruct((2 * blocks, dp, 8, LANES), BF)
    return pl.pallas_call(
        body,
        name="grad_qkv",
        out_shape=[out, out],
        grid_spec=pltpu.PrefetchScalarGridSpec(
            num_scalar_prefetch=1,
            grid=(3,),
            in_specs=[whole((total, m)), pl.BlockSpec((1, total, n), lambda j, *_: (j, 0, 0))] + [whole(v.shape) for v in (*vectors, *more)],
            out_specs=[whole(out.shape)] * 2,
            scratch_shapes=[pltpu.VMEM((m, n), F32), pltpu.VMEM((2 * dp, LANES), F32)],
        ),
        compiler_params=params(63),
        cost_estimate=pl.CostEstimate(flops=6 * total * m * n, bytes_accessed=6 * n * (total + m), transcendentals=0),
    )(core, left, right, *vectors, *more)


def add_pieces(where, groups, name):
    counts = [len(pieces([jnp.int32(0)] * 3)) for _, _, pieces, _ in groups]
    inputs = [i for g in groups for i in g[0]]
    outputs = [o for g in groups for o in g[1]]

    def body(where_ref, *refs):
        ins = refs[: len(inputs)]
        outs = refs[len(inputs) : len(inputs) + len(outputs)]
        scratch = refs[len(inputs) + len(outputs) :]
        loads, stores, sums = [], [], []
        for n, (group_in, group_out, pieces, _) in enumerate(groups):
            k_ref, g_ref, k_sem, g_sem, o_sem = scratch[5 * n : 5 * n + 5]
            for i, (a, a_at, b, b_at, o, o_at) in enumerate(pieces([where_ref[0], where_ref[1], where_ref[2]])):
                loads.append(pltpu.make_async_copy(ins[a].at[a_at], k_ref.at[i], k_sem.at[i]))
                loads.append(pltpu.make_async_copy(ins[b].at[b_at], g_ref.at[i], g_sem.at[i]))
                stores.append(pltpu.make_async_copy(k_ref.at[i], outs[o].at[o_at], o_sem.at[i]))
                sums.append((k_ref, g_ref, i))
            ins, outs = ins[len(group_in) :], outs[len(group_out) :]
        for load in loads:
            load.start()
        for i, (k_ref, g_ref, at) in enumerate(sums):
            loads[2 * i].wait()
            loads[2 * i + 1].wait()
            k_ref[at] = k_ref[at] + g_ref[at]
            stores[i].start()
        for store in stores:
            store.wait()

    scratch_shapes = []
    for (_, _, _, shape), count in zip(groups, counts):
        scratch_shapes += [pltpu.VMEM((count,) + shape, BF)] * 2 + [pltpu.SemaphoreType.DMA((count,))] * 3
    result = pl.pallas_call(
        body,
        name=name,
        out_shape=[jax.ShapeDtypeStruct(s, BF) for s in outputs],
        grid_spec=pltpu.PrefetchScalarGridSpec(
            num_scalar_prefetch=1,
            grid=(1,),
            in_specs=[ANY] * len(inputs),
            out_specs=[HBM] * len(outputs),
            scratch_shapes=scratch_shapes,
        ),
        compiler_params=params(63),
    )(where, *inputs)
    split = []
    for _, group_out, _, _ in groups:
        split.append(result[: len(group_out)])
        result = result[len(group_out) :]
    return split


def fold_first(keep, got):
    _, blocks, _, _, _, rows, lanes = keep.shape
    every = slice(None)

    def pieces(at):
        _, y, x = at
        table = []
        for role in (1, 0):
            for z in range(4):
                ax = x if role == 0 else 1 - x
                ay = y if role == 0 else 1 - y
                for half, index in ((0, (0, every, z, every, ax)), (1, (1, every, z, ay))):
                    table.append((0, index, 1, index, 2 * half + (1 - role), (every, z)))
        return table

    return (keep, got), [(blocks, 4, 2, rows, lanes)] * 4, pieces, (blocks, 2, rows, lanes)


def fold_second(parts, got):
    blocks, _, _, rows, lanes = parts[1].shape
    every = slice(None)

    def pieces(at):
        _, y, x = at
        table = []
        for role in (1, 0):
            for z in range(4):
                for half, own in ((0, y), (1, x)):
                    index = (every, z, own if role == 0 else 1 - own)
                    table.append((2 * half, index, 2 * half + 1, index, 2 * half + (1 - role), (every, z)))
        return table

    return (parts[1], got[0], parts[3], got[1]), [(blocks, 4, rows, lanes)] * 4, pieces, (blocks, rows, lanes)


def fold_third(parts, got):
    blocks, _, rows, lanes = parts[1].shape
    every = slice(None)

    def pieces(at):
        table = []
        for z in range(4):
            for half in range(2):
                table.append((2 * half, (every, z), 2 * half + 1, (every, z), 0, (z, half)))
        return table

    return (parts[1], got[0], parts[3], got[1]), [(4, 2, blocks, rows, lanes)], pieces, (blocks, rows, lanes)


def fold_last(parts, widths, name, stack=1, extra=0):
    _, _, blocks, deep, lanes = parts.shape
    chunks = sum(widths) // (2 * lanes)
    rows = (blocks * deep - extra) // (chunks * stack)

    def body(part_ref, *outs):
        def take(half, line, count, at, size):
            step = min(deep, count)
            pieces = []
            for start in range(line, line + count, step):
                total = None
                for z in range(4):
                    value = part_ref[z, half, start // deep, start % deep : start % deep + step, at : at + size].astype(F32)
                    total = value if total is None else total + value
                pieces.append(total)
            return pieces[0] if len(pieces) == 1 else jnp.concatenate(pieces, axis=0)

        base = 0
        for out, width in zip(outs, widths):
            tiles = width // 128
            for r in range(stack):
                for t in range(tiles):
                    chunk, at = (base + t * 128) // lanes, (base + t * 128) % lanes
                    line = (chunk % chunks * stack + r) * rows
                    out[pl.ds(r * rows * tiles + t, rows, stride=tiles), :] = take(chunk // chunks, line, rows, at, 128)
            base += width
        if extra:
            outs[-1][...] = take(0, blocks * deep - extra, extra, 0, lanes)

    shapes = [jax.ShapeDtypeStruct((stack * rows * w // 128, 128), F32) for w in widths]
    if extra:
        shapes.append(jax.ShapeDtypeStruct((extra, lanes), F32))
    return pl.pallas_call(body, name=name, out_shape=shapes, compiler_params=params(63))(parts)


def sync(*values):
    return lax.optimization_barrier(values)


def flip(value, bits):
    return lax.ppermute(value, "dp", [(i, i ^ bits) for i in range(16)])


def on_device(tokens, lengths, w_qkv, w_out, w_in, w_back, bias_q, value_bias, bias_out, gain1, shift1, bias_in, bias_back, gain2, shift2, cotangent):
    rows_local, half, width = tokens.shape
    dp = lax.axis_size("dp")
    dp_bits = dp.bit_length() - 1
    core = lax.axis_index("seq")
    rows = rows_local // 2
    length = 2 * half
    total = rows * length
    order_a = (0, 1) + tuple(range(2, dp_bits))
    order_b = (1, 0) + tuple(range(2, dp_bits))

    def send_rows(value):
        return swap(lax.dynamic_slice_in_dim(value, (1 - core) * rows, rows, 0))

    other = send_rows(tokens)
    cot_other = send_rows(cotangent)
    bq, bv, bo, g1, s1, bi, bb, g2, s2 = (bias_q, value_bias, bias_out, gain1, shift1, bias_in, bias_back, gain2, shift2)
    core_one = core.reshape(1).astype(jnp.int32)
    me = lax.axis_index("dp")
    fast = dp == 16 and width == 2 * LANES
    qkv, probs, full_tokens, mixed, low, hat1, inv1, inverse = attention_call(core_one, lengths, tokens, other, w_qkv, w_out, (bq, bv, bo, g1, s1))

    def flat(value):
        return value.reshape(total, value.shape[-1])

    full_tokens = flat(full_tokens)
    output, output_other, cls_own, dpre1, dmixed, g_bias_in, g_gain2, g_shift2, g_bias_back, g_gain1, g_shift1, g_bias_out, *grads = feed_call(
        core_one, lengths, flat(low), w_in, w_back, w_out, flat(mixed), flat(hat1), flat(inv1), flat(inverse), cotangent, cot_other,
        (bi.reshape(1, -1), bb, g1, g2, s2), dp, fast,
    )
    dmixed = dmixed.reshape(rows, length, width)
    cls_own = cls_own[:, : lengths.shape[1]]
    if fast:
        where = jnp.stack([me >> 2, (me >> 1) & 1, me & 1]).astype(jnp.int32)

        def view(value):
            return value.reshape((2, value.shape[0] // 2, 4, 2, 2) + value.shape[2:])

        def cross(parts, bit_a, bit_b):
            return flip(parts[0], bit_a), flip(parts[2], bit_b)

        def along_z(parts):
            return lax.all_to_all(parts, "dp", 0, 0, axis_index_groups=[[i, i + 4, i + 8, i + 12] for i in range(4)], tiled=True)

        keep_b, send_b, keep_i, send_i = grads
        got_b = swap(send_b)
        (back,) = add_pieces(where, [fold_first(view(keep_b), view(got_b))], "fold_a")
        dmixed, back, send_i, output_other = sync(dmixed, back, send_i, output_other)
        got_b = cross(back, 1, 2)
        got_i = swap(send_i)
        output_got = swap(output_other)
        dproj, *bias_a = attention_grad(qkv, probs, mixed, dmixed, 0, 1)
        dproj, got_b, got_i, keep_i, output_got = sync(dproj, got_b, got_i, keep_i, output_got)
        inner, back = add_pieces(where, [fold_first(view(keep_i), view(got_i)), fold_second(back, got_b)], "fold_b")
        dmixed, inner, back = sync(dmixed, inner, back)
        got_i = cross(inner, 1, 2)
        got_b = cross(back, 2, 1)
        dproj, *bias_b = attention_grad(qkv, probs, mixed, dmixed, 1, 1, dproj)
        keep_q, send_q = grad_proj(
            core_one, full_tokens, dproj.reshape(3, total, width),
            (bias_a[0], bias_a[1], g_bias_out, g_gain1, g_shift1, g_bias_in, g_bias_back, g_gain2, g_shift2), bias_b, dp,
        )
        send_q, keep_q, got_b, got_i = sync(send_q, keep_q, got_b, got_i)
        got_q = swap(send_q)
        inner, back = add_pieces(where, [fold_second(inner, got_i), fold_third(back, got_b)], "fold_c")
        inner, back, got_q, keep_q = sync(inner, back, got_q, keep_q)
        got_i = cross(inner, 2, 1)
        got_b = along_z(back[0])
        (proj,) = add_pieces(where, [fold_first(view(keep_q), view(got_q))], "fold_d")
        dproj, proj = sync(dproj, proj)
        got_q = cross(proj, 1, 2)
        dinput, dinput_other = input_grad_call(core_one, dproj.reshape(3, total, width), dpre1, w_qkv, half)
        output, dinput = sync(output, dinput)
        output = lax.dynamic_update_slice_in_dim(output, output_got, (1 - core) * rows, 0)
        output, dinput, dinput_other, got_i, got_q, got_b, cls_own = sync(output, dinput, dinput_other, got_i, got_q, got_b, cls_own)
        inner, proj = add_pieces(where, [fold_third(inner, got_i), fold_second(proj, got_q)], "fold_e")
        inner, proj, dinput_other, cls_own = sync(inner, proj, dinput_other, cls_own)
        got_q = cross(proj, 2, 1)
        got_i = along_z(inner[0])
        cls_got = swap(cls_own)
        dinput_got = swap(dinput_other)
        proj, got_b = sync(proj, got_b)
        (r_back,) = fold_last(got_b, (width,), "back_sum", w_back.shape[0] // width)
        r_back, got_q, cls_got, dinput_got = sync(r_back, got_q, cls_got, dinput_got)
        (proj,) = add_pieces(where, [fold_third(proj, got_q)], "fold_f")
        proj, got_i, dinput = sync(proj, got_i, dinput)
        got_q = along_z(proj[0])
        r_in, r_out = fold_last(got_i, (w_in.shape[1], width), "inner_sum")
        dinput = lax.dynamic_update_slice_in_dim(dinput, dinput_got, (1 - core) * rows, 0)
        r_in, got_q, dinput = sync(r_in, got_q, dinput)
        r_qkv, r_vec = fold_last(got_q, (3 * width,), "proj_sum", 1, 8)
        r_vec = r_vec[0, : (8 * width + w_in.shape[1]) // (2 * dp)]
    else:
        g_back, g_inner = grads
        r_back = reduce_scatter(g_back, order_a, dp, dp_bits)
        r_inner = reduce_scatter(g_inner, order_b, dp, dp_bits)
        r_in, r_out = r_inner[:, :-width], r_inner[:, -width:]
        output_got, cls_got = swap(output_other), swap(cls_own)
        dproj, g_bias_q, g_bias_v = attention_grad(qkv, probs, mixed, dmixed, 0, rows)
        dproj = dproj.reshape(3, total, width)
        g_qkv = jnp.concatenate([weight_grad(full_tokens, dproj[n], width, width, "grad_qkv") for n in range(3)], axis=1)
        r_qkv = reduce_scatter(g_qkv, order_b, dp, dp_bits)
        dinput, dinput_other = input_grad_call(core_one, dproj, dpre1, w_qkv, half)
        dinput_got = swap(dinput_other)
    if not fast:
        table = vector_table((g_bias_q, g_bias_v, g_bias_out, g_gain1, g_shift1, g_bias_in, g_bias_back, g_gain2, g_shift2), 2 * dp)
        r_vec = jnp.sum(lax.all_to_all(table, ("dp", "seq"), 0, 0, tiled=True), axis=0)[: (8 * width + w_in.shape[1]) // (2 * dp)]
        output = lax.dynamic_update_slice_in_dim(output, output_got, (1 - core) * rows, 0)
        dinput = lax.dynamic_update_slice_in_dim(dinput, dinput_got, (1 - core) * rows, 0)
    cls = jnp.where(core == 0, jnp.concatenate([cls_own, cls_got], axis=0), jnp.concatenate([cls_got, cls_own], axis=0))
    return (
        output,
        cls,
        dinput,
        r_qkv.reshape(-1),
        r_out.reshape(-1),
        r_in.reshape(-1),
        r_back.reshape(-1),
        r_vec,
    )


def solution(mesh):
    row = P("dp", "seq", None)
    both = P(("dp", "seq"))
    return jax.shard_map(
        on_device,
        mesh=mesh,
        in_specs=(row, P("dp", None)) + (P(),) * 13 + (row,),
        out_specs=(row, P("dp", None, None), row, both, both, both, both, both),
        check_vma=False,
    )
```

time: 244 us -> 236 us (0.967)
  starting transfers between devices: 36.8 us -> 31.4 us
  Pallas kernels: 164 us -> 161 us
    ppermute x21 -> x12, starting transfers between devices: 32.1 us -> 15.6 us  [flip(): return lax.ppermute(value, 'dp', [(i, i ^ bits) for i in range(16)])]
    ppermute x21 -> x12, waiting for transfers between devices: 26.6 us -> 11.8 us  [flip(): return lax.ppermute(value, 'dp', [(i, i ^ bits) for i in range(16)])]
    all_to_all x1 -> x3, waiting for transfers between devices: 0.01 us -> 12.3 us  [along_z(): lax.all_to_all(parts, 'dp', 0, 0, axis_index_groups=[[i, i + 4, i + 8, i...]
    all_to_all x1 -> x3, starting transfers between devices: 2.58 us -> 13.8 us  [along_z(): lax.all_to_all(parts, 'dp', 0, 0, axis_index_groups=[[i, i + 4, i + 8, i...]
    pallas_call x9 -> x6, Pallas kernels: 32.9 us -> 27.9 us  [add_pieces(): pl.pallas_call(body, name=name, out_shape=[jax.ShapeDtypeStruct(s, BF) fo...]
    ppermute x8, waiting for transfers between devices: 1.55 us -> 5.46 us  [swap(): return lax.ppermute(value, 'seq', [(0, 1), (1, 0)])]
    unnamed x47 -> x19, local copies, waits for them, and re-layouts: 5.12 us -> 3.88 us
    pallas_call x9 -> x7, Pallas kernels: 94.6 us -> 95.4 us  [the longest x1 54.3 us: feed_call(): pl.pallas_call(partial(feed_kernel, split), name='feed_rows', out_shape=s...]
  transfers between devices with their start and end apart: 30 -> 23, of which waited for: 9 -> 8; matrix products, arithmetic and copies ran while one was open for 3% -> 3% of each run, Pallas kernels for 44% -> 38%
where the time goes in v4:
time: 236 us; the launch traced here: 235 us
  Pallas kernels  161 us (68%)
  starting transfers between devices  31.4 us (13%)
  waiting for transfers between devices  29.6 us (13%)
  local copies, waits for them, and re-layouts  10.7 us (5%)
    pallas_call x1, Pallas kernels, feed_call(): pl.pallas_call(partial(feed_kernel, split), name='feed_rows', out_shape=s...  54.3 us
    pallas_call x1, Pallas kernels, attention_call(): pl.pallas_call(attention_kernel, name='attention_rows', out_shape=[row(3...  28.9 us
    pallas_call x6, Pallas kernels, add_pieces(): pl.pallas_call(body, name=name, out_shape=[jax.ShapeDtypeStruct(s, BF) fo...  27.9 us
    pallas_call x2, Pallas kernels, attention_grad(): pl.pallas_call(partial(attention_grad_kernel, lower), name='attention_gra...  26.8 us
    ppermute x12, starting transfers between devices, flip(): return lax.ppermute(value, 'dp', [(i, i ^ bits) for i in range(16)])  15.6 us
    all_to_all x3, starting transfers between devices, along_z(): lax.all_to_all(parts, 'dp', 0, 0, axis_index_groups=[[i, i + 4, i + 8, i...  13.8 us
    all_to_all x3, waiting for transfers between devices, along_z(): lax.all_to_all(parts, 'dp', 0, 0, axis_index_groups=[[i, i + 4, i + 8, i...  12.3 us
    ppermute x12, waiting for transfers between devices, flip(): return lax.ppermute(value, 'dp', [(i, i ^ bits) for i in range(16)])  11.8 us
  transfers between devices with their start and end apart: 23, of which 8 were waited for; matrix products, arithmetic and copies ran while one was open for 3% of the time, Pallas kernels for 38%

profile of v4, /device:TPU:0, one launch (start us, length us, event | category | flops | bytes accessed | tf_op | source)
XLA Modules:
  0.0 234.7 jit_solution(1392725562780350407)
XLA Ops:
  5.3 28.9 %attention_rows.1 = (bf16[2,512,2304]{2,1,0:T(8,128)(2,1)}, bf16[2,6,2,512,512]{4,3,2,1,0:T(8,128)(2,1)}, bf16[2,512,768]{2,1,0:T(8,128)(2,1)}, bf16[2,512,768]{...) custom-call(s32[1]{0:T(128)} %bitcast.core_ref, ...), custom_call_target="tpu_custom_call" | custom-call | flops 6442450944 | bytes 36700160 | tf_op jit(solution)/shard_map/attention_rows/pallas_call | solution.py:174
  35.0 54.3 %feed_rows.1 = (bf16[4,256,768]{2,1,0:T(8,128)(2,1)}, bf16[2,256,768]{2,1,0:T(8,128)(2,1)}, bf16[2,8,768]{2,1,0:T(8,128)(2,1)}, bf16[1024,768]{1,0:T(8,128)(2,1)...) custom-call(s32[1]{0:T(128)} %bitcast.core_ref, ...), custom_call_target="tpu_custom_call" | custom-call | flops 31406948352 | bytes 41943040 | tf_op jit(solution)/shard_map/feed_rows/pallas_call | solution.py:426
  90.3 3.9 %collective-permute-done.2 = bf16[8,16,24,384]{3,2,1,0:T(8,128)(2,1)} collective-permute-done((bf16[8,16,24,384]{3,2,1,0:T(8,128)(2,1)}, bf16[8,16,24,384]{3,2,1,0:T(8,128)(2,1)}, u32[]{:S(2)}, u32[]{:S(2)}) %collective-permute-start.2) | collective-permute-done | bytes 2359328 | tf_op jit(solution)/shard_map/ppermute | solution.py:642
  94.2 4.8 %fold_a.1 = (bf16[4,4,2,24,384]{4,3,2,1,0:T(8,128)(2,1)}, bf16[4,4,2,24,384]{4,3,2,1,0:T(8,128)(2,1)}, bf16[4,4,2,24,384]{4,3,2,1,0:T(8,128)(2,1)}, bf16[4,4,2,24,384]{4,3,2,1,0:T(8,128)(2,1)}) custom-call(s32[3]{0:T(128)} %pad_add_fusion.where_ref, bf16[2,4,4,2,2,24,384]{6,5,4,3,2,1,0:T(8,128)(2,1)} %bitcast.31, ...), custom_call_target="tpu_custom_call" | custom-call | tf_op jit(solution)/shard_map/fold_a/pallas_call | solution.py:785
  99.6 2.9 %collective-permute-start.3 = (bf16[4,4,2,24,384]{4,3,2,1,0:T(8,128)(2,1)}, bf16[4,4,2,24,384]{4,3,2,1,0:T(8,128)(2,1)}, u32[]{:S(2)}, u32[]{:S(2)}) collective-permute-start(bf16[4,4,2,24,384]{4,3,2,1,0:T(8,128)(2,1)} %get-tuple-element.163), channel_id=1, source_target_pairs={{0,2},{2,0},{4,6},{6,4},{8,10},{10,8},{12,14},{14,12},{16,18},{18,... | collective-permute-start | bytes 1769480 | tf_op jit(solution)/shard_map/ppermute | solution.py:894
  104.0 13.4 %attention_grad.2 = (bf16[3,2,512,768]{3,2,1,0:T(8,128)(2,1)}, f32[1,768]{1,0:T(1,128)}, f32[1,768]{1,0:T(1,128)}) custom-call(bf16[2,512,2304]{2,1,0:T(8,128)(2,1)} %get-tuple-element.150.qkv_ref, bf16[2,512,768]{2,1,0:T(8,128)(2,1)} %get-tuple-element.145.mixed_ref, bf16[2,512,768]{2,1,0:T(8,128)(2,1)} %bitcast.26, ...), custom_call_target="tpu_custom_call" | custom-call | flops 1610612736 | bytes 15728640 | tf_op jit(solution)/shard_map/attention_grad/pallas_call | solution.py:554
  117.9 7.1 %fold_b.1 = (bf16[5,4,2,24,384]{4,3,2,1,0:T(8,128)(2,1)}, bf16[5,4,2,24,384]{4,3,2,1,0:T(8,128)(2,1)}, bf16[5,4,2,24,384]{4,3,2,1,0:T(8,128)(2,1)}, bf16[5,4,2,2...) custom-call(s32[3]{0:T(128)} %pad_add_fusion.where_ref, ...), custom_call_target="tpu_custom_call" | custom-call | tf_op jit(solution)/shard_map/fold_b/pallas_call | solution.py:785
  129.0 13.4 %attention_grad.3 = (bf16[3,2,512,768]{3,2,1,0:T(8,128)(2,1)}, f32[1,768]{1,0:T(1,128)}, f32[1,768]{1,0:T(1,128)}) custom-call(bf16[2,512,2304]{2,1,0:T(8,128)(2,1)} %get-tuple-element.150.qkv_ref, bf16[2,512,768]{2,1,0:T(8,128)(2,1)} %get-tuple-element.145.mixed_ref, bf16[2,512,768]{2,1,0:T(8,128)(2,1)} %bitcast.27, ...), custom_call_target="tpu_custom_call", output_to_operand_aliasing={{0}: (4, {})} | custom-call | flops 1610612736 | bytes 15728640 | tf_op jit(solution)/shard_map/attention_grad/pallas_call | solution.py:554
  142.4 8.8 %grad_qkv.1 = (bf16[20,16,8,384]{3,2,1,0:T(8,128)(2,1)}, bf16[20,16,8,384]{3,2,1,0:T(8,128)(2,1)}) custom-call(s32[1]{0:T(128)} %bitcast.core_ref, bf16[1024,768]{1,0:T(8,128)(2,1)} %bitcast.41, bf16[3,1024,768]{2,1,0:T(8,128)(2,1)} %bitcast.28, f32[1,768]{1,0:T(1,128)} %get-tuple-element.187.refs_0_, f32[1,768]{1,0:T(1,128)} %get-tuple-element.188.refs_1_, ...), custom_call_target="tpu_custom_call" | custom-call | flops 3623878656 | bytes 8257536 | tf_op jit(solution)/shard_map/grad_qkv/pallas_call | solution.py:738
  152.1 4.7 %fold_c.1 = (bf16[5,4,24,384]{3,2,1,0:T(8,128)(2,1)}, bf16[5,4,24,384]{3,2,1,0:T(8,128)(2,1)}, bf16[5,4,24,384]{3,2,1,0:T(8,128)(2,1)}, bf16[5,4,24,384]{3,2,1,0:T(8,128)(2,1)}, bf16[4,2,4,24,384]{4,3,2,1,0:T(8,128)(2,1)}) custom-call(s32[3]{0:T(128)} %pad_add_fusion.where_ref, bf16[5,4,2,24,384]{4,3,2,1,0:T(8,128)(2,1)} %get-tuple-element.185.refs_0_, ...), custom_call_target="tpu_custom_call" | custom-call | tf_op jit(solution)/shard_map/fold_c/pallas_call | solution.py:785
  156.9 4.9 %all-to-all-start = ((bf16[4,2,4,24,384]{4,3,2,1,0:T(8,128)(2,1)}), bf16[4,2,4,24,384]{4,3,2,1,0:T(8,128)(2,1)S(1)}, u32[]{:S(2)}, u32[]{:S(2)}) async-start(bf16[4,2,4,24,384]{4,3,2,1,0:T(8,128)(2,1)} %get-tuple-element.235), calls=%async_computation | async-start | bytes 1179648 | tf_op jit(solution)/shard_map/all_to_all | solution.py:939
  161.7 4.3 %fold_d.1 = (bf16[10,4,2,8,384]{4,3,2,1,0:T(8,128)(2,1)}, bf16[10,4,2,8,384]{4,3,2,1,0:T(8,128)(2,1)}, bf16[10,4,2,8,384]{4,3,2,1,0:T(8,128)(2,1)}, bf16[10,4,2,8,384]{4,3,2,1,0:T(8,128)(2,1)}) custom-call(s32[3]{0:T(128)} %pad_add_fusion.where_ref, bf16[2,10,4,2,2,8,384]{6,5,4,3,2,1,0:T(8,128)(2,1)} %bitcast.32, ...), custom_call_target="tpu_custom_call" | custom-call | tf_op jit(solution)/shard_map/fold_d/pallas_call | solution.py:785
  170.2 8.5 %input_grad.1 = (bf16[4,256,768]{2,1,0:T(8,128)(2,1)}, bf16[2,256,768]{2,1,0:T(8,128)(2,1)}) custom-call(s32[1]{0:T(128)} %bitcast.core_ref, bf16[3,1024,768]{2,1,0:T(8,128)(2,1)} %bitcast.29, bf16[1024,768]{1,0:T(8,128)(2,1)} %get-tuple-element.225.d_ref, bf16[768,2304]{1,0:T(8,128)(2,1)} %w_ref.1), custom_call_target="tpu_custom_call" | custom-call | flops 3623878656 | bytes 10485760 | tf_op jit(solution)/shard_map/input_grad/pallas_call | solution.py:600
  178.8 2.1 constant_dynamic-update-slice_fusion.1
  180.8 6.3 %collective-permute-done.12.refs_1_ = bf16[5,4,24,384]{3,2,1,0:T(8,128)(2,1)S(1)} collective-permute-done((bf16[5,4,24,384]{3,2,1,0:T(8,128)(2,1)}, bf16[5,4,24,384]{3,2,1,0:T(8,128)(2,1)S(1)}, u32[]{:S(2)}, u32[]{:S(2)}) %collective-permute-start.12) | collective-permute-done | bytes 368672 | tf_op jit(solution)/shard_map/ppermute | solution.py:894
  187.9 4.3 %fold_e.1 = (bf16[4,2,5,24,384]{4,3,2,1,0:T(8,128)(2,1)}, bf16[10,4,8,384]{3,2,1,0:T(8,128)(2,1)}, bf16[10,4,8,384]{3,2,1,0:T(8,128)(2,1)}, bf16[10,4,8,384]{3,2,1,0:T(8,128)(2,1)}, bf16[10,4,8,384]{3,2,1,0:T(8,128)(2,1)}) custom-call(s32[3]{0:T(128)} %pad_add_fusion.where_ref, bf16[5,4,24,384]{3,2,1,0:T(8,128)(2,1)} %get-tuple-element.238.refs_0_, ...), custom_call_target="tpu_custom_call" | custom-call | tf_op jit(solution)/shard_map/fold_e/pallas_call | solution.py:785
  192.2 4.8 %all-to-all-start.1 = ((bf16[4,2,5,24,384]{4,3,2,1,0:T(8,128)(2,1)}), bf16[4,2,5,24,384]{4,3,2,1,0:T(8,128)(2,1)S(1)}, u32[]{:S(2)}, u32[]{:S(2)}) async-start(bf16[4,2,5,24,384]{4,3,2,1,0:T(8,128)(2,1)} %get-tuple-element.266), calls=%async_computation.1 | async-start | bytes 1474560 | tf_op jit(solution)/shard_map/all_to_all | solution.py:939
  201.9 3.7 %collective-permute-done.16.refs_1_ = bf16[10,4,8,384]{3,2,1,0:T(8,128)(2,1)S(1)} collective-permute-done((bf16[10,4,8,384]{3,2,1,0:T(8,128)(2,1)}, bf16[10,4,8,384]{3,2,1,0:T(8,128)(2,1)S(1)}, u32[]{:S(2)}, u32[]{:S(2)}) %collective-permute-start.16) | collective-permute-done | bytes 245792 | tf_op jit(solution)/shard_map/ppermute | solution.py:894
  206.9 2.7 %fold_f.1 = bf16[4,2,10,8,384]{4,3,2,1,0:T(8,128)(2,1)} custom-call(s32[3]{0:T(128)} %pad_add_fusion.where_ref, bf16[10,4,8,384]{3,2,1,0:T(8,128)(2,1)} %get-tuple-element.262.refs_0_, bf16[10,4,8,384]{3,2,1,0:T(8,128)(2,1)} %copy-done.6, bf16[10,4,8,384]{3,2,1,0:T(8,128)(2,1)} %get-tuple-element.264.refs_2_, ...), custom_call_target="tpu_custom_call" | custom-call | tf_op jit(solution)/shard_map/fold_f/pallas_call | solution.py:785
  209.7 4.6 %all-to-all-done.1.part_ref = bf16[4,2,5,24,384]{4,3,2,1,0:T(8,128)(2,1)S(1)} async-done(((bf16[4,2,5,24,384]{4,3,2,1,0:T(8,128)(2,1)}), bf16[4,2,5,24,384]{4,3,2,1,0:T(8,128)(2,1)S(1)}, u32[]{:S(2)}, u32[]{:S(2)}) %all-to-all-start.1) | async-done | bytes 737312 | tf_op jit(solution)/shard_map/all_to_all | solution.py:939
  214.3 4.1 %all-to-all-start.2 = ((bf16[4,2,10,8,384]{4,3,2,1,0:T(8,128)(2,1)}), bf16[4,2,10,8,384]{4,3,2,1,0:T(8,128)(2,1)}, u32[]{:S(2)}, u32[]{:S(2)}) async-start(bf16[4,2,10,8,384]{4,3,2,1,0:T(8,128)(2,1)} %fold_f.1), calls=%async_computation.2 | async-start | bytes 983040 | tf_op jit(solution)/shard_map/all_to_all | solution.py:939
  219.9 1.9 inner_sum.1
  221.8 2.1 constant_dynamic-update-slice_fusion
  223.9 7.7 %all-to-all-done.2.part_ref = bf16[4,2,10,8,384]{4,3,2,1,0:T(8,128)(2,1)} async-done(((bf16[4,2,10,8,384]{4,3,2,1,0:T(8,128)(2,1)}), bf16[4,2,10,8,384]{4,3,2,1,0:T(8,128)(2,1)}, u32[]{:S(2)}, u32[]{:S(2)}) %all-to-all-start.2) | async-done | bytes 491552 | tf_op jit(solution)/shard_map/all_to_all | solution.py:939
  (63 shorter events, 29.6 us)
Async XLA Ops:
  2.0 2.4 %collective-permute-start = (bf16[2,256,768]{2,1,0:T(8,128)(2,1)S(1)}, bf16[2,256,768]{2,1,0:T(8,128)(2,1)S(1)}, u32[]{:S(2)}, u32[]{:S(2)}) collective-permute-start(bf16[2,256,768]{2,1,0:T(8,128)(2,1)S(1)} %constant_dynamic-slice_fusion.1), channel_id=1, source_target_pairs={{0,1},{1,0},{2,3},{3,2},{4,5},{5,4},{6,7},{7,6},{8,9},{9,8},{10,11... | collective-permute-start | bytes 2359304 | tf_op jit(solution)/shard_map/ppermute | solution.py:642
  2.5 31.6 %collective-permute-start.1 = (bf16[2,256,768]{2,1,0:T(8,128)(2,1)S(1)}, bf16[2,256,768]{2,1,0:T(8,128)(2,1)S(1)}, u32[]{:S(2)}, u32[]{:S(2)}) collective-permute-start(bf16[2,256,768]{2,1,0:T(8,128)(2,1)S(1)} %constant_dynamic-slice_fusion), channel_id=1, source_target_pairs={{0,1},{1,0},{2,3},{3,2},{4,5},{5,4},{6,7},{7,6},{8,9},{9,8},{10,11... | collective-permute-start | bytes 2359304 | tf_op jit(solution)/shard_map/ppermute | solution.py:642
  89.3 4.9 %collective-permute-start.2 = (bf16[8,16,24,384]{3,2,1,0:T(8,128)(2,1)}, bf16[8,16,24,384]{3,2,1,0:T(8,128)(2,1)}, u32[]{:S(2)}, u32[]{:S(2)}) collective-permute-start(bf16[8,16,24,384]{3,2,1,0:T(8,128)(2,1)} %get-tuple-element.153), channel_id=1, source_target_pairs={{0,1},{1,0},{2,3},{3,2},{4,5},{5,4},{6,7},{7,6},{8,9},{9,8},{10,11... | collective-permute-start | bytes 7077896 | tf_op jit(solution)/shard_map/ppermute | solution.py:642
  99.0 18.9 %collective-permute-start.5 = (bf16[10,16,24,384]{3,2,1,0:T(8,128)(2,1)}, bf16[10,16,24,384]{3,2,1,0:T(8,128)(2,1)}, u32[]{:S(2)}, u32[]{:S(2)}) collective-permute-start(bf16[10,16,24,384]{3,2,1,0:T(8,128)(2,1)} %get-tuple-element.165), channel_id=1, source_target_pairs={{0,1},{1,0},{2,3},{3,2},{4,5},{5,4},{6,7},{7,6},{8,9},{9,8},{10,11... | collective-permute-start | bytes 8847368 | tf_op jit(solution)/shard_map/ppermute | solution.py:642
  99.4 18.4 %collective-permute-start.6 = (bf16[2,256,768]{2,1,0:T(8,128)(2,1)}, bf16[2,256,768]{2,1,0:T(8,128)(2,1)S(1)}, u32[]{:S(2)}, u32[]{:S(2)}) collective-permute-start(bf16[2,256,768]{2,1,0:T(8,128)(2,1)} %get-tuple-element.167), channel_id=1, source_target_pairs={{0,1},{1,0},{2,3},{3,2},{4,5},{5,4},{6,7},{7,6},{8,9},{9,8},{10,11... | collective-permute-start | bytes 2359304 | tf_op jit(solution)/shard_map/ppermute | solution.py:642
  99.6 17.8 %collective-permute-start.3 = (bf16[4,4,2,24,384]{4,3,2,1,0:T(8,128)(2,1)}, bf16[4,4,2,24,384]{4,3,2,1,0:T(8,128)(2,1)}, u32[]{:S(2)}, u32[]{:S(2)}) collective-permute-start(bf16[4,4,2,24,384]{4,3,2,1,0:T(8,128)(2,1)} %get-tuple-element.163), channel_id=1, source_target_pairs={{0,2},{2,0},{4,6},{6,4},{8,10},{10,8},{12,14},{14,12},{16,18},{18,... | collective-permute-start | bytes 1769480 | tf_op jit(solution)/shard_map/ppermute | solution.py:894
  102.4 15.4 %collective-permute-start.4 = (bf16[4,4,2,24,384]{4,3,2,1,0:T(8,128)(2,1)}, bf16[4,4,2,24,384]{4,3,2,1,0:T(8,128)(2,1)}, u32[]{:S(2)}, u32[]{:S(2)}) collective-permute-start(bf16[4,4,2,24,384]{4,3,2,1,0:T(8,128)(2,1)} %get-tuple-element.164), channel_id=1, source_target_pairs={{0,4},{2,6},{4,0},{6,2},{8,12},{10,14},{12,8},{14,10},{16,20},{18,... | collective-permute-start | bytes 1769480 | tf_op jit(solution)/shard_map/ppermute | solution.py:894
  117.8 7.1 %copy-start.2 = (bf16[2,256,768]{2,1,0:T(8,128)(2,1)}, bf16[2,256,768]{2,1,0:T(8,128)(2,1)S(1)}, u32[]{:S(2)}) copy-start(bf16[2,256,768]{2,1,0:T(8,128)(2,1)S(1)} %collective-permute-done.6) | copy-start | bytes 2359300
  124.9 26.3 %collective-permute-start.10 = (bf16[5,4,2,24,384]{4,3,2,1,0:T(8,128)(2,1)}, bf16[5,4,2,24,384]{4,3,2,1,0:T(8,128)(2,1)S(1)}, u32[]{:S(2)}, u32[]{:S(2)}) collective-permute-start(bf16[5,4,2,24,384]{4,3,2,1,0:T(8,128)(2,1)} %get-tuple-element.203), channel_id=1, source_target_pairs={{0,4},{2,6},{4,0},{6,2},{8,12},{10,14},{12,8},{14,10},{16,20},{18,... | collective-permute-start | bytes 2211848 | tf_op jit(solution)/shard_map/ppermute | solution.py:894
  126.5 24.8 %collective-permute-start.9 = (bf16[5,4,2,24,384]{4,3,2,1,0:T(8,128)(2,1)}, bf16[5,4,2,24,384]{4,3,2,1,0:T(8,128)(2,1)}, u32[]{:S(2)}, u32[]{:S(2)}) collective-permute-start(bf16[5,4,2,24,384]{4,3,2,1,0:T(8,128)(2,1)} %get-tuple-element.202), channel_id=1, source_target_pairs={{0,2},{2,0},{4,6},{6,4},{8,10},{10,8},{12,14},{14,12},{16,18},{18,... | collective-permute-start | bytes 2211848 | tf_op jit(solution)/shard_map/ppermute | solution.py:894
  127.0 24.2 %collective-permute-start.7 = (bf16[4,4,24,384]{3,2,1,0:T(8,128)(2,1)}, bf16[4,4,24,384]{3,2,1,0:T(8,128)(2,1)}, u32[]{:S(2)}, u32[]{:S(2)}) collective-permute-start(bf16[4,4,24,384]{3,2,1,0:T(8,128)(2,1)} %get-tuple-element.200), channel_id=1, source_target_pairs={{0,4},{2,6},{4,0},{6,2},{8,12},{10,14},{12,8},{14,10},{16,20},{18,... | collective-permute-start | bytes 884744 | tf_op jit(solution)/shard_map/ppermute | solution.py:894
  127.3 23.9 %collective-permute-start.8 = (bf16[4,4,24,384]{3,2,1,0:T(8,128)(2,1)}, bf16[4,4,24,384]{3,2,1,0:T(8,128)(2,1)}, u32[]{:S(2)}, u32[]{:S(2)}) collective-permute-start(bf16[4,4,24,384]{3,2,1,0:T(8,128)(2,1)} %get-tuple-element.201), channel_id=1, source_target_pairs={{0,2},{2,0},{4,6},{6,4},{8,10},{10,8},{12,14},{14,12},{16,18},{18,... | collective-permute-start | bytes 884744 | tf_op jit(solution)/shard_map/ppermute | solution.py:894
  151.3 5.6 %collective-permute-start.11 = (bf16[20,16,8,384]{3,2,1,0:T(8,128)(2,1)}, bf16[20,16,8,384]{3,2,1,0:T(8,128)(2,1)}, u32[]{:S(2)}, u32[]{:S(2)}) collective-permute-start(bf16[20,16,8,384]{3,2,1,0:T(8,128)(2,1)} %get-tuple-element.216), channel_id=1, source_target_pairs={{0,1},{1,0},{2,3},{3,2},{4,5},{5,4},{6,7},{7,6},{8,9},{9,8},{10,11... | collective-permute-start | bytes 5898248 | tf_op jit(solution)/shard_map/ppermute | solution.py:642
  156.9 30.3 %all-to-all-start = ((bf16[4,2,4,24,384]{4,3,2,1,0:T(8,128)(2,1)}), bf16[4,2,4,24,384]{4,3,2,1,0:T(8,128)(2,1)S(1)}, u32[]{:S(2)}, u32[]{:S(2)}) async-start(bf16[4,2,4,24,384]{4,3,2,1,0:T(8,128)(2,1)} %get-tuple-element.235), calls=%async_computation | async-start | bytes 1179648 | tf_op jit(solution)/shard_map/all_to_all | solution.py:939
  166.1 21.0 %collective-permute-start.14 = (bf16[10,4,2,8,384]{4,3,2,1,0:T(8,128)(2,1)}, bf16[10,4,2,8,384]{4,3,2,1,0:T(8,128)(2,1)}, u32[]{:S(2)}, u32[]{:S(2)}) collective-permute-start(bf16[10,4,2,8,384]{4,3,2,1,0:T(8,128)(2,1)} %get-tuple-element.233), channel_id=1, source_target_pairs={{0,2},{2,0},{4,6},{6,4},{8,10},{10,8},{12,14},{14,12},{16,18},{18,... | collective-permute-start | bytes 1474568 | tf_op jit(solution)/shard_map/ppermute | solution.py:894
  166.7 20.4 %collective-permute-start.15 = (bf16[10,4,2,8,384]{4,3,2,1,0:T(8,128)(2,1)}, bf16[10,4,2,8,384]{4,3,2,1,0:T(8,128)(2,1)}, u32[]{:S(2)}, u32[]{:S(2)}) collective-permute-start(bf16[10,4,2,8,384]{4,3,2,1,0:T(8,128)(2,1)} %get-tuple-element.234), channel_id=1, source_target_pairs={{0,4},{2,6},{4,0},{6,2},{8,12},{10,14},{12,8},{14,10},{16,20},{18,... | collective-permute-start | bytes 1474568 | tf_op jit(solution)/shard_map/ppermute | solution.py:894
  168.2 18.9 %collective-permute-start.12 = (bf16[5,4,24,384]{3,2,1,0:T(8,128)(2,1)}, bf16[5,4,24,384]{3,2,1,0:T(8,128)(2,1)S(1)}, u32[]{:S(2)}, u32[]{:S(2)}) collective-permute-start(bf16[5,4,24,384]{3,2,1,0:T(8,128)(2,1)} %get-tuple-element.231), channel_id=1, source_target_pairs={{0,4},{2,6},{4,0},{6,2},{8,12},{10,14},{12,8},{14,10},{16,20},{18,... | collective-permute-start | bytes 1105928 | tf_op jit(solution)/shard_map/ppermute | solution.py:894
  168.7 18.4 %collective-permute-start.13 = (bf16[5,4,24,384]{3,2,1,0:T(8,128)(2,1)}, bf16[5,4,24,384]{3,2,1,0:T(8,128)(2,1)}, u32[]{:S(2)}, u32[]{:S(2)}) collective-permute-start(bf16[5,4,24,384]{3,2,1,0:T(8,128)(2,1)} %get-tuple-element.232), channel_id=1, source_target_pairs={{0,2},{2,0},{4,6},{6,4},{8,10},{10,8},{12,14},{14,12},{16,18},{18,... | collective-permute-start | bytes 1105928 | tf_op jit(solution)/shard_map/ppermute | solution.py:894
  192.2 22.1 %all-to-all-start.1 = ((bf16[4,2,5,24,384]{4,3,2,1,0:T(8,128)(2,1)}), bf16[4,2,5,24,384]{4,3,2,1,0:T(8,128)(2,1)S(1)}, u32[]{:S(2)}, u32[]{:S(2)}) async-start(bf16[4,2,5,24,384]{4,3,2,1,0:T(8,128)(2,1)} %get-tuple-element.266), calls=%async_computation.1 | async-start | bytes 1474560 | tf_op jit(solution)/shard_map/all_to_all | solution.py:939
  197.0 9.9 %collective-permute-start.19 = (bf16[2,256,768]{2,1,0:T(8,128)(2,1)}, bf16[2,256,768]{2,1,0:T(8,128)(2,1)}, u32[]{:S(2)}, u32[]{:S(2)}) collective-permute-start(bf16[2,256,768]{2,1,0:T(8,128)(2,1)} %get-tuple-element.260), channel_id=1, source_target_pairs={{0,1},{1,0},{2,3},{3,2},{4,5},{5,4},{6,7},{7,6},{8,9},{9,8},{10,11... | collective-permute-start | bytes 2359304 | tf_op jit(solution)/shard_map/ppermute | solution.py:642
  197.0 8.6 %collective-permute-start.16 = (bf16[10,4,8,384]{3,2,1,0:T(8,128)(2,1)}, bf16[10,4,8,384]{3,2,1,0:T(8,128)(2,1)S(1)}, u32[]{:S(2)}, u32[]{:S(2)}) collective-permute-start(bf16[10,4,8,384]{3,2,1,0:T(8,128)(2,1)} %get-tuple-element.254), channel_id=1, source_target_pairs={{0,4},{2,6},{4,0},{6,2},{8,12},{10,14},{12,8},{14,10},{16,20},{18,... | collective-permute-start | bytes 737288 | tf_op jit(solution)/shard_map/ppermute | solution.py:894
  198.5 8.4 %collective-permute-start.17 = (bf16[10,4,8,384]{3,2,1,0:T(8,128)(2,1)}, bf16[10,4,8,384]{3,2,1,0:T(8,128)(2,1)}, u32[]{:S(2)}, u32[]{:S(2)}) collective-permute-start(bf16[10,4,8,384]{3,2,1,0:T(8,128)(2,1)} %get-tuple-element.256), channel_id=1, source_target_pairs={{0,2},{2,0},{4,6},{6,4},{8,10},{10,8},{12,14},{14,12},{16,18},{18,... | collective-permute-start | bytes 737288 | tf_op jit(solution)/shard_map/ppermute | solution.py:894
  200.0 1.9 collective-permute-start.18
  214.3 17.3 %all-to-all-start.2 = ((bf16[4,2,10,8,384]{4,3,2,1,0:T(8,128)(2,1)}), bf16[4,2,10,8,384]{4,3,2,1,0:T(8,128)(2,1)}, u32[]{:S(2)}, u32[]{:S(2)}) async-start(bf16[4,2,10,8,384]{4,3,2,1,0:T(8,128)(2,1)} %fold_f.1), calls=%async_computation.2 | async-start | bytes 983040 | tf_op jit(solution)/shard_map/all_to_all | solution.py:939
  (8 other events, 17.2 us)

commit v5 on v4

--- a/solution.py
+++ b/solution.py
@@ -141,7 +141,7 @@
         finish(2 * i + 1, ahead1_ref, 1)
         return carry
 
-    lax.fori_loop(0, pairs // 2, two_pairs, 0)
+    lax.fori_loop(0, pairs // 2, two_pairs, 0, unroll=True)
     for tail in (pairs - 2, pairs - 1):
         pltpu.make_async_copy(p_ref.at[tail % 2], probs_hbm.at[step, tail], p_sem.at[tail % 2]).wait()
 
@@ -486,83 +486,60 @@
     )(left, right)
 
 
-def attention_grad_kernel(lower, qkv_ref, mixed_ref, d_ref, probs_hbm, *rest):
-    out_ref, bq_ref, bv_ref, p_ref, p_sem = rest[-5:]
-    step = pl.program_id(0)
-    length, width = mixed_ref.shape[1:]
+def attention_grad(qkv, probs, mixed, d, lower, count, partial_out=None):
+    rows, length, width = mixed.shape
     pairs = width // 128
     scale = (width // HEADS) ** -0.5
-
-    def fetch(pair, slot):
-        return pltpu.make_async_copy(probs_hbm.at[lower + step, pair], p_ref.at[slot], p_sem.at[slot])
-
-    fetch(0, 0).start()
-
-    @pl.when(step == 0)
-    def _():
-        bq_ref[...] = jnp.zeros_like(bq_ref)
-        bv_ref[...] = jnp.zeros_like(bv_ref)
-
-    first = lax.broadcasted_iota(jnp.int32, (1, 128), 1) < 64
-
-    def pair_body(pair, carry):
-        slot = lax.rem(pair, 2)
-
-        @pl.when(pair + 1 < pairs)
-        def _():
-            fetch(pair + 1, 1 - slot).start()
-
-        at = pl.ds(pl.multiple_of(pair * 128, 128), 128)
-        q = qkv_ref[0, :, at]
-        k = qkv_ref[0, :, pl.ds(pl.multiple_of(width + pair * 128, 128), 128)]
-        v = qkv_ref[0, :, pl.ds(pl.multiple_of(2 * width + pair * 128, 128), 128)]
-        d = d_ref[0, :, at]
-        product = d.astype(F32) * mixed_ref[0, :, at].astype(F32)
+    more = [] if partial_out is None else [partial_out]
+
+    def body(q_ref, k_ref, v_ref, p_ref, m_ref, d_ref, *rest):
+        out_ref, bq_ref, bv_ref = rest[-3:]
+
+        @pl.when(pl.program_id(1) == 0)
+        def _():
+            bq_ref[...] = jnp.zeros_like(bq_ref)
+            bv_ref[...] = jnp.zeros_like(bv_ref)
+
+        first = lax.broadcasted_iota(jnp.int32, (1, 128), 1) < 64
+        q, k, v, d = q_ref[0], k_ref[0], v_ref[0], d_ref[0]
+        product = d.astype(F32) * m_ref[0].astype(F32)
         q_t, d_t, k_t = q.T, d.T, k.T
-        fetch(pair, slot).wait()
         dqs, dks, dvs = [], [], []
         for h in range(2):
             on = first if h == 0 else jnp.logical_not(first)
             part = slice(h * 64, (h + 1) * 64)
             delta = jnp.sum(jnp.where(on, product, 0.0), axis=-1, keepdims=True)
             dprobs = row_dot_t(jnp.where(on, d, jnp.zeros_like(d)), v)
-            p = p_ref[slot, h]
+            p = p_ref[0, 0, h]
             ds = (p.astype(F32) * (dprobs - delta)).astype(BF)
             dqs.append(row_dot_t(k_t[part], ds))
             dks.append(row_dot(q_t[part], ds))
             dvs.append(row_dot(d_t[part], p))
         dq = (jnp.concatenate(dqs, axis=0) * scale).T.astype(BF)
         dv = jnp.concatenate(dvs, axis=0).T.astype(BF)
-        out_ref[0, 0, :, at] = dq
-        out_ref[1, 0, :, at] = jnp.concatenate(dks, axis=0).T.astype(BF)
-        out_ref[2, 0, :, at] = dv
-        bq_ref[:, at] += jnp.sum(dq.astype(F32), axis=0, keepdims=True)
-        bv_ref[:, at] += jnp.sum(dv.astype(F32), axis=0, keepdims=True)
-        return carry
-
-    lax.fori_loop(0, pairs, pair_body, 0)
-
-
-def attention_grad(qkv, probs, mixed, d, lower, count, partial_out=None):
-    rows, length, width = mixed.shape
-    more = [] if partial_out is None else [partial_out]
-
-    def full(n):
-        return pl.BlockSpec((1, length, n), lambda r: (lower + r, 0, 0))
-
+        out_ref[0, 0] = dq
+        out_ref[1, 0] = jnp.concatenate(dks, axis=0).T.astype(BF)
+        out_ref[2, 0] = dv
+        bq_ref[...] += jnp.sum(dq.astype(F32), axis=0, keepdims=True)
+        bv_ref[...] += jnp.sum(dv.astype(F32), axis=0, keepdims=True)
+
+    def cols(base):
+        return pl.BlockSpec((1, length, 128), lambda p, r: (lower + r, 0, base + p))
+
+    vec = pl.BlockSpec((1, 128), lambda p, r: (0, p))
     one = jax.ShapeDtypeStruct((1, width), F32)
     return pl.pallas_call(
-        partial(attention_grad_kernel, lower),
+        body,
         name="attention_grad",
         out_shape=[jax.ShapeDtypeStruct((3, rows, length, width), BF), one, one],
-        grid=(count,),
-        input_output_aliases={4: 0} if more else {},
-        in_specs=[full(3 * width), full(width), full(width), ANY] + [ANY] * len(more),
-        out_specs=[pl.BlockSpec((3, 1, length, width), lambda r: (0, lower + r, 0, 0)), whole((1, width)), whole((1, width))],
-        scratch_shapes=[pltpu.VMEM((2, 2, length, length), BF), pltpu.SemaphoreType.DMA((2,))],
+        grid=(pairs, count),
+        input_output_aliases={6: 0} if more else {},
+        in_specs=[cols(0), cols(pairs), cols(2 * pairs), pl.BlockSpec((1, 1, 2, length, length), lambda p, r: (lower + r, p, 0, 0, 0)), cols(0), cols(0)]
+        + [ANY] * len(more),
+        out_specs=[pl.BlockSpec((3, 1, length, 128), lambda p, r: (0, lower + r, 0, p)), vec, vec],
         compiler_params=params(63),
         cost_estimate=pl.CostEstimate(flops=8 * count * length * length * width, bytes_accessed=(15 * count) << 20, transcendentals=0),
-    )(qkv, mixed, d, probs, *more)
+    )(qkv, qkv, qkv, probs, mixed, d, *more)
 
 
 def input_grad_call(core, dproj, dpre, w_qkv, half):
@@ -570,14 +547,20 @@
     length = 2 * half
     group = total // length
 
-    def body(core_ref, p_ref, d_ref, w_ref, own_hbm, other_hbm, acc_ref, out_ref, sem):
+    def body(core_ref, p_ref, d_hbm, w_ref, own_hbm, other_hbm, acc_ref, out_ref, d_ref, sem, d_sem):
         step = pl.program_id(0)
+        load = pltpu.make_async_copy(d_hbm, d_ref, d_sem)
         core = core_ref[0]
+
+        @pl.when(step == 0)
+        def _():
+            load.start()
+
         value = row_dot_t(p_ref[0], w_ref[...])
 
         @pl.when(step == 0)
         def _():
-            acc_ref[...] = value + d_ref[...].astype(F32)
+            acc_ref[...] = value
 
         @pl.when(step == 1)
         def _():
@@ -585,7 +568,8 @@
 
         @pl.when(step == 2)
         def _():
-            out_ref[...] = (acc_ref[...] + value).astype(BF)
+            load.wait()
+            out_ref[...] = (acc_ref[...] + value + d_ref[...].astype(F32)).astype(BF)
             stores = []
             for r in range(group):
                 other = pl.ds(pl.multiple_of(r * length + (1 - core) * half, half), half)
@@ -606,11 +590,11 @@
             grid=(3,),
             in_specs=[
                 pl.BlockSpec((1, total, width), lambda n, *_: (n, 0, 0)),
-                whole((total, width)),
+                ANY,
                 pl.BlockSpec((width, width), lambda n, *_: (0, n)),
             ],
             out_specs=[HBM, HBM],
-            scratch_shapes=[pltpu.VMEM((total, width), F32), pltpu.VMEM((total, width), BF), pltpu.SemaphoreType.DMA((2 * group,))],
+            scratch_shapes=[pltpu.VMEM((total, width), F32), pltpu.VMEM((total, width), BF), pltpu.VMEM((total, width), BF), pltpu.SemaphoreType.DMA((2 * group,)), pltpu.SemaphoreType.DMA],
         ),
         compiler_params=params(63),
         cost_estimate=pl.CostEstimate(flops=6 * total * width * width, bytes_accessed=10 << 20, transcendentals=0),
@@ -706,7 +690,7 @@
 
     def body(core_ref, l_ref, r_ref, *refs):
         ins = refs[: len(vectors) + len(more)]
-        keep_ref, send_ref, acc_ref, table_ref = refs[len(ins) :]
+        keep_hbm, send_hbm, keep_ref, send_ref, acc_ref, table_ref, o_sem = refs[len(ins) :]
         acc_ref[...] = col_dot(l_ref[...], r_ref[0])
         core = core_ref[0]
         step = pl.program_id(0)
@@ -734,6 +718,31 @@
                     ref[blocks - 1, d] = jnp.broadcast_to(line, (8, LANES))
                     ref[2 * blocks - 1, d] = jnp.zeros((8, LANES), BF)
 
+        stretches = [
+            [(0, 2 * deep), (blocks - 1, blocks), (2 * blocks - 1, 2 * blocks)],
+            [(2 * deep, 3 * deep), (blocks, blocks + deep)],
+            [(blocks + deep, blocks + 3 * deep)],
+        ]
+        stores, count = [], 0
+        for group in stretches:
+            copies = []
+            for start, stop in group:
+                for src, dst in ((keep_ref, keep_hbm), (send_ref, send_hbm)):
+                    copies.append(pltpu.make_async_copy(src.at[start:stop], dst.at[start:stop], o_sem.at[count]))
+                    count += 1
+            stores.append(copies)
+        for n, copies in enumerate(stores):
+            @pl.when(step == n)
+            def _():
+                for copy in copies:
+                    copy.start()
+
+        @pl.when(step == 2)
+        def _():
+            for copies in stores:
+                for copy in copies:
+                    copy.wait()
+
     out = jax.ShapeDtypeStruct((2 * blocks, dp, 8, LANES), BF)
     return pl.pallas_call(
         body,
@@ -743,8 +752,8 @@
             num_scalar_prefetch=1,
             grid=(3,),
             in_specs=[whole((total, m)), pl.BlockSpec((1, total, n), lambda j, *_: (j, 0, 0))] + [whole(v.shape) for v in (*vectors, *more)],
-            out_specs=[whole(out.shape)] * 2,
-            scratch_shapes=[pltpu.VMEM((m, n), F32), pltpu.VMEM((2 * dp, LANES), F32)],
+            out_specs=[HBM] * 2,
+            scratch_shapes=[pltpu.VMEM(out.shape, BF)] * 2 + [pltpu.VMEM((m, n), F32), pltpu.VMEM((2 * dp, LANES), F32), pltpu.SemaphoreType.DMA((12,))],
         ),
         compiler_params=params(63),
         cost_estimate=pl.CostEstimate(flops=6 * total * m * n, bytes_accessed=6 * n * (total + m), transcendentals=0),
@@ -768,7 +777,9 @@
                 loads.append(pltpu.make_async_copy(ins[b].at[b_at], g_ref.at[i], g_sem.at[i]))
                 stores.append(pltpu.make_async_copy(k_ref.at[i], outs[o].at[o_at], o_sem.at[i]))
                 sums.append((k_ref, g_ref, i))
-            ins, outs = ins[len(group_in) :], outs[len(group_out) :]
+            ins = ins[len(group_in) :]
+            if n + 1 < len(groups) and groups[n + 1][1]:
+                outs = outs[len(group_out) :]
         for load in loads:
             load.start()
         for i, (k_ref, g_ref, at) in enumerate(sums):
@@ -837,33 +848,55 @@
     return (parts[1], got[0], parts[3], got[1]), [(blocks, 4, rows, lanes)] * 4, pieces, (blocks, rows, lanes)
 
 
-def fold_third(parts, got):
+def fold_third(parts, got, joined=True):
     blocks, _, rows, lanes = parts[1].shape
     every = slice(None)
 
     def pieces(at):
         table = []
-        for z in range(4):
+        for n in (0, 1, 2, 3) if joined else (1, 2, 3, 0):
             for half in range(2):
-                table.append((2 * half, (every, z), 2 * half + 1, (every, z), 0, (z, half)))
+                index = (every, n if joined else at[0] ^ n)
+                table.append((2 * half, index, 2 * half + 1, index, 0 if joined else n, (n, half) if joined else (half,)))
         return table
 
-    return (parts[1], got[0], parts[3], got[1]), [(4, 2, blocks, rows, lanes)], pieces, (blocks, rows, lanes)
-
-
-def fold_last(parts, widths, name, stack=1, extra=0):
-    _, _, blocks, deep, lanes = parts.shape
+    shape = (2, blocks, rows, lanes)
+    return (parts[1], got[0], parts[3], got[1]), [(4,) + shape] if joined else [shape] * 4, pieces, (blocks, rows, lanes)
+
+
+def fold_third_pair(first, second):
+    def moved(group, lower, shapes):
+        inputs, _, pieces, shape = group
+
+        def at(where):
+            return [(a, a_at, b, b_at, 0, o_at + (slice(lower, lower + shape[0]),)) for a, a_at, b, b_at, _, o_at in pieces(where)]
+
+        return inputs, shapes, at, shape
+
+    split = first[3][0]
+    joined = (4, 2, split + second[3][0]) + first[3][1:]
+    return [moved(first, 0, [joined]), moved(second, split, [])]
+
+
+def fold_last(parts, widths, name, stack=1, extra=0, lower=0, upper=None):
+    parts = parts if isinstance(parts, list) else [parts]
+    blocks, deep, lanes = parts[0].shape[-3:]
+    blocks = (blocks if upper is None else upper) - lower
     chunks = sum(widths) // (2 * lanes)
     rows = (blocks * deep - extra) // (chunks * stack)
 
-    def body(part_ref, *outs):
+    def body(*refs):
+        ins, outs = refs[: len(parts)], refs[len(parts) :]
+        if len(ins) == 1:
+            ins = [ins[0].at[z] for z in range(4)]
+
         def take(half, line, count, at, size):
             step = min(deep, count)
             pieces = []
             for start in range(line, line + count, step):
                 total = None
-                for z in range(4):
-                    value = part_ref[z, half, start // deep, start % deep : start % deep + step, at : at + size].astype(F32)
+                for ref in ins:
+                    value = ref[half, lower + start // deep, start % deep : start % deep + step, at : at + size].astype(F32)
                     total = value if total is None else total + value
                 pieces.append(total)
             return pieces[0] if len(pieces) == 1 else jnp.concatenate(pieces, axis=0)
@@ -878,12 +911,12 @@
                     out[pl.ds(r * rows * tiles + t, rows, stride=tiles), :] = take(chunk // chunks, line, rows, at, 128)
             base += width
         if extra:
-            outs[-1][...] = take(0, blocks * deep - extra, extra, 0, lanes)
+            outs[-1][...] = take(0, blocks * deep - extra, extra, 0, lanes)[0]
 
     shapes = [jax.ShapeDtypeStruct((stack * rows * w // 128, 128), F32) for w in widths]
     if extra:
-        shapes.append(jax.ShapeDtypeStruct((extra, lanes), F32))
-    return pl.pallas_call(body, name=name, out_shape=shapes, compiler_params=params(63))(parts)
+        shapes.append(jax.ShapeDtypeStruct((lanes,), F32))
+    return pl.pallas_call(body, name=name, out_shape=shapes, compiler_params=params(63))(*parts)
 
 
 def sync(*values):
@@ -958,34 +991,34 @@
         )
         send_q, keep_q, got_b, got_i = sync(send_q, keep_q, got_b, got_i)
         got_q = swap(send_q)
-        inner, back = add_pieces(where, [fold_second(inner, got_i), fold_third(back, got_b)], "fold_c")
-        inner, back, got_q, keep_q = sync(inner, back, got_q, keep_q)
+        (inner,) = add_pieces(where, [fold_second(inner, got_i)], "fold_c")
+        inner, got_q, keep_q, cls_own = sync(inner, got_q, keep_q, cls_own)
         got_i = cross(inner, 2, 1)
-        got_b = along_z(back[0])
+        cls_got = swap(cls_own)
         (proj,) = add_pieces(where, [fold_first(view(keep_q), view(got_q))], "fold_d")
-        dproj, proj = sync(dproj, proj)
+        proj, got_i, cls_got = sync(proj, got_i, cls_got)
         got_q = cross(proj, 1, 2)
+        split = back[1].shape[0]
+        joint = add_pieces(where, fold_third_pair(fold_third(back, got_b), fold_third(inner, got_i)), "fold_e")[0][0]
+        dproj, joint = sync(dproj, joint)
+        got_i = along_z(joint)
         dinput, dinput_other = input_grad_call(core_one, dproj.reshape(3, total, width), dpre1, w_qkv, half)
-        output, dinput = sync(output, dinput)
+        dinput, dinput_other, got_q, output = sync(dinput, dinput_other, got_q, output)
+        (proj,) = add_pieces(where, [fold_second(proj, got_q)], "fold_f")
+        proj, dinput_other, output = sync(proj, dinput_other, output)
+        got_q = cross(proj, 2, 1)
+        dinput_got = swap(dinput_other)
         output = lax.dynamic_update_slice_in_dim(output, output_got, (1 - core) * rows, 0)
-        output, dinput, dinput_other, got_i, got_q, got_b, cls_own = sync(output, dinput, dinput_other, got_i, got_q, got_b, cls_own)
-        inner, proj = add_pieces(where, [fold_third(inner, got_i), fold_second(proj, got_q)], "fold_e")
-        inner, proj, dinput_other, cls_own = sync(inner, proj, dinput_other, cls_own)
-        got_q = cross(proj, 2, 1)
-        got_i = along_z(inner[0])
-        cls_got = swap(cls_own)
-        dinput_got = swap(dinput_other)
-        proj, got_b = sync(proj, got_b)
-        (r_back,) = fold_last(got_b, (width,), "back_sum", w_back.shape[0] // width)
-        r_back, got_q, cls_got, dinput_got = sync(r_back, got_q, cls_got, dinput_got)
-        (proj,) = add_pieces(where, [fold_third(proj, got_q)], "fold_f")
-        proj, got_i, dinput = sync(proj, got_i, dinput)
-        got_q = along_z(proj[0])
-        r_in, r_out = fold_last(got_i, (w_in.shape[1], width), "inner_sum")
+        output, got_q, dinput_got = sync(output, got_q, dinput_got)
+        (proj,) = add_pieces(where, [fold_third(proj, got_q, False)], "fold_g")
+        got_q = [proj[0]] + [flip(proj[n], 4 * n) for n in (1, 2, 3)]
+        dinput, proj = sync(dinput, proj)
         dinput = lax.dynamic_update_slice_in_dim(dinput, dinput_got, (1 - core) * rows, 0)
-        r_in, got_q, dinput = sync(r_in, got_q, dinput)
+        (r_back,) = fold_last(got_i, (width,), "back_sum", w_back.shape[0] // width, 0, 0, split)
+        r_in, r_out = fold_last(got_i, (w_in.shape[1], width), "inner_sum", 1, 0, split)
+        r_in, r_back, got_q, dinput = sync(r_in, r_back, got_q, dinput)
         r_qkv, r_vec = fold_last(got_q, (3 * width,), "proj_sum", 1, 8)
-        r_vec = r_vec[0, : (8 * width + w_in.shape[1]) // (2 * dp)]
+        r_vec = r_vec[: (8 * width + w_in.shape[1]) // (2 * dp)]
     else:
         g_back, g_inner = grads
         r_back = reduce_scatter(g_back, order_a, dp, dp_bits)

time: 236 us -> 219 us (0.928)
  Pallas kernels: 161 us -> 155 us
  starting transfers between devices: 31.4 us -> 25.9 us
  local copies, waits for them, and re-layouts: 10.7 us -> 7.41 us
    all_to_all x3 -> x1, waiting for transfers between devices: 12.3 us -> 0.01 us  [along_z(): lax.all_to_all(parts, 'dp', 0, 0, axis_index_groups=[[i, i + 4, i + 8, i...]
    ppermute x12 -> x15, waiting for transfers between devices: 11.8 us -> 21.7 us  [flip(): return lax.ppermute(value, 'dp', [(i, i ^ bits) for i in range(16)])]
    all_to_all x3 -> x1, starting transfers between devices: 13.8 us -> 4.91 us  [along_z(): lax.all_to_all(parts, 'dp', 0, 0, axis_index_groups=[[i, i + 4, i + 8, i...]
    pallas_call x2, Pallas kernels: 26.8 us -> 21.5 us  [attention_grad(): pl.pallas_call(body, name='attention_grad', out_shape=[jax.ShapeDtypeStru...]
    ppermute x12 -> x15, starting transfers between devices: 15.6 us -> 19.1 us  [flip(): return lax.ppermute(value, 'dp', [(i, i ^ bits) for i in range(16)])]
    pallas_call x6 -> x7, Pallas kernels: 27.9 us -> 29.5 us  [add_pieces(): pl.pallas_call(body, name=name, out_shape=[jax.ShapeDtypeStruct(s, BF) fo...]
  transfers between devices with their start and end apart: 23 -> 24, of which waited for: 8 -> 14; matrix products, arithmetic and copies ran while one was open for 3% -> 2% of each run, Pallas kernels for 38% -> 38%
where the time goes in v5:
time: 219 us; the launch traced here: 218 us
  Pallas kernels  155 us (71%)
  waiting for transfers between devices  27.8 us (13%)
  starting transfers between devices  25.9 us (12%)
  local copies, waits for them, and re-layouts  7.41 us (3%)
    pallas_call x1, Pallas kernels, feed_call(): pl.pallas_call(partial(feed_kernel, split), name='feed_rows', out_shape=s...  54.3 us
    pallas_call x7, Pallas kernels, add_pieces(): pl.pallas_call(body, name=name, out_shape=[jax.ShapeDtypeStruct(s, BF) fo...  29.5 us
    pallas_call x1, Pallas kernels, attention_call(): pl.pallas_call(attention_kernel, name='attention_rows', out_shape=[row(3...  27.7 us
    ppermute x15, waiting for transfers between devices, flip(): return lax.ppermute(value, 'dp', [(i, i ^ bits) for i in range(16)])  21.7 us
    pallas_call x2, Pallas kernels, attention_grad(): pl.pallas_call(body, name='attention_grad', out_shape=[jax.ShapeDtypeStru...  21.5 us
    ppermute x15, starting transfers between devices, flip(): return lax.ppermute(value, 'dp', [(i, i ^ bits) for i in range(16)])  19.1 us
    pallas_call x1, Pallas kernels, grad_proj(): pl.pallas_call(body, name='grad_qkv', out_shape=[out, out], grid_spec=plt...  8.39 us
    pallas_call x1, Pallas kernels, input_grad_call(): pl.pallas_call(body, name='input_grad', out_shape=[jax.ShapeDtypeStruct((...  7.98 us
  transfers between devices with their start and end apart: 24, of which 14 were waited for; matrix products, arithmetic and copies ran while one was open for 2% of the time, Pallas kernels for 38%

profile of v5, /device:TPU:0, one launch (start us, length us, event | category | flops | bytes accessed | tf_op | source)
XLA Modules:
  0.0 217.9 jit_solution(13319289957804691652)
XLA Ops:
  5.3 27.7 %attention_rows.1 = (bf16[2,512,2304]{2,1,0:T(8,128)(2,1)}, bf16[2,6,2,512,512]{4,3,2,1,0:T(8,128)(2,1)}, bf16[2,512,768]{2,1,0:T(8,128)(2,1)}, bf16[2,512,768]{...) custom-call(s32[1]{0:T(128)} %bitcast.3.core_ref, ...), custom_call_target="tpu_custom_call" | custom-call | flops 6442450944 | bytes 36700160 | tf_op jit(solution)/shard_map/attention_rows/pallas_call | solution.py:174
  33.8 54.3 %feed_rows.1 = (bf16[4,256,768]{2,1,0:T(8,128)(2,1)}, bf16[2,256,768]{2,1,0:T(8,128)(2,1)}, bf16[2,8,768]{2,1,0:T(8,128)(2,1)}, bf16[1024,768]{1,0:T(8,128)(2,1)...) custom-call(s32[1]{0:T(128)} %bitcast.3.core_ref, ...), custom_call_target="tpu_custom_call" | custom-call | flops 31406948352 | bytes 41943040 | tf_op jit(solution)/shard_map/feed_rows/pallas_call | solution.py:426
  89.1 3.9 %collective-permute-done.2 = bf16[8,16,24,384]{3,2,1,0:T(8,128)(2,1)} collective-permute-done((bf16[8,16,24,384]{3,2,1,0:T(8,128)(2,1)}, bf16[8,16,24,384]{3,2,1,0:T(8,128)(2,1)}, u32[]{:S(2)}, u32[]{:S(2)}) %collective-permute-start.2) | collective-permute-done | bytes 2359328 | tf_op jit(solution)/shard_map/ppermute | solution.py:626
  93.0 4.8 %fold_a.1 = (bf16[4,4,2,24,384]{4,3,2,1,0:T(8,128)(2,1)}, bf16[4,4,2,24,384]{4,3,2,1,0:T(8,128)(2,1)}, bf16[4,4,2,24,384]{4,3,2,1,0:T(8,128)(2,1)}, bf16[4,4,2,24,384]{4,3,2,1,0:T(8,128)(2,1)}) custom-call(s32[3]{0:T(128)} %pad_add_fusion.where_ref, bf16[2,4,4,2,2,24,384]{6,5,4,3,2,1,0:T(8,128)(2,1)} %bitcast.32, ...), custom_call_target="tpu_custom_call" | custom-call | tf_op jit(solution)/shard_map/fold_a/pallas_call | solution.py:796
  98.4 2.8 %collective-permute-start.3 = (bf16[4,4,2,24,384]{4,3,2,1,0:T(8,128)(2,1)}, bf16[4,4,2,24,384]{4,3,2,1,0:T(8,128)(2,1)}, u32[]{:S(2)}, u32[]{:S(2)}) collective-permute-start(bf16[4,4,2,24,384]{4,3,2,1,0:T(8,128)(2,1)} %get-tuple-element.159), channel_id=1, source_target_pairs={{0,2},{2,0},{4,6},{6,4},{8,10},{10,8},{12,14},{14,12},{16,18},{18,... | collective-permute-start | bytes 1769480 | tf_op jit(solution)/shard_map/ppermute | solution.py:927
  102.7 10.8 %attention_grad.2 = (bf16[3,2,512,768]{3,2,1,0:T(8,128)(2,1)}, f32[1,768]{1,0:T(1,128)}, f32[1,768]{1,0:T(1,128)}) custom-call(bf16[2,512,2304]{2,1,0:T(8,128)(2,1)} %get-tuple-element.156.q_ref.k_ref.v_ref, bf16[2,512,2304]{2,1,0:T(8,128)(2,1)} %get-tuple-element.156.q_ref.k_ref.v_ref, bf16[2,512,2304]{2,1,0:T(8,128)(2,1)} %get-tuple-element.156.q_ref.k_ref.v_ref, ...), custom_call_target="tpu_custom_call" | custom-call | flops 1610612736 | bytes 15728640 | tf_op jit(solution)/shard_map/attention_grad/pallas_call | solution.py:531
  116.6 7.0 %fold_b.1 = (bf16[5,4,2,24,384]{4,3,2,1,0:T(8,128)(2,1)}, bf16[5,4,2,24,384]{4,3,2,1,0:T(8,128)(2,1)}, bf16[5,4,2,24,384]{4,3,2,1,0:T(8,128)(2,1)}, bf16[5,4,2,2...) custom-call(s32[3]{0:T(128)} %pad_add_fusion.where_ref, ...), custom_call_target="tpu_custom_call" | custom-call | tf_op jit(solution)/shard_map/fold_b/pallas_call | solution.py:796
  127.8 10.8 %attention_grad.3 = (bf16[3,2,512,768]{3,2,1,0:T(8,128)(2,1)}, f32[1,768]{1,0:T(1,128)}, f32[1,768]{1,0:T(1,128)}) custom-call(bf16[2,512,2304]{2,1,0:T(8,128)(2,1)} %get-tuple-element.156.q_ref.k_ref.v_ref, bf16[2,512,2304]{2,1,0:T(8,128)(2,1)} %get-tuple-element.156.q_ref.k_ref.v_ref, ...), custom_call_target="tpu_custom_call", output_to_operand_aliasing={{0}: (6, {})} | custom-call | flops 1610612736 | bytes 15728640 | tf_op jit(solution)/shard_map/attention_grad/pallas_call | solution.py:531
  138.6 8.4 %grad_qkv.1 = (bf16[20,16,8,384]{3,2,1,0:T(8,128)(2,1)}, bf16[20,16,8,384]{3,2,1,0:T(8,128)(2,1)}) custom-call(s32[1]{0:T(128)} %bitcast.3.core_ref, bf16[1024,768]{1,0:T(8,128)(2,1)} %bitcast.43, bf16[3,1024,768]{2,1,0:T(8,128)(2,1)} %bitcast.29, f32[1,768]{1,0:T(1,128)} %get-tuple-element.183.refs_0_, f32[1,768]{1,0:T(1,128)} %get-tuple-element.184.refs_1_, ...), custom_call_target="tpu_custom_call" | custom-call | flops 3623878656 | bytes 8257536 | tf_op jit(solution)/shard_map/grad_qkv/pallas_call | solution.py:747
  149.0 3.7 %fold_c.1 = (bf16[5,4,24,384]{3,2,1,0:T(8,128)(2,1)}, bf16[5,4,24,384]{3,2,1,0:T(8,128)(2,1)}, bf16[5,4,24,384]{3,2,1,0:T(8,128)(2,1)}, bf16[5,4,24,384]{3,2,1,0:T(8,128)(2,1)}) custom-call(s32[3]{0:T(128)} %pad_add_fusion.where_ref, bf16[5,4,2,24,384]{4,3,2,1,0:T(8,128)(2,1)} %get-tuple-element.178.refs_0_, ...), custom_call_target="tpu_custom_call" | custom-call | tf_op jit(solution)/shard_map/fold_c/pallas_call | solution.py:796
  154.5 4.3 %fold_d.1 = (bf16[10,4,2,8,384]{4,3,2,1,0:T(8,128)(2,1)}, bf16[10,4,2,8,384]{4,3,2,1,0:T(8,128)(2,1)}, bf16[10,4,2,8,384]{4,3,2,1,0:T(8,128)(2,1)}, bf16[10,4,2,8,384]{4,3,2,1,0:T(8,128)(2,1)}) custom-call(s32[3]{0:T(128)} %pad_add_fusion.where_ref, bf16[2,10,4,2,2,8,384]{6,5,4,3,2,1,0:T(8,128)(2,1)} %bitcast.33, ...), custom_call_target="tpu_custom_call" | custom-call | tf_op jit(solution)/shard_map/fold_d/pallas_call | solution.py:796
  158.8 5.5 %collective-permute-done.12.refs_5_ = bf16[5,4,24,384]{3,2,1,0:T(8,128)(2,1)} collective-permute-done((bf16[5,4,24,384]{3,2,1,0:T(8,128)(2,1)}, bf16[5,4,24,384]{3,2,1,0:T(8,128)(2,1)}, u32[]{:S(2)}, u32[]{:S(2)}) %collective-permute-start.12) | collective-permute-done | bytes 368672 | tf_op jit(solution)/shard_map/ppermute | solution.py:927
  164.5 3.7 %fold_e.1 = bf16[4,2,9,24,384]{4,3,2,1,0:T(8,128)(2,1)} custom-call(s32[3]{0:T(128)} %pad_add_fusion.where_ref, bf16[4,4,24,384]{3,2,1,0:T(8,128)(2,1)} %get-tuple-element.220.refs_0_, bf16[4,4,24,384]{3,2,1,0:T(8,128)(2,1)} %collective-permute-done.7.refs_1_, bf16[4,4,24,384]{3,2,1,0:T(8,128)(2,1)} %get-tuple-element.222.refs_2_, ...), custom_call_target="tpu_custom_call" | custom-call | tf_op jit(solution)/shard_map/fold_e/pallas_call | solution.py:796
  168.2 4.9 %all-to-all-start = ((bf16[4,2,9,24,384]{4,3,2,1,0:T(8,128)(2,1)}), bf16[4,2,9,24,384]{4,3,2,1,0:T(8,128)(2,1)}, u32[]{:S(2)}, u32[]{:S(2)}) async-start(bf16[4,2,9,24,384]{4,3,2,1,0:T(8,128)(2,1)} %fold_e.1), calls=%async_computation | async-start | bytes 2654208 | tf_op jit(solution)/shard_map/all_to_all | solution.py:972
  175.3 8.0 %input_grad.1 = (bf16[4,256,768]{2,1,0:T(8,128)(2,1)}, bf16[2,256,768]{2,1,0:T(8,128)(2,1)}) custom-call(s32[1]{0:T(128)} %bitcast.3.core_ref, bf16[3,1024,768]{2,1,0:T(8,128)(2,1)} %bitcast.30, bf16[1024,768]{1,0:T(8,128)(2,1)} %get-tuple-element.229.d_hbm, bf16[768,2304]{1,0:T(8,128)(2,1)} %w_ref.1), custom_call_target="tpu_custom_call" | custom-call | flops 3623878656 | bytes 10485760 | tf_op jit(solution)/shard_map/input_grad/pallas_call | solution.py:584
  183.2 2.1 collective-permute-done.15.refs_1_
  185.7 3.3 %fold_f.1 = (bf16[10,4,8,384]{3,2,1,0:T(8,128)(2,1)}, bf16[10,4,8,384]{3,2,1,0:T(8,128)(2,1)}, bf16[10,4,8,384]{3,2,1,0:T(8,128)(2,1)}, bf16[10,4,8,384]{3,2,1,0:T(8,128)(2,1)}) custom-call(s32[3]{0:T(128)} %pad_add_fusion.where_ref, bf16[10,4,2,8,384]{4,3,2,1,0:T(8,128)(2,1)} %get-tuple-element.219.refs_0_, ...), custom_call_target="tpu_custom_call" | custom-call | tf_op jit(solution)/shard_map/fold_f/pallas_call | solution.py:796
  193.6 4.2 %collective-permute-done.17.refs_1_ = bf16[10,4,8,384]{3,2,1,0:T(8,128)(2,1)} collective-permute-done((bf16[10,4,8,384]{3,2,1,0:T(8,128)(2,1)}, bf16[10,4,8,384]{3,2,1,0:T(8,128)(2,1)}, u32[]{:S(2)}, u32[]{:S(2)}) %collective-permute-start.17) | collective-permute-done | bytes 245792 | tf_op jit(solution)/shard_map/ppermute | solution.py:927
  198.9 2.7 %fold_g.1 = (bf16[2,10,8,384]{3,2,1,0:T(8,128)(2,1)}, bf16[2,10,8,384]{3,2,1,0:T(8,128)(2,1)}, bf16[2,10,8,384]{3,2,1,0:T(8,128)(2,1)}, bf16[2,10,8,384]{3,2,1,0:T(8,128)(2,1)}) custom-call(s32[3]{0:T(128)} %pad_add_fusion.where_ref, bf16[10,4,8,384]{3,2,1,0:T(8,128)(2,1)} %get-tuple-element.253.refs_0_, ...), custom_call_target="tpu_custom_call" | custom-call | tf_op jit(solution)/shard_map/fold_g/pallas_call | solution.py:796
  203.4 2.4 %collective-permute-start.21 = (bf16[2,10,8,384]{3,2,1,0:T(8,128)(2,1)}, bf16[2,10,8,384]{3,2,1,0:T(8,128)(2,1)S(1)}, u32[]{:S(2)}, u32[]{:S(2)}) collective-permute-start(bf16[2,10,8,384]{3,2,1,0:T(8,128)(2,1)} %get-tuple-element.259), channel_id=1, source_target_pairs={{0,16},{2,18},{4,20},{6,22},{8,24},{10,26},{12,28},{14,30},{16,0},... | collective-permute-start | bytes 368648 | tf_op jit(solution)/shard_map/ppermute | solution.py:927
  206.1 2.1 constant_dynamic-update-slice_fusion
  208.1 2.1 inner_sum.1
  210.3 2.1 back_sum.1
  212.4 3.1 %collective-permute-done.21.refs_2_ = bf16[2,10,8,384]{3,2,1,0:T(8,128)(2,1)S(1)} collective-permute-done((bf16[2,10,8,384]{3,2,1,0:T(8,128)(2,1)}, bf16[2,10,8,384]{3,2,1,0:T(8,128)(2,1)S(1)}, u32[]{:S(2)}, u32[]{:S(2)}) %collective-permute-start.21) | collective-permute-done | bytes 122912 | tf_op jit(solution)/shard_map/ppermute | solution.py:927
  (61 shorter events, 32.6 us)
Async XLA Ops:
  2.0 2.4 %collective-permute-start = (bf16[2,256,768]{2,1,0:T(8,128)(2,1)S(1)}, bf16[2,256,768]{2,1,0:T(8,128)(2,1)S(1)}, u32[]{:S(2)}, u32[]{:S(2)}) collective-permute-start(bf16[2,256,768]{2,1,0:T(8,128)(2,1)S(1)} %constant_dynamic-slice_fusion.1), channel_id=1, source_target_pairs={{0,1},{1,0},{2,3},{3,2},{4,5},{5,4},{6,7},{7,6},{8,9},{9,8},{10,11... | collective-permute-start | bytes 2359304 | tf_op jit(solution)/shard_map/ppermute | solution.py:626
  2.5 30.4 %collective-permute-start.1 = (bf16[2,256,768]{2,1,0:T(8,128)(2,1)S(1)}, bf16[2,256,768]{2,1,0:T(8,128)(2,1)S(1)}, u32[]{:S(2)}, u32[]{:S(2)}) collective-permute-start(bf16[2,256,768]{2,1,0:T(8,128)(2,1)S(1)} %constant_dynamic-slice_fusion), channel_id=1, source_target_pairs={{0,1},{1,0},{2,3},{3,2},{4,5},{5,4},{6,7},{7,6},{8,9},{9,8},{10,11... | collective-permute-start | bytes 2359304 | tf_op jit(solution)/shard_map/ppermute | solution.py:626
  88.1 4.9 %collective-permute-start.2 = (bf16[8,16,24,384]{3,2,1,0:T(8,128)(2,1)}, bf16[8,16,24,384]{3,2,1,0:T(8,128)(2,1)}, u32[]{:S(2)}, u32[]{:S(2)}) collective-permute-start(bf16[8,16,24,384]{3,2,1,0:T(8,128)(2,1)} %get-tuple-element.148), channel_id=1, source_target_pairs={{0,1},{1,0},{2,3},{3,2},{4,5},{5,4},{6,7},{7,6},{8,9},{9,8},{10,11... | collective-permute-start | bytes 7077896 | tf_op jit(solution)/shard_map/ppermute | solution.py:626
  97.8 18.8 %collective-permute-start.5 = (bf16[10,16,24,384]{3,2,1,0:T(8,128)(2,1)}, bf16[10,16,24,384]{3,2,1,0:T(8,128)(2,1)}, u32[]{:S(2)}, u32[]{:S(2)}) collective-permute-start(bf16[10,16,24,384]{3,2,1,0:T(8,128)(2,1)} %get-tuple-element.161), channel_id=1, source_target_pairs={{0,1},{1,0},{2,3},{3,2},{4,5},{5,4},{6,7},{7,6},{8,9},{9,8},{10,11... | collective-permute-start | bytes 8847368 | tf_op jit(solution)/shard_map/ppermute | solution.py:626
  98.2 18.4 %collective-permute-start.6 = (bf16[2,256,768]{2,1,0:T(8,128)(2,1)}, bf16[2,256,768]{2,1,0:T(8,128)(2,1)S(1)}, u32[]{:S(2)}, u32[]{:S(2)}) collective-permute-start(bf16[2,256,768]{2,1,0:T(8,128)(2,1)} %get-tuple-element.163), channel_id=1, source_target_pairs={{0,1},{1,0},{2,3},{3,2},{4,5},{5,4},{6,7},{7,6},{8,9},{9,8},{10,11... | collective-permute-start | bytes 2359304 | tf_op jit(solution)/shard_map/ppermute | solution.py:626
  98.4 16.8 %collective-permute-start.3 = (bf16[4,4,2,24,384]{4,3,2,1,0:T(8,128)(2,1)}, bf16[4,4,2,24,384]{4,3,2,1,0:T(8,128)(2,1)}, u32[]{:S(2)}, u32[]{:S(2)}) collective-permute-start(bf16[4,4,2,24,384]{4,3,2,1,0:T(8,128)(2,1)} %get-tuple-element.159), channel_id=1, source_target_pairs={{0,2},{2,0},{4,6},{6,4},{8,10},{10,8},{12,14},{14,12},{16,18},{18,... | collective-permute-start | bytes 1769480 | tf_op jit(solution)/shard_map/ppermute | solution.py:927
  101.2 15.4 %collective-permute-start.4 = (bf16[4,4,2,24,384]{4,3,2,1,0:T(8,128)(2,1)}, bf16[4,4,2,24,384]{4,3,2,1,0:T(8,128)(2,1)}, u32[]{:S(2)}, u32[]{:S(2)}) collective-permute-start(bf16[4,4,2,24,384]{4,3,2,1,0:T(8,128)(2,1)} %get-tuple-element.160), channel_id=1, source_target_pairs={{0,4},{2,6},{4,0},{6,2},{8,12},{10,14},{12,8},{14,10},{16,20},{18,... | collective-permute-start | bytes 1769480 | tf_op jit(solution)/shard_map/ppermute | solution.py:927
  123.7 25.3 %collective-permute-start.10 = (bf16[5,4,2,24,384]{4,3,2,1,0:T(8,128)(2,1)}, bf16[5,4,2,24,384]{4,3,2,1,0:T(8,128)(2,1)}, u32[]{:S(2)}, u32[]{:S(2)}) collective-permute-start(bf16[5,4,2,24,384]{4,3,2,1,0:T(8,128)(2,1)} %get-tuple-element.199), channel_id=1, source_target_pairs={{0,4},{2,6},{4,0},{6,2},{8,12},{10,14},{12,8},{14,10},{16,20},{18,... | collective-permute-start | bytes 2211848 | tf_op jit(solution)/shard_map/ppermute | solution.py:927
  125.3 23.8 %collective-permute-start.9 = (bf16[5,4,2,24,384]{4,3,2,1,0:T(8,128)(2,1)}, bf16[5,4,2,24,384]{4,3,2,1,0:T(8,128)(2,1)}, u32[]{:S(2)}, u32[]{:S(2)}) collective-permute-start(bf16[5,4,2,24,384]{4,3,2,1,0:T(8,128)(2,1)} %get-tuple-element.198), channel_id=1, source_target_pairs={{0,2},{2,0},{4,6},{6,4},{8,10},{10,8},{12,14},{14,12},{16,18},{18,... | collective-permute-start | bytes 2211848 | tf_op jit(solution)/shard_map/ppermute | solution.py:927
  125.8 22.0 %collective-permute-start.7 = (bf16[4,4,24,384]{3,2,1,0:T(8,128)(2,1)}, bf16[4,4,24,384]{3,2,1,0:T(8,128)(2,1)}, u32[]{:S(2)}, u32[]{:S(2)}) collective-permute-start(bf16[4,4,24,384]{3,2,1,0:T(8,128)(2,1)} %get-tuple-element.196), channel_id=1, source_target_pairs={{0,4},{2,6},{4,0},{6,2},{8,12},{10,14},{12,8},{14,10},{16,20},{18,... | collective-permute-start | bytes 884744 | tf_op jit(solution)/shard_map/ppermute | solution.py:927
  126.1 22.9 %collective-permute-start.8 = (bf16[4,4,24,384]{3,2,1,0:T(8,128)(2,1)}, bf16[4,4,24,384]{3,2,1,0:T(8,128)(2,1)}, u32[]{:S(2)}, u32[]{:S(2)}) collective-permute-start(bf16[4,4,24,384]{3,2,1,0:T(8,128)(2,1)} %get-tuple-element.197), channel_id=1, source_target_pairs={{0,2},{2,0},{4,6},{6,4},{8,10},{10,8},{12,14},{14,12},{16,18},{18,... | collective-permute-start | bytes 884744 | tf_op jit(solution)/shard_map/ppermute | solution.py:927
  149.0 4.3 %collective-permute-start.11 = (bf16[20,16,8,384]{3,2,1,0:T(8,128)(2,1)}, bf16[20,16,8,384]{3,2,1,0:T(8,128)(2,1)}, u32[]{:S(2)}, u32[]{:S(2)}) collective-permute-start(bf16[20,16,8,384]{3,2,1,0:T(8,128)(2,1)} %get-tuple-element.207), channel_id=1, source_target_pairs={{0,1},{1,0},{2,3},{3,2},{4,5},{5,4},{6,7},{7,6},{8,9},{9,8},{10,11... | collective-permute-start | bytes 5898248 | tf_op jit(solution)/shard_map/ppermute | solution.py:626
  153.3 10.9 %collective-permute-start.12 = (bf16[5,4,24,384]{3,2,1,0:T(8,128)(2,1)}, bf16[5,4,24,384]{3,2,1,0:T(8,128)(2,1)}, u32[]{:S(2)}, u32[]{:S(2)}) collective-permute-start(bf16[5,4,24,384]{3,2,1,0:T(8,128)(2,1)} %get-tuple-element.216), channel_id=1, source_target_pairs={{0,4},{2,6},{4,0},{6,2},{8,12},{10,14},{12,8},{14,10},{16,20},{18,... | collective-permute-start | bytes 1105928 | tf_op jit(solution)/shard_map/ppermute | solution.py:927
  153.8 10.7 %collective-permute-start.13 = (bf16[5,4,24,384]{3,2,1,0:T(8,128)(2,1)}, bf16[5,4,24,384]{3,2,1,0:T(8,128)(2,1)}, u32[]{:S(2)}, u32[]{:S(2)}) collective-permute-start(bf16[5,4,24,384]{3,2,1,0:T(8,128)(2,1)} %get-tuple-element.217), channel_id=1, source_target_pairs={{0,2},{2,0},{4,6},{6,4},{8,10},{10,8},{12,14},{14,12},{16,18},{18,... | collective-permute-start | bytes 1105928 | tf_op jit(solution)/shard_map/ppermute | solution.py:927
  154.4 4.4 %collective-permute-start.14 = (bf16[2,6,768]{2,1,0:T(8,128)(2,1)S(1)}, bf16[2,6,768]{2,1,0:T(8,128)(2,1)S(1)}, u32[]{:S(2)}, u32[]{:S(2)}) collective-permute-start(bf16[2,6,768]{2,1,0:T(8,128)(2,1)S(1)} %bitcast.35), channel_id=1, source_target_pairs={{0,1},{1,0},{2,3},{3,2},{4,5},{5,4},{6,7},{7,6},{8,9},{9,8},{10,11... | collective-permute-start | bytes 55304 | tf_op jit(solution)/shard_map/ppermute | solution.py:626
  168.2 39.9 %all-to-all-start = ((bf16[4,2,9,24,384]{4,3,2,1,0:T(8,128)(2,1)}), bf16[4,2,9,24,384]{4,3,2,1,0:T(8,128)(2,1)}, u32[]{:S(2)}, u32[]{:S(2)}) async-start(bf16[4,2,9,24,384]{4,3,2,1,0:T(8,128)(2,1)} %fold_e.1), calls=%async_computation | async-start | bytes 2654208 | tf_op jit(solution)/shard_map/all_to_all | solution.py:972
  173.1 12.2 %collective-permute-start.15 = (bf16[10,4,2,8,384]{4,3,2,1,0:T(8,128)(2,1)}, bf16[10,4,2,8,384]{4,3,2,1,0:T(8,128)(2,1)}, u32[]{:S(2)}, u32[]{:S(2)}) collective-permute-start(bf16[10,4,2,8,384]{4,3,2,1,0:T(8,128)(2,1)} %get-tuple-element.232), channel_id=1, source_target_pairs={{0,2},{2,0},{4,6},{6,4},{8,10},{10,8},{12,14},{14,12},{16,18},{18,... | collective-permute-start | bytes 1474568 | tf_op jit(solution)/shard_map/ppermute | solution.py:927
  173.8 12.0 %collective-permute-start.16 = (bf16[10,4,2,8,384]{4,3,2,1,0:T(8,128)(2,1)}, bf16[10,4,2,8,384]{4,3,2,1,0:T(8,128)(2,1)}, u32[]{:S(2)}, u32[]{:S(2)}) collective-permute-start(bf16[10,4,2,8,384]{4,3,2,1,0:T(8,128)(2,1)} %get-tuple-element.233), channel_id=1, source_target_pairs={{0,4},{2,6},{4,0},{6,2},{8,12},{10,14},{12,8},{14,10},{16,20},{18,... | collective-permute-start | bytes 1474568 | tf_op jit(solution)/shard_map/ppermute | solution.py:927
  189.0 9.9 %collective-permute-start.19 = (bf16[2,256,768]{2,1,0:T(8,128)(2,1)}, bf16[2,256,768]{2,1,0:T(8,128)(2,1)}, u32[]{:S(2)}, u32[]{:S(2)}) collective-permute-start(bf16[2,256,768]{2,1,0:T(8,128)(2,1)} %get-tuple-element.248), channel_id=1, source_target_pairs={{0,1},{1,0},{2,3},{3,2},{4,5},{5,4},{6,7},{7,6},{8,9},{9,8},{10,11... | collective-permute-start | bytes 2359304 | tf_op jit(solution)/shard_map/ppermute | solution.py:626
  189.1 8.7 %collective-permute-start.17 = (bf16[10,4,8,384]{3,2,1,0:T(8,128)(2,1)}, bf16[10,4,8,384]{3,2,1,0:T(8,128)(2,1)}, u32[]{:S(2)}, u32[]{:S(2)}) collective-permute-start(bf16[10,4,8,384]{3,2,1,0:T(8,128)(2,1)} %get-tuple-element.246), channel_id=1, source_target_pairs={{0,4},{2,6},{4,0},{6,2},{8,12},{10,14},{12,8},{14,10},{16,20},{18,... | collective-permute-start | bytes 737288 | tf_op jit(solution)/shard_map/ppermute | solution.py:927
  190.6 8.3 %collective-permute-start.18 = (bf16[10,4,8,384]{3,2,1,0:T(8,128)(2,1)}, bf16[10,4,8,384]{3,2,1,0:T(8,128)(2,1)}, u32[]{:S(2)}, u32[]{:S(2)}) collective-permute-start(bf16[10,4,8,384]{3,2,1,0:T(8,128)(2,1)} %get-tuple-element.247), channel_id=1, source_target_pairs={{0,2},{2,0},{4,6},{6,4},{8,10},{10,8},{12,14},{14,12},{16,18},{18,... | collective-permute-start | bytes 737288 | tf_op jit(solution)/shard_map/ppermute | solution.py:927
  201.6 10.7 %collective-permute-start.20 = (bf16[2,10,8,384]{3,2,1,0:T(8,128)(2,1)}, bf16[2,10,8,384]{3,2,1,0:T(8,128)(2,1)S(1)}, u32[]{:S(2)}, u32[]{:S(2)}) collective-permute-start(bf16[2,10,8,384]{3,2,1,0:T(8,128)(2,1)} %get-tuple-element.258), channel_id=1, source_target_pairs={{0,8},{2,10},{4,12},{6,14},{8,0},{10,2},{12,4},{14,6},{16,24},{18,... | collective-permute-start | bytes 368648 | tf_op jit(solution)/shard_map/ppermute | solution.py:927
  203.4 12.0 %collective-permute-start.21 = (bf16[2,10,8,384]{3,2,1,0:T(8,128)(2,1)}, bf16[2,10,8,384]{3,2,1,0:T(8,128)(2,1)S(1)}, u32[]{:S(2)}, u32[]{:S(2)}) collective-permute-start(bf16[2,10,8,384]{3,2,1,0:T(8,128)(2,1)} %get-tuple-element.259), channel_id=1, source_target_pairs={{0,16},{2,18},{4,20},{6,22},{8,24},{10,26},{12,28},{14,30},{16,0},... | collective-permute-start | bytes 368648 | tf_op jit(solution)/shard_map/ppermute | solution.py:927
  205.8 9.6 %collective-permute-start.22 = (bf16[2,10,8,384]{3,2,1,0:T(8,128)(2,1)}, bf16[2,10,8,384]{3,2,1,0:T(8,128)(2,1)S(1)}, u32[]{:S(2)}, u32[]{:S(2)}) collective-permute-start(bf16[2,10,8,384]{3,2,1,0:T(8,128)(2,1)} %get-tuple-element.260), channel_id=1, source_target_pairs={{0,24},{2,26},{4,28},{6,30},{8,16},{10,18},{12,20},{14,22},{16,8},... | collective-permute-start | bytes 368648 | tf_op jit(solution)/shard_map/ppermute | solution.py:927
  (7 other events, 15.5 us)

commit v6 on v5

--- a/solution.py
+++ b/solution.py
@@ -43,7 +43,7 @@
 
 
 def params(mib):
-    return pltpu.CompilerParams(vmem_limit_bytes=mib << 20)
+    return pltpu.CompilerParams(vmem_limit_bytes=(mib << 20) + (896 << 10))
 
 
 def row_starts(len_ref, row):
@@ -979,10 +979,12 @@
         got_i = swap(send_i)
         output_got = swap(output_other)
         dproj, *bias_a = attention_grad(qkv, probs, mixed, dmixed, 0, 1)
-        dproj, got_b, got_i, keep_i, output_got = sync(dproj, got_b, got_i, keep_i, output_got)
-        inner, back = add_pieces(where, [fold_first(view(keep_i), view(got_i)), fold_second(back, got_b)], "fold_b")
-        dmixed, inner, back = sync(dmixed, inner, back)
+        dproj, got_i, keep_i, output_got = sync(dproj, got_i, keep_i, output_got)
+        (inner,) = add_pieces(where, [fold_first(view(keep_i), view(got_i))], "fold_b")
+        inner, got_b = sync(inner, got_b)
         got_i = cross(inner, 1, 2)
+        (back,) = add_pieces(where, [fold_second(back, got_b)], "fold_b2")
+        dmixed, back = sync(dmixed, back)
         got_b = cross(back, 2, 1)
         dproj, *bias_b = attention_grad(qkv, probs, mixed, dmixed, 1, 1, dproj)
         keep_q, send_q = grad_proj(

time: 219 us -> 216 us (0.986)
  waiting for transfers between devices: 27.8 us -> 22.1 us
    ppermute x15, waiting for transfers between devices: 21.7 us -> 16 us  [flip(): return lax.ppermute(value, 'dp', [(i, i ^ bits) for i in range(16)])]
    pallas_call x7 -> x8, Pallas kernels: 29.5 us -> 31.2 us  [add_pieces(): pl.pallas_call(body, name=name, out_shape=[jax.ShapeDtypeStruct(s, BF) fo...]
  transfers between devices with their start and end apart: 24 -> 24, of which waited for: 14 -> 10; matrix products, arithmetic and copies ran while one was open for 2% -> 3% of each run, Pallas kernels for 38% -> 43%
where the time goes in v6:
time: 216 us; the launch traced here: 214 us
  Pallas kernels  157 us (73%)
  starting transfers between devices  25.5 us (12%)
  waiting for transfers between devices  22.1 us (10%)
  local copies, waits for them, and re-layouts  7.93 us (4%)
    pallas_call x1, Pallas kernels, feed_call(): pl.pallas_call(partial(feed_kernel, split), name='feed_rows', out_shape=s...  54.3 us
    pallas_call x8, Pallas kernels, add_pieces(): pl.pallas_call(body, name=name, out_shape=[jax.ShapeDtypeStruct(s, BF) fo...  31.2 us
    pallas_call x1, Pallas kernels, attention_call(): pl.pallas_call(attention_kernel, name='attention_rows', out_shape=[row(3...  27.7 us
    pallas_call x2, Pallas kernels, attention_grad(): pl.pallas_call(body, name='attention_grad', out_shape=[jax.ShapeDtypeStru...  21.6 us
    ppermute x15, starting transfers between devices, flip(): return lax.ppermute(value, 'dp', [(i, i ^ bits) for i in range(16)])  18.7 us
    ppermute x15, waiting for transfers between devices, flip(): return lax.ppermute(value, 'dp', [(i, i ^ bits) for i in range(16)])  16 us
    pallas_call x1, Pallas kernels, grad_proj(): pl.pallas_call(body, name='grad_qkv', out_shape=[out, out], grid_spec=plt...  8.46 us
    pallas_call x1, Pallas kernels, input_grad_call(): pl.pallas_call(body, name='input_grad', out_shape=[jax.ShapeDtypeStruct((...  7.98 us
  transfers between devices with their start and end apart: 24, of which 10 were waited for; matrix products, arithmetic and copies ran while one was open for 3% of the time, Pallas kernels for 43%

profile of v6, /device:TPU:0, one launch (start us, length us, event | category | flops | bytes accessed | tf_op | source)
XLA Modules:
  0.0 214.3 jit_solution(719445839625632561)
XLA Ops:
  5.3 27.7 %attention_rows.1 = (bf16[2,512,2304]{2,1,0:T(8,128)(2,1)}, bf16[2,6,2,512,512]{4,3,2,1,0:T(8,128)(2,1)}, bf16[2,512,768]{2,1,0:T(8,128)(2,1)}, bf16[2,512,768]{...) custom-call(s32[1]{0:T(128)} %bitcast.3.core_ref, ...), custom_call_target="tpu_custom_call" | custom-call | flops 6442450944 | bytes 36700160 | tf_op jit(solution)/shard_map/attention_rows/pallas_call | solution.py:174
  33.9 54.3 %feed_rows.1 = (bf16[4,256,768]{2,1,0:T(8,128)(2,1)}, bf16[2,256,768]{2,1,0:T(8,128)(2,1)}, bf16[2,8,768]{2,1,0:T(8,128)(2,1)}, bf16[1024,768]{1,0:T(8,128)(2,1)...) custom-call(s32[1]{0:T(128)} %bitcast.3.core_ref, ...), custom_call_target="tpu_custom_call" | custom-call | flops 31406948352 | bytes 41943040 | tf_op jit(solution)/shard_map/feed_rows/pallas_call | solution.py:426
  89.3 3.9 %collective-permute-done.2 = bf16[8,16,24,384]{3,2,1,0:T(8,128)(2,1)} collective-permute-done((bf16[8,16,24,384]{3,2,1,0:T(8,128)(2,1)}, bf16[8,16,24,384]{3,2,1,0:T(8,128)(2,1)}, u32[]{:S(2)}, u32[]{:S(2)}) %collective-permute-start.2) | collective-permute-done | bytes 2359328 | tf_op jit(solution)/shard_map/ppermute | solution.py:626
  93.2 4.8 %fold_a.1 = (bf16[4,4,2,24,384]{4,3,2,1,0:T(8,128)(2,1)}, bf16[4,4,2,24,384]{4,3,2,1,0:T(8,128)(2,1)}, bf16[4,4,2,24,384]{4,3,2,1,0:T(8,128)(2,1)}, bf16[4,4,2,24,384]{4,3,2,1,0:T(8,128)(2,1)}) custom-call(s32[3]{0:T(128)} %pad_add_fusion.where_ref, bf16[2,4,4,2,2,24,384]{6,5,4,3,2,1,0:T(8,128)(2,1)} %bitcast.32, ...), custom_call_target="tpu_custom_call" | custom-call | tf_op jit(solution)/shard_map/fold_a/pallas_call | solution.py:796
  98.5 2.8 %collective-permute-start.5 = (bf16[4,4,2,24,384]{4,3,2,1,0:T(8,128)(2,1)}, bf16[4,4,2,24,384]{4,3,2,1,0:T(8,128)(2,1)}, u32[]{:S(2)}, u32[]{:S(2)}) collective-permute-start(bf16[4,4,2,24,384]{4,3,2,1,0:T(8,128)(2,1)} %get-tuple-element.168), channel_id=1, source_target_pairs={{0,2},{2,0},{4,6},{6,4},{8,10},{10,8},{12,14},{14,12},{16,18},{18,... | collective-permute-start | bytes 1769480 | tf_op jit(solution)/shard_map/ppermute | solution.py:927
  102.9 10.8 %attention_grad.2 = (bf16[3,2,512,768]{3,2,1,0:T(8,128)(2,1)}, f32[1,768]{1,0:T(1,128)}, f32[1,768]{1,0:T(1,128)}) custom-call(bf16[2,512,2304]{2,1,0:T(8,128)(2,1)} %get-tuple-element.141.q_ref.k_ref.v_ref, bf16[2,512,2304]{2,1,0:T(8,128)(2,1)} %get-tuple-element.141.q_ref.k_ref.v_ref, bf16[2,512,2304]{2,1,0:T(8,128)(2,1)} %get-tuple-element.141.q_ref.k_ref.v_ref, ...), custom_call_target="tpu_custom_call" | custom-call | flops 1610612736 | bytes 15728640 | tf_op jit(solution)/shard_map/attention_grad/pallas_call | solution.py:531
  113.8 5.2 %fold_b.1 = (bf16[5,4,2,24,384]{4,3,2,1,0:T(8,128)(2,1)}, bf16[5,4,2,24,384]{4,3,2,1,0:T(8,128)(2,1)}, bf16[5,4,2,24,384]{4,3,2,1,0:T(8,128)(2,1)}, bf16[5,4,2,24,384]{4,3,2,1,0:T(8,128)(2,1)}) custom-call(s32[3]{0:T(128)} %pad_add_fusion.where_ref, bf16[2,5,4,2,2,24,384]{6,5,4,3,2,1,0:T(8,128)(2,1)} %bitcast.31, ...), custom_call_target="tpu_custom_call" | custom-call | tf_op jit(solution)/shard_map/fold_b/pallas_call | solution.py:796
  119.7 3.4 %fold_b2.1 = (bf16[4,4,24,384]{3,2,1,0:T(8,128)(2,1)}, bf16[4,4,24,384]{3,2,1,0:T(8,128)(2,1)}, bf16[4,4,24,384]{3,2,1,0:T(8,128)(2,1)}, bf16[4,4,24,384]{3,2,1,0:T(8,128)(2,1)}) custom-call(s32[3]{0:T(128)} %pad_add_fusion.where_ref, bf16[4,4,2,24,384]{4,3,2,1,0:T(8,128)(2,1)} %get-tuple-element.172.refs_0_, ...), custom_call_target="tpu_custom_call" | custom-call | tf_op jit(solution)/shard_map/fold_b2/pallas_call | solution.py:796
  126.6 10.7 %attention_grad.3 = (bf16[3,2,512,768]{3,2,1,0:T(8,128)(2,1)}, f32[1,768]{1,0:T(1,128)}, f32[1,768]{1,0:T(1,128)}) custom-call(bf16[2,512,2304]{2,1,0:T(8,128)(2,1)} %get-tuple-element.141.q_ref.k_ref.v_ref, bf16[2,512,2304]{2,1,0:T(8,128)(2,1)} %get-tuple-element.141.q_ref.k_ref.v_ref, ...), custom_call_target="tpu_custom_call", output_to_operand_aliasing={{0}: (6, {})} | custom-call | flops 1610612736 | bytes 15728640 | tf_op jit(solution)/shard_map/attention_grad/pallas_call | solution.py:531
  137.4 8.5 %grad_qkv.1 = (bf16[20,16,8,384]{3,2,1,0:T(8,128)(2,1)}, bf16[20,16,8,384]{3,2,1,0:T(8,128)(2,1)}) custom-call(s32[1]{0:T(128)} %bitcast.3.core_ref, bf16[1024,768]{1,0:T(8,128)(2,1)} %bitcast.43, bf16[3,1024,768]{2,1,0:T(8,128)(2,1)} %bitcast.29, f32[1,768]{1,0:T(1,128)} %get-tuple-element.183.refs_0_, f32[1,768]{1,0:T(1,128)} %get-tuple-element.184.refs_1_, ...), custom_call_target="tpu_custom_call" | custom-call | flops 3623878656 | bytes 8257536 | tf_op jit(solution)/shard_map/grad_qkv/pallas_call | solution.py:747
  146.0 3.6 %fold_c.1 = (bf16[5,4,24,384]{3,2,1,0:T(8,128)(2,1)}, bf16[5,4,24,384]{3,2,1,0:T(8,128)(2,1)}, bf16[5,4,24,384]{3,2,1,0:T(8,128)(2,1)}, bf16[5,4,24,384]{3,2,1,0:T(8,128)(2,1)}) custom-call(s32[3]{0:T(128)} %pad_add_fusion.where_ref, bf16[5,4,2,24,384]{4,3,2,1,0:T(8,128)(2,1)} %get-tuple-element.170.refs_0_, ...), custom_call_target="tpu_custom_call" | custom-call | tf_op jit(solution)/shard_map/fold_c/pallas_call | solution.py:796
  150.9 4.3 %fold_d.1 = (bf16[10,4,2,8,384]{4,3,2,1,0:T(8,128)(2,1)}, bf16[10,4,2,8,384]{4,3,2,1,0:T(8,128)(2,1)}, bf16[10,4,2,8,384]{4,3,2,1,0:T(8,128)(2,1)}, bf16[10,4,2,8,384]{4,3,2,1,0:T(8,128)(2,1)}) custom-call(s32[3]{0:T(128)} %pad_add_fusion.where_ref, bf16[2,10,4,2,2,8,384]{6,5,4,3,2,1,0:T(8,128)(2,1)} %bitcast.33, ...), custom_call_target="tpu_custom_call" | custom-call | tf_op jit(solution)/shard_map/fold_d/pallas_call | solution.py:796
  155.2 6.0 %collective-permute-done.12.refs_5_ = bf16[5,4,24,384]{3,2,1,0:T(8,128)(2,1)} collective-permute-done((bf16[5,4,24,384]{3,2,1,0:T(8,128)(2,1)}, bf16[5,4,24,384]{3,2,1,0:T(8,128)(2,1)}, u32[]{:S(2)}, u32[]{:S(2)}) %collective-permute-start.12) | collective-permute-done | bytes 368672 | tf_op jit(solution)/shard_map/ppermute | solution.py:927
  161.4 3.8 %fold_e.1 = bf16[4,2,9,24,384]{4,3,2,1,0:T(8,128)(2,1)} custom-call(s32[3]{0:T(128)} %pad_add_fusion.where_ref, bf16[4,4,24,384]{3,2,1,0:T(8,128)(2,1)} %get-tuple-element.220.refs_0_, bf16[4,4,24,384]{3,2,1,0:T(8,128)(2,1)} %collective-permute-done.7.refs_1_, bf16[4,4,24,384]{3,2,1,0:T(8,128)(2,1)} %get-tuple-element.222.refs_2_, ...), custom_call_target="tpu_custom_call" | custom-call | tf_op jit(solution)/shard_map/fold_e/pallas_call | solution.py:796
  165.2 4.9 %all-to-all-start = ((bf16[4,2,9,24,384]{4,3,2,1,0:T(8,128)(2,1)}), bf16[4,2,9,24,384]{4,3,2,1,0:T(8,128)(2,1)}, u32[]{:S(2)}, u32[]{:S(2)}) async-start(bf16[4,2,9,24,384]{4,3,2,1,0:T(8,128)(2,1)} %fold_e.1), calls=%async_computation | async-start | bytes 2654208 | tf_op jit(solution)/shard_map/all_to_all | solution.py:972
  172.2 8.0 %input_grad.1 = (bf16[4,256,768]{2,1,0:T(8,128)(2,1)}, bf16[2,256,768]{2,1,0:T(8,128)(2,1)}) custom-call(s32[1]{0:T(128)} %bitcast.3.core_ref, bf16[3,1024,768]{2,1,0:T(8,128)(2,1)} %bitcast.30, bf16[1024,768]{1,0:T(8,128)(2,1)} %get-tuple-element.229.d_hbm, bf16[768,2304]{1,0:T(8,128)(2,1)} %w_ref.1), custom_call_target="tpu_custom_call" | custom-call | flops 3623878656 | bytes 10485760 | tf_op jit(solution)/shard_map/input_grad/pallas_call | solution.py:584
  180.2 2.2 %collective-permute-done.15.refs_1_ = bf16[10,4,2,8,384]{4,3,2,1,0:T(8,128)(2,1)} collective-permute-done((bf16[10,4,2,8,384]{4,3,2,1,0:T(8,128)(2,1)}, bf16[10,4,2,8,384]{4,3,2,1,0:T(8,128)(2,1)}, u32[]{:S(2)}, u32[]{:S(2)}) %collective-permute-start.15) | collective-permute-done | bytes 491552 | tf_op jit(solution)/shard_map/ppermute | solution.py:927
  182.6 3.3 %fold_f.1 = (bf16[10,4,8,384]{3,2,1,0:T(8,128)(2,1)}, bf16[10,4,8,384]{3,2,1,0:T(8,128)(2,1)}, bf16[10,4,8,384]{3,2,1,0:T(8,128)(2,1)}, bf16[10,4,8,384]{3,2,1,0:T(8,128)(2,1)}) custom-call(s32[3]{0:T(128)} %pad_add_fusion.where_ref, bf16[10,4,2,8,384]{4,3,2,1,0:T(8,128)(2,1)} %get-tuple-element.219.refs_0_, ...), custom_call_target="tpu_custom_call" | custom-call | tf_op jit(solution)/shard_map/fold_f/pallas_call | solution.py:796
  191.7 3.0 %collective-permute-done.17.refs_1_ = bf16[10,4,8,384]{3,2,1,0:T(8,128)(2,1)} collective-permute-done((bf16[10,4,8,384]{3,2,1,0:T(8,128)(2,1)}, bf16[10,4,8,384]{3,2,1,0:T(8,128)(2,1)}, u32[]{:S(2)}, u32[]{:S(2)}) %collective-permute-start.17) | collective-permute-done | bytes 245792 | tf_op jit(solution)/shard_map/ppermute | solution.py:927
  195.8 2.7 %fold_g.1 = (bf16[2,10,8,384]{3,2,1,0:T(8,128)(2,1)}, bf16[2,10,8,384]{3,2,1,0:T(8,128)(2,1)}, bf16[2,10,8,384]{3,2,1,0:T(8,128)(2,1)}, bf16[2,10,8,384]{3,2,1,0:T(8,128)(2,1)}) custom-call(s32[3]{0:T(128)} %pad_add_fusion.where_ref, bf16[10,4,8,384]{3,2,1,0:T(8,128)(2,1)} %get-tuple-element.253.refs_0_, ...), custom_call_target="tpu_custom_call" | custom-call | tf_op jit(solution)/shard_map/fold_g/pallas_call | solution.py:796
  200.4 2.4 %collective-permute-start.21 = (bf16[2,10,8,384]{3,2,1,0:T(8,128)(2,1)}, bf16[2,10,8,384]{3,2,1,0:T(8,128)(2,1)}, u32[]{:S(2)}, u32[]{:S(2)}) collective-permute-start(bf16[2,10,8,384]{3,2,1,0:T(8,128)(2,1)} %get-tuple-element.259), channel_id=1, source_target_pairs={{0,16},{2,18},{4,20},{6,22},{8,24},{10,26},{12,28},{14,30},{16,0},... | collective-permute-start | bytes 368648 | tf_op jit(solution)/shard_map/ppermute | solution.py:927
  205.1 2.1 inner_sum.1
  207.2 2.1 back_sum.1
  209.3 3.2 %collective-permute-done.21.refs_2_ = bf16[2,10,8,384]{3,2,1,0:T(8,128)(2,1)} collective-permute-done((bf16[2,10,8,384]{3,2,1,0:T(8,128)(2,1)}, bf16[2,10,8,384]{3,2,1,0:T(8,128)(2,1)}, u32[]{:S(2)}, u32[]{:S(2)}) %collective-permute-start.21) | collective-permute-done | bytes 122912 | tf_op jit(solution)/shard_map/ppermute | solution.py:927
  (56 shorter events, 29.7 us)
Async XLA Ops:
  2.0 2.4 %collective-permute-start = (bf16[2,256,768]{2,1,0:T(8,128)(2,1)S(1)}, bf16[2,256,768]{2,1,0:T(8,128)(2,1)S(1)}, u32[]{:S(2)}, u32[]{:S(2)}) collective-permute-start(bf16[2,256,768]{2,1,0:T(8,128)(2,1)S(1)} %constant_dynamic-slice_fusion.1), channel_id=1, source_target_pairs={{0,1},{1,0},{2,3},{3,2},{4,5},{5,4},{6,7},{7,6},{8,9},{9,8},{10,11... | collective-permute-start | bytes 2359304 | tf_op jit(solution)/shard_map/ppermute | solution.py:626
  2.5 30.5 %collective-permute-start.1 = (bf16[2,256,768]{2,1,0:T(8,128)(2,1)S(1)}, bf16[2,256,768]{2,1,0:T(8,128)(2,1)S(1)}, u32[]{:S(2)}, u32[]{:S(2)}) collective-permute-start(bf16[2,256,768]{2,1,0:T(8,128)(2,1)S(1)} %constant_dynamic-slice_fusion), channel_id=1, source_target_pairs={{0,1},{1,0},{2,3},{3,2},{4,5},{5,4},{6,7},{7,6},{8,9},{9,8},{10,11... | collective-permute-start | bytes 2359304 | tf_op jit(solution)/shard_map/ppermute | solution.py:626
  88.2 4.9 %collective-permute-start.2 = (bf16[8,16,24,384]{3,2,1,0:T(8,128)(2,1)}, bf16[8,16,24,384]{3,2,1,0:T(8,128)(2,1)}, u32[]{:S(2)}, u32[]{:S(2)}) collective-permute-start(bf16[8,16,24,384]{3,2,1,0:T(8,128)(2,1)} %get-tuple-element.150), channel_id=1, source_target_pairs={{0,1},{1,0},{2,3},{3,2},{4,5},{5,4},{6,7},{7,6},{8,9},{9,8},{10,11... | collective-permute-start | bytes 7077896 | tf_op jit(solution)/shard_map/ppermute | solution.py:626
  97.9 15.8 %collective-permute-start.3 = (bf16[10,16,24,384]{3,2,1,0:T(8,128)(2,1)}, bf16[10,16,24,384]{3,2,1,0:T(8,128)(2,1)}, u32[]{:S(2)}, u32[]{:S(2)}) collective-permute-start(bf16[10,16,24,384]{3,2,1,0:T(8,128)(2,1)} %get-tuple-element.159), channel_id=1, source_target_pairs={{0,1},{1,0},{2,3},{3,2},{4,5},{5,4},{6,7},{7,6},{8,9},{9,8},{10,11... | collective-permute-start | bytes 8847368 | tf_op jit(solution)/shard_map/ppermute | solution.py:626
  98.4 15.4 %collective-permute-start.4 = (bf16[2,256,768]{2,1,0:T(8,128)(2,1)}, bf16[2,256,768]{2,1,0:T(8,128)(2,1)}, u32[]{:S(2)}, u32[]{:S(2)}) collective-permute-start(bf16[2,256,768]{2,1,0:T(8,128)(2,1)} %get-tuple-element.161), channel_id=1, source_target_pairs={{0,1},{1,0},{2,3},{3,2},{4,5},{5,4},{6,7},{7,6},{8,9},{9,8},{10,11... | collective-permute-start | bytes 2359304 | tf_op jit(solution)/shard_map/ppermute | solution.py:626
  98.5 20.5 %collective-permute-start.5 = (bf16[4,4,2,24,384]{4,3,2,1,0:T(8,128)(2,1)}, bf16[4,4,2,24,384]{4,3,2,1,0:T(8,128)(2,1)}, u32[]{:S(2)}, u32[]{:S(2)}) collective-permute-start(bf16[4,4,2,24,384]{4,3,2,1,0:T(8,128)(2,1)} %get-tuple-element.168), channel_id=1, source_target_pairs={{0,2},{2,0},{4,6},{6,4},{8,10},{10,8},{12,14},{14,12},{16,18},{18,... | collective-permute-start | bytes 1769480 | tf_op jit(solution)/shard_map/ppermute | solution.py:927
  101.4 17.6 %collective-permute-start.6 = (bf16[4,4,2,24,384]{4,3,2,1,0:T(8,128)(2,1)}, bf16[4,4,2,24,384]{4,3,2,1,0:T(8,128)(2,1)}, u32[]{:S(2)}, u32[]{:S(2)}) collective-permute-start(bf16[4,4,2,24,384]{4,3,2,1,0:T(8,128)(2,1)} %get-tuple-element.169), channel_id=1, source_target_pairs={{0,4},{2,6},{4,0},{6,2},{8,12},{10,14},{12,8},{14,10},{16,20},{18,... | collective-permute-start | bytes 1769480 | tf_op jit(solution)/shard_map/ppermute | solution.py:927
  119.0 26.9 %collective-permute-start.10 = (bf16[5,4,2,24,384]{4,3,2,1,0:T(8,128)(2,1)}, bf16[5,4,2,24,384]{4,3,2,1,0:T(8,128)(2,1)}, u32[]{:S(2)}, u32[]{:S(2)}) collective-permute-start(bf16[5,4,2,24,384]{4,3,2,1,0:T(8,128)(2,1)} %get-tuple-element.199), channel_id=1, source_target_pairs={{0,4},{2,6},{4,0},{6,2},{8,12},{10,14},{12,8},{14,10},{16,20},{18,... | collective-permute-start | bytes 2211848 | tf_op jit(solution)/shard_map/ppermute | solution.py:927
  119.6 26.3 %collective-permute-start.9 = (bf16[5,4,2,24,384]{4,3,2,1,0:T(8,128)(2,1)}, bf16[5,4,2,24,384]{4,3,2,1,0:T(8,128)(2,1)}, u32[]{:S(2)}, u32[]{:S(2)}) collective-permute-start(bf16[5,4,2,24,384]{4,3,2,1,0:T(8,128)(2,1)} %get-tuple-element.198), channel_id=1, source_target_pairs={{0,2},{2,0},{4,6},{6,4},{8,10},{10,8},{12,14},{14,12},{16,18},{18,... | collective-permute-start | bytes 2211848 | tf_op jit(solution)/shard_map/ppermute | solution.py:927
  123.1 22.7 %collective-permute-start.7 = (bf16[4,4,24,384]{3,2,1,0:T(8,128)(2,1)}, bf16[4,4,24,384]{3,2,1,0:T(8,128)(2,1)}, u32[]{:S(2)}, u32[]{:S(2)}) collective-permute-start(bf16[4,4,24,384]{3,2,1,0:T(8,128)(2,1)} %get-tuple-element.196), channel_id=1, source_target_pairs={{0,4},{2,6},{4,0},{6,2},{8,12},{10,14},{12,8},{14,10},{16,20},{18,... | collective-permute-start | bytes 884744 | tf_op jit(solution)/shard_map/ppermute | solution.py:927
  125.1 20.7 %collective-permute-start.8 = (bf16[4,4,24,384]{3,2,1,0:T(8,128)(2,1)}, bf16[4,4,24,384]{3,2,1,0:T(8,128)(2,1)}, u32[]{:S(2)}, u32[]{:S(2)}) collective-permute-start(bf16[4,4,24,384]{3,2,1,0:T(8,128)(2,1)} %get-tuple-element.197), channel_id=1, source_target_pairs={{0,2},{2,0},{4,6},{6,4},{8,10},{10,8},{12,14},{14,12},{16,18},{18,... | collective-permute-start | bytes 884744 | tf_op jit(solution)/shard_map/ppermute | solution.py:927
  145.9 4.4 %collective-permute-start.11 = (bf16[20,16,8,384]{3,2,1,0:T(8,128)(2,1)}, bf16[20,16,8,384]{3,2,1,0:T(8,128)(2,1)}, u32[]{:S(2)}, u32[]{:S(2)}) collective-permute-start(bf16[20,16,8,384]{3,2,1,0:T(8,128)(2,1)} %get-tuple-element.207), channel_id=1, source_target_pairs={{0,1},{1,0},{2,3},{3,2},{4,5},{5,4},{6,7},{7,6},{8,9},{9,8},{10,11... | collective-permute-start | bytes 5898248 | tf_op jit(solution)/shard_map/ppermute | solution.py:626
  150.3 10.9 %collective-permute-start.12 = (bf16[5,4,24,384]{3,2,1,0:T(8,128)(2,1)}, bf16[5,4,24,384]{3,2,1,0:T(8,128)(2,1)}, u32[]{:S(2)}, u32[]{:S(2)}) collective-permute-start(bf16[5,4,24,384]{3,2,1,0:T(8,128)(2,1)} %get-tuple-element.216), channel_id=1, source_target_pairs={{0,4},{2,6},{4,0},{6,2},{8,12},{10,14},{12,8},{14,10},{16,20},{18,... | collective-permute-start | bytes 1105928 | tf_op jit(solution)/shard_map/ppermute | solution.py:927
  150.8 10.7 %collective-permute-start.13 = (bf16[5,4,24,384]{3,2,1,0:T(8,128)(2,1)}, bf16[5,4,24,384]{3,2,1,0:T(8,128)(2,1)}, u32[]{:S(2)}, u32[]{:S(2)}) collective-permute-start(bf16[5,4,24,384]{3,2,1,0:T(8,128)(2,1)} %get-tuple-element.217), channel_id=1, source_target_pairs={{0,2},{2,0},{4,6},{6,4},{8,10},{10,8},{12,14},{14,12},{16,18},{18,... | collective-permute-start | bytes 1105928 | tf_op jit(solution)/shard_map/ppermute | solution.py:927
  150.9 4.3 %collective-permute-start.14 = (bf16[2,6,768]{2,1,0:T(8,128)(2,1)S(1)}, bf16[2,6,768]{2,1,0:T(8,128)(2,1)S(1)}, u32[]{:S(2)}, u32[]{:S(2)}) collective-permute-start(bf16[2,6,768]{2,1,0:T(8,128)(2,1)S(1)} %bitcast.35), channel_id=1, source_target_pairs={{0,1},{1,0},{2,3},{3,2},{4,5},{5,4},{6,7},{7,6},{8,9},{9,8},{10,11... | collective-permute-start | bytes 55304 | tf_op jit(solution)/shard_map/ppermute | solution.py:626
  165.2 39.9 %all-to-all-start = ((bf16[4,2,9,24,384]{4,3,2,1,0:T(8,128)(2,1)}), bf16[4,2,9,24,384]{4,3,2,1,0:T(8,128)(2,1)}, u32[]{:S(2)}, u32[]{:S(2)}) async-start(bf16[4,2,9,24,384]{4,3,2,1,0:T(8,128)(2,1)} %fold_e.1), calls=%async_computation | async-start | bytes 2654208 | tf_op jit(solution)/shard_map/all_to_all | solution.py:972
  170.1 12.3 %collective-permute-start.15 = (bf16[10,4,2,8,384]{4,3,2,1,0:T(8,128)(2,1)}, bf16[10,4,2,8,384]{4,3,2,1,0:T(8,128)(2,1)}, u32[]{:S(2)}, u32[]{:S(2)}) collective-permute-start(bf16[10,4,2,8,384]{4,3,2,1,0:T(8,128)(2,1)} %get-tuple-element.232), channel_id=1, source_target_pairs={{0,2},{2,0},{4,6},{6,4},{8,10},{10,8},{12,14},{14,12},{16,18},{18,... | collective-permute-start | bytes 1474568 | tf_op jit(solution)/shard_map/ppermute | solution.py:927
  170.6 12.0 %collective-permute-start.16 = (bf16[10,4,2,8,384]{4,3,2,1,0:T(8,128)(2,1)}, bf16[10,4,2,8,384]{4,3,2,1,0:T(8,128)(2,1)}, u32[]{:S(2)}, u32[]{:S(2)}) collective-permute-start(bf16[10,4,2,8,384]{4,3,2,1,0:T(8,128)(2,1)} %get-tuple-element.233), channel_id=1, source_target_pairs={{0,4},{2,6},{4,0},{6,2},{8,12},{10,14},{12,8},{14,10},{16,20},{18,... | collective-permute-start | bytes 1474568 | tf_op jit(solution)/shard_map/ppermute | solution.py:927
  185.9 9.9 %collective-permute-start.19 = (bf16[2,256,768]{2,1,0:T(8,128)(2,1)}, bf16[2,256,768]{2,1,0:T(8,128)(2,1)}, u32[]{:S(2)}, u32[]{:S(2)}) collective-permute-start(bf16[2,256,768]{2,1,0:T(8,128)(2,1)} %get-tuple-element.248), channel_id=1, source_target_pairs={{0,1},{1,0},{2,3},{3,2},{4,5},{5,4},{6,7},{7,6},{8,9},{9,8},{10,11... | collective-permute-start | bytes 2359304 | tf_op jit(solution)/shard_map/ppermute | solution.py:626
  186.0 8.7 %collective-permute-start.17 = (bf16[10,4,8,384]{3,2,1,0:T(8,128)(2,1)}, bf16[10,4,8,384]{3,2,1,0:T(8,128)(2,1)}, u32[]{:S(2)}, u32[]{:S(2)}) collective-permute-start(bf16[10,4,8,384]{3,2,1,0:T(8,128)(2,1)} %get-tuple-element.246), channel_id=1, source_target_pairs={{0,4},{2,6},{4,0},{6,2},{8,12},{10,14},{12,8},{14,10},{16,20},{18,... | collective-permute-start | bytes 737288 | tf_op jit(solution)/shard_map/ppermute | solution.py:927
  187.5 8.3 %collective-permute-start.18 = (bf16[10,4,8,384]{3,2,1,0:T(8,128)(2,1)}, bf16[10,4,8,384]{3,2,1,0:T(8,128)(2,1)}, u32[]{:S(2)}, u32[]{:S(2)}) collective-permute-start(bf16[10,4,8,384]{3,2,1,0:T(8,128)(2,1)} %get-tuple-element.247), channel_id=1, source_target_pairs={{0,2},{2,0},{4,6},{6,4},{8,10},{10,8},{12,14},{14,12},{16,18},{18,... | collective-permute-start | bytes 737288 | tf_op jit(solution)/shard_map/ppermute | solution.py:927
  198.6 10.7 %collective-permute-start.20 = (bf16[2,10,8,384]{3,2,1,0:T(8,128)(2,1)}, bf16[2,10,8,384]{3,2,1,0:T(8,128)(2,1)}, u32[]{:S(2)}, u32[]{:S(2)}) collective-permute-start(bf16[2,10,8,384]{3,2,1,0:T(8,128)(2,1)} %get-tuple-element.258), channel_id=1, source_target_pairs={{0,8},{2,10},{4,12},{6,14},{8,0},{10,2},{12,4},{14,6},{16,24},{18,... | collective-permute-start | bytes 368648 | tf_op jit(solution)/shard_map/ppermute | solution.py:927
  200.4 12.1 %collective-permute-start.21 = (bf16[2,10,8,384]{3,2,1,0:T(8,128)(2,1)}, bf16[2,10,8,384]{3,2,1,0:T(8,128)(2,1)}, u32[]{:S(2)}, u32[]{:S(2)}) collective-permute-start(bf16[2,10,8,384]{3,2,1,0:T(8,128)(2,1)} %get-tuple-element.259), channel_id=1, source_target_pairs={{0,16},{2,18},{4,20},{6,22},{8,24},{10,26},{12,28},{14,30},{16,0},... | collective-permute-start | bytes 368648 | tf_op jit(solution)/shard_map/ppermute | solution.py:927
  202.7 9.7 %collective-permute-start.22 = (bf16[2,10,8,384]{3,2,1,0:T(8,128)(2,1)}, bf16[2,10,8,384]{3,2,1,0:T(8,128)(2,1)}, u32[]{:S(2)}, u32[]{:S(2)}) collective-permute-start(bf16[2,10,8,384]{3,2,1,0:T(8,128)(2,1)} %get-tuple-element.260), channel_id=1, source_target_pairs={{0,24},{2,26},{4,28},{6,30},{8,16},{10,18},{12,20},{14,22},{16,8},... | collective-permute-start | bytes 368648 | tf_op jit(solution)/shard_map/ppermute | solution.py:927
  (4 other events, 8.7 us)

commit v7 on v6

--- a/solution.py
+++ b/solution.py
@@ -771,28 +771,34 @@
         scratch = refs[len(inputs) + len(outputs) :]
         loads, stores, sums = [], [], []
         for n, (group_in, group_out, pieces, _) in enumerate(groups):
-            k_ref, g_ref, k_sem, g_sem, o_sem = scratch[5 * n : 5 * n + 5]
-            for i, (a, a_at, b, b_at, o, o_at) in enumerate(pieces([where_ref[0], where_ref[1], where_ref[2]])):
-                loads.append(pltpu.make_async_copy(ins[a].at[a_at], k_ref.at[i], k_sem.at[i]))
-                loads.append(pltpu.make_async_copy(ins[b].at[b_at], g_ref.at[i], g_sem.at[i]))
+            k_ref, g_ref, h_ref, k_sem, g_sem, h_sem, o_sem = scratch[7 * n : 7 * n + 7]
+            for i, (a, a_at, b, b_at, o, o_at, *third) in enumerate(pieces([where_ref[0], where_ref[1], where_ref[2]])):
+                loads.append([pltpu.make_async_copy(ins[a].at[a_at], k_ref.at[i], k_sem.at[i])])
+                loads[-1].append(pltpu.make_async_copy(ins[b].at[b_at], g_ref.at[i], g_sem.at[i]))
+                if third:
+                    loads[-1].append(pltpu.make_async_copy(ins[third[0]].at[third[1]], h_ref.at[i], h_sem.at[i]))
                 stores.append(pltpu.make_async_copy(k_ref.at[i], outs[o].at[o_at], o_sem.at[i]))
-                sums.append((k_ref, g_ref, i))
+                sums.append((k_ref, g_ref, h_ref if third else None, i))
             ins = ins[len(group_in) :]
             if n + 1 < len(groups) and groups[n + 1][1]:
                 outs = outs[len(group_out) :]
-        for load in loads:
-            load.start()
-        for i, (k_ref, g_ref, at) in enumerate(sums):
-            loads[2 * i].wait()
-            loads[2 * i + 1].wait()
-            k_ref[at] = k_ref[at] + g_ref[at]
+        for copies in loads:
+            for copy in copies:
+                copy.start()
+        for i, (k_ref, g_ref, h_ref, at) in enumerate(sums):
+            for copy in loads[i]:
+                copy.wait()
+            value = k_ref[at] + g_ref[at]
+            k_ref[at] = value if h_ref is None else value + h_ref[at]
             stores[i].start()
         for store in stores:
             store.wait()
 
     scratch_shapes = []
-    for (_, _, _, shape), count in zip(groups, counts):
-        scratch_shapes += [pltpu.VMEM((count,) + shape, BF)] * 2 + [pltpu.SemaphoreType.DMA((count,))] * 3
+    for (_, _, pieces, shape), count in zip(groups, counts):
+        third = count if len(pieces([jnp.int32(0)] * 3)[0]) > 6 else 1
+        scratch_shapes += [pltpu.VMEM((n,) + shape, BF) for n in (count, count, third)]
+        scratch_shapes += [pltpu.SemaphoreType.DMA((n,)) for n in (count, count, third, count)]
     result = pl.pallas_call(
         body,
         name=name,
@@ -820,32 +826,30 @@
     def pieces(at):
         _, y, x = at
         table = []
-        for role in (1, 0):
-            for z in range(4):
-                ax = x if role == 0 else 1 - x
-                ay = y if role == 0 else 1 - y
-                for half, index in ((0, (0, every, z, every, ax)), (1, (1, every, z, ay))):
-                    table.append((0, index, 1, index, 2 * half + (1 - role), (every, z)))
+        for z in range(4):
+            for half, index in ((0, (0, every, z, every, 1 - x)), (1, (1, every, z, 1 - y))):
+                table.append((0, index, 1, index, half, (every, z)))
         return table
 
-    return (keep, got), [(blocks, 4, 2, rows, lanes)] * 4, pieces, (blocks, 2, rows, lanes)
-
-
-def fold_second(parts, got):
-    blocks, _, _, rows, lanes = parts[1].shape
+    return (keep, got), [(blocks, 4, 2, rows, lanes)] * 2, pieces, (blocks, 2, rows, lanes)
+
+
+def fold_second(keep, got, arrived):
+    _, blocks, _, _, _, rows, lanes = keep.shape
     every = slice(None)
 
     def pieces(at):
         _, y, x = at
         table = []
         for role in (1, 0):
+            ax = x if role == 0 else 1 - x
+            ay = y if role == 0 else 1 - y
             for z in range(4):
-                for half, own in ((0, y), (1, x)):
-                    index = (every, z, own if role == 0 else 1 - own)
-                    table.append((2 * half, index, 2 * half + 1, index, 2 * half + (1 - role), (every, z)))
+                for half, index, inner in ((0, (0, every, z, ay, x), ay), (1, (1, every, z, y, ax), ax)):
+                    table.append((0, index, 1, index, 2 * half + (1 - role), (every, z), 2 + half, (every, z, inner)))
         return table
 
-    return (parts[1], got[0], parts[3], got[1]), [(blocks, 4, rows, lanes)] * 4, pieces, (blocks, rows, lanes)
+    return (keep, got, *arrived), [(blocks, 4, rows, lanes)] * 4, pieces, (blocks, rows, lanes)
 
 
 def fold_third(parts, got, joined=True):
@@ -966,24 +970,26 @@
             return value.reshape((2, value.shape[0] // 2, 4, 2, 2) + value.shape[2:])
 
         def cross(parts, bit_a, bit_b):
-            return flip(parts[0], bit_a), flip(parts[2], bit_b)
+            return flip(parts[0], bit_a), flip(parts[len(parts) // 2], bit_b)
 
         def along_z(parts):
             return lax.all_to_all(parts, "dp", 0, 0, axis_index_groups=[[i, i + 4, i + 8, i + 12] for i in range(4)], tiled=True)
 
         keep_b, send_b, keep_i, send_i = grads
         got_b = swap(send_b)
-        (back,) = add_pieces(where, [fold_first(view(keep_b), view(got_b))], "fold_a")
+        base_b = view(keep_b), view(got_b)
+        (back,) = add_pieces(where, [fold_first(*base_b)], "fold_a")
         dmixed, back, send_i, output_other = sync(dmixed, back, send_i, output_other)
         got_b = cross(back, 1, 2)
         got_i = swap(send_i)
         output_got = swap(output_other)
         dproj, *bias_a = attention_grad(qkv, probs, mixed, dmixed, 0, 1)
         dproj, got_i, keep_i, output_got = sync(dproj, got_i, keep_i, output_got)
-        (inner,) = add_pieces(where, [fold_first(view(keep_i), view(got_i))], "fold_b")
+        base_i = view(keep_i), view(got_i)
+        (inner,) = add_pieces(where, [fold_first(*base_i)], "fold_b")
         inner, got_b = sync(inner, got_b)
         got_i = cross(inner, 1, 2)
-        (back,) = add_pieces(where, [fold_second(back, got_b)], "fold_b2")
+        (back,) = add_pieces(where, [fold_second(*base_b, got_b)], "fold_b2")
         dmixed, back = sync(dmixed, back)
         got_b = cross(back, 2, 1)
         dproj, *bias_b = attention_grad(qkv, probs, mixed, dmixed, 1, 1, dproj)
@@ -993,11 +999,12 @@
         )
         send_q, keep_q, got_b, got_i = sync(send_q, keep_q, got_b, got_i)
         got_q = swap(send_q)
-        (inner,) = add_pieces(where, [fold_second(inner, got_i)], "fold_c")
+        (inner,) = add_pieces(where, [fold_second(*base_i, got_i)], "fold_c")
         inner, got_q, keep_q, cls_own = sync(inner, got_q, keep_q, cls_own)
         got_i = cross(inner, 2, 1)
         cls_got = swap(cls_own)
-        (proj,) = add_pieces(where, [fold_first(view(keep_q), view(got_q))], "fold_d")
+        base_q = view(keep_q), view(got_q)
+        (proj,) = add_pieces(where, [fold_first(*base_q)], "fold_d")
         proj, got_i, cls_got = sync(proj, got_i, cls_got)
         got_q = cross(proj, 1, 2)
         split = back[1].shape[0]
@@ -1006,7 +1013,7 @@
         got_i = along_z(joint)
         dinput, dinput_other = input_grad_call(core_one, dproj.reshape(3, total, width), dpre1, w_qkv, half)
         dinput, dinput_other, got_q, output = sync(dinput, dinput_other, got_q, output)
-        (proj,) = add_pieces(where, [fold_second(proj, got_q)], "fold_f")
+        (proj,) = add_pieces(where, [fold_second(*base_q, got_q)], "fold_f")
         proj, dinput_other, output = sync(proj, dinput_other, output)
         got_q = cross(proj, 2, 1)
         dinput_got = swap(dinput_other)

time: 216 us -> 214 us (level)
  Pallas kernels: 157 us -> 154 us
    pallas_call x8, Pallas kernels: 31.2 us -> 28.7 us  [add_pieces(): pl.pallas_call(body, name=name, out_shape=[jax.ShapeDtypeStruct(s, BF) fo...]
  transfers between devices with their start and end apart: 24 -> 24, of which waited for: 10 -> 9; matrix products, arithmetic and copies ran while one was open for 3% -> 3% of each run, Pallas kernels for 43% -> 43%
where the time goes in v7:
time: 214 us; the launch traced here: 213 us
  Pallas kernels  154 us (72%)
  starting transfers between devices  25.5 us (12%)
  waiting for transfers between devices  23.5 us (11%)
  local copies, waits for them, and re-layouts  7.88 us (4%)
    pallas_call x1, Pallas kernels, feed_call(): pl.pallas_call(partial(feed_kernel, split), name='feed_rows', out_shape=s...  54.2 us
    pallas_call x8, Pallas kernels, add_pieces(): pl.pallas_call(body, name=name, out_shape=[jax.ShapeDtypeStruct(s, BF) fo...  28.7 us
    pallas_call x1, Pallas kernels, attention_call(): pl.pallas_call(attention_kernel, name='attention_rows', out_shape=[row(3...  27.7 us
    pallas_call x2, Pallas kernels, attention_grad(): pl.pallas_call(body, name='attention_grad', out_shape=[jax.ShapeDtypeStru...  21.5 us
    ppermute x15, starting transfers between devices, flip(): return lax.ppermute(value, 'dp', [(i, i ^ bits) for i in range(16)])  18.7 us
    ppermute x15, waiting for transfers between devices, flip(): return lax.ppermute(value, 'dp', [(i, i ^ bits) for i in range(16)])  18 us
    pallas_call x1, Pallas kernels, grad_proj(): pl.pallas_call(body, name='grad_qkv', out_shape=[out, out], grid_spec=plt...  8.36 us
    pallas_call x1, Pallas kernels, input_grad_call(): pl.pallas_call(body, name='input_grad', out_shape=[jax.ShapeDtypeStruct((...  7.98 us
  transfers between devices with their start and end apart: 24, of which 9 were waited for; matrix products, arithmetic and copies ran while one was open for 3% of the time, Pallas kernels for 43%

profile of v7, /device:TPU:0, one launch (start us, length us, event | category | flops | bytes accessed | tf_op | source)
XLA Modules:
  0.0 212.8 jit_solution(13969756642585606059)
XLA Ops:
  5.3 27.7 %attention_rows.1 = (bf16[2,512,2304]{2,1,0:T(8,128)(2,1)}, bf16[2,6,2,512,512]{4,3,2,1,0:T(8,128)(2,1)}, bf16[2,512,768]{2,1,0:T(8,128)(2,1)}, bf16[2,512,768]{...) custom-call(s32[1]{0:T(128)} %bitcast.3.core_ref, ...), custom_call_target="tpu_custom_call" | custom-call | flops 6442450944 | bytes 36700160 | tf_op jit(solution)/shard_map/attention_rows/pallas_call | solution.py:174
  33.9 54.2 %feed_rows.1 = (bf16[4,256,768]{2,1,0:T(8,128)(2,1)}, bf16[2,256,768]{2,1,0:T(8,128)(2,1)}, bf16[2,8,768]{2,1,0:T(8,128)(2,1)}, bf16[1024,768]{1,0:T(8,128)(2,1)...) custom-call(s32[1]{0:T(128)} %bitcast.3.core_ref, ...), custom_call_target="tpu_custom_call" | custom-call | flops 31406948352 | bytes 41943040 | tf_op jit(solution)/shard_map/feed_rows/pallas_call | solution.py:426
  89.0 4.0 %collective-permute-done.2 = bf16[8,16,24,384]{3,2,1,0:T(8,128)(2,1)} collective-permute-done((bf16[8,16,24,384]{3,2,1,0:T(8,128)(2,1)}, bf16[8,16,24,384]{3,2,1,0:T(8,128)(2,1)}, u32[]{:S(2)}, u32[]{:S(2)}) %collective-permute-start.2) | collective-permute-done | bytes 2359328 | tf_op jit(solution)/shard_map/ppermute | solution.py:626
  93.0 3.3 %fold_a.1 = (bf16[4,4,2,24,384]{4,3,2,1,0:T(8,128)(2,1)}, bf16[4,4,2,24,384]{4,3,2,1,0:T(8,128)(2,1)}) custom-call(s32[3]{0:T(128)} %pad_add_fusion.where_ref, bf16[2,4,4,2,2,24,384]{6,5,4,3,2,1,0:T(8,128)(2,1)} %bitcast.28, bf16[2,4,4,2,2,24,384]{6,5,4,3,2,1,0:T(8,128)(2,1)} %bitcast.12.refs_1_), custom_call_target="tpu_custom_call" | custom-call | tf_op jit(solution)/shard_map/fold_a/pallas_call | solution.py:802
  96.9 2.9 %collective-permute-start.5 = (bf16[4,4,2,24,384]{4,3,2,1,0:T(8,128)(2,1)}, bf16[4,4,2,24,384]{4,3,2,1,0:T(8,128)(2,1)}, u32[]{:S(2)}, u32[]{:S(2)}) collective-permute-start(bf16[4,4,2,24,384]{4,3,2,1,0:T(8,128)(2,1)} %get-tuple-element.153), channel_id=1, source_target_pairs={{0,2},{2,0},{4,6},{6,4},{8,10},{10,8},{12,14},{14,12},{16,18},{18,... | collective-permute-start | bytes 1769480 | tf_op jit(solution)/shard_map/ppermute | solution.py:931
  101.2 10.7 %attention_grad.2 = (bf16[3,2,512,768]{3,2,1,0:T(8,128)(2,1)}, f32[1,768]{1,0:T(1,128)}, f32[1,768]{1,0:T(1,128)}) custom-call(bf16[2,512,2304]{2,1,0:T(8,128)(2,1)} %get-tuple-element.129.q_ref.k_ref.v_ref, bf16[2,512,2304]{2,1,0:T(8,128)(2,1)} %get-tuple-element.129.q_ref.k_ref.v_ref, bf16[2,512,2304]{2,1,0:T(8,128)(2,1)} %get-tuple-element.129.q_ref.k_ref.v_ref, ...), custom_call_target="tpu_custom_call" | custom-call | flops 1610612736 | bytes 15728640 | tf_op jit(solution)/shard_map/attention_grad/pallas_call | solution.py:531
  112.0 3.5 %fold_b.1 = (bf16[5,4,2,24,384]{4,3,2,1,0:T(8,128)(2,1)}, bf16[5,4,2,24,384]{4,3,2,1,0:T(8,128)(2,1)}) custom-call(s32[3]{0:T(128)} %pad_add_fusion.where_ref, bf16[2,5,4,2,2,24,384]{6,5,4,3,2,1,0:T(8,128)(2,1)} %bitcast.26, bf16[2,5,4,2,2,24,384]{6,5,4,3,2,1,0:T(8,128)(2,1)} %bitcast.14.refs_1_), custom_call_target="tpu_custom_call" | custom-call | tf_op jit(solution)/shard_map/fold_b/pallas_call | solution.py:802
  117.2 4.0 %fold_b2.1 = (bf16[4,4,24,384]{3,2,1,0:T(8,128)(2,1)}, bf16[4,4,24,384]{3,2,1,0:T(8,128)(2,1)}, bf16[4,4,24,384]{3,2,1,0:T(8,128)(2,1)}, bf16[4,4,24,384]{3,2,1,0:T(8,128)(2,1)}) custom-call(s32[3]{0:T(128)} %pad_add_fusion.where_ref, bf16[2,4,4,2,2,24,384]{6,5,4,3,2,1,0:T(8,128)(2,1)} %bitcast.29, bf16[2,4,4,2,2,24,384]{6,5,4,3,2,1,0:T(8,128)(2,1)} %bitcast.12.refs_1_, ...), custom_call_target="tpu_custom_call" | custom-call | tf_op jit(solution)/shard_map/fold_b2/pallas_call | solution.py:802
  123.7 10.7 %attention_grad.3 = (bf16[3,2,512,768]{3,2,1,0:T(8,128)(2,1)}, f32[1,768]{1,0:T(1,128)}, f32[1,768]{1,0:T(1,128)}) custom-call(bf16[2,512,2304]{2,1,0:T(8,128)(2,1)} %get-tuple-element.129.q_ref.k_ref.v_ref, bf16[2,512,2304]{2,1,0:T(8,128)(2,1)} %get-tuple-element.129.q_ref.k_ref.v_ref, ...), custom_call_target="tpu_custom_call", output_to_operand_aliasing={{0}: (6, {})} | custom-call | flops 1610612736 | bytes 15728640 | tf_op jit(solution)/shard_map/attention_grad/pallas_call | solution.py:531
  134.4 8.4 %grad_qkv.1 = (bf16[20,16,8,384]{3,2,1,0:T(8,128)(2,1)}, bf16[20,16,8,384]{3,2,1,0:T(8,128)(2,1)}) custom-call(s32[1]{0:T(128)} %bitcast.3.core_ref, bf16[1024,768]{1,0:T(8,128)(2,1)} %bitcast.46, bf16[3,1024,768]{2,1,0:T(8,128)(2,1)} %bitcast.35, f32[1,768]{1,0:T(1,128)} %get-tuple-element.164.refs_0_, f32[1,768]{1,0:T(1,128)} %get-tuple-element.165.refs_1_, ...), custom_call_target="tpu_custom_call" | custom-call | flops 3623878656 | bytes 8257536 | tf_op jit(solution)/shard_map/grad_qkv/pallas_call | solution.py:747
  143.0 4.5 %fold_c.1 = (bf16[5,4,24,384]{3,2,1,0:T(8,128)(2,1)}, bf16[5,4,24,384]{3,2,1,0:T(8,128)(2,1)}, bf16[5,4,24,384]{3,2,1,0:T(8,128)(2,1)}, bf16[5,4,24,384]{3,2,1,0:T(8,128)(2,1)}) custom-call(s32[3]{0:T(128)} %pad_add_fusion.where_ref, bf16[2,5,4,2,2,24,384]{6,5,4,3,2,1,0:T(8,128)(2,1)} %bitcast.27, bf16[2,5,4,2,2,24,384]{6,5,4,3,2,1,0:T(8,128)(2,1)} %bitcast.14.refs_1_, ...), custom_call_target="tpu_custom_call" | custom-call | tf_op jit(solution)/shard_map/fold_c/pallas_call | solution.py:802
  149.1 3.2 %fold_d.1 = (bf16[10,4,2,8,384]{4,3,2,1,0:T(8,128)(2,1)}, bf16[10,4,2,8,384]{4,3,2,1,0:T(8,128)(2,1)}) custom-call(s32[3]{0:T(128)} %pad_add_fusion.where_ref, bf16[2,10,4,2,2,8,384]{6,5,4,3,2,1,0:T(8,128)(2,1)} %bitcast.30, bf16[2,10,4,2,2,8,384]{6,5,4,3,2,1,0:T(8,128)(2,1)} %bitcast.18.refs_1_), custom_call_target="tpu_custom_call" | custom-call | tf_op jit(solution)/shard_map/fold_d/pallas_call | solution.py:802
  152.3 6.5 %collective-permute-done.12.refs_5_ = bf16[5,4,24,384]{3,2,1,0:T(8,128)(2,1)} collective-permute-done((bf16[5,4,24,384]{3,2,1,0:T(8,128)(2,1)}, bf16[5,4,24,384]{3,2,1,0:T(8,128)(2,1)}, u32[]{:S(2)}, u32[]{:S(2)}) %collective-permute-start.12) | collective-permute-done | bytes 368672 | tf_op jit(solution)/shard_map/ppermute | solution.py:931
  159.6 3.8 %fold_e.1 = bf16[4,2,9,24,384]{4,3,2,1,0:T(8,128)(2,1)} custom-call(s32[3]{0:T(128)} %pad_add_fusion.where_ref, bf16[4,4,24,384]{3,2,1,0:T(8,128)(2,1)} %get-tuple-element.192.refs_0_, bf16[4,4,24,384]{3,2,1,0:T(8,128)(2,1)} %collective-permute-done.7.refs_1_, bf16[4,4,24,384]{3,2,1,0:T(8,128)(2,1)} %get-tuple-element.194.refs_2_, ...), custom_call_target="tpu_custom_call" | custom-call | tf_op jit(solution)/shard_map/fold_e/pallas_call | solution.py:802
  163.4 4.9 %all-to-all-start = ((bf16[4,2,9,24,384]{4,3,2,1,0:T(8,128)(2,1)}), bf16[4,2,9,24,384]{4,3,2,1,0:T(8,128)(2,1)}, u32[]{:S(2)}, u32[]{:S(2)}) async-start(bf16[4,2,9,24,384]{4,3,2,1,0:T(8,128)(2,1)} %fold_e.1), calls=%async_computation | async-start | bytes 2654208 | tf_op jit(solution)/shard_map/all_to_all | solution.py:976
  169.7 8.0 %input_grad.1 = (bf16[4,256,768]{2,1,0:T(8,128)(2,1)}, bf16[2,256,768]{2,1,0:T(8,128)(2,1)}) custom-call(s32[1]{0:T(128)} %bitcast.3.core_ref, bf16[3,1024,768]{2,1,0:T(8,128)(2,1)} %bitcast.36, bf16[1024,768]{1,0:T(8,128)(2,1)} %get-tuple-element.206.d_hbm, bf16[768,2304]{1,0:T(8,128)(2,1)} %w_ref.1), custom_call_target="tpu_custom_call" | custom-call | flops 3623878656 | bytes 10485760 | tf_op jit(solution)/shard_map/input_grad/pallas_call | solution.py:584
  177.7 3.1 %collective-permute-done.15.refs_2_ = bf16[10,4,2,8,384]{4,3,2,1,0:T(8,128)(2,1)} collective-permute-done((bf16[10,4,2,8,384]{4,3,2,1,0:T(8,128)(2,1)}, bf16[10,4,2,8,384]{4,3,2,1,0:T(8,128)(2,1)}, u32[]{:S(2)}, u32[]{:S(2)}) %collective-permute-start.15) | collective-permute-done | bytes 491552 | tf_op jit(solution)/shard_map/ppermute | solution.py:931
  181.1 3.8 %fold_f.1 = (bf16[10,4,8,384]{3,2,1,0:T(8,128)(2,1)}, bf16[10,4,8,384]{3,2,1,0:T(8,128)(2,1)}, bf16[10,4,8,384]{3,2,1,0:T(8,128)(2,1)}, bf16[10,4,8,384]{3,2,1,0:T(8,128)(2,1)}) custom-call(s32[3]{0:T(128)} %pad_add_fusion.where_ref, bf16[2,10,4,2,2,8,384]{6,5,4,3,2,1,0:T(8,128)(2,1)} %bitcast.31, bf16[2,10,4,2,2,8,384]{6,5,4,3,2,1,0:T(8,128)(2,1)} %bitcast.18.refs_1_, ...), custom_call_target="tpu_custom_call" | custom-call | tf_op jit(solution)/shard_map/fold_f/pallas_call | solution.py:802
  190.2 3.5 %collective-permute-done.17.refs_1_ = bf16[10,4,8,384]{3,2,1,0:T(8,128)(2,1)} collective-permute-done((bf16[10,4,8,384]{3,2,1,0:T(8,128)(2,1)}, bf16[10,4,8,384]{3,2,1,0:T(8,128)(2,1)}, u32[]{:S(2)}, u32[]{:S(2)}) %collective-permute-start.17) | collective-permute-done | bytes 245792 | tf_op jit(solution)/shard_map/ppermute | solution.py:931
  194.3 2.7 %fold_g.1 = (bf16[2,10,8,384]{3,2,1,0:T(8,128)(2,1)}, bf16[2,10,8,384]{3,2,1,0:T(8,128)(2,1)}, bf16[2,10,8,384]{3,2,1,0:T(8,128)(2,1)}, bf16[2,10,8,384]{3,2,1,0:T(8,128)(2,1)}) custom-call(s32[3]{0:T(128)} %pad_add_fusion.where_ref, bf16[10,4,8,384]{3,2,1,0:T(8,128)(2,1)} %get-tuple-element.229.refs_0_, ...), custom_call_target="tpu_custom_call" | custom-call | tf_op jit(solution)/shard_map/fold_g/pallas_call | solution.py:802
  198.9 2.4 %collective-permute-start.21 = (bf16[2,10,8,384]{3,2,1,0:T(8,128)(2,1)}, bf16[2,10,8,384]{3,2,1,0:T(8,128)(2,1)}, u32[]{:S(2)}, u32[]{:S(2)}) collective-permute-start(bf16[2,10,8,384]{3,2,1,0:T(8,128)(2,1)} %get-tuple-element.235), channel_id=1, source_target_pairs={{0,16},{2,18},{4,20},{6,22},{8,24},{10,26},{12,28},{14,30},{16,0},... | collective-permute-start | bytes 368648 | tf_op jit(solution)/shard_map/ppermute | solution.py:931
  203.6 2.1 back_sum.1
  205.7 2.1 inner_sum.1
  207.8 3.2 %collective-permute-done.21.refs_2_ = bf16[2,10,8,384]{3,2,1,0:T(8,128)(2,1)} collective-permute-done((bf16[2,10,8,384]{3,2,1,0:T(8,128)(2,1)}, bf16[2,10,8,384]{3,2,1,0:T(8,128)(2,1)}, u32[]{:S(2)}, u32[]{:S(2)}) %collective-permute-start.21) | collective-permute-done | bytes 122912 | tf_op jit(solution)/shard_map/ppermute | solution.py:931
  (56 shorter events, 29.0 us)
Async XLA Ops:
  2.0 2.4 %collective-permute-start = (bf16[2,256,768]{2,1,0:T(8,128)(2,1)S(1)}, bf16[2,256,768]{2,1,0:T(8,128)(2,1)S(1)}, u32[]{:S(2)}, u32[]{:S(2)}) collective-permute-start(bf16[2,256,768]{2,1,0:T(8,128)(2,1)S(1)} %constant_dynamic-slice_fusion.1), channel_id=1, source_target_pairs={{0,1},{1,0},{2,3},{3,2},{4,5},{5,4},{6,7},{7,6},{8,9},{9,8},{10,11... | collective-permute-start | bytes 2359304 | tf_op jit(solution)/shard_map/ppermute | solution.py:626
  2.5 30.4 %collective-permute-start.1 = (bf16[2,256,768]{2,1,0:T(8,128)(2,1)S(1)}, bf16[2,256,768]{2,1,0:T(8,128)(2,1)S(1)}, u32[]{:S(2)}, u32[]{:S(2)}) collective-permute-start(bf16[2,256,768]{2,1,0:T(8,128)(2,1)S(1)} %constant_dynamic-slice_fusion), channel_id=1, source_target_pairs={{0,1},{1,0},{2,3},{3,2},{4,5},{5,4},{6,7},{7,6},{8,9},{9,8},{10,11... | collective-permute-start | bytes 2359304 | tf_op jit(solution)/shard_map/ppermute | solution.py:626
  88.1 4.9 %collective-permute-start.2 = (bf16[8,16,24,384]{3,2,1,0:T(8,128)(2,1)}, bf16[8,16,24,384]{3,2,1,0:T(8,128)(2,1)}, u32[]{:S(2)}, u32[]{:S(2)}) collective-permute-start(bf16[8,16,24,384]{3,2,1,0:T(8,128)(2,1)} %get-tuple-element.138), channel_id=1, source_target_pairs={{0,1},{1,0},{2,3},{3,2},{4,5},{5,4},{6,7},{7,6},{8,9},{9,8},{10,11... | collective-permute-start | bytes 7077896 | tf_op jit(solution)/shard_map/ppermute | solution.py:626
  96.3 15.7 %collective-permute-start.3 = (bf16[10,16,24,384]{3,2,1,0:T(8,128)(2,1)}, bf16[10,16,24,384]{3,2,1,0:T(8,128)(2,1)}, u32[]{:S(2)}, u32[]{:S(2)}) collective-permute-start(bf16[10,16,24,384]{3,2,1,0:T(8,128)(2,1)} %get-tuple-element.145), channel_id=1, source_target_pairs={{0,1},{1,0},{2,3},{3,2},{4,5},{5,4},{6,7},{7,6},{8,9},{9,8},{10,11... | collective-permute-start | bytes 8847368 | tf_op jit(solution)/shard_map/ppermute | solution.py:626
  96.7 15.3 %collective-permute-start.4 = (bf16[2,256,768]{2,1,0:T(8,128)(2,1)}, bf16[2,256,768]{2,1,0:T(8,128)(2,1)}, u32[]{:S(2)}, u32[]{:S(2)}) collective-permute-start(bf16[2,256,768]{2,1,0:T(8,128)(2,1)} %get-tuple-element.147), channel_id=1, source_target_pairs={{0,1},{1,0},{2,3},{3,2},{4,5},{5,4},{6,7},{7,6},{8,9},{9,8},{10,11... | collective-permute-start | bytes 2359304 | tf_op jit(solution)/shard_map/ppermute | solution.py:626
  96.9 18.6 %collective-permute-start.5 = (bf16[4,4,2,24,384]{4,3,2,1,0:T(8,128)(2,1)}, bf16[4,4,2,24,384]{4,3,2,1,0:T(8,128)(2,1)}, u32[]{:S(2)}, u32[]{:S(2)}) collective-permute-start(bf16[4,4,2,24,384]{4,3,2,1,0:T(8,128)(2,1)} %get-tuple-element.153), channel_id=1, source_target_pairs={{0,2},{2,0},{4,6},{6,4},{8,10},{10,8},{12,14},{14,12},{16,18},{18,... | collective-permute-start | bytes 1769480 | tf_op jit(solution)/shard_map/ppermute | solution.py:931
  99.7 15.8 %collective-permute-start.6 = (bf16[4,4,2,24,384]{4,3,2,1,0:T(8,128)(2,1)}, bf16[4,4,2,24,384]{4,3,2,1,0:T(8,128)(2,1)}, u32[]{:S(2)}, u32[]{:S(2)}) collective-permute-start(bf16[4,4,2,24,384]{4,3,2,1,0:T(8,128)(2,1)} %get-tuple-element.154), channel_id=1, source_target_pairs={{0,4},{2,6},{4,0},{6,2},{8,12},{10,14},{12,8},{14,10},{16,20},{18,... | collective-permute-start | bytes 1769480 | tf_op jit(solution)/shard_map/ppermute | solution.py:931
  115.5 27.3 %collective-permute-start.9 = (bf16[5,4,2,24,384]{4,3,2,1,0:T(8,128)(2,1)}, bf16[5,4,2,24,384]{4,3,2,1,0:T(8,128)(2,1)}, u32[]{:S(2)}, u32[]{:S(2)}) collective-permute-start(bf16[5,4,2,24,384]{4,3,2,1,0:T(8,128)(2,1)} %get-tuple-element.179), channel_id=1, source_target_pairs={{0,2},{2,0},{4,6},{6,4},{8,10},{10,8},{12,14},{14,12},{16,18},{18,... | collective-permute-start | bytes 2211848 | tf_op jit(solution)/shard_map/ppermute | solution.py:931
  116.1 26.8 %collective-permute-start.10 = (bf16[5,4,2,24,384]{4,3,2,1,0:T(8,128)(2,1)}, bf16[5,4,2,24,384]{4,3,2,1,0:T(8,128)(2,1)}, u32[]{:S(2)}, u32[]{:S(2)}) collective-permute-start(bf16[5,4,2,24,384]{4,3,2,1,0:T(8,128)(2,1)} %get-tuple-element.180), channel_id=1, source_target_pairs={{0,4},{2,6},{4,0},{6,2},{8,12},{10,14},{12,8},{14,10},{16,20},{18,... | collective-permute-start | bytes 2211848 | tf_op jit(solution)/shard_map/ppermute | solution.py:931
  121.2 21.6 %collective-permute-start.7 = (bf16[4,4,24,384]{3,2,1,0:T(8,128)(2,1)}, bf16[4,4,24,384]{3,2,1,0:T(8,128)(2,1)}, u32[]{:S(2)}, u32[]{:S(2)}) collective-permute-start(bf16[4,4,24,384]{3,2,1,0:T(8,128)(2,1)} %get-tuple-element.177), channel_id=1, source_target_pairs={{0,4},{2,6},{4,0},{6,2},{8,12},{10,14},{12,8},{14,10},{16,20},{18,... | collective-permute-start | bytes 884744 | tf_op jit(solution)/shard_map/ppermute | solution.py:931
  122.2 20.6 %collective-permute-start.8 = (bf16[4,4,24,384]{3,2,1,0:T(8,128)(2,1)}, bf16[4,4,24,384]{3,2,1,0:T(8,128)(2,1)}, u32[]{:S(2)}, u32[]{:S(2)}) collective-permute-start(bf16[4,4,24,384]{3,2,1,0:T(8,128)(2,1)} %get-tuple-element.178), channel_id=1, source_target_pairs={{0,2},{2,0},{4,6},{6,4},{8,10},{10,8},{12,14},{14,12},{16,18},{18,... | collective-permute-start | bytes 884744 | tf_op jit(solution)/shard_map/ppermute | solution.py:931
  142.9 4.5 %collective-permute-start.11 = (bf16[20,16,8,384]{3,2,1,0:T(8,128)(2,1)}, bf16[20,16,8,384]{3,2,1,0:T(8,128)(2,1)}, u32[]{:S(2)}, u32[]{:S(2)}) collective-permute-start(bf16[20,16,8,384]{3,2,1,0:T(8,128)(2,1)} %get-tuple-element.187), channel_id=1, source_target_pairs={{0,1},{1,0},{2,3},{3,2},{4,5},{5,4},{6,7},{7,6},{8,9},{9,8},{10,11... | collective-permute-start | bytes 5898248 | tf_op jit(solution)/shard_map/ppermute | solution.py:626
  147.4 11.4 %collective-permute-start.12 = (bf16[5,4,24,384]{3,2,1,0:T(8,128)(2,1)}, bf16[5,4,24,384]{3,2,1,0:T(8,128)(2,1)}, u32[]{:S(2)}, u32[]{:S(2)}) collective-permute-start(bf16[5,4,24,384]{3,2,1,0:T(8,128)(2,1)} %get-tuple-element.199), channel_id=1, source_target_pairs={{0,4},{2,6},{4,0},{6,2},{8,12},{10,14},{12,8},{14,10},{16,20},{18,... | collective-permute-start | bytes 1105928 | tf_op jit(solution)/shard_map/ppermute | solution.py:931
  148.6 11.0 %collective-permute-start.13 = (bf16[5,4,24,384]{3,2,1,0:T(8,128)(2,1)}, bf16[5,4,24,384]{3,2,1,0:T(8,128)(2,1)}, u32[]{:S(2)}, u32[]{:S(2)}) collective-permute-start(bf16[5,4,24,384]{3,2,1,0:T(8,128)(2,1)} %get-tuple-element.200), channel_id=1, source_target_pairs={{0,2},{2,0},{4,6},{6,4},{8,10},{10,8},{12,14},{14,12},{16,18},{18,... | collective-permute-start | bytes 1105928 | tf_op jit(solution)/shard_map/ppermute | solution.py:931
  149.1 3.2 %collective-permute-start.14 = (bf16[2,6,768]{2,1,0:T(8,128)(2,1)S(1)}, bf16[2,6,768]{2,1,0:T(8,128)(2,1)S(1)}, u32[]{:S(2)}, u32[]{:S(2)}) collective-permute-start(bf16[2,6,768]{2,1,0:T(8,128)(2,1)S(1)} %bitcast.38), channel_id=1, source_target_pairs={{0,1},{1,0},{2,3},{3,2},{4,5},{5,4},{6,7},{7,6},{8,9},{9,8},{10,11... | collective-permute-start | bytes 55304 | tf_op jit(solution)/shard_map/ppermute | solution.py:626
  163.4 40.2 %all-to-all-start = ((bf16[4,2,9,24,384]{4,3,2,1,0:T(8,128)(2,1)}), bf16[4,2,9,24,384]{4,3,2,1,0:T(8,128)(2,1)}, u32[]{:S(2)}, u32[]{:S(2)}) async-start(bf16[4,2,9,24,384]{4,3,2,1,0:T(8,128)(2,1)} %fold_e.1), calls=%async_computation | async-start | bytes 2654208 | tf_op jit(solution)/shard_map/all_to_all | solution.py:976
  168.3 12.6 %collective-permute-start.15 = (bf16[10,4,2,8,384]{4,3,2,1,0:T(8,128)(2,1)}, bf16[10,4,2,8,384]{4,3,2,1,0:T(8,128)(2,1)}, u32[]{:S(2)}, u32[]{:S(2)}) collective-permute-start(bf16[10,4,2,8,384]{4,3,2,1,0:T(8,128)(2,1)} %get-tuple-element.209), channel_id=1, source_target_pairs={{0,2},{2,0},{4,6},{6,4},{8,10},{10,8},{12,14},{14,12},{16,18},{18,... | collective-permute-start | bytes 1474568 | tf_op jit(solution)/shard_map/ppermute | solution.py:931
  168.8 12.3 %collective-permute-start.16 = (bf16[10,4,2,8,384]{4,3,2,1,0:T(8,128)(2,1)}, bf16[10,4,2,8,384]{4,3,2,1,0:T(8,128)(2,1)}, u32[]{:S(2)}, u32[]{:S(2)}) collective-permute-start(bf16[10,4,2,8,384]{4,3,2,1,0:T(8,128)(2,1)} %get-tuple-element.210), channel_id=1, source_target_pairs={{0,4},{2,6},{4,0},{6,2},{8,12},{10,14},{12,8},{14,10},{16,20},{18,... | collective-permute-start | bytes 1474568 | tf_op jit(solution)/shard_map/ppermute | solution.py:931
  184.9 9.4 %collective-permute-start.19 = (bf16[2,256,768]{2,1,0:T(8,128)(2,1)}, bf16[2,256,768]{2,1,0:T(8,128)(2,1)}, u32[]{:S(2)}, u32[]{:S(2)}) collective-permute-start(bf16[2,256,768]{2,1,0:T(8,128)(2,1)} %get-tuple-element.224), channel_id=1, source_target_pairs={{0,1},{1,0},{2,3},{3,2},{4,5},{5,4},{6,7},{7,6},{8,9},{9,8},{10,11... | collective-permute-start | bytes 2359304 | tf_op jit(solution)/shard_map/ppermute | solution.py:626
  184.9 8.7 %collective-permute-start.17 = (bf16[10,4,8,384]{3,2,1,0:T(8,128)(2,1)}, bf16[10,4,8,384]{3,2,1,0:T(8,128)(2,1)}, u32[]{:S(2)}, u32[]{:S(2)}) collective-permute-start(bf16[10,4,8,384]{3,2,1,0:T(8,128)(2,1)} %get-tuple-element.222), channel_id=1, source_target_pairs={{0,4},{2,6},{4,0},{6,2},{8,12},{10,14},{12,8},{14,10},{16,20},{18,... | collective-permute-start | bytes 737288 | tf_op jit(solution)/shard_map/ppermute | solution.py:931
  186.0 8.3 %collective-permute-start.18 = (bf16[10,4,8,384]{3,2,1,0:T(8,128)(2,1)}, bf16[10,4,8,384]{3,2,1,0:T(8,128)(2,1)}, u32[]{:S(2)}, u32[]{:S(2)}) collective-permute-start(bf16[10,4,8,384]{3,2,1,0:T(8,128)(2,1)} %get-tuple-element.223), channel_id=1, source_target_pairs={{0,2},{2,0},{4,6},{6,4},{8,10},{10,8},{12,14},{14,12},{16,18},{18,... | collective-permute-start | bytes 737288 | tf_op jit(solution)/shard_map/ppermute | solution.py:931
  197.0 10.7 %collective-permute-start.20 = (bf16[2,10,8,384]{3,2,1,0:T(8,128)(2,1)}, bf16[2,10,8,384]{3,2,1,0:T(8,128)(2,1)}, u32[]{:S(2)}, u32[]{:S(2)}) collective-permute-start(bf16[2,10,8,384]{3,2,1,0:T(8,128)(2,1)} %get-tuple-element.234), channel_id=1, source_target_pairs={{0,8},{2,10},{4,12},{6,14},{8,0},{10,2},{12,4},{14,6},{16,24},{18,... | collective-permute-start | bytes 368648 | tf_op jit(solution)/shard_map/ppermute | solution.py:931
  198.9 12.1 %collective-permute-start.21 = (bf16[2,10,8,384]{3,2,1,0:T(8,128)(2,1)}, bf16[2,10,8,384]{3,2,1,0:T(8,128)(2,1)}, u32[]{:S(2)}, u32[]{:S(2)}) collective-permute-start(bf16[2,10,8,384]{3,2,1,0:T(8,128)(2,1)} %get-tuple-element.235), channel_id=1, source_target_pairs={{0,16},{2,18},{4,20},{6,22},{8,24},{10,26},{12,28},{14,30},{16,0},... | collective-permute-start | bytes 368648 | tf_op jit(solution)/shard_map/ppermute | solution.py:931
  201.2 9.7 %collective-permute-start.22 = (bf16[2,10,8,384]{3,2,1,0:T(8,128)(2,1)}, bf16[2,10,8,384]{3,2,1,0:T(8,128)(2,1)}, u32[]{:S(2)}, u32[]{:S(2)}) collective-permute-start(bf16[2,10,8,384]{3,2,1,0:T(8,128)(2,1)} %get-tuple-element.236), channel_id=1, source_target_pairs={{0,24},{2,26},{4,28},{6,30},{8,16},{10,18},{12,20},{14,22},{16,8},... | collective-permute-start | bytes 368648 | tf_op jit(solution)/shard_map/ppermute | solution.py:931
  (4 other events, 9.9 us)

commit v8 on v7

--- a/solution.py
+++ b/solution.py
@@ -202,7 +202,7 @@
                 pltpu.SemaphoreType.DMA,
             ],
         ),
-        compiler_params=params(60),
+        compiler_params=params(62),
         cost_estimate=pl.CostEstimate(
             flops=8 * rows * length * width * width + 4 * rows * length * length * width,
             bytes_accessed=35 << 20,
@@ -457,7 +457,7 @@
                 pltpu.SemaphoreType.DMA((2,)),
             ],
         ),
-        compiler_params=params(60),
+        compiler_params=params(61),
         cost_estimate=pl.CostEstimate(flops=2 * total * width * (6 * hidden + 2 * width), bytes_accessed=40 << 20, transcendentals=2 * total * hidden),
     )(core, lengths, low, w_in, w_back, w_out, mixed, hat1, inv1, scale, cot, cot_other, *vectors)
 

time: 214 us -> 214 us (level)
  no operation moved by 1% of the time
where the time goes in v8:
time: 214 us; the launch traced here: 212 us
  Pallas kernels  155 us (72%)
  starting transfers between devices  25.6 us (12%)
  waiting for transfers between devices  23.3 us (11%)
  local copies, waits for them, and re-layouts  7 us (3%)
    pallas_call x1, Pallas kernels, feed_call(): pl.pallas_call(partial(feed_kernel, split), name='feed_rows', out_shape=s...  54.3 us
    pallas_call x8, Pallas kernels, add_pieces(): pl.pallas_call(body, name=name, out_shape=[jax.ShapeDtypeStruct(s, BF) fo...  28.8 us
    pallas_call x1, Pallas kernels, attention_call(): pl.pallas_call(attention_kernel, name='attention_rows', out_shape=[row(3...  27.7 us
    pallas_call x2, Pallas kernels, attention_grad(): pl.pallas_call(body, name='attention_grad', out_shape=[jax.ShapeDtypeStru...  21.6 us
    ppermute x15, starting transfers between devices, flip(): return lax.ppermute(value, 'dp', [(i, i ^ bits) for i in range(16)])  18.7 us
    ppermute x15, waiting for transfers between devices, flip(): return lax.ppermute(value, 'dp', [(i, i ^ bits) for i in range(16)])  17.9 us
    pallas_call x1, Pallas kernels, grad_proj(): pl.pallas_call(body, name='grad_qkv', out_shape=[out, out], grid_spec=plt...  8.37 us
    pallas_call x1, Pallas kernels, input_grad_call(): pl.pallas_call(body, name='input_grad', out_shape=[jax.ShapeDtypeStruct((...  7.98 us
  transfers between devices with their start and end apart: 24, of which 9 were waited for; matrix products, arithmetic and copies ran while one was open for 3% of the time, Pallas kernels for 43%

profile of v8, /device:TPU:0, one launch (start us, length us, event | category | flops | bytes accessed | tf_op | source)
XLA Modules:
  0.0 212.1 jit_solution(12547188692718029344)
XLA Ops:
  5.3 27.7 %attention_rows.1 = (bf16[2,512,2304]{2,1,0:T(8,128)(2,1)}, bf16[2,6,2,512,512]{4,3,2,1,0:T(8,128)(2,1)}, bf16[2,512,768]{2,1,0:T(8,128)(2,1)}, bf16[2,512,768]{...) custom-call(s32[1]{0:T(128)} %bitcast.3.core_ref, ...), custom_call_target="tpu_custom_call" | custom-call | flops 6442450944 | bytes 36700160 | tf_op jit(solution)/shard_map/attention_rows/pallas_call | solution.py:174
  33.0 54.3 %feed_rows.1 = (bf16[4,256,768]{2,1,0:T(8,128)(2,1)}, bf16[2,256,768]{2,1,0:T(8,128)(2,1)}, bf16[2,8,768]{2,1,0:T(8,128)(2,1)}, bf16[1024,768]{1,0:T(8,128)(2,1)...) custom-call(s32[1]{0:T(128)} %bitcast.3.core_ref, ...), custom_call_target="tpu_custom_call" | custom-call | flops 31406948352 | bytes 41943040 | tf_op jit(solution)/shard_map/feed_rows/pallas_call | solution.py:426
  88.4 3.9 %collective-permute-done.2 = bf16[8,16,24,384]{3,2,1,0:T(8,128)(2,1)} collective-permute-done((bf16[8,16,24,384]{3,2,1,0:T(8,128)(2,1)}, bf16[8,16,24,384]{3,2,1,0:T(8,128)(2,1)}, u32[]{:S(2)}, u32[]{:S(2)}) %collective-permute-start.2) | collective-permute-done | bytes 2359328 | tf_op jit(solution)/shard_map/ppermute | solution.py:626
  92.2 3.3 %fold_a.1 = (bf16[4,4,2,24,384]{4,3,2,1,0:T(8,128)(2,1)}, bf16[4,4,2,24,384]{4,3,2,1,0:T(8,128)(2,1)}) custom-call(s32[3]{0:T(128)} %pad_add_fusion.where_ref, bf16[2,4,4,2,2,24,384]{6,5,4,3,2,1,0:T(8,128)(2,1)} %bitcast.28, bf16[2,4,4,2,2,24,384]{6,5,4,3,2,1,0:T(8,128)(2,1)} %bitcast.12.refs_1_), custom_call_target="tpu_custom_call" | custom-call | tf_op jit(solution)/shard_map/fold_a/pallas_call | solution.py:802
  96.1 2.8 %collective-permute-start.5 = (bf16[4,4,2,24,384]{4,3,2,1,0:T(8,128)(2,1)}, bf16[4,4,2,24,384]{4,3,2,1,0:T(8,128)(2,1)}, u32[]{:S(2)}, u32[]{:S(2)}) collective-permute-start(bf16[4,4,2,24,384]{4,3,2,1,0:T(8,128)(2,1)} %get-tuple-element.153), channel_id=1, source_target_pairs={{0,2},{2,0},{4,6},{6,4},{8,10},{10,8},{12,14},{14,12},{16,18},{18,... | collective-permute-start | bytes 1769480 | tf_op jit(solution)/shard_map/ppermute | solution.py:931
  100.4 10.8 %attention_grad.2 = (bf16[3,2,512,768]{3,2,1,0:T(8,128)(2,1)}, f32[1,768]{1,0:T(1,128)}, f32[1,768]{1,0:T(1,128)}) custom-call(bf16[2,512,2304]{2,1,0:T(8,128)(2,1)} %get-tuple-element.129.q_ref.k_ref.v_ref, bf16[2,512,2304]{2,1,0:T(8,128)(2,1)} %get-tuple-element.129.q_ref.k_ref.v_ref, bf16[2,512,2304]{2,1,0:T(8,128)(2,1)} %get-tuple-element.129.q_ref.k_ref.v_ref, ...), custom_call_target="tpu_custom_call" | custom-call | flops 1610612736 | bytes 15728640 | tf_op jit(solution)/shard_map/attention_grad/pallas_call | solution.py:531
  111.2 3.5 %fold_b.1 = (bf16[5,4,2,24,384]{4,3,2,1,0:T(8,128)(2,1)}, bf16[5,4,2,24,384]{4,3,2,1,0:T(8,128)(2,1)}) custom-call(s32[3]{0:T(128)} %pad_add_fusion.where_ref, bf16[2,5,4,2,2,24,384]{6,5,4,3,2,1,0:T(8,128)(2,1)} %bitcast.26, bf16[2,5,4,2,2,24,384]{6,5,4,3,2,1,0:T(8,128)(2,1)} %bitcast.14.refs_1_), custom_call_target="tpu_custom_call" | custom-call | tf_op jit(solution)/shard_map/fold_b/pallas_call | solution.py:802
  116.4 4.0 %fold_b2.1 = (bf16[4,4,24,384]{3,2,1,0:T(8,128)(2,1)}, bf16[4,4,24,384]{3,2,1,0:T(8,128)(2,1)}, bf16[4,4,24,384]{3,2,1,0:T(8,128)(2,1)}, bf16[4,4,24,384]{3,2,1,0:T(8,128)(2,1)}) custom-call(s32[3]{0:T(128)} %pad_add_fusion.where_ref, bf16[2,4,4,2,2,24,384]{6,5,4,3,2,1,0:T(8,128)(2,1)} %bitcast.29, bf16[2,4,4,2,2,24,384]{6,5,4,3,2,1,0:T(8,128)(2,1)} %bitcast.12.refs_1_, ...), custom_call_target="tpu_custom_call" | custom-call | tf_op jit(solution)/shard_map/fold_b2/pallas_call | solution.py:802
  123.0 10.8 %attention_grad.3 = (bf16[3,2,512,768]{3,2,1,0:T(8,128)(2,1)}, f32[1,768]{1,0:T(1,128)}, f32[1,768]{1,0:T(1,128)}) custom-call(bf16[2,512,2304]{2,1,0:T(8,128)(2,1)} %get-tuple-element.129.q_ref.k_ref.v_ref, bf16[2,512,2304]{2,1,0:T(8,128)(2,1)} %get-tuple-element.129.q_ref.k_ref.v_ref, ...), custom_call_target="tpu_custom_call", output_to_operand_aliasing={{0}: (6, {})} | custom-call | flops 1610612736 | bytes 15728640 | tf_op jit(solution)/shard_map/attention_grad/pallas_call | solution.py:531
  133.7 8.4 %grad_qkv.1 = (bf16[20,16,8,384]{3,2,1,0:T(8,128)(2,1)}, bf16[20,16,8,384]{3,2,1,0:T(8,128)(2,1)}) custom-call(s32[1]{0:T(128)} %bitcast.3.core_ref, bf16[1024,768]{1,0:T(8,128)(2,1)} %bitcast.46, bf16[3,1024,768]{2,1,0:T(8,128)(2,1)} %bitcast.35, f32[1,768]{1,0:T(1,128)} %get-tuple-element.164.refs_0_, f32[1,768]{1,0:T(1,128)} %get-tuple-element.165.refs_1_, ...), custom_call_target="tpu_custom_call" | custom-call | flops 3623878656 | bytes 8257536 | tf_op jit(solution)/shard_map/grad_qkv/pallas_call | solution.py:747
  142.3 4.5 %fold_c.1 = (bf16[5,4,24,384]{3,2,1,0:T(8,128)(2,1)}, bf16[5,4,24,384]{3,2,1,0:T(8,128)(2,1)}, bf16[5,4,24,384]{3,2,1,0:T(8,128)(2,1)}, bf16[5,4,24,384]{3,2,1,0:T(8,128)(2,1)}) custom-call(s32[3]{0:T(128)} %pad_add_fusion.where_ref, bf16[2,5,4,2,2,24,384]{6,5,4,3,2,1,0:T(8,128)(2,1)} %bitcast.27, bf16[2,5,4,2,2,24,384]{6,5,4,3,2,1,0:T(8,128)(2,1)} %bitcast.14.refs_1_, ...), custom_call_target="tpu_custom_call" | custom-call | tf_op jit(solution)/shard_map/fold_c/pallas_call | solution.py:802
  148.4 3.2 %fold_d.1 = (bf16[10,4,2,8,384]{4,3,2,1,0:T(8,128)(2,1)}, bf16[10,4,2,8,384]{4,3,2,1,0:T(8,128)(2,1)}) custom-call(s32[3]{0:T(128)} %pad_add_fusion.where_ref, bf16[2,10,4,2,2,8,384]{6,5,4,3,2,1,0:T(8,128)(2,1)} %bitcast.30, bf16[2,10,4,2,2,8,384]{6,5,4,3,2,1,0:T(8,128)(2,1)} %bitcast.18.refs_1_), custom_call_target="tpu_custom_call" | custom-call | tf_op jit(solution)/shard_map/fold_d/pallas_call | solution.py:802
  151.6 6.5 %collective-permute-done.12.refs_5_ = bf16[5,4,24,384]{3,2,1,0:T(8,128)(2,1)} collective-permute-done((bf16[5,4,24,384]{3,2,1,0:T(8,128)(2,1)}, bf16[5,4,24,384]{3,2,1,0:T(8,128)(2,1)}, u32[]{:S(2)}, u32[]{:S(2)}) %collective-permute-start.12) | collective-permute-done | bytes 368672 | tf_op jit(solution)/shard_map/ppermute | solution.py:931
  158.9 3.8 %fold_e.1 = bf16[4,2,9,24,384]{4,3,2,1,0:T(8,128)(2,1)} custom-call(s32[3]{0:T(128)} %pad_add_fusion.where_ref, bf16[4,4,24,384]{3,2,1,0:T(8,128)(2,1)} %get-tuple-element.192.refs_0_, bf16[4,4,24,384]{3,2,1,0:T(8,128)(2,1)} %collective-permute-done.7.refs_1_, bf16[4,4,24,384]{3,2,1,0:T(8,128)(2,1)} %get-tuple-element.194.refs_2_, ...), custom_call_target="tpu_custom_call" | custom-call | tf_op jit(solution)/shard_map/fold_e/pallas_call | solution.py:802
  162.7 4.9 %all-to-all-start = ((bf16[4,2,9,24,384]{4,3,2,1,0:T(8,128)(2,1)}), bf16[4,2,9,24,384]{4,3,2,1,0:T(8,128)(2,1)}, u32[]{:S(2)}, u32[]{:S(2)}) async-start(bf16[4,2,9,24,384]{4,3,2,1,0:T(8,128)(2,1)} %fold_e.1), calls=%async_computation | async-start | bytes 2654208 | tf_op jit(solution)/shard_map/all_to_all | solution.py:976
  169.1 8.0 %input_grad.1 = (bf16[4,256,768]{2,1,0:T(8,128)(2,1)}, bf16[2,256,768]{2,1,0:T(8,128)(2,1)}) custom-call(s32[1]{0:T(128)} %bitcast.3.core_ref, bf16[3,1024,768]{2,1,0:T(8,128)(2,1)} %bitcast.36, bf16[1024,768]{1,0:T(8,128)(2,1)} %get-tuple-element.206.d_hbm, bf16[768,2304]{1,0:T(8,128)(2,1)} %w_ref.1), custom_call_target="tpu_custom_call" | custom-call | flops 3623878656 | bytes 10485760 | tf_op jit(solution)/shard_map/input_grad/pallas_call | solution.py:584
  177.1 3.0 %collective-permute-done.15.refs_2_ = bf16[10,4,2,8,384]{4,3,2,1,0:T(8,128)(2,1)} collective-permute-done((bf16[10,4,2,8,384]{4,3,2,1,0:T(8,128)(2,1)}, bf16[10,4,2,8,384]{4,3,2,1,0:T(8,128)(2,1)}, u32[]{:S(2)}, u32[]{:S(2)}) %collective-permute-start.15) | collective-permute-done | bytes 491552 | tf_op jit(solution)/shard_map/ppermute | solution.py:931
  180.4 3.8 %fold_f.1 = (bf16[10,4,8,384]{3,2,1,0:T(8,128)(2,1)}, bf16[10,4,8,384]{3,2,1,0:T(8,128)(2,1)}, bf16[10,4,8,384]{3,2,1,0:T(8,128)(2,1)}, bf16[10,4,8,384]{3,2,1,0:T(8,128)(2,1)}) custom-call(s32[3]{0:T(128)} %pad_add_fusion.where_ref, bf16[2,10,4,2,2,8,384]{6,5,4,3,2,1,0:T(8,128)(2,1)} %bitcast.31, bf16[2,10,4,2,2,8,384]{6,5,4,3,2,1,0:T(8,128)(2,1)} %bitcast.18.refs_1_, ...), custom_call_target="tpu_custom_call" | custom-call | tf_op jit(solution)/shard_map/fold_f/pallas_call | solution.py:802
  189.5 3.4 %collective-permute-done.17.refs_1_ = bf16[10,4,8,384]{3,2,1,0:T(8,128)(2,1)} collective-permute-done((bf16[10,4,8,384]{3,2,1,0:T(8,128)(2,1)}, bf16[10,4,8,384]{3,2,1,0:T(8,128)(2,1)}, u32[]{:S(2)}, u32[]{:S(2)}) %collective-permute-start.17) | collective-permute-done | bytes 245792 | tf_op jit(solution)/shard_map/ppermute | solution.py:931
  193.7 2.7 %fold_g.1 = (bf16[2,10,8,384]{3,2,1,0:T(8,128)(2,1)}, bf16[2,10,8,384]{3,2,1,0:T(8,128)(2,1)}, bf16[2,10,8,384]{3,2,1,0:T(8,128)(2,1)}, bf16[2,10,8,384]{3,2,1,0:T(8,128)(2,1)}) custom-call(s32[3]{0:T(128)} %pad_add_fusion.where_ref, bf16[10,4,8,384]{3,2,1,0:T(8,128)(2,1)} %get-tuple-element.229.refs_0_, ...), custom_call_target="tpu_custom_call" | custom-call | tf_op jit(solution)/shard_map/fold_g/pallas_call | solution.py:802
  198.2 2.4 %collective-permute-start.21 = (bf16[2,10,8,384]{3,2,1,0:T(8,128)(2,1)}, bf16[2,10,8,384]{3,2,1,0:T(8,128)(2,1)}, u32[]{:S(2)}, u32[]{:S(2)}) collective-permute-start(bf16[2,10,8,384]{3,2,1,0:T(8,128)(2,1)} %get-tuple-element.235), channel_id=1, source_target_pairs={{0,16},{2,18},{4,20},{6,22},{8,24},{10,26},{12,28},{14,30},{16,0},... | collective-permute-start | bytes 368648 | tf_op jit(solution)/shard_map/ppermute | solution.py:931
  202.9 2.1 back_sum.1
  205.0 2.1 inner_sum.1
  207.2 3.2 %collective-permute-done.21.refs_2_ = bf16[2,10,8,384]{3,2,1,0:T(8,128)(2,1)} collective-permute-done((bf16[2,10,8,384]{3,2,1,0:T(8,128)(2,1)}, bf16[2,10,8,384]{3,2,1,0:T(8,128)(2,1)}, u32[]{:S(2)}, u32[]{:S(2)}) %collective-permute-start.21) | collective-permute-done | bytes 122912 | tf_op jit(solution)/shard_map/ppermute | solution.py:931
  (54 shorter events, 28.3 us)
Async XLA Ops:
  2.0 2.4 %collective-permute-start = (bf16[2,256,768]{2,1,0:T(8,128)(2,1)S(1)}, bf16[2,256,768]{2,1,0:T(8,128)(2,1)S(1)}, u32[]{:S(2)}, u32[]{:S(2)}) collective-permute-start(bf16[2,256,768]{2,1,0:T(8,128)(2,1)S(1)} %constant_dynamic-slice_fusion.1), channel_id=1, source_target_pairs={{0,1},{1,0},{2,3},{3,2},{4,5},{5,4},{6,7},{7,6},{8,9},{9,8},{10,11... | collective-permute-start | bytes 2359304 | tf_op jit(solution)/shard_map/ppermute | solution.py:626
  2.5 30.4 %collective-permute-start.1 = (bf16[2,256,768]{2,1,0:T(8,128)(2,1)S(1)}, bf16[2,256,768]{2,1,0:T(8,128)(2,1)}, u32[]{:S(2)}, u32[]{:S(2)}) collective-permute-start(bf16[2,256,768]{2,1,0:T(8,128)(2,1)S(1)} %constant_dynamic-slice_fusion), channel_id=1, source_target_pairs={{0,1},{1,0},{2,3},{3,2},{4,5},{5,4},{6,7},{7,6},{8,9},{9,8},{10,11... | collective-permute-start | bytes 2359304 | tf_op jit(solution)/shard_map/ppermute | solution.py:626
  87.3 4.9 %collective-permute-start.2 = (bf16[8,16,24,384]{3,2,1,0:T(8,128)(2,1)}, bf16[8,16,24,384]{3,2,1,0:T(8,128)(2,1)}, u32[]{:S(2)}, u32[]{:S(2)}) collective-permute-start(bf16[8,16,24,384]{3,2,1,0:T(8,128)(2,1)} %get-tuple-element.138), channel_id=1, source_target_pairs={{0,1},{1,0},{2,3},{3,2},{4,5},{5,4},{6,7},{7,6},{8,9},{9,8},{10,11... | collective-permute-start | bytes 7077896 | tf_op jit(solution)/shard_map/ppermute | solution.py:626
  95.5 15.7 %collective-permute-start.3 = (bf16[10,16,24,384]{3,2,1,0:T(8,128)(2,1)}, bf16[10,16,24,384]{3,2,1,0:T(8,128)(2,1)}, u32[]{:S(2)}, u32[]{:S(2)}) collective-permute-start(bf16[10,16,24,384]{3,2,1,0:T(8,128)(2,1)} %get-tuple-element.145), channel_id=1, source_target_pairs={{0,1},{1,0},{2,3},{3,2},{4,5},{5,4},{6,7},{7,6},{8,9},{9,8},{10,11... | collective-permute-start | bytes 8847368 | tf_op jit(solution)/shard_map/ppermute | solution.py:626
  95.9 15.3 %collective-permute-start.4 = (bf16[2,256,768]{2,1,0:T(8,128)(2,1)}, bf16[2,256,768]{2,1,0:T(8,128)(2,1)}, u32[]{:S(2)}, u32[]{:S(2)}) collective-permute-start(bf16[2,256,768]{2,1,0:T(8,128)(2,1)} %get-tuple-element.147), channel_id=1, source_target_pairs={{0,1},{1,0},{2,3},{3,2},{4,5},{5,4},{6,7},{7,6},{8,9},{9,8},{10,11... | collective-permute-start | bytes 2359304 | tf_op jit(solution)/shard_map/ppermute | solution.py:626
  96.1 18.6 %collective-permute-start.5 = (bf16[4,4,2,24,384]{4,3,2,1,0:T(8,128)(2,1)}, bf16[4,4,2,24,384]{4,3,2,1,0:T(8,128)(2,1)}, u32[]{:S(2)}, u32[]{:S(2)}) collective-permute-start(bf16[4,4,2,24,384]{4,3,2,1,0:T(8,128)(2,1)} %get-tuple-element.153), channel_id=1, source_target_pairs={{0,2},{2,0},{4,6},{6,4},{8,10},{10,8},{12,14},{14,12},{16,18},{18,... | collective-permute-start | bytes 1769480 | tf_op jit(solution)/shard_map/ppermute | solution.py:931
  98.9 15.8 %collective-permute-start.6 = (bf16[4,4,2,24,384]{4,3,2,1,0:T(8,128)(2,1)}, bf16[4,4,2,24,384]{4,3,2,1,0:T(8,128)(2,1)}, u32[]{:S(2)}, u32[]{:S(2)}) collective-permute-start(bf16[4,4,2,24,384]{4,3,2,1,0:T(8,128)(2,1)} %get-tuple-element.154), channel_id=1, source_target_pairs={{0,4},{2,6},{4,0},{6,2},{8,12},{10,14},{12,8},{14,10},{16,20},{18,... | collective-permute-start | bytes 1769480 | tf_op jit(solution)/shard_map/ppermute | solution.py:931
  114.7 27.4 %collective-permute-start.9 = (bf16[5,4,2,24,384]{4,3,2,1,0:T(8,128)(2,1)}, bf16[5,4,2,24,384]{4,3,2,1,0:T(8,128)(2,1)}, u32[]{:S(2)}, u32[]{:S(2)}) collective-permute-start(bf16[5,4,2,24,384]{4,3,2,1,0:T(8,128)(2,1)} %get-tuple-element.179), channel_id=1, source_target_pairs={{0,2},{2,0},{4,6},{6,4},{8,10},{10,8},{12,14},{14,12},{16,18},{18,... | collective-permute-start | bytes 2211848 | tf_op jit(solution)/shard_map/ppermute | solution.py:931
  115.3 26.8 %collective-permute-start.10 = (bf16[5,4,2,24,384]{4,3,2,1,0:T(8,128)(2,1)}, bf16[5,4,2,24,384]{4,3,2,1,0:T(8,128)(2,1)}, u32[]{:S(2)}, u32[]{:S(2)}) collective-permute-start(bf16[5,4,2,24,384]{4,3,2,1,0:T(8,128)(2,1)} %get-tuple-element.180), channel_id=1, source_target_pairs={{0,4},{2,6},{4,0},{6,2},{8,12},{10,14},{12,8},{14,10},{16,20},{18,... | collective-permute-start | bytes 2211848 | tf_op jit(solution)/shard_map/ppermute | solution.py:931
  120.4 21.7 %collective-permute-start.7 = (bf16[4,4,24,384]{3,2,1,0:T(8,128)(2,1)}, bf16[4,4,24,384]{3,2,1,0:T(8,128)(2,1)}, u32[]{:S(2)}, u32[]{:S(2)}) collective-permute-start(bf16[4,4,24,384]{3,2,1,0:T(8,128)(2,1)} %get-tuple-element.177), channel_id=1, source_target_pairs={{0,4},{2,6},{4,0},{6,2},{8,12},{10,14},{12,8},{14,10},{16,20},{18,... | collective-permute-start | bytes 884744 | tf_op jit(solution)/shard_map/ppermute | solution.py:931
  121.5 20.6 %collective-permute-start.8 = (bf16[4,4,24,384]{3,2,1,0:T(8,128)(2,1)}, bf16[4,4,24,384]{3,2,1,0:T(8,128)(2,1)}, u32[]{:S(2)}, u32[]{:S(2)}) collective-permute-start(bf16[4,4,24,384]{3,2,1,0:T(8,128)(2,1)} %get-tuple-element.178), channel_id=1, source_target_pairs={{0,2},{2,0},{4,6},{6,4},{8,10},{10,8},{12,14},{14,12},{16,18},{18,... | collective-permute-start | bytes 884744 | tf_op jit(solution)/shard_map/ppermute | solution.py:931
  142.2 4.6 %collective-permute-start.11 = (bf16[20,16,8,384]{3,2,1,0:T(8,128)(2,1)}, bf16[20,16,8,384]{3,2,1,0:T(8,128)(2,1)}, u32[]{:S(2)}, u32[]{:S(2)}) collective-permute-start(bf16[20,16,8,384]{3,2,1,0:T(8,128)(2,1)} %get-tuple-element.187), channel_id=1, source_target_pairs={{0,1},{1,0},{2,3},{3,2},{4,5},{5,4},{6,7},{7,6},{8,9},{9,8},{10,11... | collective-permute-start | bytes 5898248 | tf_op jit(solution)/shard_map/ppermute | solution.py:626
  146.8 11.4 %collective-permute-start.12 = (bf16[5,4,24,384]{3,2,1,0:T(8,128)(2,1)}, bf16[5,4,24,384]{3,2,1,0:T(8,128)(2,1)}, u32[]{:S(2)}, u32[]{:S(2)}) collective-permute-start(bf16[5,4,24,384]{3,2,1,0:T(8,128)(2,1)} %get-tuple-element.199), channel_id=1, source_target_pairs={{0,4},{2,6},{4,0},{6,2},{8,12},{10,14},{12,8},{14,10},{16,20},{18,... | collective-permute-start | bytes 1105928 | tf_op jit(solution)/shard_map/ppermute | solution.py:931
  147.9 11.0 %collective-permute-start.13 = (bf16[5,4,24,384]{3,2,1,0:T(8,128)(2,1)}, bf16[5,4,24,384]{3,2,1,0:T(8,128)(2,1)}, u32[]{:S(2)}, u32[]{:S(2)}) collective-permute-start(bf16[5,4,24,384]{3,2,1,0:T(8,128)(2,1)} %get-tuple-element.200), channel_id=1, source_target_pairs={{0,2},{2,0},{4,6},{6,4},{8,10},{10,8},{12,14},{14,12},{16,18},{18,... | collective-permute-start | bytes 1105928 | tf_op jit(solution)/shard_map/ppermute | solution.py:931
  148.4 3.2 %collective-permute-start.14 = (bf16[2,6,768]{2,1,0:T(8,128)(2,1)S(1)}, bf16[2,6,768]{2,1,0:T(8,128)(2,1)S(1)}, u32[]{:S(2)}, u32[]{:S(2)}) collective-permute-start(bf16[2,6,768]{2,1,0:T(8,128)(2,1)S(1)} %bitcast.38), channel_id=1, source_target_pairs={{0,1},{1,0},{2,3},{3,2},{4,5},{5,4},{6,7},{7,6},{8,9},{9,8},{10,11... | collective-permute-start | bytes 55304 | tf_op jit(solution)/shard_map/ppermute | solution.py:626
  162.7 40.3 %all-to-all-start = ((bf16[4,2,9,24,384]{4,3,2,1,0:T(8,128)(2,1)}), bf16[4,2,9,24,384]{4,3,2,1,0:T(8,128)(2,1)}, u32[]{:S(2)}, u32[]{:S(2)}) async-start(bf16[4,2,9,24,384]{4,3,2,1,0:T(8,128)(2,1)} %fold_e.1), calls=%async_computation | async-start | bytes 2654208 | tf_op jit(solution)/shard_map/all_to_all | solution.py:976
  167.5 12.6 %collective-permute-start.15 = (bf16[10,4,2,8,384]{4,3,2,1,0:T(8,128)(2,1)}, bf16[10,4,2,8,384]{4,3,2,1,0:T(8,128)(2,1)}, u32[]{:S(2)}, u32[]{:S(2)}) collective-permute-start(bf16[10,4,2,8,384]{4,3,2,1,0:T(8,128)(2,1)} %get-tuple-element.209), channel_id=1, source_target_pairs={{0,2},{2,0},{4,6},{6,4},{8,10},{10,8},{12,14},{14,12},{16,18},{18,... | collective-permute-start | bytes 1474568 | tf_op jit(solution)/shard_map/ppermute | solution.py:931
  168.1 12.3 %collective-permute-start.16 = (bf16[10,4,2,8,384]{4,3,2,1,0:T(8,128)(2,1)}, bf16[10,4,2,8,384]{4,3,2,1,0:T(8,128)(2,1)}, u32[]{:S(2)}, u32[]{:S(2)}) collective-permute-start(bf16[10,4,2,8,384]{4,3,2,1,0:T(8,128)(2,1)} %get-tuple-element.210), channel_id=1, source_target_pairs={{0,4},{2,6},{4,0},{6,2},{8,12},{10,14},{12,8},{14,10},{16,20},{18,... | collective-permute-start | bytes 1474568 | tf_op jit(solution)/shard_map/ppermute | solution.py:931
  184.2 9.5 %collective-permute-start.19 = (bf16[2,256,768]{2,1,0:T(8,128)(2,1)}, bf16[2,256,768]{2,1,0:T(8,128)(2,1)}, u32[]{:S(2)}, u32[]{:S(2)}) collective-permute-start(bf16[2,256,768]{2,1,0:T(8,128)(2,1)} %get-tuple-element.224), channel_id=1, source_target_pairs={{0,1},{1,0},{2,3},{3,2},{4,5},{5,4},{6,7},{7,6},{8,9},{9,8},{10,11... | collective-permute-start | bytes 2359304 | tf_op jit(solution)/shard_map/ppermute | solution.py:626
  184.3 8.7 %collective-permute-start.17 = (bf16[10,4,8,384]{3,2,1,0:T(8,128)(2,1)}, bf16[10,4,8,384]{3,2,1,0:T(8,128)(2,1)}, u32[]{:S(2)}, u32[]{:S(2)}) collective-permute-start(bf16[10,4,8,384]{3,2,1,0:T(8,128)(2,1)} %get-tuple-element.222), channel_id=1, source_target_pairs={{0,4},{2,6},{4,0},{6,2},{8,12},{10,14},{12,8},{14,10},{16,20},{18,... | collective-permute-start | bytes 737288 | tf_op jit(solution)/shard_map/ppermute | solution.py:931
  185.3 8.3 %collective-permute-start.18 = (bf16[10,4,8,384]{3,2,1,0:T(8,128)(2,1)}, bf16[10,4,8,384]{3,2,1,0:T(8,128)(2,1)}, u32[]{:S(2)}, u32[]{:S(2)}) collective-permute-start(bf16[10,4,8,384]{3,2,1,0:T(8,128)(2,1)} %get-tuple-element.223), channel_id=1, source_target_pairs={{0,2},{2,0},{4,6},{6,4},{8,10},{10,8},{12,14},{14,12},{16,18},{18,... | collective-permute-start | bytes 737288 | tf_op jit(solution)/shard_map/ppermute | solution.py:931
  196.4 10.7 %collective-permute-start.20 = (bf16[2,10,8,384]{3,2,1,0:T(8,128)(2,1)}, bf16[2,10,8,384]{3,2,1,0:T(8,128)(2,1)}, u32[]{:S(2)}, u32[]{:S(2)}) collective-permute-start(bf16[2,10,8,384]{3,2,1,0:T(8,128)(2,1)} %get-tuple-element.234), channel_id=1, source_target_pairs={{0,8},{2,10},{4,12},{6,14},{8,0},{10,2},{12,4},{14,6},{16,24},{18,... | collective-permute-start | bytes 368648 | tf_op jit(solution)/shard_map/ppermute | solution.py:931
  198.2 12.1 %collective-permute-start.21 = (bf16[2,10,8,384]{3,2,1,0:T(8,128)(2,1)}, bf16[2,10,8,384]{3,2,1,0:T(8,128)(2,1)}, u32[]{:S(2)}, u32[]{:S(2)}) collective-permute-start(bf16[2,10,8,384]{3,2,1,0:T(8,128)(2,1)} %get-tuple-element.235), channel_id=1, source_target_pairs={{0,16},{2,18},{4,20},{6,22},{8,24},{10,26},{12,28},{14,30},{16,0},... | collective-permute-start | bytes 368648 | tf_op jit(solution)/shard_map/ppermute | solution.py:931
  200.6 9.7 %collective-permute-start.22 = (bf16[2,10,8,384]{3,2,1,0:T(8,128)(2,1)}, bf16[2,10,8,384]{3,2,1,0:T(8,128)(2,1)}, u32[]{:S(2)}, u32[]{:S(2)}) collective-permute-start(bf16[2,10,8,384]{3,2,1,0:T(8,128)(2,1)} %get-tuple-element.236), channel_id=1, source_target_pairs={{0,24},{2,26},{4,28},{6,30},{8,16},{10,18},{12,20},{14,22},{16,8},... | collective-permute-start | bytes 368648 | tf_op jit(solution)/shard_map/ppermute | solution.py:931
  (3 other events, 9.0 us)
